TPU v7x, 32 devices: a whole 2x2x4 slice. The times are simulated.
32 devices in a mesh: gx: 2 (over core), gy: 4 (over y, x), gz: 4 (over z).
Axes of the slice: x: 2, y: 2, z: 4, core: 2. Of those that a mesh axis runs over, the one named last changes fastest.
Arguments:
- orbitals: bfloat16 [2, 128, 64000], P(None, ('gx', 'gy', 'gz')), may hold values from -6 to 6
- dest: int32 [128], replicated, may hold values from 0 to 31, as said below
- partners: int32 [128, 2], replicated, may hold values from 0 to 127, as said below
- anchors: int32 [128, 3], replicated, may hold values from 0 to 767, as said below
Outputs:
- exchange: float32 [2, 224, 64000], P(None, ('gx', 'gy', 'gz'))
Inputs may be any that keep to these rules, and one draw needn't show every extreme that they name: `dest`: box i goes to its first device or to the device just before or just after it in the numbering; a device passes at most 2 boxes to the device before and at most 1 to the device after, and holds at most 7 boxes after the move; every device holds one or more; each of these three bounds is reached in every draw. A box's partners (the box itself or the same box twice may occur) sit at first on the same device as the box or on one next to it in the numbering, and after the move likewise. Before the move and after it, exactly 1 of the boxes of a device are partners of boxes on the device after it, and exactly 1 are partners of boxes on the device before it (where that device exists). `anchors`: columns are the three grid dimensions, each within its own grid extent; along each, a partner's anchor differs from its box's by at most 20 cells, the difference taken modulo the grid.
All inputs are finite; a program needn't handle non-finite values.
Results may differ from a plain program's by a relative error of at most 0.0072.
Values may be sent and summed in bfloat16 or wider, within the bound.
No kernel may reach another device: no remote copies, remote signals or barrier semaphores. Data moves between devices by JAX's collectives and lax.ppermute only.
A program may use at most 64 MiB of HBM per device.

v0:
```python
import jax
import jax.numpy as jnp
from jax import lax
from jax.sharding import PartitionSpec as P

EDGE = 40
PARTNERS = 2
GRID_X = 768
GRID_Y = 384
GRID_Z = 384
BOX_DEV = 4
BACK = 2
AHEAD = 1
CAP = 7


SCREEN = 0.001
FINEST = lax.Precision.HIGHEST


def from_behind(value, axis, steps):
    count = lax.axis_size(axis)
    initial, last = (max(0, -steps), min(count, count - steps))
    return lax.ppermute(value, axis, [(source, source + steps) for source in range(initial, last)])


def sine_basis(edge_cells):
    counter = jnp.arange(edge_cells, dtype=jnp.float32) + 1.0
    angles = jnp.pi * counter[:, None] * counter[None, :] / (edge_cells + 1.0)
    sine_table = (jnp.sqrt(2.0 / (edge_cells + 1.0)) * jnp.sin(angles)).astype(jnp.bfloat16)
    levels = 2.0 - 2.0 * jnp.cos(jnp.pi * counter / (edge_cells + 1.0))
    spectrum = levels[:, None, None] + levels[None, :, None] + levels[None, None, :] + SCREEN
    return (sine_table, spectrum)


def sine_pass(volume, sine_table):
    volume = jnp.einsum(
        "ak,psabc->pskbc", sine_table, volume, preferred_element_type=jnp.float32
    ).astype(jnp.bfloat16)
    volume = jnp.einsum(
        "bk,psabc->psakc", sine_table, volume, preferred_element_type=jnp.float32
    ).astype(jnp.bfloat16)
    return jnp.einsum("ck,psabc->psabk", sine_table, volume, preferred_element_type=jnp.float32)


def pair_sum(center, partner_boxes, deltas, sine_table, spectrum):
    spin_count = center.shape[0]
    edge_cells = sine_table.shape[0]
    cube_shape = (spin_count, edge_cells, edge_cells, edge_cells)
    center_cube = center.astype(jnp.float32).reshape(cube_shape)
    moving = partner_boxes.reshape((partner_boxes.shape[0],) + cube_shape)
    cell_line = jnp.arange(edge_cells, dtype=jnp.int32)
    shifters = [
        (
            cell_line[None, None, :]
            == cell_line[None, :, None] - deltas[:, dimension][:, None, None]
        ).astype(jnp.bfloat16)
        for dimension in range(3)
    ]
    moving = jnp.einsum(
        "pxa,psabc->psxbc", shifters[0], moving, preferred_element_type=jnp.float32
    ).astype(jnp.bfloat16)
    moving = jnp.einsum(
        "pyb,psxbc->psxyc", shifters[1], moving, preferred_element_type=jnp.float32
    ).astype(jnp.bfloat16)
    shifted = jnp.einsum(
        "pzc,psxyc->psxyz", shifters[2], moving, preferred_element_type=jnp.float32
    )
    density = (center_cube[None] * shifted).astype(jnp.bfloat16)
    spectral = (sine_pass(density, sine_table) / spectrum).astype(jnp.bfloat16)
    potential = sine_pass(spectral, sine_table)
    return jnp.sum(potential * shifted, axis=0).reshape(spin_count, -1)


def wrapped(difference):
    extent = jnp.array([GRID_X, GRID_Y, GRID_Z], jnp.int32)
    return (difference + extent // 2) % extent - extent // 2


def routing(dest, device):
    filler = jnp.full((2 * BOX_DEV,), -1, jnp.int32)
    padded = jnp.concatenate([filler, dest, filler])
    nearby = lax.dynamic_slice_in_dim(padded, device * BOX_DEV, 5 * BOX_DEV)
    window_pos = jnp.arange(5 * BOX_DEV, dtype=jnp.int32)
    blocks = window_pos // BOX_DEV
    earlier = (nearby[:, None] == nearby[None, :]) & (window_pos[None, :] < window_pos[:, None])
    rankings = jnp.sum(earlier.astype(jnp.int32), axis=1)
    inside = jnp.sum((earlier & (blocks[:, None] == blocks[None, :])).astype(jnp.int32), axis=1)
    return (nearby, rankings, inside)


def select_rows(wanted, inside, row_count):
    counter = jnp.arange(row_count, dtype=jnp.int32)
    return (wanted[None, :] & (inside[None, :] == counter[:, None])).astype(jnp.float32)


def arrival(match_part, inside_part, row_count):
    counter = jnp.arange(row_count, dtype=jnp.int32)
    picker = (inside_part[:, None] == counter[None, :]).astype(jnp.float32)
    return jnp.dot(match_part, picker, precision=FINEST)


def combine(placers, portions):
    summed = 0
    for placer, portion in zip(placers, portions):
        summed = summed + jnp.einsum(
            "ka,sac->skc", placer, portion, preferred_element_type=jnp.float32, precision=FINEST
        )
    return summed


def fetch_box(prev_boxes, self_boxes, next_boxes, side_code, row_index):
    from_prev = lax.dynamic_index_in_dim(prev_boxes, row_index, 1, keepdims=False)
    from_self = lax.dynamic_index_in_dim(self_boxes, row_index, 1, keepdims=False)
    from_next = lax.dynamic_index_in_dim(next_boxes, row_index, 1, keepdims=False)
    return jnp.where(side_code < 0, from_prev, jnp.where(side_code == 0, from_self, from_next))


def neighbour_rows(source, full_rows):
    prev_rows = from_behind(source, ("gx", "gy", "gz"), 1)
    next_rows = from_behind(source, ("gx", "gy", "gz"), -1)
    return (prev_rows, next_rows, full_rows, full_rows)


def shards(orbitals, dest, partners, anchors):
    device = lax.axis_index(("gx", "gy", "gz"))
    sine_table, spectrum = sine_basis(EDGE)
    nearby, rankings, inside = routing(dest, device)
    own_dest = nearby[2 * BOX_DEV : 3 * BOX_DEV]
    own_inside = inside[2 * BOX_DEV : 3 * BOX_DEV]
    pick_ahead = select_rows(own_dest == device + 1, own_inside, AHEAD)
    pick_back = select_rows(own_dest == device - 1, own_inside, BACK)
    slot_line = jnp.arange(CAP, dtype=jnp.int32)
    matches = (nearby[None, :] == device) & (rankings[None, :] == slot_line[:, None])
    match_values = matches.astype(jnp.float32)
    placers = (
        arrival(match_values[:, BOX_DEV : 2 * BOX_DEV], inside[BOX_DEV : 2 * BOX_DEV], AHEAD),
        match_values[:, 2 * BOX_DEV : 3 * BOX_DEV],
        arrival(
            match_values[:, 3 * BOX_DEV : 4 * BOX_DEV], inside[3 * BOX_DEV : 4 * BOX_DEV], BACK
        ),
    )
    own_ids = device * BOX_DEV + jnp.arange(BOX_DEV, dtype=jnp.int32)
    partner_ids = lax.dynamic_slice_in_dim(partners, device * BOX_DEV, BOX_DEV, axis=0)
    relative = jnp.clip(partner_ids - (device - 1) * BOX_DEV, 0, 3 * BOX_DEV - 1)
    side_codes = relative // BOX_DEV - 1
    partner_rows = relative % BOX_DEV
    deltas = wrapped(
        jnp.take(anchors, partner_ids, axis=0) - jnp.take(anchors, own_ids, axis=0)[:, None, :]
    )
    prev_boxes, next_boxes, prev_index, next_index = neighbour_rows(orbitals, partner_rows)
    row_pick = jnp.where(
        side_codes < 0, prev_index, jnp.where(side_codes == 0, partner_rows, next_index)
    )

    def one_box(box_items):
        row_index, side_row, row_slots, delta_row = box_items
        center = lax.dynamic_index_in_dim(orbitals, row_index, 1, keepdims=False)
        partner_boxes = jnp.stack(
            [
                fetch_box(prev_boxes, orbitals, next_boxes, side_row[number], row_slots[number])
                for number in range(PARTNERS)
            ]
        )
        return pair_sum(center, partner_boxes, delta_row, sine_table, spectrum)

    box_terms = lax.map(
        one_box, (jnp.arange(BOX_DEV, dtype=jnp.int32), side_codes, row_pick, deltas)
    )
    own_terms = jnp.moveaxis(box_terms, 0, 1)
    ahead_terms = jnp.einsum("ar,src->sac", pick_ahead, own_terms, precision=FINEST)
    back_terms = jnp.einsum("ar,src->sac", pick_back, own_terms, precision=FINEST)
    arrived_prev = from_behind(ahead_terms, ("gx", "gy", "gz"), 1)
    arrived_next = from_behind(back_terms, ("gx", "gy", "gz"), -1)
    exchange = combine(placers, (arrived_prev, own_terms, arrived_next))
    return exchange


def solution(mesh):
    return jax.shard_map(
        shards,
        mesh=mesh,
        in_specs=(P(None, ("gx", "gy", "gz"), None), P(), P(), P()),
        out_specs=P(None, ("gx", "gy", "gz"), None),
        check_vma=False,
    )
```

profile of v0, /device:TPU:4, one launch (start us, length us, event | category | flops | bytes accessed | tf_op | source)
XLA Modules:
  0.0 346.7 jit_solution(8992167310822296772)
XLA Ops:
  0.0 2.1 copy.58
  2.1 3.5 %collective-permute-start = (bf16[2,4,64000]{2,0,1:T(2,128)(2,1)S(1)}, bf16[2,4,64000]{2,0,1:T(2,128)(2,1)S(1)}, u32[]{:S(2)}, u32[]{:S(2)}) collective-permute-start(bf16[2,4,64000]{2,0,1:T(2,128)(2,1)S(1)} %copy.58), channel_id=1, source_target_pairs={{0,1},{1,2},{2,3},{3,4},{4,5},{5,6},{6,7},{7,8},{8,9},{9,10},{10,1... | collective-permute-start | bytes 3072008 | tf_op jit(solution)/shard_map/ppermute | solution.py:24
  5.6 6.0 %collective-permute-start.1 = (bf16[2,4,64000]{2,0,1:T(2,128)(2,1)S(1)}, bf16[2,4,64000]{2,0,1:T(2,128)(2,1)}, u32[]{:S(2)}, u32[]{:S(2)}) collective-permute-start(bf16[2,4,64000]{2,0,1:T(2,128)(2,1)S(1)} %copy.58), channel_id=1, source_target_pairs={{1,0},{2,1},{3,2},{4,3},{5,4},{6,5},{7,6},{8,7},{9,8},{10,9},{11,1... | collective-permute-start | bytes 3072008 | tf_op jit(solution)/shard_map/ppermute | solution.py:24
  14.4 18.8 %collective-permute-done = bf16[2,4,64000]{2,0,1:T(2,128)(2,1)S(1)} collective-permute-done((bf16[2,4,64000]{2,0,1:T(2,128)(2,1)S(1)}, bf16[2,4,64000]{2,0,1:T(2,128)(2,1)S(1)}, u32[]{:S(2)}, u32[]{:S(2)}) %collective-permute-start) | collective-permute-done | bytes 1024032 | tf_op jit(solution)/shard_map/ppermute | solution.py:24
  33.1 20.0 %collective-permute-done.1 = bf16[2,4,64000]{2,0,1:T(2,128)(2,1)} collective-permute-done((bf16[2,4,64000]{2,0,1:T(2,128)(2,1)S(1)}, bf16[2,4,64000]{2,0,1:T(2,128)(2,1)}, u32[]{:S(2)}, u32[]{:S(2)}) %collective-permute-start.1) | collective-permute-done | bytes 1024032 | tf_op jit(solution)/shard_map/ppermute | solution.py:24
  53.1 243.4 %while.12 = (s32[]{:T(128)}, f32[4,2,64000]{2,1,0:T(2,128)}, s32[4]{0:T(128)S(1)}, bf16[2,4,64000]{2,0,1:T(2,128)(2,1)S(1)}, s32[4,2]{0,1:T(2,128)S(1)}, /*index...) while((s32[]{:T(128)}, f32[4,2,64000]{2,1,0:T(2,128)}, ...), condition=%wide.region_2.3_spmd.clone.clone, body=%wide.region_0.2_spmd.clone.clone.sunk | while | flops 188336256 | bytes 38666924 | solution.py:167
  63.1 2.8 broadcast_select_fusion.6
  65.8 1.2 select_n.250
  67.7 1.2 select_n.251
  70.6 3.7 %copy.97 = bf16[2,2,40,40,40]{3,4,2,1,0:T(8,128)(2,1)} copy(bf16[2,2,40,40,40]{2,4,3,1,0:T(8,128)(2,1)S(1)} %fusion.154) | data formatting | bytes 1024000 | tf_op jit(solution)/shard_map/while/body/eval_jaxpr/convert_element_type | solution.py:62
  74.3 2.7 reshape.373
  77.1 4.2 %multiply_convert_fusion.3 = (bf16[2,2,40,40,40]{4,3,2,1,0:T(8,128)(2,1)}, f32[2,2,40,40,40]{4,3,2,1,0:T(8,128)S(1)}) fusion(f32[2,40,40,40]{3,2,1,0:T(8,128)} %reshape.373, s32[2,40]{1,0:T(2,128)S(1)} %get-tuple-element.351, bf16[2,2,40,40,40]{3,4,2,1,0:T(8,128)(2,1)} %copy.97, s32[2,40]{1,0:T(2,128)S(1)} %get-tuple-element.355), kind=kOutput, calls=%fused_computation.6.clone.1 | convolution fusion | flops 41734400 | bytes 2560640 | tf_op jit(solution)/shard_map/while/body/eval_jaxpr/pzc,psxyc->psxyz/dot_general | solution.py:66
  81.3 3.9 %fusion.155 = bf16[2,2,40,40,40]{2,4,3,1,0:T(8,128)(2,1)} fusion(bf16[2,2,40,40,40]{4,3,2,1,0:T(8,128)(2,1)} %get-tuple-element.357, f32[40]{0:T(128)S(1)} %get-tuple-element.401, f32[40]{0:T(128)S(1)} %get-tuple-element.402), kind=kOutput, calls=%fused_computation.23.clone.1 | convolution fusion | flops 20742400 | bytes 1024320 | tf_op jit(solution)/shard_map/while/body/eval_jaxpr/ak,psabc->pskbc/dot_general | solution.py:37
  85.2 4.8 %copy.98 = bf16[2,2,40,40,40]{3,4,2,1,0:T(8,128)(2,1)} copy(bf16[2,2,40,40,40]{2,4,3,1,0:T(8,128)(2,1)} %fusion.155) | data formatting | bytes 1024000 | tf_op jit(solution)/shard_map/while/body/eval_jaxpr/convert_element_type | solution.py:39
  91.2 5.2 %divide_convert_fusion.2 = bf16[2,2,40,40,40]{4,3,2,1,0:T(8,128)(2,1)} fusion(f32[40,40,40]{2,1,0:T(8,128)} %add_add_fusion.2, bf16[2,2,40,40,40]{3,4,2,1,0:T(8,128)(2,1)} %copy.98, f32[40]{0:T(128)S(1)} %get-tuple-element.401, f32[40]{0:T(128)S(1)} %get-tuple-element.402), kind=kOutput, calls=%fused_computation.5.clone.1 | convolution fusion | flops 41740800 | bytes 1280320 | tf_op jit(solution)/shard_map/while/body/eval_jaxpr/ck,psabc->psabk/dot_general | solution.py:43
  96.4 3.9 %fusion.156 = bf16[2,2,40,40,40]{2,4,3,1,0:T(8,128)(2,1)} fusion(bf16[2,2,40,40,40]{4,3,2,1,0:T(8,128)(2,1)} %divide_convert_fusion.2, f32[40]{0:T(128)S(1)} %get-tuple-element.401, f32[40]{0:T(128)S(1)} %get-tuple-element.402), kind=kOutput, calls=%fused_computation.24.clone.1 | convolution fusion | flops 20742400 | bytes 1024320 | tf_op jit(solution)/shard_map/while/body/eval_jaxpr/ak,psabc->pskbc/dot_general | solution.py:37
  100.3 4.8 %copy.99 = bf16[2,2,40,40,40]{3,4,2,1,0:T(8,128)(2,1)} copy(bf16[2,2,40,40,40]{2,4,3,1,0:T(8,128)(2,1)} %fusion.156) | data formatting | bytes 1024000 | tf_op jit(solution)/shard_map/while/body/eval_jaxpr/convert_element_type | solution.py:39
  105.1 5.1 %multiply_reduce_fusion.2 = f32[2,40,40,40]{3,2,1,0:T(8,128)} fusion(f32[2,2,40,40,40]{4,3,2,1,0:T(8,128)S(1)} %get-tuple-element.356, bf16[2,2,40,40,40]{3,4,2,1,0:T(8,128)(2,1)} %copy.99, f32[40]{0:T(128)S(1)} %get-tuple-element.401, f32[40]{0:T(128)S(1)} %get-tuple-element.402), kind=kOutput, calls=%fused_computation.4.clone.1 | convolution fusion | flops 41612800 | bytes 2048320 | tf_op jit(solution)/shard_map/while/body/eval_jaxpr/ck,psabc->psabk/dot_general | solution.py:43
  110.3 2.9 broadcast_in_dim.27
  123.9 2.8 broadcast_select_fusion.6
  126.7 1.2 select_n.250
  128.6 1.2 select_n.251
  131.5 3.7 %copy.97 = bf16[2,2,40,40,40]{3,4,2,1,0:T(8,128)(2,1)} copy(bf16[2,2,40,40,40]{2,4,3,1,0:T(8,128)(2,1)S(1)} %fusion.154) | data formatting | bytes 1024000 | tf_op jit(solution)/shard_map/while/body/eval_jaxpr/convert_element_type | solution.py:62
  135.2 2.7 reshape.373
  137.9 4.2 %multiply_convert_fusion.3 = (bf16[2,2,40,40,40]{4,3,2,1,0:T(8,128)(2,1)}, f32[2,2,40,40,40]{4,3,2,1,0:T(8,128)S(1)}) fusion(f32[2,40,40,40]{3,2,1,0:T(8,128)} %reshape.373, s32[2,40]{1,0:T(2,128)S(1)} %get-tuple-element.351, bf16[2,2,40,40,40]{3,4,2,1,0:T(8,128)(2,1)} %copy.97, s32[2,40]{1,0:T(2,128)S(1)} %get-tuple-element.355), kind=kOutput, calls=%fused_computation.6.clone.1 | convolution fusion | flops 41734400 | bytes 2560640 | tf_op jit(solution)/shard_map/while/body/eval_jaxpr/pzc,psxyc->psxyz/dot_general | solution.py:66
  142.1 3.9 %fusion.155 = bf16[2,2,40,40,40]{2,4,3,1,0:T(8,128)(2,1)} fusion(bf16[2,2,40,40,40]{4,3,2,1,0:T(8,128)(2,1)} %get-tuple-element.357, f32[40]{0:T(128)S(1)} %get-tuple-element.401, f32[40]{0:T(128)S(1)} %get-tuple-element.402), kind=kOutput, calls=%fused_computation.23.clone.1 | convolution fusion | flops 20742400 | bytes 1024320 | tf_op jit(solution)/shard_map/while/body/eval_jaxpr/ak,psabc->pskbc/dot_general | solution.py:37
  146.0 4.8 %copy.98 = bf16[2,2,40,40,40]{3,4,2,1,0:T(8,128)(2,1)} copy(bf16[2,2,40,40,40]{2,4,3,1,0:T(8,128)(2,1)} %fusion.155) | data formatting | bytes 1024000 | tf_op jit(solution)/shard_map/while/body/eval_jaxpr/convert_element_type | solution.py:39
  152.1 5.2 %divide_convert_fusion.2 = bf16[2,2,40,40,40]{4,3,2,1,0:T(8,128)(2,1)} fusion(f32[40,40,40]{2,1,0:T(8,128)} %add_add_fusion.2, bf16[2,2,40,40,40]{3,4,2,1,0:T(8,128)(2,1)} %copy.98, f32[40]{0:T(128)S(1)} %get-tuple-element.401, f32[40]{0:T(128)S(1)} %get-tuple-element.402), kind=kOutput, calls=%fused_computation.5.clone.1 | convolution fusion | flops 41740800 | bytes 1280320 | tf_op jit(solution)/shard_map/while/body/eval_jaxpr/ck,psabc->psabk/dot_general | solution.py:43
  157.3 3.9 %fusion.156 = bf16[2,2,40,40,40]{2,4,3,1,0:T(8,128)(2,1)} fusion(bf16[2,2,40,40,40]{4,3,2,1,0:T(8,128)(2,1)} %divide_convert_fusion.2, f32[40]{0:T(128)S(1)} %get-tuple-element.401, f32[40]{0:T(128)S(1)} %get-tuple-element.402), kind=kOutput, calls=%fused_computation.24.clone.1 | convolution fusion | flops 20742400 | bytes 1024320 | tf_op jit(solution)/shard_map/while/body/eval_jaxpr/ak,psabc->pskbc/dot_general | solution.py:37
  161.2 4.8 %copy.99 = bf16[2,2,40,40,40]{3,4,2,1,0:T(8,128)(2,1)} copy(bf16[2,2,40,40,40]{2,4,3,1,0:T(8,128)(2,1)} %fusion.156) | data formatting | bytes 1024000 | tf_op jit(solution)/shard_map/while/body/eval_jaxpr/convert_element_type | solution.py:39
  166.0 5.1 %multiply_reduce_fusion.2 = f32[2,40,40,40]{3,2,1,0:T(8,128)} fusion(f32[2,2,40,40,40]{4,3,2,1,0:T(8,128)S(1)} %get-tuple-element.356, bf16[2,2,40,40,40]{3,4,2,1,0:T(8,128)(2,1)} %copy.99, f32[40]{0:T(128)S(1)} %get-tuple-element.401, f32[40]{0:T(128)S(1)} %get-tuple-element.402), kind=kOutput, calls=%fused_computation.4.clone.1 | convolution fusion | flops 41612800 | bytes 2048320 | tf_op jit(solution)/shard_map/while/body/eval_jaxpr/ck,psabc->psabk/dot_general | solution.py:43
  171.1 2.9 broadcast_in_dim.27
  184.7 2.8 broadcast_select_fusion.6
  187.5 1.2 select_n.250
  192.3 3.7 %copy.97 = bf16[2,2,40,40,40]{3,4,2,1,0:T(8,128)(2,1)} copy(bf16[2,2,40,40,40]{2,4,3,1,0:T(8,128)(2,1)S(1)} %fusion.154) | data formatting | bytes 1024000 | tf_op jit(solution)/shard_map/while/body/eval_jaxpr/convert_element_type | solution.py:62
  196.0 2.7 reshape.373
  198.7 4.2 %multiply_convert_fusion.3 = (bf16[2,2,40,40,40]{4,3,2,1,0:T(8,128)(2,1)}, f32[2,2,40,40,40]{4,3,2,1,0:T(8,128)S(1)}) fusion(f32[2,40,40,40]{3,2,1,0:T(8,128)} %reshape.373, s32[2,40]{1,0:T(2,128)S(1)} %get-tuple-element.351, bf16[2,2,40,40,40]{3,4,2,1,0:T(8,128)(2,1)} %copy.97, s32[2,40]{1,0:T(2,128)S(1)} %get-tuple-element.355), kind=kOutput, calls=%fused_computation.6.clone.1 | convolution fusion | flops 41734400 | bytes 2560640 | tf_op jit(solution)/shard_map/while/body/eval_jaxpr/pzc,psxyc->psxyz/dot_general | solution.py:66
  203.0 3.9 %fusion.155 = bf16[2,2,40,40,40]{2,4,3,1,0:T(8,128)(2,1)} fusion(bf16[2,2,40,40,40]{4,3,2,1,0:T(8,128)(2,1)} %get-tuple-element.357, f32[40]{0:T(128)S(1)} %get-tuple-element.401, f32[40]{0:T(128)S(1)} %get-tuple-element.402), kind=kOutput, calls=%fused_computation.23.clone.1 | convolution fusion | flops 20742400 | bytes 1024320 | tf_op jit(solution)/shard_map/while/body/eval_jaxpr/ak,psabc->pskbc/dot_general | solution.py:37
  206.9 4.8 %copy.98 = bf16[2,2,40,40,40]{3,4,2,1,0:T(8,128)(2,1)} copy(bf16[2,2,40,40,40]{2,4,3,1,0:T(8,128)(2,1)} %fusion.155) | data formatting | bytes 1024000 | tf_op jit(solution)/shard_map/while/body/eval_jaxpr/convert_element_type | solution.py:39
  212.9 5.2 %divide_convert_fusion.2 = bf16[2,2,40,40,40]{4,3,2,1,0:T(8,128)(2,1)} fusion(f32[40,40,40]{2,1,0:T(8,128)} %add_add_fusion.2, bf16[2,2,40,40,40]{3,4,2,1,0:T(8,128)(2,1)} %copy.98, f32[40]{0:T(128)S(1)} %get-tuple-element.401, f32[40]{0:T(128)S(1)} %get-tuple-element.402), kind=kOutput, calls=%fused_computation.5.clone.1 | convolution fusion | flops 41740800 | bytes 1280320 | tf_op jit(solution)/shard_map/while/body/eval_jaxpr/ck,psabc->psabk/dot_general | solution.py:43
  218.1 3.9 %fusion.156 = bf16[2,2,40,40,40]{2,4,3,1,0:T(8,128)(2,1)} fusion(bf16[2,2,40,40,40]{4,3,2,1,0:T(8,128)(2,1)} %divide_convert_fusion.2, f32[40]{0:T(128)S(1)} %get-tuple-element.401, f32[40]{0:T(128)S(1)} %get-tuple-element.402), kind=kOutput, calls=%fused_computation.24.clone.1 | convolution fusion | flops 20742400 | bytes 1024320 | tf_op jit(solution)/shard_map/while/body/eval_jaxpr/ak,psabc->pskbc/dot_general | solution.py:37
  222.0 4.8 %copy.99 = bf16[2,2,40,40,40]{3,4,2,1,0:T(8,128)(2,1)} copy(bf16[2,2,40,40,40]{2,4,3,1,0:T(8,128)(2,1)} %fusion.156) | data formatting | bytes 1024000 | tf_op jit(solution)/shard_map/while/body/eval_jaxpr/convert_element_type | solution.py:39
  226.8 5.1 %multiply_reduce_fusion.2 = f32[2,40,40,40]{3,2,1,0:T(8,128)} fusion(f32[2,2,40,40,40]{4,3,2,1,0:T(8,128)S(1)} %get-tuple-element.356, bf16[2,2,40,40,40]{3,4,2,1,0:T(8,128)(2,1)} %copy.99, f32[40]{0:T(128)S(1)} %get-tuple-element.401, f32[40]{0:T(128)S(1)} %get-tuple-element.402), kind=kOutput, calls=%fused_computation.4.clone.1 | convolution fusion | flops 41612800 | bytes 2048320 | tf_op jit(solution)/shard_map/while/body/eval_jaxpr/ck,psabc->psabk/dot_general | solution.py:43
  232.0 2.9 broadcast_in_dim.27
  245.6 2.8 broadcast_select_fusion.6
  248.4 1.2 select_n.250
  253.2 3.7 %copy.97 = bf16[2,2,40,40,40]{3,4,2,1,0:T(8,128)(2,1)} copy(bf16[2,2,40,40,40]{2,4,3,1,0:T(8,128)(2,1)S(1)} %fusion.154) | data formatting | bytes 1024000 | tf_op jit(solution)/shard_map/while/body/eval_jaxpr/convert_element_type | solution.py:62
  256.8 2.7 reshape.373
  259.6 4.2 %multiply_convert_fusion.3 = (bf16[2,2,40,40,40]{4,3,2,1,0:T(8,128)(2,1)}, f32[2,2,40,40,40]{4,3,2,1,0:T(8,128)S(1)}) fusion(f32[2,40,40,40]{3,2,1,0:T(8,128)} %reshape.373, s32[2,40]{1,0:T(2,128)S(1)} %get-tuple-element.351, bf16[2,2,40,40,40]{3,4,2,1,0:T(8,128)(2,1)} %copy.97, s32[2,40]{1,0:T(2,128)S(1)} %get-tuple-element.355), kind=kOutput, calls=%fused_computation.6.clone.1 | convolution fusion | flops 41734400 | bytes 2560640 | tf_op jit(solution)/shard_map/while/body/eval_jaxpr/pzc,psxyc->psxyz/dot_general | solution.py:66
  263.8 3.9 %fusion.155 = bf16[2,2,40,40,40]{2,4,3,1,0:T(8,128)(2,1)} fusion(bf16[2,2,40,40,40]{4,3,2,1,0:T(8,128)(2,1)} %get-tuple-element.357, f32[40]{0:T(128)S(1)} %get-tuple-element.401, f32[40]{0:T(128)S(1)} %get-tuple-element.402), kind=kOutput, calls=%fused_computation.23.clone.1 | convolution fusion | flops 20742400 | bytes 1024320 | tf_op jit(solution)/shard_map/while/body/eval_jaxpr/ak,psabc->pskbc/dot_general | solution.py:37
  267.7 4.8 %copy.98 = bf16[2,2,40,40,40]{3,4,2,1,0:T(8,128)(2,1)} copy(bf16[2,2,40,40,40]{2,4,3,1,0:T(8,128)(2,1)} %fusion.155) | data formatting | bytes 1024000 | tf_op jit(solution)/shard_map/while/body/eval_jaxpr/convert_element_type | solution.py:39
  273.7 5.2 %divide_convert_fusion.2 = bf16[2,2,40,40,40]{4,3,2,1,0:T(8,128)(2,1)} fusion(f32[40,40,40]{2,1,0:T(8,128)} %add_add_fusion.2, bf16[2,2,40,40,40]{3,4,2,1,0:T(8,128)(2,1)} %copy.98, f32[40]{0:T(128)S(1)} %get-tuple-element.401, f32[40]{0:T(128)S(1)} %get-tuple-element.402), kind=kOutput, calls=%fused_computation.5.clone.1 | convolution fusion | flops 41740800 | bytes 1280320 | tf_op jit(solution)/shard_map/while/body/eval_jaxpr/ck,psabc->psabk/dot_general | solution.py:43
  278.9 3.9 %fusion.156 = bf16[2,2,40,40,40]{2,4,3,1,0:T(8,128)(2,1)} fusion(bf16[2,2,40,40,40]{4,3,2,1,0:T(8,128)(2,1)} %divide_convert_fusion.2, f32[40]{0:T(128)S(1)} %get-tuple-element.401, f32[40]{0:T(128)S(1)} %get-tuple-element.402), kind=kOutput, calls=%fused_computation.24.clone.1 | convolution fusion | flops 20742400 | bytes 1024320 | tf_op jit(solution)/shard_map/while/body/eval_jaxpr/ak,psabc->pskbc/dot_general | solution.py:37
  282.8 4.8 %copy.99 = bf16[2,2,40,40,40]{3,4,2,1,0:T(8,128)(2,1)} copy(bf16[2,2,40,40,40]{2,4,3,1,0:T(8,128)(2,1)} %fusion.156) | data formatting | bytes 1024000 | tf_op jit(solution)/shard_map/while/body/eval_jaxpr/convert_element_type | solution.py:39
  287.7 5.1 %multiply_reduce_fusion.2 = f32[2,40,40,40]{3,2,1,0:T(8,128)} fusion(f32[2,2,40,40,40]{4,3,2,1,0:T(8,128)S(1)} %get-tuple-element.356, bf16[2,2,40,40,40]{3,4,2,1,0:T(8,128)(2,1)} %copy.99, f32[40]{0:T(128)S(1)} %get-tuple-element.401, f32[40]{0:T(128)S(1)} %get-tuple-element.402), kind=kOutput, calls=%fused_computation.4.clone.1 | convolution fusion | flops 41612800 | bytes 2048320 | tf_op jit(solution)/shard_map/while/body/eval_jaxpr/ck,psabc->psabk/dot_general | solution.py:43
  292.8 2.9 broadcast_in_dim.27
  296.5 3.9 %convolution_bitcast_fusion = f32[2,2,64000]{2,1,0:T(2,128)S(1)} fusion(f32[2,4,64000]{2,0,1:T(2,128)} %bitcast.150, pred[4]{0:T(512)(128)(4,1)S(1)} %slice_compare_fusion, s32[4]{0:T(128)S(1)} %get-tuple-element.244), kind=kOutput, calls=%fused_computation.74 | convolution fusion | flops 12288016 | bytes 3072020 | tf_op jit(solution)/shard_map/ar,src->sac/dot_general | solution.py:172
  300.4 4.5 %collective-permute-start.3 = (f32[2,2,64000]{2,1,0:T(2,128)S(1)}, f32[2,2,64000]{2,1,0:T(2,128)S(1)}, u32[]{:S(2)}, u32[]{:S(2)}) collective-permute-start(f32[2,2,64000]{2,1,0:T(2,128)S(1)} %convolution_bitcast_fusion), channel_id=1, source_target_pairs={{1,0},{2,1},{3,2},{4,3},{5,4},{6,5},{7,6},{8,7},{9,8},{10,9},{11,1... | collective-permute-start | bytes 3072008 | tf_op jit(solution)/shard_map/ppermute | solution.py:24
  305.0 2.3 fusion.73
  307.5 1.9 collective-permute-start.2
  309.9 2.2 fusion.75
  312.1 25.8 %collective-permute-done.2 = f32[2,1,64000]{2,0,1:T(2,128)S(1)} collective-permute-done((f32[2,1,64000]{2,0,1:T(2,128)S(1)}, f32[2,1,64000]{2,0,1:T(2,128)S(1)}, u32[]{:S(2)}, u32[]{:S(2)}) %collective-permute-start.2) | collective-permute-done | bytes 512032 | tf_op jit(solution)/shard_map/ppermute | solution.py:24
  337.9 4.2 %add_bitcast_fusion = f32[2,7,64000]{2,1,0:T(8,128)S(1)} fusion(f32[2,64000,7]{1,2,0:T(8,128)S(1)} %fusion.75, f32[7]{0:T(128)S(1)} %convolution_bitcast_fusion.2, f32[2,64000]{1,0:T(2,128)S(1)} %bitcast.153, f32[2,2,64000]{2,1,0:T(2,128)S(1)} %collective-permute-done.3, f32[7,2,1]{0,1,2:T(2,128)S(1)} %convolution_bitcast_fusion.1), kind=kOutput, calls=%fused_computation.75 | convolution fusion | flops 24192000 | bytes 8704084 | tf_op jit(solution)/shard_map/ka,sac->skc/dot_general | solution.py:106
  342.1 4.6 %copy.61 = f32[2,7,64000]{2,0,1:T(2,128)} copy(f32[2,7,64000]{2,1,0:T(8,128)S(1)} %add_bitcast_fusion) | data formatting | bytes 7168000 | tf_op jit(solution)/shard_map/add | solution.py:106
  (139 shorter events, 31.1 us)
Async XLA Ops:
  0.0 14.0 %copy-start.8 = (s32[3]{0:T(128)S(1)}, s32[3]{0:T(128)}, u32[]{:S(2)}) copy-start(s32[3]{0:T(128)} %constant.193) | copy-start | bytes 40
  0.0 14.0 %copy-start.9 = (s32[3]{0:T(128)S(1)}, s32[3]{0:T(128)}, u32[]{:S(2)}) copy-start(s32[3]{0:T(128)} %constant.195) | copy-start | bytes 40
  0.0 14.0 %copy-start.10 = (s32[3]{0:T(128)S(1)}, s32[3]{0:T(128)}, u32[]{:S(2)}) copy-start(s32[3]{0:T(128)} %constant.198) | copy-start | bytes 40
  0.0 11.7 %copy-start.6 = (s32[128,2]{0,1:T(2,128)S(1)}, s32[128,2]{0,1:T(2,128)}, u32[]{:S(2)}) copy-start(s32[128,2]{0,1:T(2,128)} %param.9) | copy-start | bytes 3076
  0.0 12.0 %copy-start.11 = (s32[128]{0:T(128)S(1)}, s32[128]{0:T(128)}, u32[]{:S(2)}) copy-start(s32[128]{0:T(128)} %param.8) | copy-start | bytes 1540
  0.0 12.3 %copy-start.7 = (s32[128,3]{0,1:T(4,128)S(1)}, s32[128,3]{0,1:T(4,128)}, u32[]{:S(2)}) copy-start(s32[128,3]{0,1:T(4,128)} %param.10) | copy-start | bytes 4612
  2.1 31.0 %collective-permute-start = (bf16[2,4,64000]{2,0,1:T(2,128)(2,1)S(1)}, bf16[2,4,64000]{2,0,1:T(2,128)(2,1)S(1)}, u32[]{:S(2)}, u32[]{:S(2)}) collective-permute-start(bf16[2,4,64000]{2,0,1:T(2,128)(2,1)S(1)} %copy.58), channel_id=1, source_target_pairs={{0,1},{1,2},{2,3},{3,4},{4,5},{5,6},{6,7},{7,8},{8,9},{9,10},{10,1... | collective-permute-start | bytes 3072008 | tf_op jit(solution)/shard_map/ppermute | solution.py:24
  5.6 47.5 %collective-permute-start.1 = (bf16[2,4,64000]{2,0,1:T(2,128)(2,1)S(1)}, bf16[2,4,64000]{2,0,1:T(2,128)(2,1)}, u32[]{:S(2)}, u32[]{:S(2)}) collective-permute-start(bf16[2,4,64000]{2,0,1:T(2,128)(2,1)S(1)} %copy.58), channel_id=1, source_target_pairs={{1,0},{2,1},{3,2},{4,3},{5,4},{6,5},{7,6},{8,7},{9,8},{10,9},{11,1... | collective-permute-start | bytes 3072008 | tf_op jit(solution)/shard_map/ppermute | solution.py:24
  53.1 12.7 %copy-start.1 = (bf16[2,4,64000]{2,0,1:T(2,128)(2,1)}, bf16[2,4,64000]{2,0,1:T(2,128)(2,1)S(1)}, u32[]{:S(2)}) copy-start(bf16[2,4,64000]{2,0,1:T(2,128)(2,1)S(1)} %get-tuple-element.395) | copy-start | bytes 3072004 | tf_op jit(solution)/shard_map/while
  53.2 12.7 %copy-start.4 = (bf16[2,4,64000]{2,0,1:T(2,128)(2,1)}, bf16[2,4,64000]{2,0,1:T(2,128)(2,1)S(1)}, u32[]{:S(2)}) copy-start(bf16[2,4,64000]{2,0,1:T(2,128)(2,1)S(1)} %get-tuple-element.398) | copy-start | bytes 3072004 | tf_op jit(solution)/shard_map/while
  70.6 3.7 %copy-start = (f32[2,1,64000]{2,0,1:T(2,128)S(1)}, f32[2,1,64000]{2,0,1:T(2,128)}, u32[]{:S(2)}) copy-start(f32[2,1,64000]{2,0,1:T(2,128)} %get-tuple-element.348) | copy-start | bytes 1536004 | tf_op jit(solution)/shard_map/while
  110.3 3.7 %copy-start.2 = (bf16[2,4,64000]{2,0,1:T(2,128)(2,1)S(1)}, bf16[2,4,64000]{2,0,1:T(2,128)(2,1)}, u32[]{:S(2)}) copy-start(bf16[2,4,64000]{2,0,1:T(2,128)(2,1)} %copy-done.1) | copy-start | bytes 3072004 | tf_op jit(solution)/shard_map/while
  110.3 3.7 %copy-start.5 = (bf16[2,4,64000]{2,0,1:T(2,128)(2,1)S(1)}, bf16[2,4,64000]{2,0,1:T(2,128)(2,1)}, u32[]{:S(2)}) copy-start(bf16[2,4,64000]{2,0,1:T(2,128)(2,1)} %copy-done.4) | copy-start | bytes 3072004 | tf_op jit(solution)/shard_map/while
  114.0 12.7 %copy-start.1 = (bf16[2,4,64000]{2,0,1:T(2,128)(2,1)}, bf16[2,4,64000]{2,0,1:T(2,128)(2,1)S(1)}, u32[]{:S(2)}) copy-start(bf16[2,4,64000]{2,0,1:T(2,128)(2,1)S(1)} %get-tuple-element.395) | copy-start | bytes 3072004 | tf_op jit(solution)/shard_map/while
  114.0 12.7 %copy-start.4 = (bf16[2,4,64000]{2,0,1:T(2,128)(2,1)}, bf16[2,4,64000]{2,0,1:T(2,128)(2,1)S(1)}, u32[]{:S(2)}) copy-start(bf16[2,4,64000]{2,0,1:T(2,128)(2,1)S(1)} %get-tuple-element.398) | copy-start | bytes 3072004 | tf_op jit(solution)/shard_map/while
  131.5 3.7 %copy-start = (f32[2,1,64000]{2,0,1:T(2,128)S(1)}, f32[2,1,64000]{2,0,1:T(2,128)}, u32[]{:S(2)}) copy-start(f32[2,1,64000]{2,0,1:T(2,128)} %get-tuple-element.348) | copy-start | bytes 1536004 | tf_op jit(solution)/shard_map/while
  171.1 3.7 %copy-start.2 = (bf16[2,4,64000]{2,0,1:T(2,128)(2,1)S(1)}, bf16[2,4,64000]{2,0,1:T(2,128)(2,1)}, u32[]{:S(2)}) copy-start(bf16[2,4,64000]{2,0,1:T(2,128)(2,1)} %copy-done.1) | copy-start | bytes 3072004 | tf_op jit(solution)/shard_map/while
  171.1 3.7 %copy-start.5 = (bf16[2,4,64000]{2,0,1:T(2,128)(2,1)S(1)}, bf16[2,4,64000]{2,0,1:T(2,128)(2,1)}, u32[]{:S(2)}) copy-start(bf16[2,4,64000]{2,0,1:T(2,128)(2,1)} %copy-done.4) | copy-start | bytes 3072004 | tf_op jit(solution)/shard_map/while
  174.8 12.7 %copy-start.1 = (bf16[2,4,64000]{2,0,1:T(2,128)(2,1)}, bf16[2,4,64000]{2,0,1:T(2,128)(2,1)S(1)}, u32[]{:S(2)}) copy-start(bf16[2,4,64000]{2,0,1:T(2,128)(2,1)S(1)} %get-tuple-element.395) | copy-start | bytes 3072004 | tf_op jit(solution)/shard_map/while
  174.8 12.7 %copy-start.4 = (bf16[2,4,64000]{2,0,1:T(2,128)(2,1)}, bf16[2,4,64000]{2,0,1:T(2,128)(2,1)S(1)}, u32[]{:S(2)}) copy-start(bf16[2,4,64000]{2,0,1:T(2,128)(2,1)S(1)} %get-tuple-element.398) | copy-start | bytes 3072004 | tf_op jit(solution)/shard_map/while
  192.3 3.7 %copy-start = (f32[2,1,64000]{2,0,1:T(2,128)S(1)}, f32[2,1,64000]{2,0,1:T(2,128)}, u32[]{:S(2)}) copy-start(f32[2,1,64000]{2,0,1:T(2,128)} %get-tuple-element.348) | copy-start | bytes 1536004 | tf_op jit(solution)/shard_map/while
  232.0 3.7 %copy-start.2 = (bf16[2,4,64000]{2,0,1:T(2,128)(2,1)S(1)}, bf16[2,4,64000]{2,0,1:T(2,128)(2,1)}, u32[]{:S(2)}) copy-start(bf16[2,4,64000]{2,0,1:T(2,128)(2,1)} %copy-done.1) | copy-start | bytes 3072004 | tf_op jit(solution)/shard_map/while
  232.0 3.7 %copy-start.5 = (bf16[2,4,64000]{2,0,1:T(2,128)(2,1)S(1)}, bf16[2,4,64000]{2,0,1:T(2,128)(2,1)}, u32[]{:S(2)}) copy-start(bf16[2,4,64000]{2,0,1:T(2,128)(2,1)} %copy-done.4) | copy-start | bytes 3072004 | tf_op jit(solution)/shard_map/while
  235.7 12.7 %copy-start.1 = (bf16[2,4,64000]{2,0,1:T(2,128)(2,1)}, bf16[2,4,64000]{2,0,1:T(2,128)(2,1)S(1)}, u32[]{:S(2)}) copy-start(bf16[2,4,64000]{2,0,1:T(2,128)(2,1)S(1)} %get-tuple-element.395) | copy-start | bytes 3072004 | tf_op jit(solution)/shard_map/while
  235.7 12.7 %copy-start.4 = (bf16[2,4,64000]{2,0,1:T(2,128)(2,1)}, bf16[2,4,64000]{2,0,1:T(2,128)(2,1)S(1)}, u32[]{:S(2)}) copy-start(bf16[2,4,64000]{2,0,1:T(2,128)(2,1)S(1)} %get-tuple-element.398) | copy-start | bytes 3072004 | tf_op jit(solution)/shard_map/while
  253.2 3.7 %copy-start = (f32[2,1,64000]{2,0,1:T(2,128)S(1)}, f32[2,1,64000]{2,0,1:T(2,128)}, u32[]{:S(2)}) copy-start(f32[2,1,64000]{2,0,1:T(2,128)} %get-tuple-element.348) | copy-start | bytes 1536004 | tf_op jit(solution)/shard_map/while
  292.8 3.7 %copy-start.2 = (bf16[2,4,64000]{2,0,1:T(2,128)(2,1)S(1)}, bf16[2,4,64000]{2,0,1:T(2,128)(2,1)}, u32[]{:S(2)}) copy-start(bf16[2,4,64000]{2,0,1:T(2,128)(2,1)} %copy-done.1) | copy-start | bytes 3072004 | tf_op jit(solution)/shard_map/while
  292.8 3.7 %copy-start.5 = (bf16[2,4,64000]{2,0,1:T(2,128)(2,1)S(1)}, bf16[2,4,64000]{2,0,1:T(2,128)(2,1)}, u32[]{:S(2)}) copy-start(bf16[2,4,64000]{2,0,1:T(2,128)(2,1)} %copy-done.4) | copy-start | bytes 3072004 | tf_op jit(solution)/shard_map/while
  296.5 8.5 %copy-start.3 = (f32[4,2,64000]{2,1,0:T(2,128)S(1)}, f32[4,2,64000]{2,1,0:T(2,128)}, u32[]{:S(2)}) copy-start(f32[4,2,64000]{2,1,0:T(2,128)} %get-tuple-element.77) | copy-start | bytes 6144004
  300.4 37.5 %collective-permute-start.3 = (f32[2,2,64000]{2,1,0:T(2,128)S(1)}, f32[2,2,64000]{2,1,0:T(2,128)S(1)}, u32[]{:S(2)}, u32[]{:S(2)}) collective-permute-start(f32[2,2,64000]{2,1,0:T(2,128)S(1)} %convolution_bitcast_fusion), channel_id=1, source_target_pairs={{1,0},{2,1},{3,2},{4,3},{5,4},{6,5},{7,6},{8,7},{9,8},{10,9},{11,1... | collective-permute-start | bytes 3072008 | tf_op jit(solution)/shard_map/ppermute | solution.py:24
  307.5 30.4 %collective-permute-start.2 = (f32[2,1,64000]{2,0,1:T(2,128)S(1)}, f32[2,1,64000]{2,0,1:T(2,128)S(1)}, u32[]{:S(2)}, u32[]{:S(2)}) collective-permute-start(f32[2,1,64000]{2,0,1:T(2,128)S(1)} %bitcast.154), channel_id=1, source_target_pairs={{0,1},{1,2},{2,3},{3,4},{4,5},{5,6},{6,7},{7,8},{8,9},{9,10},{10,1... | collective-permute-start | bytes 1536008 | tf_op jit(solution)/shard_map/ppermute | solution.py:24
where the time goes:
time: 350 us; the launch traced here: 347 us
  local copies, waits for them, and re-layouts  111 us (32%)
  matrix products  105 us (30%)
  waiting for transfers between devices  64.6 us (18%)
  loops' own time  32.3 us (9%)
  other arithmetic  17.7 us (5%)
  starting transfers between devices  15.8 us (5%)
    ppermute x4, waiting for transfers between devices, from_behind(): lax.ppermute(value, axis, [(source, source + steps) for source in range(i...  64.6 us
    dot_general x8, matrix products, sine_pass(): jnp.einsum('ck,psabc->psabk', sine_table, volume, preferred_element_type=...  41.4 us
    convert_element_type x8, local copies, waits for them, and re-layouts, sine_pass(): volume = jnp.einsum('ak,psabc->pskbc', sine_table, volume, preferred_elem...  38.7 us
    another operation x1, loops' own time, shards(): lax.map(one_box, (jnp.arange(BOX_DEV, dtype=jnp.int32), side_codes, row_p...  32.3 us
    dot_general x8, matrix products, sine_pass(): jnp.einsum('ak,psabc->pskbc', sine_table, volume, preferred_element_type=...  31.1 us
    dot_general x4, matrix products, pair_sum(): jnp.einsum('pzc,psxyc->psxyz', shifters[2], moving, preferred_element_typ...  17 us
    ppermute x4, starting transfers between devices, from_behind(): lax.ppermute(value, axis, [(source, source + steps) for source in range(i...  15.8 us
    select_n x16, local copies, waits for them, and re-layouts, fetch_box(): jnp.where(side_code < 0, from_prev, jnp.where(side_code == 0, from_self,...  15 us
  transfers between devices with their start and end apart: 4, of which 3 were waited for; matrix products, arithmetic and copies ran while one was open for 2% of the time, Pallas kernels for 0%

commit v1 on v0

v1 whole, which is shorter than its diff:
```python
import jax
import jax.numpy as jnp
import numpy as np
from jax import lax
from jax.experimental import pallas as pl
from jax.experimental.pallas import tpu as pltpu
from jax.sharding import PartitionSpec as P

EDGE = 40
PARTNERS = 2
GRID_X = 768
GRID_Y = 384
GRID_Z = 384
BACK = 2
AHEAD = 1
CAP = 7
SCREEN = 0.001

AXES = ("gx", "gy", "gz")
LANES = 128
FACE = EDGE * EDGE
TILES = -(-FACE // LANES)
WIDE = TILES * LANES
NCHUNK = 256
NSTEPS = -(-FACE // NCHUNK)
NWIDE = NSTEPS * NCHUNK
FLAT = EDGE ** 3 // LANES
HALF = EDGE // 2
PAIRT = 2 * FACE // LANES
PAD = 24
ROWS = EDGE + 2 * PAD
ZERO_TILES = 7
BF = jnp.bfloat16
F32 = jnp.float32


def tables():
    counter = np.arange(EDGE, dtype=np.float32) + 1.0
    angles = np.float32(np.pi) * counter[:, None] * counter[None, :] / np.float32(EDGE + 1.0)
    sine = (np.sqrt(np.float32(2.0 / (EDGE + 1.0))) * np.sin(angles)).astype(jnp.bfloat16)
    sine = sine.astype(np.float32)
    levels = 2.0 - 2.0 * np.cos(np.pi * counter.astype(np.float64) / (EDGE + 1.0))
    lam = levels[:, None, None] + levels[None, :, None] + levels[None, None, :] + SCREEN
    inverse = np.zeros((EDGE, NWIDE), np.float32)
    inverse[:, :FACE] = (1.0 / lam).reshape(EDGE, FACE)
    repeated = np.zeros((EDGE, NWIDE), np.float32)
    repeated[:, :FACE] = np.repeat(sine, EDGE, axis=1)
    tiled = np.zeros((EDGE, NWIDE), np.float32)
    tiled[:, :FACE] = np.tile(sine, (1, EDGE))
    return sine, inverse, repeated, tiled


def lane_iota():
    return lax.broadcasted_iota(jnp.int32, (1, LANES), 1)


def split_boxes(orb_ref, flat_ref, spin, boxes):
    def step(i, _):
        base = pl.multiple_of(i * PAIRT * LANES, LANES)
        x = orb_ref[spin, :, pl.ds(base, PAIRT * LANES)].astype(F32)
        for j in range(PAIRT):
            flat_ref[pl.ds(pl.multiple_of((i * PAIRT + j) * 8, 8), boxes), :] = x[:, j * LANES:(j + 1) * LANES]
        return 0
    lax.fori_loop(0, HALF, step, 0)


def flat_to_slabs(load, store):
    low = lane_iota() < LANES // 2
    rolled = None
    for t in range(PAIRT):
        x = load(t)
        if t < TILES:
            store(t, 0, x)
        if t >= TILES - 1:
            turned = pltpu.roll(x, LANES // 2, 1)
            if rolled is not None:
                store(t - TILES, 1, jnp.where(low, rolled, turned))
            rolled = turned
    store(TILES - 1, 1, rolled)


def slabs_to_flat(load, store):
    low = lane_iota() < LANES // 2
    for t in range(TILES - 1):
        store(t, load(t, 0))
    before = load(TILES - 1, 0)
    for v in range(TILES):
        turned = pltpu.roll(load(v, 1), LANES // 2, 1)
        store(TILES - 1 + v, jnp.where(low, before, turned))
        before = turned


def window_kernel(win_ref, orb_ref, ahead_ref, back_ref, flat_ref):
    boxes = orb_ref.shape[1]
    for spin in range(2):
        split_boxes(orb_ref, flat_ref, spin, boxes)
        ahead_ref[spin] = flat_ref[pl.ds(win_ref[0], FLAT, stride=8), :].astype(BF)
        back_ref[spin] = flat_ref[pl.ds(win_ref[1], FLAT, stride=8), :].astype(BF)


def prepare_kernel(orb_ref, rep_ref, til_ref, own_ref, kron_ref, flat_ref):
    boxes = orb_ref.shape[1]
    for spin in range(2):
        split_boxes(orb_ref, flat_ref, spin, boxes)

        def one(box, _):
            flat_to_slabs(
                lambda t: flat_ref[pl.ds(box + 8 * t, HALF, stride=8 * PAIRT), :],
                lambda u, parity, x: own_ref.__setitem__((box, spin, u, pl.ds(parity, HALF, stride=2), slice(None)), x),
            )
            return 0
        lax.fori_loop(0, boxes, one, 0)

    def build(i, _):
        row = pl.multiple_of(i * 2 * EDGE, 16)
        for c in range(NSTEPS):
            cols = slice(c * NCHUNK, (c + 1) * NCHUNK)
            til = til_ref[:, cols]
            first = rep_ref[pl.ds(2 * i, 1), cols] * til
            second = rep_ref[pl.ds(2 * i + 1, 1), cols] * til
            kron_ref[pl.ds(row, 2 * EDGE), cols] = jnp.concatenate([first, second], axis=0).astype(BF)
        return 0
    lax.fori_loop(0, HALF, build, 0)
    kron_ref[FACE:, :] = jnp.zeros((WIDE - FACE, NWIDE), BF)


def pair_kernel(tab_ref, own_ref, kron_ref, prev_ref, next_ref, diag_ref, inv_ref,
                out_ref, sent_ahead_ref, sent_back_ref,
                pad_ref, mov_ref, x_ref, y_ref, flat_ref, res_ref):
    boxes = own_ref.shape[0]
    body = pl.ds(PAD, EDGE)
    lanes = lane_iota()
    rows = lax.broadcasted_iota(jnp.int32, (EDGE, 1), 0)

    def stage(box, _):
        for spin in range(2):
            for u in range(TILES):
                pad_ref[box, spin, u, body, :] = own_ref[box, spin, u]
        return 0
    lax.fori_loop(0, boxes, stage, 0)
    for side, ref in ((0, prev_ref), (1, next_ref)):
        for spin in range(2):
            flat_ref[...] = ref[spin].astype(F32)
            flat_to_slabs(
                lambda t: flat_ref[pl.ds(t, HALF, stride=PAIRT), :],
                lambda u, parity, x: pad_ref.__setitem__(
                    (boxes + side, spin, u, pl.ds(PAD + parity, HALF, stride=2), slice(None)), x),
            )

    def dense(box, _):
        keep, places = [], []
        for number in range(PARTNERS):
            base = 1 + (box * PARTNERS + number) * 4
            source = tab_ref[base]
            da, db, dc = tab_ref[base + 1], tab_ref[base + 2], tab_ref[base + 3]
            offset = ZERO_TILES * LANES - (db * EDGE + dc)
            quotient, rest = offset // LANES, offset % LANES
            row_ok = (rows >= da) & (rows < da + EDGE)
            places.append((source, da, db, dc, quotient, rest, row_ok))
        for spin in range(2):
            last = [None] * PARTNERS
            for u in range(TILES + 1):
                values = []
                for number in range(PARTNERS):
                    source, da, db, dc, quotient, rest, row_ok = places[number]
                    tile = jnp.clip(quotient + (u - ZERO_TILES), 0, TILES - 1)
                    x = pad_ref[source, spin, tile, pl.ds(PAD - da, EDGE), :]
                    turned = pltpu.roll(x, (LANES - rest) % LANES, 1)
                    if u > 0:
                        cell = lanes + (u - 1) * LANES
                        b = (cell * 52429) >> 21
                        c = cell - b * EDGE
                        ok = (b >= db) & (b < db + EDGE) & (c >= dc) & (c < dc + EDGE) & (b < EDGE)
                        moved = jnp.where(row_ok & ok, jnp.where(lanes < LANES - rest, last[number], turned), 0.0)
                        mov_ref[box, spin, number, u - 1] = moved
                        values.append(own_ref[box, spin, u - 1] * moved)
                    last[number] = turned
                if u > 0:
                    both = jnp.concatenate(values, axis=0)
                    if u == TILES:
                        both = jnp.where(lanes < FACE - (TILES - 1) * LANES, both, 0.0)
                    x_ref[pl.ds(pl.multiple_of((box * 2 + spin) * PARTNERS * EDGE, 16), PARTNERS * EDGE),
                          (u - 1) * LANES:u * LANES] = both.astype(BF)
        return 0
    lax.fori_loop(0, boxes, dense, 0)

    group = 2 * PARTNERS * EDGE
    diag = diag_ref[...]

    def first_pass(box, _):
        where = pl.ds(pl.multiple_of(box * group, 16), group)
        y_ref[where, :WIDE] = jnp.dot(diag, x_ref[where, :WIDE], preferred_element_type=F32).astype(BF)
        return 0
    lax.fori_loop(0, boxes, first_pass, 0)

    cubes = boxes * 2 * PARTNERS

    def forward(n, _):
        cols = pl.ds(pl.multiple_of(n * NCHUNK, NCHUNK), NCHUNK)
        z = jnp.dot(y_ref[:, :WIDE], kron_ref[:, cols], preferred_element_type=F32)
        z = z.reshape(cubes, EDGE, NCHUNK) * inv_ref[:, cols][None]
        x_ref[:, cols] = z.reshape(cubes * EDGE, NCHUNK).astype(BF)
        return 0
    lax.fori_loop(0, NSTEPS, forward, 0)

    def backward(n, _):
        cols = pl.ds(pl.multiple_of(n * NCHUNK, NCHUNK), NCHUNK)
        y_ref[:, cols] = jnp.dot(x_ref[:, :WIDE], kron_ref[:, cols], preferred_element_type=F32).astype(BF)
        return 0
    lax.fori_loop(0, NSTEPS, backward, 0)

    def finish(box, _):
        where = pl.ds(pl.multiple_of(box * group, 16), group)
        for u in range(TILES):
            potential = jnp.dot(diag, y_ref[where, u * LANES:(u + 1) * LANES], preferred_element_type=F32)
            for spin in range(2):
                total = 0.0
                for number in range(PARTNERS):
                    first = (spin * PARTNERS + number) * EDGE
                    total = total + potential[first:first + EDGE] * mov_ref[box, spin, number, u]
                res_ref[spin, u] = total
        for spin in range(2):
            slabs_to_flat(
                lambda u, parity: res_ref[spin, u, pl.ds(parity, HALF, stride=2), :],
                lambda t, x: out_ref.__setitem__(
                    (box, pl.ds(2 * t + spin, HALF, stride=2 * PAIRT), slice(None)), x),
            )
        return 0
    lax.fori_loop(0, boxes, finish, 0)
    base = 1 + boxes * PARTNERS * 4
    for k in range(AHEAD):
        sent_ahead_ref[k] = out_ref[tab_ref[base + k]].astype(BF)
    for k in range(BACK):
        sent_back_ref[k] = out_ref[tab_ref[base + AHEAD + k]].astype(BF)


def place_kernel(code_ref, own_ref, prev_ref, next_ref, out_ref):
    boxes = own_ref.shape[0]
    code = code_ref[pl.program_id(0)]

    @pl.when(code < boxes)
    def _():
        out_ref[0] = own_ref[jnp.minimum(code, boxes - 1)]

    @pl.when((code >= boxes) & (code < boxes + AHEAD))
    def _():
        out_ref[0] = prev_ref[jnp.clip(code - boxes, 0, AHEAD - 1)].astype(F32)

    @pl.when((code >= boxes + AHEAD) & (code < boxes + AHEAD + BACK))
    def _():
        out_ref[0] = next_ref[jnp.clip(code - boxes - AHEAD, 0, BACK - 1)].astype(F32)

    @pl.when(code >= boxes + AHEAD + BACK)
    def _():
        out_ref[...] = jnp.zeros_like(out_ref)


def from_behind(value, steps):
    count = lax.axis_size(AXES)
    initial, last = (max(0, -steps), min(count, count - steps))
    return lax.ppermute(value, AXES, [(source, source + steps) for source in range(initial, last)])


def whole(count):
    return [pl.BlockSpec(memory_space=pltpu.VMEM)] * count


SCALARS = pl.BlockSpec(memory_space=pltpu.SMEM)


def shards(orbitals, dest, partners, anchors):
    boxes = orbitals.shape[1]
    device = lax.axis_index(AXES)
    sine, inverse, repeated, tiled = tables()

    around = lax.dynamic_slice_in_dim(
        jnp.pad(partners, ((boxes, boxes), (0, 0)), constant_values=-1), device * boxes, 3 * boxes, axis=0)
    local = around - device * boxes
    mine = jnp.where((local >= 0) & (local < boxes), local, 0)
    window = jnp.stack([jnp.max(mine[2 * boxes:]), jnp.max(mine[:boxes])]).astype(jnp.int32)

    ahead_box, back_box = pl.pallas_call(
        window_kernel,
        out_shape=[jax.ShapeDtypeStruct((2, FLAT, LANES), BF)] * 2,
        in_specs=[SCALARS] + whole(1),
        out_specs=whole(2),
        scratch_shapes=[pltpu.VMEM((FLAT * 8, LANES), F32)],
        compiler_params=pltpu.CompilerParams(vmem_limit_bytes=8 << 20),
        name="window",
    )(window, orbitals)
    prev_box = from_behind(ahead_box, 1)
    next_box = from_behind(back_box, -1)

    own, kron = pl.pallas_call(
        prepare_kernel,
        out_shape=[jax.ShapeDtypeStruct((boxes, 2, TILES, EDGE, LANES), F32),
                   jax.ShapeDtypeStruct((WIDE, NWIDE), BF)],
        in_specs=whole(3),
        out_specs=whole(2),
        scratch_shapes=[pltpu.VMEM((FLAT * 8, LANES), F32)],
        compiler_params=pltpu.CompilerParams(vmem_limit_bytes=16 << 20),
        cost_estimate=pl.CostEstimate(flops=10_000_000, bytes_accessed=10_000_000, transcendentals=0),
        name="prepare",
    )(orbitals, repeated, tiled)

    pairs = local[boxes:2 * boxes]
    side = pairs // boxes
    source = jnp.where(side < 0, boxes, jnp.where(side > 0, boxes + 1, pairs))
    spots = lax.dynamic_slice_in_dim(
        jnp.pad(anchors, ((boxes, boxes), (0, 0))), device * boxes, 3 * boxes, axis=0)
    pick = (jnp.clip(pairs + boxes, 0, 3 * boxes - 1)[:, :, None] == jnp.arange(3 * boxes, dtype=jnp.int32))
    there = jnp.sum(jnp.where(pick[..., None], spots[None, None], 0), axis=2)
    extent = jnp.array([GRID_X, GRID_Y, GRID_Z], jnp.int32)
    difference = there - spots[boxes:2 * boxes, None, :]
    delta = (difference + extent // 2) % extent - extent // 2
    delta = jnp.clip(delta, -(PAD - 4), PAD - 4)
    pair_table = jnp.concatenate([source[..., None], delta], axis=-1).reshape(-1)

    nearby = lax.dynamic_slice_in_dim(
        jnp.pad(dest, (boxes, boxes), constant_values=-1), device * boxes, 3 * boxes)
    place = jnp.arange(3 * boxes, dtype=jnp.int32)
    earlier = (nearby[:, None] == nearby[None, :]) & (place[None, :] < place[:, None])
    same = (place[:, None] // boxes) == (place[None, :] // boxes)
    rank = jnp.sum(earlier.astype(jnp.int32), axis=1)
    inside = jnp.sum((earlier & same).astype(jnp.int32), axis=1)
    block = place // boxes
    code = jnp.where(block == 1, place - boxes,
                     jnp.where(block == 0, boxes + inside, boxes + AHEAD + inside))
    slot = jnp.arange(CAP, dtype=jnp.int32)
    taken = (nearby[None, :] == device) & (rank[None, :] == slot[:, None])
    none = boxes + AHEAD + BACK
    codes = none + jnp.sum(jnp.where(taken, code[None, :] - none, 0), axis=1)
    goes = nearby[boxes:2 * boxes]
    order = inside[boxes:2 * boxes]
    box_line = jnp.arange(boxes, dtype=jnp.int32)
    leave_ahead = [jnp.sum(jnp.where((goes == device + 1) & (order == k), box_line, 0)) for k in range(AHEAD)]
    leave_back = [jnp.sum(jnp.where((goes == device - 1) & (order == k), box_line, 0)) for k in range(BACK)]
    table = jnp.concatenate([device[None].astype(jnp.int32), pair_table,
                             jnp.stack(leave_ahead + leave_back)]).astype(jnp.int32)

    diag = np.kron(np.eye(2 * PARTNERS, dtype=np.float32), sine).astype(jnp.bfloat16)
    cubes = boxes * 2 * PARTNERS
    terms, sent_ahead, sent_back = pl.pallas_call(
        pair_kernel,
        out_shape=[jax.ShapeDtypeStruct((boxes, 2 * FLAT, LANES), F32),
                   jax.ShapeDtypeStruct((AHEAD, 2 * FLAT, LANES), BF),
                   jax.ShapeDtypeStruct((BACK, 2 * FLAT, LANES), BF)],
        in_specs=[SCALARS] + whole(6),
        out_specs=whole(3),
        scratch_shapes=[
            pltpu.VMEM((boxes + 2, 2, TILES, ROWS, LANES), F32),
            pltpu.VMEM((boxes, 2, PARTNERS, TILES, EDGE, LANES), F32),
            pltpu.VMEM((cubes * EDGE, NWIDE), BF),
            pltpu.VMEM((cubes * EDGE, NWIDE), BF),
            pltpu.VMEM((FLAT, LANES), F32),
            pltpu.VMEM((2, TILES, EDGE, LANES), F32),
        ],
        compiler_params=pltpu.CompilerParams(vmem_limit_bytes=48 << 20),
        name="pairs",
    )(table, own, kron, prev_box, next_box, diag, inverse)
    from_prev = from_behind(sent_ahead, 1)
    from_next = from_behind(sent_back, -1)

    placed = pl.pallas_call(
        place_kernel,
        out_shape=jax.ShapeDtypeStruct((CAP, 2 * FLAT, LANES), F32),
        grid=(CAP,),
        in_specs=[SCALARS] + whole(3),
        out_specs=pl.BlockSpec((1, 2 * FLAT, LANES), lambda i: (i, 0, 0)),
        compiler_params=pltpu.CompilerParams(vmem_limit_bytes=16 << 20),
        name="place",
    )(codes, terms, from_prev, from_next)
    placed = placed.reshape(CAP, FLAT, 2, LANES)
    return placed.transpose(2, 0, 1, 3).reshape(2, CAP, FLAT * LANES)


def solution(mesh):
    return jax.shard_map(
        shards,
        mesh=mesh,
        in_specs=(P(None, AXES, None), P(), P(), P()),
        out_specs=P(None, AXES, None),
        check_vma=False,
    )
```

time: 350 us -> 80.1 us (0.23)
  matrix products: 105 us -> 0 us
  local copies, waits for them, and re-layouts: 111 us -> 20.6 us
  waiting for transfers between devices: 64.6 us -> 14.2 us
  loops' own time: 32.3 us -> 0 us
  Pallas kernels: 0 us -> 23.4 us
  other arithmetic: 17.7 us -> 5.81 us
    dot_general x30 -> x0, matrix products: 105 us -> none  [the longest x8 41.4 us: sine_pass(): jnp.einsum('ck,psabc->psabk', sine_table, volume, preferred_element_type=...]
    convert_element_type x16 -> x0, local copies, waits for them, and re-layouts: 64 us -> none  [the longest x8 38.7 us: sine_pass(): volume = jnp.einsum('ak,psabc->pskbc', sine_table, volume, preferred_elem...]
    ppermute x4, waiting for transfers between devices: 64.6 us -> 14.2 us  [from_behind(): lax.ppermute(value, AXES, [(source, source + steps) for source in range(i...]
    another operation x1 -> x0, loops' own time: 32.3 us -> none  [shards(): lax.map(one_box, (jnp.arange(BOX_DEV, dtype=jnp.int32), side_codes, row_p...]
    pallas_call x0 -> x4, Pallas kernels: none -> 23.4 us  [the longest x1 19 us: shards(): pl.pallas_call(pair_kernel, out_shape=[jax.ShapeDtypeStruct((boxes, 2 * F...]
    select_n x17 -> x0, local copies, waits for them, and re-layouts: 15.1 us -> none  [the longest x16 15 us: fetch_box(): jnp.where(side_code < 0, from_prev, jnp.where(side_code == 0, from_self,...]
    broadcast_in_dim x5 -> x0, local copies, waits for them, and re-layouts: 11.5 us -> none  [the longest x4 11.4 us: shards(): lax.map(one_box, (jnp.arange(BOX_DEV, dtype=jnp.int32), side_codes, row_p...]
    select_n x8 -> x3, other arithmetic: 11.3 us -> 1.48 us  [the longest x1 0.75 us: shards(): mine = jnp.where((local >= 0) & (local < boxes), local, 0)]
  transfers between devices with their start and end apart: 4 -> 4, of which waited for: 3 -> 2; matrix products, arithmetic and copies ran while one was open for 2% -> 8% of each run, Pallas kernels for 0% -> 3%
where the time goes in v1:
time: 80.1 us; the launch traced here: 79.4 us
  Pallas kernels  23.4 us (29%)
  local copies, waits for them, and re-layouts  20.6 us (26%)
  starting transfers between devices  15.3 us (19%)
  waiting for transfers between devices  14.2 us (18%)
  other arithmetic  5.81 us (7%)
    pallas_call x1, Pallas kernels, shards(): pl.pallas_call(pair_kernel, out_shape=[jax.ShapeDtypeStruct((boxes, 2 * F...  19 us
    ppermute x4, starting transfers between devices, from_behind(): lax.ppermute(value, AXES, [(source, source + steps) for source in range(i...  15.3 us
    ppermute x4, waiting for transfers between devices, from_behind(): lax.ppermute(value, AXES, [(source, source + steps) for source in range(i...  14.2 us
    unnamed x14, local copies, waits for them, and re-layouts  8.72 us
    reshape x1, local copies, waits for them, and re-layouts, shards(): return placed.transpose(2, 0, 1, 3).reshape(2, CAP, FLAT * LANES)  6.88 us
    pallas_call x1, Pallas kernels, shards(): pl.pallas_call(prepare_kernel, out_shape=[jax.ShapeDtypeStruct((boxes, 2,...  2.06 us
    reshape x1, local copies, waits for them, and re-layouts, shards(): placed = placed.reshape(CAP, FLAT, 2, LANES)  2.02 us
    concatenate x1, local copies, waits for them, and re-layouts, shards(): jnp.concatenate([device[None].astype(jnp.int32), pair_table, jnp.stack(le...  1.96 us
  transfers between devices with their start and end apart: 4, of which 2 were waited for; matrix products, arithmetic and copies ran while one was open for 8% of the time, Pallas kernels for 3%

profile of v1, /device:TPU:4, one launch (start us, length us, event | category | flops | bytes accessed | tf_op | source)
XLA Modules:
  0.0 79.4 jit_solution(2597612411765418227)
XLA Ops:
  0.0 0.8 and_select_fusion
  0.8 0.7 compare_select_fusion.1
  1.5 1.3 %pad_add_fusion.1.win_ref = s32[2]{0:T(128)S(1)} fusion(s32[1]{0:T(128)} %bitcast.7, s32[1]{0:T(128)} %bitcast.6), kind=kLoop, calls=%fused_computation.39 | loop fusion | flops 2 | bytes 16 | tf_op jit(solution)/shard_map/stack | solution.py:280
  2.8 0.0 copy-start.1
  2.8 1.2 %copy-done.1 = bf16[2,4,64000]{2,1,0:T(4,128)(2,1)S(1)} copy-done((bf16[2,4,64000]{2,1,0:T(4,128)(2,1)S(1)}, bf16[2,4,64000]{2,1,0:T(4,128)(2,1)}, u32[]{:S(2)}) %copy-start.1) | copy-done | bytes 1024024
  4.0 1.3 %window.1 = (bf16[2,500,128]{2,1,0:T(8,128)(2,1)S(1)}, bf16[2,500,128]{2,1,0:T(8,128)(2,1)S(1)}) custom-call(s32[2]{0:T(128)S(1)} %pad_add_fusion.1.win_ref, bf16[2,4,64000]{2,1,0:T(4,128)(2,1)S(1)} %copy-done.1), custom_call_target="tpu_custom_call" | custom-call | tf_op jit(solution)/shard_map/window/pallas_call | solution.py:282
  5.3 3.5 %collective-permute-start = (bf16[2,500,128]{2,1,0:T(8,128)(2,1)S(1)}, bf16[2,500,128]{2,1,0:T(8,128)(2,1)S(1)}, u32[]{:S(2)}, u32[]{:S(2)}) collective-permute-start(bf16[2,500,128]{2,1,0:T(8,128)(2,1)S(1)} %get-tuple-element.14), channel_id=1, source_target_pairs={{0,1},{1,2},{2,3},{3,4},{4,5},{5,6},{6,7},{7,8},{8,9},{9,10},{10,1... | collective-permute-start | bytes 768008 | tf_op jit(solution)/shard_map/ppermute | solution.py:261
  8.8 6.0 %collective-permute-start.1 = (bf16[2,500,128]{2,1,0:T(8,128)(2,1)S(1)}, bf16[2,500,128]{2,1,0:T(8,128)(2,1)S(1)}, u32[]{:S(2)}, u32[]{:S(2)}) collective-permute-start(bf16[2,500,128]{2,1,0:T(8,128)(2,1)S(1)} %get-tuple-element.15), channel_id=1, source_target_pairs={{1,0},{2,1},{3,2},{4,3},{5,4},{6,5},{7,6},{8,7},{9,8},{10,9},{11,1... | collective-permute-start | bytes 768008 | tf_op jit(solution)/shard_map/ppermute | solution.py:261
  14.7 0.7 broadcast_compare_fusion
  15.5 0.1 iota_compare_fusion.1
  15.5 0.8 pad_dynamic-slice_fusion
  16.3 0.1 slice.19
  16.4 0.2 select_reduce_fusion
  16.6 0.9 %fusion.2 = s32[4,2,3]{0,2,1:T(4,128)S(1)} fusion(s32[4,2,3]{0,2,1:T(4,128)S(1)} %select_reduce_fusion, s32[3]{0:T(128)} %constant.158, s32[3]{0:T(128)} %constant.155, s32[3]{0:T(128)} %constant.153, s32[4,3]{0,1:T(4,128)S(1)} %slice.19), kind=kLoop, calls=%fused_computation.8 | loop fusion | flops 240 | bytes 276 | tf_op jit(solution)/shard_map/jit(clip)/min | solution.py:316
  17.5 0.1 copy.21
  17.6 0.1 reshape.114
  17.7 0.2 convert_reduce_fusion.1
  17.9 0.8 fusion.8
  18.6 2.0 %concatenate.7.tab_ref = s32[36]{0:T(128)S(1)} concatenate(s32[1]{0:T(128)} %bitcast, s32[32]{0:T(128)S(1)} %reshape.114, s32[1]{0:T(128)} %bitcast.3, s32[1]{0:T(128)} %bitcast.4, s32[1]{0:T(128)} %bitcast.5), dimensions={0} | concatenate | bytes 288 | tf_op jit(solution)/shard_map/concatenate | solution.py:338
  20.6 0.0 copy-start.2
  20.6 1.2 %copy-done.2 = bf16[2,4,64000]{2,1,0:T(4,128)(2,1)S(1)} copy-done((bf16[2,4,64000]{2,1,0:T(4,128)(2,1)S(1)}, bf16[2,4,64000]{2,1,0:T(4,128)(2,1)}, u32[]{:S(2)}) %copy-start.2) | copy-done | bytes 1024024
  21.8 0.0 copy-start.3
  21.8 1.0 %copy-done.3 = f32[40,1792]{1,0:T(8,128)S(1)} copy-done((f32[40,1792]{1,0:T(8,128)S(1)}, f32[40,1792]{1,0:T(8,128)}, u32[]{:S(2)}) %copy-start.3) | copy-done | bytes 286744
  22.8 0.0 copy-start.4
  22.8 1.0 %copy-done.4 = f32[40,1792]{1,0:T(8,128)S(1)} copy-done((f32[40,1792]{1,0:T(8,128)S(1)}, f32[40,1792]{1,0:T(8,128)}, u32[]{:S(2)}) %copy-start.4) | copy-done | bytes 286744
  23.7 2.1 %prepare.1 = (f32[4,2,13,40,128]{4,3,2,1,0:T(8,128)S(1)}, bf16[1664,1792]{1,0:T(8,128)(2,1)S(1)}) custom-call(bf16[2,4,64000]{2,1,0:T(4,128)(2,1)S(1)} %copy-done.2, f32[40,1792]{1,0:T(8,128)S(1)} %copy-done.4, f32[40,1792]{1,0:T(8,128)S(1)} %copy-done.3), custom_call_target="tpu_custom_call" | custom-call | flops 10000000 | bytes 10000000 | tf_op jit(solution)/shard_map/prepare/pallas_call | solution.py:294
  25.8 0.0 copy-start
  25.8 2.5 %copy-done = bf16[1664,1792]{1,0:T(8,128)(2,1)} copy-done((bf16[1664,1792]{1,0:T(8,128)(2,1)}, bf16[1664,1792]{1,0:T(8,128)(2,1)S(1)}, u32[]{:S(2)}) %copy-start) | copy-done | bytes 5963800
  28.3 0.0 collective-permute-done.prev_ref
  28.3 0.0 collective-permute-done.1.next_ref
  28.4 0.0 copy-start.5
  28.4 1.0 %copy-done.5 = f32[40,1792]{1,0:T(8,128)S(1)} copy-done((f32[40,1792]{1,0:T(8,128)S(1)}, f32[40,1792]{1,0:T(8,128)}, u32[]{:S(2)}) %copy-start.5) | copy-done | bytes 286744
  29.3 0.0 copy-start.6
  29.3 0.9 %copy-done.6 = bf16[160,160]{1,0:T(8,128)(2,1)S(1)} copy-done((bf16[160,160]{1,0:T(8,128)(2,1)S(1)}, bf16[160,160]{1,0:T(8,128)(2,1)}, u32[]{:S(2)}) %copy-start.6) | copy-done | bytes 51224
  30.2 19.0 %pairs.1 = (f32[4,1000,128]{2,1,0:T(8,128)S(1)}, bf16[1,1000,128]{2,1,0:T(8,128)(2,1)S(1)}, bf16[2,1000,128]{2,1,0:T(8,128)(2,1)S(1)}) custom-call(s32[36]{0:T(128)S(1)} %concatenate.7.tab_ref, f32[4,2,13,40,128]{4,3,2,1,0:T(8,128)S(1)} %get-tuple-element.12.own_ref, bf16[1664,1792]{1,0:T(8,128)(2,1)} %copy-done, ...), custom_call_target="tpu_custom_call" | custom-call | tf_op jit(solution)/shard_map/pairs/pallas_call | solution.py:343
  49.2 2.8 %collective-permute-start.3 = (bf16[2,1000,128]{2,1,0:T(8,128)(2,1)S(1)}, bf16[2,1000,128]{2,1,0:T(8,128)(2,1)S(1)}, u32[]{:S(2)}, u32[]{:S(2)}) collective-permute-start(bf16[2,1000,128]{2,1,0:T(8,128)(2,1)S(1)} %get-tuple-element.18), channel_id=1, source_target_pairs={{1,0},{2,1},{3,2},{4,3},{5,4},{6,5},{7,6},{8,7},{9,8},{10,9},{11,1... | collective-permute-start | bytes 1536008 | tf_op jit(solution)/shard_map/ppermute | solution.py:261
  52.0 3.0 %collective-permute-start.2 = (bf16[1,1000,128]{2,1,0:T(8,128)(2,1)S(1)}, bf16[1,1000,128]{2,1,0:T(8,128)(2,1)S(1)}, u32[]{:S(2)}, u32[]{:S(2)}) collective-permute-start(bf16[1,1000,128]{2,1,0:T(8,128)(2,1)S(1)} %get-tuple-element.17), channel_id=1, source_target_pairs={{0,1},{1,2},{2,3},{3,4},{4,5},{5,6},{6,7},{7,8},{8,9},{9,10},{10,1... | collective-permute-start | bytes 768008 | tf_op jit(solution)/shard_map/ppermute | solution.py:261
  55.1 0.1 select_reduce_fusion.1
  55.2 13.5 %collective-permute-done.2.prev_ref = bf16[1,1000,128]{2,1,0:T(8,128)(2,1)S(1)} collective-permute-done((bf16[1,1000,128]{2,1,0:T(8,128)(2,1)S(1)}, bf16[1,1000,128]{2,1,0:T(8,128)(2,1)S(1)}, u32[]{:S(2)}, u32[]{:S(2)}) %collective-permute-start.2) | collective-permute-done | bytes 256032 | tf_op jit(solution)/shard_map/ppermute | solution.py:261
  68.7 0.7 collective-permute-done.3.next_ref
  69.4 1.1 %place.1 = f32[7,1000,128]{2,1,0:T(8,128)S(1)} custom-call(s32[7]{0:T(128)S(1)} %broadcast_add_fusion.code_ref, f32[4,1000,128]{2,1,0:T(8,128)S(1)} %get-tuple-element.16.own_ref, bf16[1,1000,128]{2,1,0:T(8,128)(2,1)S(1)} %collective-permute-done.2.prev_ref, bf16[2,1000,128]{2,1,0:T(8,128)(2,1)S(1)} %collective-permute-done.3.next_ref), custom_call_target="tpu_custom_call" | custom-call | tf_op jit(solution)/shard_map/place/pallas_call | solution.py:364
  70.5 2.0 %copy.24 = f32[7,500,2,128]{3,1,2,0:T(8,128)} copy(f32[7,500,2,128]{3,2,1,0:T(2,128)S(1)} %bitcast.15) | data formatting | bytes 7168000 | tf_op jit(solution)/shard_map/reshape | solution.py:373
  72.5 6.9 %reshape.116 = f32[2,7,64000]{2,0,1:T(2,128)} reshape(f32[2,7,500,128]{3,2,0,1:T(8,128)} %bitcast.16) | data formatting | bytes 7168000 | tf_op jit(solution)/shard_map/reshape | solution.py:374
  (4 shorter events, 0.0 us)
Async XLA Ops:
  2.8 1.2 %copy-start.1 = (bf16[2,4,64000]{2,1,0:T(4,128)(2,1)S(1)}, bf16[2,4,64000]{2,1,0:T(4,128)(2,1)}, u32[]{:S(2)}) copy-start(bf16[2,4,64000]{2,1,0:T(4,128)(2,1)} %orb_ref.3) | copy-start | bytes 3072004
  5.3 23.1 %collective-permute-start = (bf16[2,500,128]{2,1,0:T(8,128)(2,1)S(1)}, bf16[2,500,128]{2,1,0:T(8,128)(2,1)S(1)}, u32[]{:S(2)}, u32[]{:S(2)}) collective-permute-start(bf16[2,500,128]{2,1,0:T(8,128)(2,1)S(1)} %get-tuple-element.14), channel_id=1, source_target_pairs={{0,1},{1,2},{2,3},{3,4},{4,5},{5,6},{6,7},{7,8},{8,9},{9,10},{10,1... | collective-permute-start | bytes 768008 | tf_op jit(solution)/shard_map/ppermute | solution.py:261
  8.8 19.6 %collective-permute-start.1 = (bf16[2,500,128]{2,1,0:T(8,128)(2,1)S(1)}, bf16[2,500,128]{2,1,0:T(8,128)(2,1)S(1)}, u32[]{:S(2)}, u32[]{:S(2)}) collective-permute-start(bf16[2,500,128]{2,1,0:T(8,128)(2,1)S(1)} %get-tuple-element.15), channel_id=1, source_target_pairs={{1,0},{2,1},{3,2},{4,3},{5,4},{6,5},{7,6},{8,7},{9,8},{10,9},{11,1... | collective-permute-start | bytes 768008 | tf_op jit(solution)/shard_map/ppermute | solution.py:261
  20.6 1.2 %copy-start.2 = (bf16[2,4,64000]{2,1,0:T(4,128)(2,1)S(1)}, bf16[2,4,64000]{2,1,0:T(4,128)(2,1)}, u32[]{:S(2)}) copy-start(bf16[2,4,64000]{2,1,0:T(4,128)(2,1)} %orb_ref.3) | copy-start | bytes 3072004
  21.8 1.0 %copy-start.3 = (f32[40,1792]{1,0:T(8,128)S(1)}, f32[40,1792]{1,0:T(8,128)}, u32[]{:S(2)}) copy-start(f32[40,1792]{1,0:T(8,128)} %constant.128.clone.til_ref) | copy-start | bytes 860164
  22.8 1.0 %copy-start.4 = (f32[40,1792]{1,0:T(8,128)S(1)}, f32[40,1792]{1,0:T(8,128)}, u32[]{:S(2)}) copy-start(f32[40,1792]{1,0:T(8,128)} %constant.127.clone.rep_ref) | copy-start | bytes 860164
  25.8 2.5 %copy-start = (bf16[1664,1792]{1,0:T(8,128)(2,1)}, bf16[1664,1792]{1,0:T(8,128)(2,1)S(1)}, u32[]{:S(2)}) copy-start(bf16[1664,1792]{1,0:T(8,128)(2,1)S(1)} %get-tuple-element.13.kron_ref) | copy-start | bytes 17891332
  28.4 1.0 %copy-start.5 = (f32[40,1792]{1,0:T(8,128)S(1)}, f32[40,1792]{1,0:T(8,128)}, u32[]{:S(2)}) copy-start(f32[40,1792]{1,0:T(8,128)} %constant.131.clone.inv_ref) | copy-start | bytes 860164
  29.3 0.9 %copy-start.6 = (bf16[160,160]{1,0:T(8,128)(2,1)S(1)}, bf16[160,160]{1,0:T(8,128)(2,1)}, u32[]{:S(2)}) copy-start(bf16[160,160]{1,0:T(8,128)(2,1)} %constant.130.clone.diag_ref) | copy-start | bytes 153604
  49.2 20.2 %collective-permute-start.3 = (bf16[2,1000,128]{2,1,0:T(8,128)(2,1)S(1)}, bf16[2,1000,128]{2,1,0:T(8,128)(2,1)S(1)}, u32[]{:S(2)}, u32[]{:S(2)}) collective-permute-start(bf16[2,1000,128]{2,1,0:T(8,128)(2,1)S(1)} %get-tuple-element.18), channel_id=1, source_target_pairs={{1,0},{2,1},{3,2},{4,3},{5,4},{6,5},{7,6},{8,7},{9,8},{10,9},{11,1... | collective-permute-start | bytes 1536008 | tf_op jit(solution)/shard_map/ppermute | solution.py:261
  52.0 16.7 %collective-permute-start.2 = (bf16[1,1000,128]{2,1,0:T(8,128)(2,1)S(1)}, bf16[1,1000,128]{2,1,0:T(8,128)(2,1)S(1)}, u32[]{:S(2)}, u32[]{:S(2)}) collective-permute-start(bf16[1,1000,128]{2,1,0:T(8,128)(2,1)S(1)} %get-tuple-element.17), channel_id=1, source_target_pairs={{0,1},{1,2},{2,3},{3,4},{4,5},{5,6},{6,7},{7,8},{8,9},{9,10},{10,1... | collective-permute-start | bytes 768008 | tf_op jit(solution)/shard_map/ppermute | solution.py:261

commit v2 on v1

v2 whole, which is shorter than its diff:
```python
import jax
import jax.numpy as jnp
import numpy as np
from jax import lax
from jax.experimental import pallas as pl
from jax.experimental.pallas import tpu as pltpu
from jax.sharding import PartitionSpec as P


EDGE = 40
PARTNERS = 2
GRID_X = 768
GRID_Y = 384
GRID_Z = 384
BACK = 2
AHEAD = 1
CAP = 7
SCREEN = 0.001

AXES = ("gx", "gy", "gz")
LANES = 128
FACE = EDGE * EDGE
TILES = -(-FACE // LANES)
WIDE = TILES * LANES
NCHUNK = 256
NSTEPS = -(-FACE // NCHUNK)
NWIDE = NSTEPS * NCHUNK
FLAT = EDGE ** 3 // LANES
HALF = EDGE // 2
PAIRT = 2 * FACE // LANES
PAD = 24
ROWS = EDGE + 2 * PAD
ZERO_TILES = 7
BF = jnp.bfloat16
F32 = jnp.float32


def tables():
    counter = np.arange(EDGE, dtype=np.float32) + 1.0
    angles = np.float32(np.pi) * counter[:, None] * counter[None, :] / np.float32(EDGE + 1.0)
    sine = (np.sqrt(np.float32(2.0 / (EDGE + 1.0))) * np.sin(angles)).astype(jnp.bfloat16)
    sine = sine.astype(np.float32)
    levels = 2.0 - 2.0 * np.cos(np.pi * counter.astype(np.float64) / (EDGE + 1.0))
    lam = levels[:, None, None] + levels[None, :, None] + levels[None, None, :] + SCREEN
    inverse = np.zeros((EDGE, NWIDE), np.float32)
    inverse[:, :FACE] = (1.0 / lam).reshape(EDGE, FACE)
    repeated = np.zeros((EDGE, NWIDE), np.float32)
    repeated[:, :FACE] = np.repeat(sine, EDGE, axis=1)
    tiled = np.zeros((EDGE, NWIDE), np.float32)
    tiled[:, :FACE] = np.tile(sine, (1, EDGE))
    return sine, inverse, repeated, tiled


def lane_iota():
    return lax.broadcasted_iota(jnp.int32, (1, LANES), 1)


def split_boxes(orb_ref, flat_ref, spin, boxes):
    def step(i, _):
        base = pl.multiple_of(i * PAIRT * LANES, LANES)
        x = orb_ref[spin, :, pl.ds(base, PAIRT * LANES)].astype(F32)
        for j in range(PAIRT):
            flat_ref[pl.ds(pl.multiple_of((i * PAIRT + j) * 8, 8), boxes), :] = x[:, j * LANES:(j + 1) * LANES]
        return 0

    lax.fori_loop(0, HALF, step, 0)


def flat_to_slabs(load, store):
    low = lane_iota() < LANES // 2
    rolled = None
    for t in range(PAIRT):
        x = load(t)
        if t < TILES:
            store(t, 0, x)
        if t >= TILES - 1:
            turned = pltpu.roll(x, LANES // 2, 1)
            if rolled is not None:
                store(t - TILES, 1, jnp.where(low, rolled, turned))
            rolled = turned
    store(TILES - 1, 1, rolled)


def slabs_to_flat(load, store):
    low = lane_iota() < LANES // 2
    for t in range(TILES - 1):
        store(t, load(t, 0))
    before = load(TILES - 1, 0)
    for v in range(TILES):
        turned = pltpu.roll(load(v, 1), LANES // 2, 1)
        store(TILES - 1 + v, jnp.where(low, before, turned))
        before = turned


def window_kernel(part_ref, orb_ref, *refs):
    outs, (orb, flat_ref, sems) = refs[:4], refs[4:]
    boxes = orb_ref.shape[1]
    total = part_ref.shape[1]
    device = lax.axis_index(AXES)
    copies = [pltpu.make_async_copy(orb_ref.at[spin], orb.at[spin], sems.at[spin]) for spin in range(2)]
    for copy in copies:
        copy.start()
    wanted = []
    for step in (1, -1):
        found = jnp.int32(0)
        for k in range(boxes):
            other = (device + step) * boxes + k
            inside = (other >= 0) & (other < total)
            for number in range(PARTNERS):
                local = part_ref[number, jnp.clip(other, 0, total - 1)] - device * boxes
                found = jnp.where(inside & (local >= 0) & (local < boxes), local, found)
        wanted.append(found)
    for spin in range(2):
        copies[spin].wait()
        split_boxes(orb, flat_ref, spin, boxes)
        for side in range(2):
            outs[2 * spin + side][...] = flat_ref[pl.ds(wanted[side], FLAT, stride=8), :].astype(BF)


def table_layout(boxes):
    pairs = 0
    codes = pairs + boxes * PARTNERS * 4
    slots = codes + CAP + 1
    leaves = slots + AHEAD + BACK + 1
    return pairs, codes, slots, leaves, leaves + AHEAD + BACK + 1


def prepare_kernel(dest_ref, part_ref, anc_ref, orb_ref, rep_ref, til_ref, own_ref, kron_ref, tab_ref, flat_ref):
    boxes = orb_ref.shape[1]
    total = part_ref.shape[1]
    device = lax.axis_index(AXES)
    pairs, codes, slots, leaves, _ = table_layout(boxes)
    for box in range(boxes):
        me = device * boxes + box
        for number in range(PARTNERS):
            other = part_ref[number, me]
            local = other - device * boxes
            base = pairs + (box * PARTNERS + number) * 4
            tab_ref[base] = jnp.where(local < 0, boxes, jnp.where(local >= boxes, boxes + 1, local))
            for axis, extent in enumerate((GRID_X, GRID_Y, GRID_Z)):
                moved = anc_ref[axis, other] - anc_ref[axis, me] + extent // 2
                moved = jnp.where(moved < 0, moved + extent, jnp.where(moved >= extent, moved - extent, moved))
                tab_ref[base + 1 + axis] = jnp.clip(moved - extent // 2, -(PAD - 4), PAD - 4)
    for k in range(CAP + 1):
        tab_ref[codes + k] = boxes + AHEAD + BACK
    for k in range(AHEAD + BACK + 1):
        tab_ref[slots + k] = CAP
        tab_ref[leaves + k] = 0
    count = jnp.int32(0)
    for block in range(3):
        arrived = jnp.int32(0)
        ahead, back = jnp.int32(0), jnp.int32(0)
        for k in range(boxes):
            box = (device + (block - 1)) * boxes + k
            inside = (box >= 0) & (box < total)
            goes = dest_ref[jnp.clip(box, 0, total - 1)]
            hit = inside & (goes == device)
            if block == 1:
                code = jnp.int32(k)
                leaves_ahead, leaves_back = goes == device + 1, goes == device - 1
                spare = leaves + AHEAD + BACK
                tab_ref[jnp.where(leaves_ahead, leaves + jnp.minimum(ahead, AHEAD - 1), spare)] = jnp.int32(k)
                tab_ref[jnp.where(leaves_back, leaves + AHEAD + jnp.minimum(back, BACK - 1), spare)] = jnp.int32(k)
                ahead = ahead + leaves_ahead.astype(jnp.int32)
                back = back + leaves_back.astype(jnp.int32)
            else:
                first, most = (0, AHEAD) if block == 0 else (AHEAD, BACK)
                where = first + jnp.minimum(arrived, most - 1)
                code = boxes + where
                tab_ref[jnp.where(hit, slots + where, slots + AHEAD + BACK)] = count
                arrived = arrived + hit.astype(jnp.int32)
            tab_ref[jnp.where(hit, codes + jnp.minimum(count, CAP - 1), codes + CAP)] = code
            count = count + hit.astype(jnp.int32)

    for spin in range(2):
        split_boxes(orb_ref, flat_ref, spin, boxes)

        def one(box, _):
            flat_to_slabs(
                lambda t: flat_ref[pl.ds(box + 8 * t, HALF, stride=8 * PAIRT), :],
                lambda u, parity, x: own_ref.__setitem__((box, spin, u, pl.ds(parity, HALF, stride=2), slice(None)), x),
            )
            return 0

        lax.fori_loop(0, boxes, one, 0)

    def build(i, _):
        row = pl.multiple_of(i * 2 * EDGE, 16)
        for c in range(NSTEPS):
            cols = slice(c * NCHUNK, (c + 1) * NCHUNK)
            til = til_ref[:, cols]
            first = rep_ref[pl.ds(2 * i, 1), cols] * til
            second = rep_ref[pl.ds(2 * i + 1, 1), cols] * til
            kron_ref[pl.ds(row, 2 * EDGE), cols] = jnp.concatenate([first, second], axis=0).astype(BF)
        return 0

    lax.fori_loop(0, HALF, build, 0)
    kron_ref[FACE:, :] = jnp.zeros((WIDE - FACE, NWIDE), BF)


def pair_kernel(spin, tab_ref, own_ref, kron_ref, prev_ref, next_ref, diag_ref, inv_ref,
                out_ref, sent_ahead_ref, sent_back_ref,
                pad_ref, mov_ref, x_ref, y_ref, flat_ref, res_ref):
    boxes = own_ref.shape[0]
    pairs, _, _, leaves, _ = table_layout(boxes)
    body = pl.ds(PAD, EDGE)
    lanes = lane_iota()
    rows = lax.broadcasted_iota(jnp.int32, (EDGE, 1), 0)

    def stage(box, _):
        for u in range(TILES):
            pad_ref[box, u, body, :] = own_ref[box, spin, u]
        return 0

    lax.fori_loop(0, boxes, stage, 0)
    for side, ref in ((0, prev_ref), (1, next_ref)):
        flat_ref[...] = ref[...].astype(F32)
        flat_to_slabs(
            lambda t: flat_ref[pl.ds(t, HALF, stride=PAIRT), :],
            lambda u, parity, x: pad_ref.__setitem__(
                (boxes + side, u, pl.ds(PAD + parity, HALF, stride=2), slice(None)), x),
        )

    def dense(box, _):
        places = []
        for number in range(PARTNERS):
            base = pairs + (box * PARTNERS + number) * 4
            source = tab_ref[base]
            da, db, dc = tab_ref[base + 1], tab_ref[base + 2], tab_ref[base + 3]
            offset = ZERO_TILES * LANES - (db * EDGE + dc)
            row_ok = jnp.abs(2 * (rows - da) - (EDGE - 1)) < EDGE
            places.append((source, da, db, dc, offset // LANES, offset % LANES, row_ok))
        last = [None] * PARTNERS
        for u in range(TILES + 1):
            values = []
            for number in range(PARTNERS):
                source, da, db, dc, quotient, rest, row_ok = places[number]
                tile = jnp.clip(quotient + (u - ZERO_TILES), 0, TILES - 1)
                x = pad_ref[source, tile, pl.ds(PAD - da, EDGE), :]
                turned = pltpu.roll(x, (LANES - rest) % LANES, 1)
                if u > 0:
                    cell = lanes + (u - 1) * LANES
                    b = (cell * 52429) >> 21
                    c = cell - b * EDGE
                    ok = (jnp.abs(2 * (b - db) - (EDGE - 1)) < EDGE) & (jnp.abs(2 * (c - dc) - (EDGE - 1)) < EDGE)
                    if u == TILES:
                        ok = ok & (lanes < FACE - (TILES - 1) * LANES)
                    moved = jnp.where(row_ok & ok, jnp.where(lanes < LANES - rest, last[number], turned), 0.0)
                    mov_ref[box, number, u - 1] = moved
                    values.append(own_ref[box, spin, u - 1] * moved)
                last[number] = turned
            if u > 0:
                both = jnp.concatenate(values, axis=0)
                if u == TILES:
                    both = jnp.where(lanes < FACE - (TILES - 1) * LANES, both, 0.0)
                x_ref[pl.ds(pl.multiple_of(box * PARTNERS * EDGE, 16), PARTNERS * EDGE),
                      (u - 1) * LANES:u * LANES] = both.astype(BF)
        return 0

    lax.fori_loop(0, boxes, dense, 0)

    group = diag_ref.shape[0]
    cubes = boxes * PARTNERS
    diag = diag_ref[...]

    def first_pass(i, _):
        where = pl.ds(pl.multiple_of(i * group, 16), group)
        y_ref[where, :WIDE] = jnp.dot(diag, x_ref[where, :WIDE], preferred_element_type=F32).astype(BF)
        return 0

    lax.fori_loop(0, cubes * EDGE // group, first_pass, 0)

    def forward(n, _):
        cols = pl.ds(pl.multiple_of(n * NCHUNK, NCHUNK), NCHUNK)
        z = jnp.dot(y_ref[:, :WIDE], kron_ref[:, cols], preferred_element_type=F32)
        z = z.reshape(cubes, EDGE, NCHUNK) * inv_ref[:, cols][None]
        x_ref[:, cols] = z.reshape(cubes * EDGE, NCHUNK).astype(BF)
        return 0

    lax.fori_loop(0, NSTEPS, forward, 0)

    def backward(n, _):
        cols = pl.ds(pl.multiple_of(n * NCHUNK, NCHUNK), NCHUNK)
        y_ref[:, cols] = jnp.dot(x_ref[:, :WIDE], kron_ref[:, cols], preferred_element_type=F32).astype(BF)
        return 0

    lax.fori_loop(0, NSTEPS, backward, 0)

    held = group // (PARTNERS * EDGE)

    def finish(i, _):
        where = pl.ds(pl.multiple_of(i * group, 16), group)
        for u in range(TILES):
            potential = jnp.dot(diag, y_ref[where, u * LANES:(u + 1) * LANES], preferred_element_type=F32)
            for k in range(held):
                total = 0.0
                for number in range(PARTNERS):
                    first = (k * PARTNERS + number) * EDGE
                    total = total + potential[first:first + EDGE] * mov_ref[i * held + k, number, u]
                res_ref[k, u] = total
        for k in range(held):
            slabs_to_flat(
                lambda u, parity: res_ref[k, u, pl.ds(parity, HALF, stride=2), :],
                lambda t, x: out_ref.__setitem__((i * held + k, pl.ds(t, HALF, stride=PAIRT), slice(None)), x),
            )
        return 0

    lax.fori_loop(0, boxes // held, finish, 0)
    for k in range(AHEAD):
        sent_ahead_ref[k] = out_ref[tab_ref[leaves + k]].astype(BF)
    for k in range(BACK):
        sent_back_ref[k] = out_ref[tab_ref[leaves + AHEAD + k]].astype(BF)


def interleave(out, both_ref, load):
    for spin in range(2):
        both_ref[pl.ds(spin, FLAT, stride=2), :] = load(spin)

    def step(i, _):
        base = pl.multiple_of(i * PAIRT * LANES, LANES)
        chunk = both_ref[pl.ds(pl.multiple_of(i * 2 * PAIRT, 2), 2 * PAIRT), :]
        for j in range(PAIRT):
            out[:, pl.ds(pl.multiple_of(base + j * LANES, LANES), LANES)] = chunk[2 * j:2 * j + 2]
        return 0

    lax.fori_loop(0, HALF, step, 0)


def keep_kernel(tab_ref, low_ref, high_ref, out_ref, both_ref):
    boxes = low_ref.shape[0]
    code = tab_ref[table_layout(boxes)[1] + pl.program_id(0)]

    @pl.when(code < boxes)
    def _():
        box = jnp.minimum(code, boxes - 1)
        interleave(out_ref.at[0], both_ref, lambda spin: (low_ref, high_ref)[spin][box])

    @pl.when(code >= boxes + AHEAD + BACK)
    def _():
        out_ref[...] = jnp.zeros_like(out_ref)


def place_kernel(boxes, tab_ref, prev_low, next_low, prev_high, next_high, kept_ref, out_ref, form_ref, both_ref, sems):
    slots = table_layout(boxes)[2]
    copies = []
    for k in range(AHEAD + BACK):
        pair, row = ((prev_low, prev_high), k) if k < AHEAD else ((next_low, next_high), k - AHEAD)
        slot = tab_ref[slots + k]
        copy = pltpu.make_async_copy(form_ref.at[k], out_ref.at[jnp.minimum(slot, CAP - 1)], sems.at[k])

        @pl.when(slot < CAP)
        def _():
            interleave(form_ref.at[k], both_ref, lambda spin: pair[spin][row].astype(F32))
            copy.start()

        copies.append((slot, copy))
    for slot, copy in copies:
        @pl.when(slot < CAP)
        def _():
            copy.wait()


def from_behind(value, steps):
    count = lax.axis_size(AXES)
    initial, last = (max(0, -steps), min(count, count - steps))
    return lax.ppermute(value, AXES, [(source, source + steps) for source in range(initial, last)])


def whole(count):
    return [pl.BlockSpec(memory_space=pltpu.VMEM)] * count


SCALARS = pl.BlockSpec(memory_space=pltpu.SMEM)
ANYWHERE = pl.BlockSpec(memory_space=pltpu.MemorySpace.HBM)


def cost(flops, size):
    return pl.CostEstimate(flops=flops, bytes_accessed=size, transcendentals=0)


def shards(orbitals, dest, partners, anchors):
    boxes = orbitals.shape[1]
    sine, inverse, repeated, tiled = tables()
    partners_t, anchors_t = partners.T, anchors.T

    windows = pl.pallas_call(
        window_kernel,
        out_shape=[jax.ShapeDtypeStruct((FLAT, LANES), BF)] * 4,
        in_specs=[SCALARS, ANYWHERE],
        out_specs=whole(4),
        scratch_shapes=[pltpu.VMEM(orbitals.shape, BF), pltpu.VMEM((FLAT * 8, LANES), F32),
                        pltpu.SemaphoreType.DMA((2,))],
        compiler_params=pltpu.CompilerParams(vmem_limit_bytes=8 << 20),
        name="window",
    )(partners_t, orbitals)
    halos = []
    for spin in range(2):
        ahead = from_behind(windows[2 * spin], 1)
        back = from_behind(windows[2 * spin + 1], -1)
        halos.append((ahead, back))

    own, kron, table = pl.pallas_call(
        prepare_kernel,
        out_shape=[jax.ShapeDtypeStruct((boxes, 2, TILES, EDGE, LANES), F32),
                   jax.ShapeDtypeStruct((WIDE, NWIDE), BF),
                   jax.ShapeDtypeStruct((table_layout(boxes)[-1],), jnp.int32)],
        in_specs=[SCALARS] * 3 + whole(3),
        out_specs=whole(2) + [SCALARS],
        scratch_shapes=[pltpu.VMEM((FLAT * 8, LANES), F32)],
        compiler_params=pltpu.CompilerParams(vmem_limit_bytes=14 << 20),
        cost_estimate=cost(10_000_000, 10_000_000),
        name="prepare",
    )(dest, partners_t, anchors_t, orbitals, repeated, tiled)

    held = 2 if boxes % 2 == 0 else 1
    diag = np.kron(np.eye(held * PARTNERS, dtype=np.float32), sine).astype(jnp.bfloat16)
    cubes = boxes * PARTNERS
    terms, arrived = [], []
    for spin in range(2):
        solve = pl.pallas_call(
            lambda *refs, spin=spin: pair_kernel(spin, *refs),
            out_shape=[jax.ShapeDtypeStruct((boxes, FLAT, LANES), F32),
                       jax.ShapeDtypeStruct((AHEAD, FLAT, LANES), BF),
                       jax.ShapeDtypeStruct((BACK, FLAT, LANES), BF)],
            in_specs=[SCALARS] + whole(6),
            out_specs=whole(3),
            scratch_shapes=[
                pltpu.VMEM((boxes + 2, TILES, ROWS, LANES), F32),
                pltpu.VMEM((boxes, PARTNERS, TILES, EDGE, LANES), F32),
                pltpu.VMEM((cubes * EDGE, NWIDE), BF),
                pltpu.VMEM((cubes * EDGE, NWIDE), BF),
                pltpu.VMEM((FLAT, LANES), F32),
                pltpu.VMEM((held, TILES, EDGE, LANES), F32),
            ],
            compiler_params=pltpu.CompilerParams(vmem_limit_bytes=24 << 20),
            cost_estimate=cost(4 * cubes * EDGE * FACE * FACE, 10_000_000),
        )
        mine, sent_ahead, sent_back = solve(table, own, kron, *halos[spin], diag, inverse)
        terms.append(mine)
        ahead = from_behind(sent_ahead, 1)
        back = from_behind(sent_back, -1)
        arrived += [ahead, back]

    shape = jax.ShapeDtypeStruct((CAP, 2, FLAT * LANES), F32)
    kept = pl.pallas_call(
        keep_kernel,
        out_shape=shape,
        grid=(CAP,),
        in_specs=[SCALARS] + whole(2),
        out_specs=pl.BlockSpec((1, 2, FLAT * LANES), lambda i: (i, 0, 0)),
        scratch_shapes=[pltpu.VMEM((2 * FLAT, LANES), F32)],
        compiler_params=pltpu.CompilerParams(vmem_limit_bytes=8 << 20),
        cost_estimate=cost(1_000_000, 8_000_000),
        name="keep",
    )(table, *terms)
    placed = pl.pallas_call(
        lambda *refs: place_kernel(boxes, *refs),
        out_shape=shape,
        in_specs=[SCALARS] + whole(4) + [ANYWHERE],
        out_specs=ANYWHERE,
        scratch_shapes=[pltpu.VMEM((AHEAD + BACK, 2, FLAT * LANES), F32), pltpu.VMEM((2 * FLAT, LANES), F32),
                        pltpu.SemaphoreType.DMA((AHEAD + BACK,))],
        input_output_aliases={5: 0},
        compiler_params=pltpu.CompilerParams(vmem_limit_bytes=8 << 20),
        cost_estimate=cost(1_000_000, 4_000_000),
        name="place",
    )(table, *arrived, kept)
    return jnp.transpose(placed, (1, 0, 2))


def solution(mesh):
    return jax.shard_map(
        shards,
        mesh=mesh,
        in_specs=(P(None, AXES, None), P(), P(), P()),
        out_specs=P(None, AXES, None),
        check_vma=False,
    )
```

time: 80.1 us -> 75.4 us (0.941)
  starting transfers between devices: 15.3 us -> 30.6 us
  waiting for transfers between devices: 14.2 us -> 2.01 us
  local copies, waits for them, and re-layouts: 20.6 us -> 8.88 us
  Pallas kernels: 23.4 us -> 33 us
  other arithmetic: 5.81 us -> 0 us
    ppermute x4 -> x8, starting transfers between devices: 15.3 us -> 30.6 us  [from_behind(): lax.ppermute(value, AXES, [(source, source + steps) for source in range(i...]
    ppermute x4 -> x8, waiting for transfers between devices: 14.2 us -> 2.01 us  [from_behind(): lax.ppermute(value, AXES, [(source, source + steps) for source in range(i...]
    reshape x3 -> x0, local copies, waits for them, and re-layouts: 8.98 us -> none  [the longest x1 6.88 us: shards(): return placed.transpose(2, 0, 1, 3).reshape(2, CAP, FLAT * LANES)]
    pallas_call x3 -> x5, Pallas kernels: 21.3 us -> 29.5 us  [the longest x2 20.3 us: shards(): solve(table, own, kron, *halos[spin], diag, inverse)]
    concatenate x2 -> x0, local copies, waits for them, and re-layouts: 2.06 us -> none  [the longest x1 1.96 us: shards(): jnp.concatenate([device[None].astype(jnp.int32), pair_table, jnp.stack(le...]
    select_n x3 -> x0, other arithmetic: 1.48 us -> none  [the longest x1 0.75 us: shards(): mine = jnp.where((local >= 0) & (local < boxes), local, 0)]
    pallas_call x1, Pallas kernels: 2.06 us -> 3.46 us  [shards(): pl.pallas_call(prepare_kernel, out_shape=[jax.ShapeDtypeStruct((boxes, 2,...]
    another operation x1 -> x0, other arithmetic: 1.32 us -> none  [shards(): jnp.stack([jnp.max(mine[2 * boxes:]), jnp.max(mine[:boxes])])]
  transfers between devices with their start and end apart: 4 -> 8, of which waited for: 2 -> 1; matrix products, arithmetic and copies ran while one was open for 8% -> 0% of each run, Pallas kernels for 3% -> 38%
where the time goes in v2:
time: 75.4 us; the launch traced here: 74.6 us
  Pallas kernels  33 us (44%)
  starting transfers between devices  30.6 us (41%)
  local copies, waits for them, and re-layouts  8.88 us (12%)
  waiting for transfers between devices  2.01 us (3%)
    ppermute x8, starting transfers between devices, from_behind(): lax.ppermute(value, AXES, [(source, source + steps) for source in range(i...  30.6 us
    pallas_call x2, Pallas kernels, shards(): solve(table, own, kron, *halos[spin], diag, inverse)  20.3 us
    unnamed x24, local copies, waits for them, and re-layouts  8.88 us
    pallas_call x1, Pallas kernels, shards(): pl.pallas_call(keep_kernel, out_shape=shape, grid=(CAP,), in_specs=[SCALA...  4.51 us
    pallas_call x1, Pallas kernels, shards(): pl.pallas_call(prepare_kernel, out_shape=[jax.ShapeDtypeStruct((boxes, 2,...  3.46 us
    pallas_call x1, Pallas kernels, shards(): pl.pallas_call(lambda *refs: place_kernel(boxes, *refs), out_shape=shape,...  2.71 us
    pallas_call x1, Pallas kernels, shards(): pl.pallas_call(window_kernel, out_shape=[jax.ShapeDtypeStruct((FLAT, LANE...  2.04 us
    ppermute x8, waiting for transfers between devices, from_behind(): lax.ppermute(value, AXES, [(source, source + steps) for source in range(i...  2.01 us
  transfers between devices with their start and end apart: 8, of which 1 were waited for; matrix products, arithmetic and copies ran while one was open for 0% of the time, Pallas kernels for 38%

profile of v2, /device:TPU:4, one launch (start us, length us, event | category | flops | bytes accessed | tf_op | source)
XLA Modules:
  0.0 74.6 jit_solution(9023253984755633726)
XLA Ops:
  0.0 0.0 copy-start
  0.0 1.2 %copy-done = bf16[2,4,64000]{2,1,0:T(4,128)(2,1)S(1)} copy-done((bf16[2,4,64000]{2,1,0:T(4,128)(2,1)S(1)}, bf16[2,4,64000]{2,1,0:T(4,128)(2,1)}, u32[]{:S(2)}) %copy-start) | copy-done | bytes 1024024
  1.2 0.0 copy-start.4
  1.2 0.7 copy-done.4
  1.9 2.0 %window.1 = (bf16[500,128]{1,0:T(8,128)(2,1)S(1)}, bf16[500,128]{1,0:T(8,128)(2,1)S(1)}, bf16[500,128]{1,0:T(8,128)(2,1)S(1)}, bf16[500,128]{1,0:T(8,128)(2,1)S(1)}) custom-call(s32[2,128]{1,0:T(2,128)S(1)} %bitcast.3, bf16[2,4,64000]{2,1,0:T(4,128)(2,1)S(1)} %copy-done), custom_call_target="tpu_custom_call" | custom-call | tf_op jit(solution)/shard_map/window/pallas_call | solution.py:386
  3.9 3.5 %collective-permute-start.4 = (bf16[500,128]{1,0:T(8,128)(2,1)S(1)}, bf16[500,128]{1,0:T(8,128)(2,1)S(1)}, u32[]{:S(2)}, u32[]{:S(2)}) collective-permute-start(bf16[500,128]{1,0:T(8,128)(2,1)S(1)} %get-tuple-element.25), channel_id=1, source_target_pairs={{0,1},{1,2},{2,3},{3,4},{4,5},{5,6},{6,7},{7,8},{8,9},{9,10},{10,1... | collective-permute-start | bytes 384008 | tf_op jit(solution)/shard_map/ppermute | solution.py:366
  7.4 6.0 %collective-permute-start.5 = (bf16[500,128]{1,0:T(8,128)(2,1)S(1)}, bf16[500,128]{1,0:T(8,128)(2,1)S(1)}, u32[]{:S(2)}, u32[]{:S(2)}) collective-permute-start(bf16[500,128]{1,0:T(8,128)(2,1)S(1)} %get-tuple-element.26), channel_id=1, source_target_pairs={{1,0},{2,1},{3,2},{4,3},{5,4},{6,5},{7,6},{8,7},{9,8},{10,9},{11,1... | collective-permute-start | bytes 384008 | tf_op jit(solution)/shard_map/ppermute | solution.py:366
  13.4 1.9 %collective-permute-start = (bf16[500,128]{1,0:T(8,128)(2,1)S(1)}, bf16[500,128]{1,0:T(8,128)(2,1)S(1)}, u32[]{:S(2)}, u32[]{:S(2)}) collective-permute-start(bf16[500,128]{1,0:T(8,128)(2,1)S(1)} %get-tuple-element.21), channel_id=1, source_target_pairs={{0,1},{1,2},{2,3},{3,4},{4,5},{5,6},{6,7},{7,8},{8,9},{9,10},{10,1... | collective-permute-start | bytes 384008 | tf_op jit(solution)/shard_map/ppermute | solution.py:366
  15.3 7.5 %collective-permute-start.1 = (bf16[500,128]{1,0:T(8,128)(2,1)S(1)}, bf16[500,128]{1,0:T(8,128)(2,1)S(1)}, u32[]{:S(2)}, u32[]{:S(2)}) collective-permute-start(bf16[500,128]{1,0:T(8,128)(2,1)S(1)} %get-tuple-element.22), channel_id=1, source_target_pairs={{1,0},{2,1},{3,2},{4,3},{5,4},{6,5},{7,6},{8,7},{9,8},{10,9},{11,1... | collective-permute-start | bytes 384008 | tf_op jit(solution)/shard_map/ppermute | solution.py:366
  22.8 0.0 copy-start.1
  22.9 1.2 %copy-done.1 = bf16[2,4,64000]{2,1,0:T(4,128)(2,1)S(1)} copy-done((bf16[2,4,64000]{2,1,0:T(4,128)(2,1)S(1)}, bf16[2,4,64000]{2,1,0:T(4,128)(2,1)}, u32[]{:S(2)}) %copy-start.1) | copy-done | bytes 1024024
  24.1 0.0 copy-start.2
  24.1 1.0 %copy-done.2 = f32[40,1792]{1,0:T(8,128)S(1)} copy-done((f32[40,1792]{1,0:T(8,128)S(1)}, f32[40,1792]{1,0:T(8,128)}, u32[]{:S(2)}) %copy-start.2) | copy-done | bytes 286744
  25.0 0.0 copy-start.3
  25.0 1.0 %copy-done.3 = f32[40,1792]{1,0:T(8,128)S(1)} copy-done((f32[40,1792]{1,0:T(8,128)S(1)}, f32[40,1792]{1,0:T(8,128)}, u32[]{:S(2)}) %copy-start.3) | copy-done | bytes 286744
  26.0 0.0 copy-start.5
  26.0 0.7 copy-done.5
  26.7 0.0 copy-start.6
  26.7 0.7 copy-done.6
  27.3 0.0 copy-start.7
  27.4 0.7 copy-done.7
  28.0 3.5 %prepare.1 = (f32[4,2,13,40,128]{4,3,2,1,0:T(8,128)S(1)}, bf16[1664,1792]{1,0:T(8,128)(2,1)S(1)}, s32[48]{0:T(128)S(1)}) custom-call(s32[128]{0:T(128)S(1)} %copy-done.7, s32[2,128]{1,0:T(2,128)S(1)} %bitcast.4, s32[3,128]{1,0:T(4,128)S(1)} %bitcast.5, bf16[2,4,64000]{2,1,0:T(4,128)(2,1)S(1)} %copy-done.1, f32[40,1792]{1,0:T(8,128)S(1)} %copy-done.3, ...), custom_call_target="tpu_custom_call" | custom-call | flops 10000000 | bytes 10000000 | tf_op jit(solution)/shard_map/prepare/pallas_call | solution.py:402
  31.5 0.0 collective-permute-done.4.refs_3_
  31.5 0.0 collective-permute-done.5.refs_4_
  31.5 0.0 copy-start.8
  31.5 0.9 %copy-done.8 = f32[40,1792]{1,0:T(8,128)S(1)} copy-done((f32[40,1792]{1,0:T(8,128)S(1)}, f32[40,1792]{1,0:T(8,128)}, u32[]{:S(2)}) %copy-start.8) | copy-done | bytes 286744
  32.5 0.0 copy-start.10
  32.5 0.9 %copy-done.10 = bf16[160,160]{1,0:T(8,128)(2,1)S(1)} copy-done((bf16[160,160]{1,0:T(8,128)(2,1)S(1)}, bf16[160,160]{1,0:T(8,128)(2,1)}, u32[]{:S(2)}) %copy-start.10) | copy-done | bytes 51224
  33.3 0.0 copy-start.9
  33.3 0.0 copy-start.11
  33.3 10.1 %shard_map.83 = (f32[4,500,128]{2,1,0:T(8,128)S(1)}, bf16[1,500,128]{2,1,0:T(8,128)(2,1)S(1)}, bf16[2,500,128]{2,1,0:T(8,128)(2,1)S(1)}) custom-call(s32[48]{0:T(128)S(1)} %get-tuple-element.18.refs_0_.tab_ref, f32[4,2,13,40,128]{4,3,2,1,0:T(8,128)S(1)} %get-tuple-element.19.refs_1_, bf16[1664,1792]{1,0:T(8,128)(2,1)S(1)} %get-tuple-element.20.refs_2_, ...), custom_call_target="tpu_custom_call" | custom-call | flops 3276800000 | bytes 10000000 | tf_op jit(solution)/shard_map/pallas_call | solution.py:438
  43.5 1.9 %collective-permute-start.7 = (bf16[2,500,128]{2,1,0:T(8,128)(2,1)S(1)}, bf16[2,500,128]{2,1,0:T(8,128)(2,1)S(1)}, u32[]{:S(2)}, u32[]{:S(2)}) collective-permute-start(bf16[2,500,128]{2,1,0:T(8,128)(2,1)S(1)} %get-tuple-element.28), channel_id=1, source_target_pairs={{1,0},{2,1},{3,2},{4,3},{5,4},{6,5},{7,6},{8,7},{9,8},{10,9},{11,1... | collective-permute-start | bytes 768008 | tf_op jit(solution)/shard_map/ppermute | solution.py:366
  45.4 0.0 collective-permute-done.refs_3_
  45.4 0.0 collective-permute-done.1.refs_4_
  45.4 0.0 copy-done.9
  45.4 0.0 copy-done.11
  45.5 10.1 %shard_map.82 = (f32[4,500,128]{2,1,0:T(8,128)S(1)}, bf16[1,500,128]{2,1,0:T(8,128)(2,1)S(1)}, bf16[2,500,128]{2,1,0:T(8,128)(2,1)S(1)}) custom-call(s32[48]{0:T(128)S(1)} %get-tuple-element.18.refs_0_.tab_ref, f32[4,2,13,40,128]{4,3,2,1,0:T(8,128)S(1)} %get-tuple-element.19.refs_1_, bf16[1664,1792]{1,0:T(8,128)(2,1)S(1)} %get-tuple-element.20.refs_2_, ...), custom_call_target="tpu_custom_call" | custom-call | flops 3276800000 | bytes 10000000 | tf_op jit(solution)/shard_map/pallas_call | solution.py:438
  55.6 1.9 %collective-permute-start.3 = (bf16[2,500,128]{2,1,0:T(8,128)(2,1)S(1)}, bf16[2,500,128]{2,1,0:T(8,128)(2,1)S(1)}, u32[]{:S(2)}, u32[]{:S(2)}) collective-permute-start(bf16[2,500,128]{2,1,0:T(8,128)(2,1)S(1)} %get-tuple-element.24), channel_id=1, source_target_pairs={{1,0},{2,1},{3,2},{4,3},{5,4},{6,5},{7,6},{8,7},{9,8},{10,9},{11,1... | collective-permute-start | bytes 768008 | tf_op jit(solution)/shard_map/ppermute | solution.py:366
  57.5 3.9 %collective-permute-start.6 = (bf16[1,500,128]{2,1,0:T(8,128)(2,1)S(1)}, bf16[1,500,128]{2,1,0:T(8,128)(2,1)S(1)}, u32[]{:S(2)}, u32[]{:S(2)}) collective-permute-start(bf16[1,500,128]{2,1,0:T(8,128)(2,1)S(1)} %get-tuple-element.27), channel_id=1, source_target_pairs={{0,1},{1,2},{2,3},{3,4},{4,5},{5,6},{6,7},{7,8},{8,9},{9,10},{10,1... | collective-permute-start | bytes 384008 | tf_op jit(solution)/shard_map/ppermute | solution.py:366
  61.5 3.9 %collective-permute-start.2 = (bf16[1,500,128]{2,1,0:T(8,128)(2,1)S(1)}, bf16[1,500,128]{2,1,0:T(8,128)(2,1)S(1)}, u32[]{:S(2)}, u32[]{:S(2)}) collective-permute-start(bf16[1,500,128]{2,1,0:T(8,128)(2,1)S(1)} %get-tuple-element.23), channel_id=1, source_target_pairs={{0,1},{1,2},{2,3},{3,4},{4,5},{5,6},{6,7},{7,8},{8,9},{9,10},{10,1... | collective-permute-start | bytes 384008 | tf_op jit(solution)/shard_map/ppermute | solution.py:366
  65.4 4.5 %keep.1.refs_5_ = f32[7,2,64000]{2,1,0:T(2,128)} custom-call(s32[48]{0:T(128)S(1)} %get-tuple-element.18.refs_0_.tab_ref, f32[4,500,128]{2,1,0:T(8,128)S(1)} %get-tuple-element.29.low_ref, f32[4,500,128]{2,1,0:T(8,128)S(1)} %get-tuple-element.30.high_ref), custom_call_target="tpu_custom_call" | custom-call | flops 1000000 | bytes 8000000 | tf_op jit(solution)/shard_map/keep/pallas_call | solution.py:445
  69.9 0.0 collective-permute-done.6.refs_3_
  69.9 2.0 %collective-permute-done.2.refs_1_ = bf16[1,500,128]{2,1,0:T(8,128)(2,1)S(1)} collective-permute-done((bf16[1,500,128]{2,1,0:T(8,128)(2,1)S(1)}, bf16[1,500,128]{2,1,0:T(8,128)(2,1)S(1)}, u32[]{:S(2)}, u32[]{:S(2)}) %collective-permute-start.2) | collective-permute-done | bytes 128032 | tf_op jit(solution)/shard_map/ppermute | solution.py:366
  71.9 0.0 collective-permute-done.7.refs_4_
  71.9 0.0 collective-permute-done.3.refs_2_
  71.9 2.7 %place.1 = f32[7,2,64000]{2,1,0:T(2,128)} custom-call(s32[48]{0:T(128)S(1)} %get-tuple-element.18.refs_0_.tab_ref, bf16[1,500,128]{2,1,0:T(8,128)(2,1)S(1)} %collective-permute-done.2.refs_1_, bf16[2,500,128]{2,1,0:T(8,128)(2,1)S(1)} %collective-permute-done.3.refs_2_, ...), custom_call_target="tpu_custom_call", output_to_operand_aliasing={{}: (5, {})} | custom-call | flops 1000000 | bytes 4000000 | tf_op jit(solution)/shard_map/place/pallas_call | solution.py:456
Async XLA Ops:
  0.0 1.2 %copy-start = (bf16[2,4,64000]{2,1,0:T(4,128)(2,1)S(1)}, bf16[2,4,64000]{2,1,0:T(4,128)(2,1)}, u32[]{:S(2)}) copy-start(bf16[2,4,64000]{2,1,0:T(4,128)(2,1)} %orb_ref.3) | copy-start | bytes 3072004
  1.2 0.7 copy-start.4
  3.9 27.5 %collective-permute-start.4 = (bf16[500,128]{1,0:T(8,128)(2,1)S(1)}, bf16[500,128]{1,0:T(8,128)(2,1)S(1)}, u32[]{:S(2)}, u32[]{:S(2)}) collective-permute-start(bf16[500,128]{1,0:T(8,128)(2,1)S(1)} %get-tuple-element.25), channel_id=1, source_target_pairs={{0,1},{1,2},{2,3},{3,4},{4,5},{5,6},{6,7},{7,8},{8,9},{9,10},{10,1... | collective-permute-start | bytes 384008 | tf_op jit(solution)/shard_map/ppermute | solution.py:366
  7.4 24.0 %collective-permute-start.5 = (bf16[500,128]{1,0:T(8,128)(2,1)S(1)}, bf16[500,128]{1,0:T(8,128)(2,1)S(1)}, u32[]{:S(2)}, u32[]{:S(2)}) collective-permute-start(bf16[500,128]{1,0:T(8,128)(2,1)S(1)} %get-tuple-element.26), channel_id=1, source_target_pairs={{1,0},{2,1},{3,2},{4,3},{5,4},{6,5},{7,6},{8,7},{9,8},{10,9},{11,1... | collective-permute-start | bytes 384008 | tf_op jit(solution)/shard_map/ppermute | solution.py:366
  13.4 32.0 %collective-permute-start = (bf16[500,128]{1,0:T(8,128)(2,1)S(1)}, bf16[500,128]{1,0:T(8,128)(2,1)S(1)}, u32[]{:S(2)}, u32[]{:S(2)}) collective-permute-start(bf16[500,128]{1,0:T(8,128)(2,1)S(1)} %get-tuple-element.21), channel_id=1, source_target_pairs={{0,1},{1,2},{2,3},{3,4},{4,5},{5,6},{6,7},{7,8},{8,9},{9,10},{10,1... | collective-permute-start | bytes 384008 | tf_op jit(solution)/shard_map/ppermute | solution.py:366
  15.3 30.1 %collective-permute-start.1 = (bf16[500,128]{1,0:T(8,128)(2,1)S(1)}, bf16[500,128]{1,0:T(8,128)(2,1)S(1)}, u32[]{:S(2)}, u32[]{:S(2)}) collective-permute-start(bf16[500,128]{1,0:T(8,128)(2,1)S(1)} %get-tuple-element.22), channel_id=1, source_target_pairs={{1,0},{2,1},{3,2},{4,3},{5,4},{6,5},{7,6},{8,7},{9,8},{10,9},{11,1... | collective-permute-start | bytes 384008 | tf_op jit(solution)/shard_map/ppermute | solution.py:366
  22.8 1.2 %copy-start.1 = (bf16[2,4,64000]{2,1,0:T(4,128)(2,1)S(1)}, bf16[2,4,64000]{2,1,0:T(4,128)(2,1)}, u32[]{:S(2)}) copy-start(bf16[2,4,64000]{2,1,0:T(4,128)(2,1)} %orb_ref.3) | copy-start | bytes 3072004
  24.1 1.0 %copy-start.2 = (f32[40,1792]{1,0:T(8,128)S(1)}, f32[40,1792]{1,0:T(8,128)}, u32[]{:S(2)}) copy-start(f32[40,1792]{1,0:T(8,128)} %constant.9.clone.til_ref) | copy-start | bytes 860164
  25.0 1.0 %copy-start.3 = (f32[40,1792]{1,0:T(8,128)S(1)}, f32[40,1792]{1,0:T(8,128)}, u32[]{:S(2)}) copy-start(f32[40,1792]{1,0:T(8,128)} %constant.8.clone.rep_ref) | copy-start | bytes 860164
  26.0 0.7 copy-start.5
  26.7 0.7 copy-start.6
  27.3 0.7 copy-start.7
  31.5 1.0 %copy-start.8 = (f32[40,1792]{1,0:T(8,128)S(1)}, f32[40,1792]{1,0:T(8,128)}, u32[]{:S(2)}) copy-start(f32[40,1792]{1,0:T(8,128)} %constant.11.clone.refs_6_) | copy-start | bytes 860164
  32.5 0.9 %copy-start.10 = (bf16[160,160]{1,0:T(8,128)(2,1)S(1)}, bf16[160,160]{1,0:T(8,128)(2,1)}, u32[]{:S(2)}) copy-start(bf16[160,160]{1,0:T(8,128)(2,1)} %constant.10.clone.refs_5_) | copy-start | bytes 153604
  33.3 12.1 %copy-start.9 = (f32[40,1792]{1,0:T(8,128)S(1)}, f32[40,1792]{1,0:T(8,128)}, u32[]{:S(2)}) copy-start(f32[40,1792]{1,0:T(8,128)} %constant.11.clone.refs_6_) | copy-start | bytes 860164
  33.3 12.1 %copy-start.11 = (bf16[160,160]{1,0:T(8,128)(2,1)S(1)}, bf16[160,160]{1,0:T(8,128)(2,1)}, u32[]{:S(2)}) copy-start(bf16[160,160]{1,0:T(8,128)(2,1)} %constant.10.clone.refs_5_) | copy-start | bytes 153604
  43.5 28.4 %collective-permute-start.7 = (bf16[2,500,128]{2,1,0:T(8,128)(2,1)S(1)}, bf16[2,500,128]{2,1,0:T(8,128)(2,1)S(1)}, u32[]{:S(2)}, u32[]{:S(2)}) collective-permute-start(bf16[2,500,128]{2,1,0:T(8,128)(2,1)S(1)} %get-tuple-element.28), channel_id=1, source_target_pairs={{1,0},{2,1},{3,2},{4,3},{5,4},{6,5},{7,6},{8,7},{9,8},{10,9},{11,1... | collective-permute-start | bytes 768008 | tf_op jit(solution)/shard_map/ppermute | solution.py:366
  55.6 16.3 %collective-permute-start.3 = (bf16[2,500,128]{2,1,0:T(8,128)(2,1)S(1)}, bf16[2,500,128]{2,1,0:T(8,128)(2,1)S(1)}, u32[]{:S(2)}, u32[]{:S(2)}) collective-permute-start(bf16[2,500,128]{2,1,0:T(8,128)(2,1)S(1)} %get-tuple-element.24), channel_id=1, source_target_pairs={{1,0},{2,1},{3,2},{4,3},{5,4},{6,5},{7,6},{8,7},{9,8},{10,9},{11,1... | collective-permute-start | bytes 768008 | tf_op jit(solution)/shard_map/ppermute | solution.py:366
  57.5 12.4 %collective-permute-start.6 = (bf16[1,500,128]{2,1,0:T(8,128)(2,1)S(1)}, bf16[1,500,128]{2,1,0:T(8,128)(2,1)S(1)}, u32[]{:S(2)}, u32[]{:S(2)}) collective-permute-start(bf16[1,500,128]{2,1,0:T(8,128)(2,1)S(1)} %get-tuple-element.27), channel_id=1, source_target_pairs={{0,1},{1,2},{2,3},{3,4},{4,5},{5,6},{6,7},{7,8},{8,9},{9,10},{10,1... | collective-permute-start | bytes 384008 | tf_op jit(solution)/shard_map/ppermute | solution.py:366
  61.5 10.4 %collective-permute-start.2 = (bf16[1,500,128]{2,1,0:T(8,128)(2,1)S(1)}, bf16[1,500,128]{2,1,0:T(8,128)(2,1)S(1)}, u32[]{:S(2)}, u32[]{:S(2)}) collective-permute-start(bf16[1,500,128]{2,1,0:T(8,128)(2,1)S(1)} %get-tuple-element.23), channel_id=1, source_target_pairs={{0,1},{1,2},{2,3},{3,4},{4,5},{5,6},{6,7},{7,8},{8,9},{9,10},{10,1... | collective-permute-start | bytes 384008 | tf_op jit(solution)/shard_map/ppermute | solution.py:366

commit v3 on v2

v3 whole, which is shorter than its diff:
```python
import jax
import jax.numpy as jnp
import numpy as np
from jax import lax
from jax.experimental import pallas as pl
from jax.experimental.pallas import tpu as pltpu
from jax.sharding import PartitionSpec as P


EDGE = 40
PARTNERS = 2
GRID_X = 768
GRID_Y = 384
GRID_Z = 384
BACK = 2
AHEAD = 1
CAP = 7
SCREEN = 0.001

AXES = ("gx", "gy", "gz")
LANES = 128
FACE = EDGE * EDGE
TILES = -(-FACE // LANES)
WIDE = TILES * LANES
NCHUNK = 256
NSTEPS = -(-FACE // NCHUNK)
NWIDE = NSTEPS * NCHUNK
FLAT = EDGE ** 3 // LANES
HALF = EDGE // 2
PAIRT = 2 * FACE // LANES
PAD = 24
ROWS = EDGE + 2 * PAD
ZERO_TILES = 7
BF = jnp.bfloat16
F32 = jnp.float32


def tables():
    counter = np.arange(EDGE, dtype=np.float32) + 1.0
    angles = np.float32(np.pi) * counter[:, None] * counter[None, :] / np.float32(EDGE + 1.0)
    sine = (np.sqrt(np.float32(2.0 / (EDGE + 1.0))) * np.sin(angles)).astype(jnp.bfloat16)
    sine = sine.astype(np.float32)
    levels = 2.0 - 2.0 * np.cos(np.pi * counter.astype(np.float64) / (EDGE + 1.0))
    lam = levels[:, None, None] + levels[None, :, None] + levels[None, None, :] + SCREEN
    inverse = np.zeros((EDGE, NWIDE), np.float32)
    inverse[:, :FACE] = (1.0 / lam).reshape(EDGE, FACE)
    repeated = np.zeros((EDGE, NWIDE), np.float32)
    repeated[:, :FACE] = np.repeat(sine, EDGE, axis=1)
    tiled = np.zeros((EDGE, NWIDE), np.float32)
    tiled[:, :FACE] = np.tile(sine, (1, EDGE))
    return sine, inverse, repeated, tiled


def lane_iota():
    return lax.broadcasted_iota(jnp.int32, (1, LANES), 1)


def split_boxes(orb_ref, flat_ref, spin, boxes):
    def step(i, _):
        base = pl.multiple_of(i * PAIRT * LANES, LANES)
        x = orb_ref[spin, :, pl.ds(base, PAIRT * LANES)].astype(F32)
        for j in range(PAIRT):
            flat_ref[pl.ds(pl.multiple_of((i * PAIRT + j) * 8, 8), boxes), :] = x[:, j * LANES:(j + 1) * LANES]
        return 0

    lax.fori_loop(0, HALF, step, 0)


def flat_to_slabs(load, store):
    low = lane_iota() < LANES // 2
    rolled = None
    for t in range(PAIRT):
        x = load(t)
        if t < TILES:
            store(t, 0, x)
        if t >= TILES - 1:
            turned = pltpu.roll(x, LANES // 2, 1)
            if rolled is not None:
                store(t - TILES, 1, jnp.where(low, rolled, turned))
            rolled = turned
    store(TILES - 1, 1, rolled)


def slabs_to_flat(load, store):
    low = lane_iota() < LANES // 2
    for t in range(TILES - 1):
        store(t, load(t, 0))
    before = load(TILES - 1, 0)
    for v in range(TILES):
        turned = pltpu.roll(load(v, 1), LANES // 2, 1)
        store(TILES - 1 + v, jnp.where(low, before, turned))
        before = turned


def window_kernel(part_ref, orb_ref, *refs):
    outs, (orb, flat_ref, sems) = refs[:2], refs[2:]
    boxes = orb_ref.shape[1]
    total = part_ref.shape[1]
    device = lax.axis_index(AXES)
    copies = [pltpu.make_async_copy(orb_ref.at[spin], orb.at[spin], sems.at[spin]) for spin in range(2)]
    for copy in copies:
        copy.start()
    wanted = []
    for step in (1, -1):
        found = jnp.int32(0)
        for k in range(boxes):
            other = (device + step) * boxes + k
            inside = (other >= 0) & (other < total)
            for number in range(PARTNERS):
                local = part_ref[number, jnp.clip(other, 0, total - 1)] - device * boxes
                found = jnp.where(inside & (local >= 0) & (local < boxes), local, found)
        wanted.append(found)
    for spin in range(2):
        copies[spin].wait()
        split_boxes(orb, flat_ref, spin, boxes)
        for side in range(2):
            outs[side][spin] = flat_ref[pl.ds(wanted[side], FLAT, stride=8), :].astype(BF)


def table_layout(boxes):
    pairs = 0
    codes = pairs + boxes * PARTNERS * 4
    slots = codes + CAP + 1
    leaves = slots + AHEAD + BACK + 1
    order = leaves + AHEAD + BACK + 1
    return pairs, codes, slots, leaves, order, order + boxes


def prepare_kernel(dest_ref, part_ref, anc_ref, orb_ref, rep_ref, pad_ref, kron_ref, tab_ref, flat_ref):
    boxes = orb_ref.shape[1]
    total = part_ref.shape[1]
    device = lax.axis_index(AXES)
    pairs, codes, slots, leaves, order, _ = table_layout(boxes)
    one, none = jnp.int32(1), jnp.int32(0)
    for k in range(CAP + 1):
        tab_ref[codes + k] = boxes + AHEAD + BACK
    for k in range(AHEAD + BACK + 1):
        tab_ref[slots + k] = CAP
        tab_ref[leaves + k] = 0
    goes = [dest_ref[device * boxes + k] for k in range(boxes)]
    ahead_all, back_all = none, none
    for k in range(boxes):
        ahead_all = ahead_all + jnp.where(goes[k] == device + 1, one, none)
        back_all = back_all + jnp.where(goes[k] == device - 1, one, none)
    ahead, back, stay = none, none, none
    spots = []
    for k in range(boxes):
        is_ahead, is_back = goes[k] == device + 1, goes[k] == device - 1
        spot = jnp.where(is_ahead, ahead, jnp.where(is_back, ahead_all + back, ahead_all + back_all + stay))
        spots.append(spot)
        tab_ref[order + spot] = k
        spare = leaves + AHEAD + BACK
        tab_ref[jnp.where(is_ahead, leaves + jnp.minimum(ahead, AHEAD - 1), spare)] = spot
        tab_ref[jnp.where(is_back, leaves + AHEAD + jnp.minimum(back, BACK - 1), spare)] = spot
        ahead = ahead + jnp.where(is_ahead, one, none)
        back = back + jnp.where(is_back, one, none)
        stay = stay + jnp.where(is_ahead | is_back, none, one)
    count = none
    for block in range(3):
        arrived = none
        for k in range(boxes):
            box = (device + (block - 1)) * boxes + k
            hit = (box >= 0) & (box < total) & (dest_ref[jnp.clip(box, 0, total - 1)] == device)
            if block == 1:
                code = spots[k]
            else:
                first, most = (0, AHEAD) if block == 0 else (AHEAD, BACK)
                where = first + jnp.minimum(arrived, most - 1)
                code = boxes + where
                tab_ref[jnp.where(hit, slots + where, slots + AHEAD + BACK)] = count
                arrived = arrived + jnp.where(hit, one, none)
            tab_ref[jnp.where(hit, codes + jnp.minimum(count, CAP - 1), codes + CAP)] = code
            count = count + jnp.where(hit, one, none)
    for box in range(boxes):
        me = device * boxes + box
        for number in range(PARTNERS):
            other = part_ref[number, me]
            local = other - device * boxes
            base = pairs + (box * PARTNERS + number) * 4
            tab_ref[base] = jnp.where(local < 0, boxes, jnp.where(local >= boxes, boxes + 1, local))
            for axis, extent in enumerate((GRID_X, GRID_Y, GRID_Z)):
                moved = anc_ref[axis, other] - anc_ref[axis, me] + extent // 2
                moved = jnp.where(moved < 0, moved + extent, jnp.where(moved >= extent, moved - extent, moved))
                tab_ref[base + 1 + axis] = jnp.clip(moved - extent // 2, -(PAD - 4), PAD - 4)

    for spin in range(2):
        split_boxes(orb_ref, flat_ref, spin, boxes)

        def slabs(box, _):
            flat_to_slabs(
                lambda t: flat_ref[pl.ds(box + 8 * t, HALF, stride=8 * PAIRT), :],
                lambda u, parity, x: pad_ref.__setitem__(
                    (box, spin, u, pl.ds(PAD + parity, HALF, stride=2), slice(None)), x),
            )
            return 0

        lax.fori_loop(0, boxes, slabs, 0)

    def build(i, _):
        row = pl.multiple_of(i * 2 * EDGE, 16)
        for c in range(NSTEPS):
            cols = slice(c * NCHUNK, (c + 1) * NCHUNK)
            til = rep_ref[1, :, cols]
            first = rep_ref[0, pl.ds(2 * i, 1), cols] * til
            second = rep_ref[0, pl.ds(2 * i + 1, 1), cols] * til
            kron_ref[pl.ds(row, 2 * EDGE), cols] = jnp.concatenate([first, second], axis=0).astype(BF)
        return 0

    lax.fori_loop(0, HALF, build, 0)
    kron_ref[FACE:, :] = jnp.zeros((WIDE - FACE, NWIDE), BF)


def fill_kernel(old_ref, prev_ref, next_ref, pad_ref, flat_ref):
    boxes = pad_ref.shape[0] - 2
    for side, ref in ((0, prev_ref), (1, next_ref)):
        for spin in range(2):
            flat_ref[...] = ref[spin].astype(F32)
            flat_to_slabs(
                lambda t: flat_ref[pl.ds(t, HALF, stride=PAIRT), :],
                lambda u, parity, x: pad_ref.__setitem__(
                    (boxes + side, spin, u, pl.ds(PAD + parity, HALF, stride=2), slice(None)), x),
            )


def pair_kernel(start, held, spins, tab_ref, pad_ref, kron_ref, diag_ref, inv_ref, out_ref, *refs):
    sends, (mov_ref, x_ref, y_ref, res_ref) = refs[:-4], refs[-4:]
    boxes = pad_ref.shape[0] - 2
    pairs, _, _, leaves, order, _ = table_layout(boxes)
    lanes = lane_iota()
    rows = lax.broadcasted_iota(jnp.int32, (EDGE, 1), 0)

    def dense(index, _):
        box = tab_ref[order + start + index]
        places = []
        for number in range(PARTNERS):
            base = pairs + (box * PARTNERS + number) * 4
            source = tab_ref[base]
            da, db, dc = tab_ref[base + 1], tab_ref[base + 2], tab_ref[base + 3]
            offset = ZERO_TILES * LANES - (db * EDGE + dc)
            row_ok = jnp.abs(2 * (rows - da) - (EDGE - 1)) < EDGE
            places.append((source, da, db, dc, offset // LANES, offset % LANES, row_ok))
        last = [[None] * PARTNERS for _ in spins]
        for u in range(TILES + 1):
            keep = []
            for number in range(PARTNERS):
                source, da, db, dc, quotient, rest, row_ok = places[number]
                if u > 0:
                    cell = lanes + (u - 1) * LANES
                    b = (cell * 52429) >> 21
                    c = cell - b * EDGE
                    ok = (jnp.abs(2 * (b - db) - (EDGE - 1)) < EDGE) & (jnp.abs(2 * (c - dc) - (EDGE - 1)) < EDGE)
                    if u == TILES:
                        ok = ok & (lanes < FACE - (TILES - 1) * LANES)
                    keep.append(row_ok & ok)
            for at, spin in enumerate(spins):
                values = []
                for number in range(PARTNERS):
                    source, da, db, dc, quotient, rest, row_ok = places[number]
                    tile = jnp.clip(quotient + (u - ZERO_TILES), 0, TILES - 1)
                    x = pad_ref[source, spin, tile, pl.ds(PAD - da, EDGE), :]
                    turned = pltpu.roll(x, (LANES - rest) % LANES, 1)
                    if u > 0:
                        moved = jnp.where(keep[number], jnp.where(lanes < LANES - rest, last[at][number], turned), 0.0)
                        mov_ref[index, at, number, u - 1] = moved
                        values.append(pad_ref[box, spin, u - 1, pl.ds(PAD, EDGE), :] * moved)
                    last[at][number] = turned
                if u > 0:
                    both = jnp.concatenate(values, axis=0)
                    if u == TILES:
                        both = jnp.where(lanes < FACE - (TILES - 1) * LANES, both, 0.0)
                    first = (index * len(spins) + at) * PARTNERS * EDGE
                    x_ref[pl.ds(pl.multiple_of(first, 16), PARTNERS * EDGE),
                          (u - 1) * LANES:u * LANES] = both.astype(BF)
        return 0

    lax.fori_loop(0, held, dense, 0)

    cubes = held * len(spins) * PARTNERS
    diag = diag_ref[...]
    for c in range(NSTEPS):
        cols = slice(c * NCHUNK, min((c + 1) * NCHUNK, WIDE))
        y_ref[:, cols] = jnp.dot(diag, x_ref[:, cols], preferred_element_type=F32).astype(BF)

    def forward(n, _):
        cols = pl.ds(pl.multiple_of(n * NCHUNK, NCHUNK), NCHUNK)
        z = jnp.dot(y_ref[:, :WIDE], kron_ref[:, cols], preferred_element_type=F32)
        z = z.reshape(cubes, EDGE, NCHUNK) * inv_ref[:, cols][None]
        x_ref[:, cols] = z.reshape(cubes * EDGE, NCHUNK).astype(BF)
        return 0

    lax.fori_loop(0, NSTEPS, forward, 0)

    def backward(n, _):
        cols = pl.ds(pl.multiple_of(n * NCHUNK, NCHUNK), NCHUNK)
        y_ref[:, cols] = jnp.dot(x_ref[:, :WIDE], kron_ref[:, cols], preferred_element_type=F32).astype(BF)
        return 0

    lax.fori_loop(0, NSTEPS, backward, 0)

    for u in range(TILES):
        potential = jnp.dot(diag, y_ref[:, u * LANES:(u + 1) * LANES], preferred_element_type=F32)
        for index in range(held):
            for at in range(len(spins)):
                total = 0.0
                for number in range(PARTNERS):
                    first = ((index * len(spins) + at) * PARTNERS + number) * EDGE
                    total = total + potential[first:first + EDGE] * mov_ref[index, at, number, u]
                res_ref[index * len(spins) + at, u] = total

    def flatten(row, _):
        slabs_to_flat(
            lambda u, parity: res_ref[row, u, pl.ds(parity, HALF, stride=2), :],
            lambda t, x: out_ref.__setitem__((row, pl.ds(t, HALF, stride=PAIRT), slice(None)), x),
        )
        return 0

    lax.fori_loop(0, held * len(spins), flatten, 0)
    if sends:
        for k in range(AHEAD):
            sends[0][k] = out_ref[tab_ref[leaves + k]].astype(BF)
        for k in range(BACK):
            sends[1][k] = out_ref[tab_ref[leaves + AHEAD + k]].astype(BF)


def interleave(out, both_ref, load):
    for spin in range(2):
        both_ref[pl.ds(spin, FLAT, stride=2), :] = load(spin)

    def step(i, _):
        base = pl.multiple_of(i * PAIRT * LANES, LANES)
        chunk = both_ref[pl.ds(pl.multiple_of(i * 2 * PAIRT, 2), 2 * PAIRT), :]
        for j in range(PAIRT):
            out[:, pl.ds(pl.multiple_of(base + j * LANES, LANES), LANES)] = chunk[2 * j:2 * j + 2]
        return 0

    lax.fori_loop(0, HALF, step, 0)


def keep_kernel(tab_ref, low_ref, high_ref, rest_ref, out_ref, both_ref):
    first = low_ref.shape[0]
    boxes = first + rest_ref.shape[0] // 2
    code = tab_ref[table_layout(boxes)[1] + pl.program_id(0)]

    @pl.when(code < first)
    def _():
        spot = jnp.minimum(code, first - 1)
        interleave(out_ref.at[0], both_ref, lambda spin: (low_ref, high_ref)[spin][spot])

    @pl.when((code >= first) & (code < boxes))
    def _():
        spot = jnp.clip(code - first, 0, boxes - first - 1)
        interleave(out_ref.at[0], both_ref, lambda spin: rest_ref[2 * spot + spin])

    @pl.when(code >= boxes + AHEAD + BACK)
    def _():
        out_ref[...] = jnp.zeros_like(out_ref)


def place_kernel(boxes, tab_ref, prev_low, next_low, prev_high, next_high, kept_ref, out_ref, form_ref, both_ref, sems):
    slots = table_layout(boxes)[2]
    copies = []
    for k in range(AHEAD + BACK):
        pair, row = ((prev_low, prev_high), k) if k < AHEAD else ((next_low, next_high), k - AHEAD)
        slot = tab_ref[slots + k]
        copy = pltpu.make_async_copy(form_ref.at[k], out_ref.at[jnp.minimum(slot, CAP - 1)], sems.at[k])

        @pl.when(slot < CAP)
        def _():
            interleave(form_ref.at[k], both_ref, lambda spin: pair[spin][row].astype(F32))
            copy.start()

        copies.append((slot, copy))
    for slot, copy in copies:
        @pl.when(slot < CAP)
        def _():
            copy.wait()


def from_behind(value, steps):
    count = lax.axis_size(AXES)
    return lax.ppermute(value, AXES, [(source, (source + steps) % count) for source in range(count)])


def whole(count):
    return [pl.BlockSpec(memory_space=pltpu.VMEM)] * count


SCALARS = pl.BlockSpec(memory_space=pltpu.SMEM)
ANYWHERE = pl.BlockSpec(memory_space=pltpu.MemorySpace.HBM)


def cost(flops, size):
    return pl.CostEstimate(flops=flops, bytes_accessed=size, transcendentals=0)


def shards(orbitals, dest, partners, anchors):
    boxes = orbitals.shape[1]
    sine, inverse, repeated, tiled = tables()
    partners_t, anchors_t = partners.T, anchors.T

    windows = pl.pallas_call(
        window_kernel,
        out_shape=[jax.ShapeDtypeStruct((2, FLAT, LANES), BF)] * 2,
        in_specs=[SCALARS, ANYWHERE],
        out_specs=whole(2),
        scratch_shapes=[pltpu.VMEM(orbitals.shape, BF), pltpu.VMEM((FLAT * 8, LANES), F32),
                        pltpu.SemaphoreType.DMA((2,))],
        compiler_params=pltpu.CompilerParams(vmem_limit_bytes=66_300_000),
        name="window",
    )(partners_t, orbitals)
    from_prev = from_behind(windows[0], 1)
    from_next = from_behind(windows[1], -1)

    slabs = jax.ShapeDtypeStruct((boxes + 2, 2, TILES, ROWS, LANES), F32)
    pad, kron, table = pl.pallas_call(
        prepare_kernel,
        out_shape=[slabs,
                   jax.ShapeDtypeStruct((WIDE, NWIDE), BF),
                   jax.ShapeDtypeStruct((table_layout(boxes)[-1],), jnp.int32)],
        in_specs=[SCALARS] * 3 + whole(2),
        out_specs=whole(2) + [SCALARS],
        scratch_shapes=[pltpu.VMEM((FLAT * 8, LANES), F32)],
        compiler_params=pltpu.CompilerParams(vmem_limit_bytes=20 << 20),
        cost_estimate=cost(10_000_000, 10_000_000),
        name="prepare",
    )(dest, partners_t, anchors_t, orbitals, np.stack([repeated, tiled]))
    pad = pl.pallas_call(
        fill_kernel,
        out_shape=slabs,
        in_specs=whole(3),
        out_specs=pl.BlockSpec(memory_space=pltpu.VMEM),
        scratch_shapes=[pltpu.VMEM((FLAT, LANES), F32)],
        input_output_aliases={0: 0},
        compiler_params=pltpu.CompilerParams(vmem_limit_bytes=12 << 20),
        cost_estimate=cost(1_000_000, 2_000_000),
        name="fill",
    )(pad, from_prev, from_next)

    moving = AHEAD + BACK

    def solve(start, held, spins, send):
        cubes = held * len(spins) * PARTNERS
        diag = np.kron(np.eye(cubes, dtype=np.float32), sine).astype(jnp.bfloat16)
        shapes = [jax.ShapeDtypeStruct((held * len(spins), FLAT, LANES), F32)]
        if send:
            shapes += [jax.ShapeDtypeStruct((count, FLAT, LANES), BF) for count in (AHEAD, BACK)]
        return pl.pallas_call(
            lambda *refs: pair_kernel(start, held, spins, *refs),
            out_shape=shapes,
            in_specs=[SCALARS] + whole(4),
            out_specs=whole(len(shapes)),
            scratch_shapes=[
                pltpu.VMEM((held, len(spins), PARTNERS, TILES, EDGE, LANES), F32),
                pltpu.VMEM((cubes * EDGE, NWIDE), BF),
                pltpu.VMEM((cubes * EDGE, NWIDE), BF),
                pltpu.VMEM((held * len(spins), TILES, EDGE, LANES), F32),
            ],
            compiler_params=pltpu.CompilerParams(vmem_limit_bytes=20 << 20),
            cost_estimate=cost(4 * cubes * EDGE * FACE * FACE, 10_000_000),
        )(table, pad, kron, diag, inverse)

    terms, arrived = [], []
    for spin in range(2):
        mine, sent_ahead, sent_back = solve(0, moving, (spin,), True)
        terms.append(mine)
        ahead = from_behind(sent_ahead, 1)
        back = from_behind(sent_back, -1)
        arrived += [ahead, back]
    terms += solve(moving, boxes - moving, (0, 1), False)

    shape = jax.ShapeDtypeStruct((CAP, 2, FLAT * LANES), F32)
    kept = pl.pallas_call(
        keep_kernel,
        out_shape=shape,
        grid=(CAP,),
        in_specs=[SCALARS] + whole(3),
        out_specs=pl.BlockSpec((1, 2, FLAT * LANES), lambda i: (i, 0, 0)),
        scratch_shapes=[pltpu.VMEM((2 * FLAT, LANES), F32)],
        compiler_params=pltpu.CompilerParams(vmem_limit_bytes=8 << 20),
        cost_estimate=cost(1_000_000, 8_000_000),
        name="keep",
    )(table, *terms)
    placed = pl.pallas_call(
        lambda *refs: place_kernel(boxes, *refs),
        out_shape=shape,
        in_specs=[SCALARS] + whole(4) + [ANYWHERE],
        out_specs=ANYWHERE,
        scratch_shapes=[pltpu.VMEM((AHEAD + BACK, 2, FLAT * LANES), F32), pltpu.VMEM((2 * FLAT, LANES), F32),
                        pltpu.SemaphoreType.DMA((AHEAD + BACK,))],
        input_output_aliases={5: 0},
        compiler_params=pltpu.CompilerParams(vmem_limit_bytes=8 << 20),
        cost_estimate=cost(1_000_000, 4_000_000),
        name="place",
    )(table, *arrived, kept)
    return jnp.transpose(placed, (1, 0, 2))


def solution(mesh):
    return jax.shard_map(
        shards,
        mesh=mesh,
        in_specs=(P(None, AXES, None), P(), P(), P()),
        out_specs=P(None, AXES, None),
        check_vma=False,
    )
```

time: 75.4 us -> 61.8 us (0.82)
  the two profiles are of different devices: /device:TPU:4 before, /device:TPU:1 now
where the time goes in v3:
time: 61.8 us; the launch traced here: 61.5 us
  Pallas kernels  38 us (61%)
  starting transfers between devices  13.9 us (22%)
  local copies, waits for them, and re-layouts  5.04 us (8%)
  waiting for transfers between devices  4.55 us (7%)
    pallas_call x3, Pallas kernels, solve(): pl.pallas_call(lambda *refs: pair_kernel(start, held, spins, *refs), out_...  23.1 us
    ppermute x6, starting transfers between devices, from_behind(): lax.ppermute(value, AXES, [(source, (source + steps) % count) for source...  13.9 us
    unnamed x16, local copies, waits for them, and re-layouts  5.04 us
    ppermute x6, waiting for transfers between devices, from_behind(): lax.ppermute(value, AXES, [(source, (source + steps) % count) for source...  4.55 us
    pallas_call x1, Pallas kernels, shards(): pl.pallas_call(keep_kernel, out_shape=shape, grid=(CAP,), in_specs=[SCALA...  4.5 us
    pallas_call x1, Pallas kernels, shards(): pl.pallas_call(prepare_kernel, out_shape=[slabs, jax.ShapeDtypeStruct((WI...  3.58 us
    pallas_call x1, Pallas kernels, shards(): pl.pallas_call(lambda *refs: place_kernel(boxes, *refs), out_shape=shape,...  3.39 us
    pallas_call x1, Pallas kernels, shards(): pl.pallas_call(window_kernel, out_shape=[jax.ShapeDtypeStruct((2, FLAT, L...  3.22 us
  transfers between devices with their start and end apart: 6, of which 3 were waited for; matrix products, arithmetic and copies ran while one was open for 0% of the time, Pallas kernels for 24%

profile of v3, /device:TPU:1, one launch (start us, length us, event | category | flops | bytes accessed | tf_op | source)
XLA Modules:
  0.0 61.5 jit_solution(11916001429822484045)
XLA Ops:
  0.0 3.2 %window.1 = (bf16[2,500,128]{2,1,0:T(8,128)(2,1)}, bf16[2,500,128]{2,1,0:T(8,128)(2,1)}) custom-call(s32[2,128]{1,0:T(2,128)} %bitcast.3, bf16[2,4,64000]{2,1,0:T(4,128)(2,1)} %orb_ref.3), custom_call_target="tpu_custom_call" | custom-call | tf_op jit(solution)/shard_map/window/pallas_call | solution.py:401
  3.2 2.2 %collective-permute-start = (bf16[2,500,128]{2,1,0:T(8,128)(2,1)}, bf16[2,500,128]{2,1,0:T(8,128)(2,1)S(1)}, u32[]{:S(2)}, u32[]{:S(2)}) collective-permute-start(bf16[2,500,128]{2,1,0:T(8,128)(2,1)} %get-tuple-element.18), channel_id=1, source_target_pairs={{0,1},{1,2},{2,3},{3,4},{4,5},{5,6},{6,7},{7,8},{8,9},{9,10},{10,1... | collective-permute-start | bytes 768008 | tf_op jit(solution)/shard_map/ppermute | solution.py:381
  5.4 4.5 %collective-permute-start.1 = (bf16[2,500,128]{2,1,0:T(8,128)(2,1)}, bf16[2,500,128]{2,1,0:T(8,128)(2,1)S(1)}, u32[]{:S(2)}, u32[]{:S(2)}) collective-permute-start(bf16[2,500,128]{2,1,0:T(8,128)(2,1)} %get-tuple-element.19), channel_id=1, source_target_pairs={{0,31},{1,0},{2,1},{3,2},{4,3},{5,4},{6,5},{7,6},{8,7},{9,8},{10,9... | collective-permute-start | bytes 768008 | tf_op jit(solution)/shard_map/ppermute | solution.py:381
  9.9 0.0 copy-start
  9.9 1.2 %copy-done = bf16[2,4,64000]{2,1,0:T(4,128)(2,1)S(1)} copy-done((bf16[2,4,64000]{2,1,0:T(4,128)(2,1)S(1)}, bf16[2,4,64000]{2,1,0:T(4,128)(2,1)}, u32[]{:S(2)}) %copy-start) | copy-done | bytes 1024024
  11.1 0.0 copy-start.2
  11.1 1.1 %copy-done.2 = f32[2,40,1792]{2,1,0:T(8,128)S(1)} copy-done((f32[2,40,1792]{2,1,0:T(8,128)S(1)}, f32[2,40,1792]{2,1,0:T(8,128)}, u32[]{:S(2)}) %copy-start.2) | copy-done | bytes 573464
  12.2 0.0 copy-start.5
  12.2 0.7 %copy-done.5 = s32[128,2]{0,1:T(2,128)S(1)} copy-done((s32[128,2]{0,1:T(2,128)S(1)}, s32[128,2]{0,1:T(2,128)}, u32[]{:S(2)}) %copy-start.5) | copy-done | bytes 1048
  12.9 0.0 copy-start.6
  12.9 0.7 %copy-done.6 = s32[128,3]{0,1:T(4,128)S(1)} copy-done((s32[128,3]{0,1:T(4,128)S(1)}, s32[128,3]{0,1:T(4,128)}, u32[]{:S(2)}) %copy-start.6) | copy-done | bytes 1560
  13.6 0.0 copy-start.7
  13.6 0.7 %copy-done.7 = s32[128]{0:T(128)S(1)} copy-done((s32[128]{0:T(128)S(1)}, s32[128]{0:T(128)}, u32[]{:S(2)}) %copy-start.7) | copy-done | bytes 536
  14.2 3.6 %prepare.1 = (f32[6,2,13,88,128]{4,3,2,1,0:T(8,128)S(1)}, bf16[1664,1792]{1,0:T(8,128)(2,1)S(1)}, s32[52]{0:T(128)S(1)}) custom-call(s32[128]{0:T(128)S(1)} %copy-done.7, s32[2,128]{1,0:T(2,128)S(1)} %bitcast.4, s32[3,128]{1,0:T(4,128)S(1)} %bitcast.5, bf16[2,4,64000]{2,1,0:T(4,128)(2,1)S(1)} %copy-done, f32[2,40,1792]{2,1,0:T(8,128)S(1)} %copy-done.2), custom_call_target="tpu_custom_call" | custom-call | flops 10000000 | bytes 10000000 | tf_op jit(solution)/shard_map/prepare/pallas_call | solution.py:415
  17.8 0.0 collective-permute-done.prev_ref
  17.8 0.1 collective-permute-done.1.next_ref
  18.0 0.0 copy-start.1
  18.0 0.0 copy-start.3
  18.0 0.2 fill.1.refs_1_
  18.2 0.7 %copy-done.1 = f32[40,1792]{1,0:T(8,128)S(1)} copy-done((f32[40,1792]{1,0:T(8,128)S(1)}, f32[40,1792]{1,0:T(8,128)}, u32[]{:S(2)}) %copy-start.1) | copy-done | bytes 286744
  18.9 0.0 copy-done.3
  18.9 8.3 %shard_map.92 = (f32[3,500,128]{2,1,0:T(8,128)S(1)}, bf16[1,500,128]{2,1,0:T(8,128)(2,1)S(1)}, bf16[2,500,128]{2,1,0:T(8,128)(2,1)S(1)}) custom-call(s32[52]{0:T(128)S(1)} %get-tuple-element.16.refs_0_.tab_ref, f32[6,2,13,88,128]{4,3,2,1,0:T(8,128)S(1)} %fill.1.refs_1_, bf16[1664,1792]{1,0:T(8,128)(2,1)S(1)} %get-tuple-element.20.refs_2_, ...), custom_call_target="tpu_custom_call" | custom-call | flops 2457600000 | bytes 10000000 | tf_op jit(solution)/shard_map/pallas_call | solution.py:447
  27.2 0.0 copy-start.4
  27.2 8.3 %shard_map.91 = (f32[3,500,128]{2,1,0:T(8,128)S(1)}, bf16[1,500,128]{2,1,0:T(8,128)(2,1)S(1)}, bf16[2,500,128]{2,1,0:T(8,128)(2,1)S(1)}) custom-call(s32[52]{0:T(128)S(1)} %get-tuple-element.16.refs_0_.tab_ref, f32[6,2,13,88,128]{4,3,2,1,0:T(8,128)S(1)} %fill.1.refs_1_, bf16[1664,1792]{1,0:T(8,128)(2,1)S(1)} %get-tuple-element.20.refs_2_, ...), custom_call_target="tpu_custom_call" | custom-call | flops 2457600000 | bytes 10000000 | tf_op jit(solution)/shard_map/pallas_call | solution.py:447
  35.6 5.7 %collective-permute-start.5 = (bf16[2,500,128]{2,1,0:T(8,128)(2,1)S(1)}, bf16[2,500,128]{2,1,0:T(8,128)(2,1)S(1)}, u32[]{:S(2)}, u32[]{:S(2)}) collective-permute-start(bf16[2,500,128]{2,1,0:T(8,128)(2,1)S(1)} %get-tuple-element.24), channel_id=1, source_target_pairs={{0,31},{1,0},{2,1},{3,2},{4,3},{5,4},{6,5},{7,6},{8,7},{9,8},{10,9... | collective-permute-start | bytes 768008 | tf_op jit(solution)/shard_map/ppermute | solution.py:381
  41.2 0.5 collective-permute-start.3
  41.7 1.0 %collective-permute-start.4 = (bf16[1,500,128]{2,1,0:T(8,128)(2,1)S(1)}, bf16[1,500,128]{2,1,0:T(8,128)(2,1)S(1)}, u32[]{:S(2)}, u32[]{:S(2)}) collective-permute-start(bf16[1,500,128]{2,1,0:T(8,128)(2,1)S(1)} %get-tuple-element.23), channel_id=1, source_target_pairs={{0,1},{1,2},{2,3},{3,4},{4,5},{5,6},{6,7},{7,8},{8,9},{9,10},{10,1... | collective-permute-start | bytes 384008 | tf_op jit(solution)/shard_map/ppermute | solution.py:381
  42.7 0.0 collective-permute-start.2
  42.7 0.0 copy-done.4
  42.7 6.5 %shard_map.93.rest_ref = f32[2,500,128]{2,1,0:T(8,128)S(1)} custom-call(s32[52]{0:T(128)S(1)} %get-tuple-element.16.refs_0_.tab_ref, f32[6,2,13,88,128]{4,3,2,1,0:T(8,128)S(1)} %fill.1.refs_1_, bf16[1664,1792]{1,0:T(8,128)(2,1)S(1)} %get-tuple-element.20.refs_2_, bf16[160,160]{1,0:T(8,128)(2,1)S(1)} %copy-done.4, f32[40,1792]{1,0:T(8,128)S(1)} %copy-done.1), custom_call_target="tpu_custom_call" | custom-call | flops 1638400000 | bytes 10000000 | tf_op jit(solution)/shard_map/pallas_call | solution.py:447
  49.2 4.5 %keep.1.refs_5_ = f32[7,2,64000]{2,1,0:T(2,128)} custom-call(s32[52]{0:T(128)S(1)} %get-tuple-element.16.refs_0_.tab_ref, f32[3,500,128]{2,1,0:T(8,128)S(1)} %get-tuple-element.25.low_ref, f32[3,500,128]{2,1,0:T(8,128)S(1)} %get-tuple-element.26.high_ref, f32[2,500,128]{2,1,0:T(8,128)S(1)} %shard_map.93.rest_ref), custom_call_target="tpu_custom_call" | custom-call | flops 1000000 | bytes 8000000 | tf_op jit(solution)/shard_map/keep/pallas_call | solution.py:472
  53.7 3.0 %collective-permute-done.4.refs_3_ = bf16[1,500,128]{2,1,0:T(8,128)(2,1)S(1)} collective-permute-done((bf16[1,500,128]{2,1,0:T(8,128)(2,1)S(1)}, bf16[1,500,128]{2,1,0:T(8,128)(2,1)S(1)}, u32[]{:S(2)}, u32[]{:S(2)}) %collective-permute-start.4) | collective-permute-done | bytes 128032 | tf_op jit(solution)/shard_map/ppermute | solution.py:381
  56.7 1.4 %collective-permute-done.2.refs_1_ = bf16[1,500,128]{2,1,0:T(8,128)(2,1)S(1)} collective-permute-done((bf16[1,500,128]{2,1,0:T(8,128)(2,1)S(1)}, bf16[1,500,128]{2,1,0:T(8,128)(2,1)S(1)}, u32[]{:S(2)}, u32[]{:S(2)}) %collective-permute-start.2) | collective-permute-done | bytes 128032 | tf_op jit(solution)/shard_map/ppermute | solution.py:381
  58.1 0.0 collective-permute-done.5.refs_4_
  58.1 0.0 collective-permute-done.3.refs_2_
  58.1 3.4 %place.1 = f32[7,2,64000]{2,1,0:T(2,128)} custom-call(s32[52]{0:T(128)S(1)} %get-tuple-element.16.refs_0_.tab_ref, bf16[1,500,128]{2,1,0:T(8,128)(2,1)S(1)} %collective-permute-done.2.refs_1_, bf16[2,500,128]{2,1,0:T(8,128)(2,1)S(1)} %collective-permute-done.3.refs_2_, ...), custom_call_target="tpu_custom_call", output_to_operand_aliasing={{}: (5, {})} | custom-call | flops 1000000 | bytes 4000000 | tf_op jit(solution)/shard_map/place/pallas_call | solution.py:483
Async XLA Ops:
  3.2 14.6 %collective-permute-start = (bf16[2,500,128]{2,1,0:T(8,128)(2,1)}, bf16[2,500,128]{2,1,0:T(8,128)(2,1)S(1)}, u32[]{:S(2)}, u32[]{:S(2)}) collective-permute-start(bf16[2,500,128]{2,1,0:T(8,128)(2,1)} %get-tuple-element.18), channel_id=1, source_target_pairs={{0,1},{1,2},{2,3},{3,4},{4,5},{5,6},{6,7},{7,8},{8,9},{9,10},{10,1... | collective-permute-start | bytes 768008 | tf_op jit(solution)/shard_map/ppermute | solution.py:381
  5.4 12.6 %collective-permute-start.1 = (bf16[2,500,128]{2,1,0:T(8,128)(2,1)}, bf16[2,500,128]{2,1,0:T(8,128)(2,1)S(1)}, u32[]{:S(2)}, u32[]{:S(2)}) collective-permute-start(bf16[2,500,128]{2,1,0:T(8,128)(2,1)} %get-tuple-element.19), channel_id=1, source_target_pairs={{0,31},{1,0},{2,1},{3,2},{4,3},{5,4},{6,5},{7,6},{8,7},{9,8},{10,9... | collective-permute-start | bytes 768008 | tf_op jit(solution)/shard_map/ppermute | solution.py:381
  9.9 1.2 %copy-start = (bf16[2,4,64000]{2,1,0:T(4,128)(2,1)S(1)}, bf16[2,4,64000]{2,1,0:T(4,128)(2,1)}, u32[]{:S(2)}) copy-start(bf16[2,4,64000]{2,1,0:T(4,128)(2,1)} %orb_ref.3) | copy-start | bytes 3072004
  11.1 1.1 %copy-start.2 = (f32[2,40,1792]{2,1,0:T(8,128)S(1)}, f32[2,40,1792]{2,1,0:T(8,128)}, u32[]{:S(2)}) copy-start(f32[2,40,1792]{2,1,0:T(8,128)} %constant.8.clone.rep_ref) | copy-start | bytes 1720324
  12.2 0.7 %copy-start.5 = (s32[128,2]{0,1:T(2,128)S(1)}, s32[128,2]{0,1:T(2,128)}, u32[]{:S(2)}) copy-start(s32[128,2]{0,1:T(2,128)} %param.11) | copy-start | bytes 3076
  12.9 0.7 %copy-start.6 = (s32[128,3]{0,1:T(4,128)S(1)}, s32[128,3]{0,1:T(4,128)}, u32[]{:S(2)}) copy-start(s32[128,3]{0,1:T(4,128)} %param.12) | copy-start | bytes 4612
  13.6 0.7 %copy-start.7 = (s32[128]{0:T(128)S(1)}, s32[128]{0:T(128)}, u32[]{:S(2)}) copy-start(s32[128]{0:T(128)} %dest_ref.1) | copy-start | bytes 1540
  18.0 1.0 %copy-start.1 = (f32[40,1792]{1,0:T(8,128)S(1)}, f32[40,1792]{1,0:T(8,128)}, u32[]{:S(2)}) copy-start(f32[40,1792]{1,0:T(8,128)} %constant.10.clone.refs_4_) | copy-start | bytes 860164
  18.0 1.0 %copy-start.3 = (bf16[240,240]{1,0:T(8,128)(2,1)S(1)}, bf16[240,240]{1,0:T(8,128)(2,1)}, u32[]{:S(2)}) copy-start(bf16[240,240]{1,0:T(8,128)(2,1)} %constant.9.clone.refs_3_) | copy-start | bytes 345604
  27.2 15.5 %copy-start.4 = (bf16[160,160]{1,0:T(8,128)(2,1)S(1)}, bf16[160,160]{1,0:T(8,128)(2,1)}, u32[]{:S(2)}) copy-start(bf16[160,160]{1,0:T(8,128)(2,1)} %constant.11.clone.refs_3_) | copy-start | bytes 153604
  35.6 22.6 %collective-permute-start.5 = (bf16[2,500,128]{2,1,0:T(8,128)(2,1)S(1)}, bf16[2,500,128]{2,1,0:T(8,128)(2,1)S(1)}, u32[]{:S(2)}, u32[]{:S(2)}) collective-permute-start(bf16[2,500,128]{2,1,0:T(8,128)(2,1)S(1)} %get-tuple-element.24), channel_id=1, source_target_pairs={{0,31},{1,0},{2,1},{3,2},{4,3},{5,4},{6,5},{7,6},{8,7},{9,8},{10,9... | collective-permute-start | bytes 768008 | tf_op jit(solution)/shard_map/ppermute | solution.py:381
  41.2 16.9 %collective-permute-start.3 = (bf16[2,500,128]{2,1,0:T(8,128)(2,1)S(1)}, bf16[2,500,128]{2,1,0:T(8,128)(2,1)S(1)}, u32[]{:S(2)}, u32[]{:S(2)}) collective-permute-start(bf16[2,500,128]{2,1,0:T(8,128)(2,1)S(1)} %get-tuple-element.22), channel_id=1, source_target_pairs={{0,31},{1,0},{2,1},{3,2},{4,3},{5,4},{6,5},{7,6},{8,7},{9,8},{10,9... | collective-permute-start | bytes 768008 | tf_op jit(solution)/shard_map/ppermute | solution.py:381
  41.7 15.1 %collective-permute-start.4 = (bf16[1,500,128]{2,1,0:T(8,128)(2,1)S(1)}, bf16[1,500,128]{2,1,0:T(8,128)(2,1)S(1)}, u32[]{:S(2)}, u32[]{:S(2)}) collective-permute-start(bf16[1,500,128]{2,1,0:T(8,128)(2,1)S(1)} %get-tuple-element.23), channel_id=1, source_target_pairs={{0,1},{1,2},{2,3},{3,4},{4,5},{5,6},{6,7},{7,8},{8,9},{9,10},{10,1... | collective-permute-start | bytes 384008 | tf_op jit(solution)/shard_map/ppermute | solution.py:381
  42.7 15.4 %collective-permute-start.2 = (bf16[1,500,128]{2,1,0:T(8,128)(2,1)S(1)}, bf16[1,500,128]{2,1,0:T(8,128)(2,1)S(1)}, u32[]{:S(2)}, u32[]{:S(2)}) collective-permute-start(bf16[1,500,128]{2,1,0:T(8,128)(2,1)S(1)} %get-tuple-element.21), channel_id=1, source_target_pairs={{0,1},{1,2},{2,3},{3,4},{4,5},{5,6},{6,7},{7,8},{8,9},{9,10},{10,1... | collective-permute-start | bytes 384008 | tf_op jit(solution)/shard_map/ppermute | solution.py:381

commit v4 on v3

--- a/solution.py
+++ b/solution.py
@@ -55,10 +55,10 @@
     return lax.broadcasted_iota(jnp.int32, (1, LANES), 1)
 
 
-def split_boxes(orb_ref, flat_ref, spin, boxes):
+def split_boxes(orb_ref, flat_ref, boxes):
     def step(i, _):
         base = pl.multiple_of(i * PAIRT * LANES, LANES)
-        x = orb_ref[spin, :, pl.ds(base, PAIRT * LANES)].astype(F32)
+        x = orb_ref[:, pl.ds(base, PAIRT * LANES)].astype(F32)
         for j in range(PAIRT):
             flat_ref[pl.ds(pl.multiple_of((i * PAIRT + j) * 8, 8), boxes), :] = x[:, j * LANES:(j + 1) * LANES]
         return 0
@@ -92,14 +92,9 @@
         before = turned
 
 
-def window_kernel(part_ref, orb_ref, *refs):
-    outs, (orb, flat_ref, sems) = refs[:2], refs[2:]
-    boxes = orb_ref.shape[1]
+def wanted_boxes(part_ref, boxes):
     total = part_ref.shape[1]
     device = lax.axis_index(AXES)
-    copies = [pltpu.make_async_copy(orb_ref.at[spin], orb.at[spin], sems.at[spin]) for spin in range(2)]
-    for copy in copies:
-        copy.start()
     wanted = []
     for step in (1, -1):
         found = jnp.int32(0)
@@ -110,11 +105,26 @@
                 local = part_ref[number, jnp.clip(other, 0, total - 1)] - device * boxes
                 found = jnp.where(inside & (local >= 0) & (local < boxes), local, found)
         wanted.append(found)
-    for spin in range(2):
-        copies[spin].wait()
-        split_boxes(orb, flat_ref, spin, boxes)
-        for side in range(2):
-            outs[side][spin] = flat_ref[pl.ds(wanted[side], FLAT, stride=8), :].astype(BF)
+    return wanted
+
+
+def window_kernel(dest_hbm, part_hbm, anc_hbm, orb_hbm, ahead_low, back_low, ahead_high, back_high, tab_ref,
+                  dest_ref, part_ref, anc_ref, orb_ref, flat_ref, sems):
+    boxes = orb_ref.shape[1]
+    small = [pltpu.make_async_copy(source, target, sems.at[k]) for k, (source, target) in enumerate(
+        ((part_hbm, part_ref), (dest_hbm, dest_ref), (anc_hbm, anc_ref)))]
+    large = [pltpu.make_async_copy(orb_hbm.at[spin], orb_ref.at[spin], sems.at[3 + spin]) for spin in range(2)]
+    for copy in (small[0], large[0], small[1], small[2], large[1]):
+        copy.start()
+    for copy in small:
+        copy.wait()
+    wanted = wanted_boxes(part_ref, boxes)
+    build_tables(dest_ref, part_ref, anc_ref, tab_ref, boxes)
+    for spin, refs in enumerate(((ahead_low, back_low), (ahead_high, back_high))):
+        large[spin].wait()
+        split_boxes(orb_ref.at[spin], flat_ref, boxes)
+        for side, ref in enumerate(refs):
+            ref[...] = flat_ref[pl.ds(wanted[side], FLAT, stride=8), :].astype(BF)
 
 
 def table_layout(boxes):
@@ -126,8 +136,7 @@
     return pairs, codes, slots, leaves, order, order + boxes
 
 
-def prepare_kernel(dest_ref, part_ref, anc_ref, orb_ref, rep_ref, pad_ref, kron_ref, tab_ref, flat_ref):
-    boxes = orb_ref.shape[1]
+def build_tables(dest_ref, part_ref, anc_ref, tab_ref, boxes):
     total = part_ref.shape[1]
     device = lax.axis_index(AXES)
     pairs, codes, slots, leaves, order, _ = table_layout(boxes)
@@ -183,18 +192,28 @@
                 moved = jnp.where(moved < 0, moved + extent, jnp.where(moved >= extent, moved - extent, moved))
                 tab_ref[base + 1 + axis] = jnp.clip(moved - extent // 2, -(PAD - 4), PAD - 4)
 
-    for spin in range(2):
-        split_boxes(orb_ref, flat_ref, spin, boxes)
+
+def prepare_kernel(orb_hbm, rep_hbm, low_ref, high_ref, kron_ref, orb_ref, rep_ref, flat_ref, sems):
+    boxes = orb_ref.shape[1]
+    copies = [pltpu.make_async_copy(orb_hbm.at[spin], orb_ref.at[spin], sems.at[spin]) for spin in range(2)]
+    copies.append(pltpu.make_async_copy(rep_hbm, rep_ref, sems.at[2]))
+    for copy in copies:
+        copy.start()
+    for spin, pad_ref in enumerate((low_ref, high_ref)):
+        copies[spin].wait()
+        split_boxes(orb_ref.at[spin], flat_ref, boxes)
 
         def slabs(box, _):
             flat_to_slabs(
                 lambda t: flat_ref[pl.ds(box + 8 * t, HALF, stride=8 * PAIRT), :],
                 lambda u, parity, x: pad_ref.__setitem__(
-                    (box, spin, u, pl.ds(PAD + parity, HALF, stride=2), slice(None)), x),
+                    (box, u, pl.ds(PAD + parity, HALF, stride=2), slice(None)), x),
             )
             return 0
 
         lax.fori_loop(0, boxes, slabs, 0)
+
+    copies[2].wait()
 
     def build(i, _):
         row = pl.multiple_of(i * 2 * EDGE, 16)
@@ -213,18 +232,18 @@
 def fill_kernel(old_ref, prev_ref, next_ref, pad_ref, flat_ref):
     boxes = pad_ref.shape[0] - 2
     for side, ref in ((0, prev_ref), (1, next_ref)):
-        for spin in range(2):
-            flat_ref[...] = ref[spin].astype(F32)
-            flat_to_slabs(
-                lambda t: flat_ref[pl.ds(t, HALF, stride=PAIRT), :],
-                lambda u, parity, x: pad_ref.__setitem__(
-                    (boxes + side, spin, u, pl.ds(PAD + parity, HALF, stride=2), slice(None)), x),
-            )
-
-
-def pair_kernel(start, held, spins, tab_ref, pad_ref, kron_ref, diag_ref, inv_ref, out_ref, *refs):
-    sends, (mov_ref, x_ref, y_ref, res_ref) = refs[:-4], refs[-4:]
-    boxes = pad_ref.shape[0] - 2
+        flat_ref[...] = ref[...].astype(F32)
+        flat_to_slabs(
+            lambda t: flat_ref[pl.ds(t, HALF, stride=PAIRT), :],
+            lambda u, parity, x: pad_ref.__setitem__(
+                (boxes + side, u, pl.ds(PAD + parity, HALF, stride=2), slice(None)), x),
+        )
+
+
+def pair_kernel(start, held, spins, tab_ref, kron_ref, diag_ref, inv_ref, *refs):
+    pads, out_ref, sends = refs[:len(spins)], refs[len(spins)], refs[len(spins) + 1:-4]
+    mov_ref, x_ref, y_ref, res_ref = refs[-4:]
+    boxes = pads[0].shape[0] - 2
     pairs, _, _, leaves, order, _ = table_layout(boxes)
     lanes = lane_iota()
     rows = lax.broadcasted_iota(jnp.int32, (EDGE, 1), 0)
@@ -252,17 +271,17 @@
                     if u == TILES:
                         ok = ok & (lanes < FACE - (TILES - 1) * LANES)
                     keep.append(row_ok & ok)
-            for at, spin in enumerate(spins):
+            for at, pad_ref in enumerate(pads):
                 values = []
                 for number in range(PARTNERS):
                     source, da, db, dc, quotient, rest, row_ok = places[number]
                     tile = jnp.clip(quotient + (u - ZERO_TILES), 0, TILES - 1)
-                    x = pad_ref[source, spin, tile, pl.ds(PAD - da, EDGE), :]
+                    x = pad_ref[source, tile, pl.ds(PAD - da, EDGE), :]
                     turned = pltpu.roll(x, (LANES - rest) % LANES, 1)
                     if u > 0:
                         moved = jnp.where(keep[number], jnp.where(lanes < LANES - rest, last[at][number], turned), 0.0)
                         mov_ref[index, at, number, u - 1] = moved
-                        values.append(pad_ref[box, spin, u - 1, pl.ds(PAD, EDGE), :] * moved)
+                        values.append(pad_ref[box, u - 1, pl.ds(PAD, EDGE), :] * moved)
                     last[at][number] = turned
                 if u > 0:
                     both = jnp.concatenate(values, axis=0)
@@ -322,21 +341,7 @@
             sends[1][k] = out_ref[tab_ref[leaves + AHEAD + k]].astype(BF)
 
 
-def interleave(out, both_ref, load):
-    for spin in range(2):
-        both_ref[pl.ds(spin, FLAT, stride=2), :] = load(spin)
-
-    def step(i, _):
-        base = pl.multiple_of(i * PAIRT * LANES, LANES)
-        chunk = both_ref[pl.ds(pl.multiple_of(i * 2 * PAIRT, 2), 2 * PAIRT), :]
-        for j in range(PAIRT):
-            out[:, pl.ds(pl.multiple_of(base + j * LANES, LANES), LANES)] = chunk[2 * j:2 * j + 2]
-        return 0
-
-    lax.fori_loop(0, HALF, step, 0)
-
-
-def keep_kernel(tab_ref, low_ref, high_ref, rest_ref, out_ref, both_ref):
+def keep_kernel(tab_ref, low_ref, high_ref, rest_ref, out_ref):
     first = low_ref.shape[0]
     boxes = first + rest_ref.shape[0] // 2
     code = tab_ref[table_layout(boxes)[1] + pl.program_id(0)]
@@ -344,19 +349,21 @@
     @pl.when(code < first)
     def _():
         spot = jnp.minimum(code, first - 1)
-        interleave(out_ref.at[0], both_ref, lambda spin: (low_ref, high_ref)[spin][spot])
+        for spin, ref in enumerate((low_ref, high_ref)):
+            out_ref[0, pl.ds(spin, FLAT, stride=2), :] = ref[spot]
 
     @pl.when((code >= first) & (code < boxes))
     def _():
         spot = jnp.clip(code - first, 0, boxes - first - 1)
-        interleave(out_ref.at[0], both_ref, lambda spin: rest_ref[2 * spot + spin])
+        for spin in range(2):
+            out_ref[0, pl.ds(spin, FLAT, stride=2), :] = rest_ref[2 * spot + spin]
 
     @pl.when(code >= boxes + AHEAD + BACK)
     def _():
         out_ref[...] = jnp.zeros_like(out_ref)
 
 
-def place_kernel(boxes, tab_ref, prev_low, next_low, prev_high, next_high, kept_ref, out_ref, form_ref, both_ref, sems):
+def place_kernel(boxes, tab_ref, prev_low, next_low, prev_high, next_high, kept_ref, out_ref, form_ref, sems):
     slots = table_layout(boxes)[2]
     copies = []
     for k in range(AHEAD + BACK):
@@ -366,7 +373,8 @@
 
         @pl.when(slot < CAP)
         def _():
-            interleave(form_ref.at[k], both_ref, lambda spin: pair[spin][row].astype(F32))
+            for spin, ref in enumerate(pair):
+                form_ref[k, pl.ds(spin, FLAT, stride=2), :] = ref[row].astype(F32)
             copy.start()
 
         copies.append((slot, copy))
@@ -389,6 +397,10 @@
 ANYWHERE = pl.BlockSpec(memory_space=pltpu.MemorySpace.HBM)
 
 
+def in_place(value):
+    return pltpu.with_memory_space_constraint(jnp.asarray(value), pltpu.HBM)
+
+
 def cost(flops, size):
     return pl.CostEstimate(flops=flops, bytes_accessed=size, transcendentals=0)
 
@@ -398,43 +410,48 @@
     sine, inverse, repeated, tiled = tables()
     partners_t, anchors_t = partners.T, anchors.T
 
-    windows = pl.pallas_call(
+    box = jax.ShapeDtypeStruct((FLAT, LANES), BF)
+    splitter = pltpu.VMEM((FLAT * 8, LANES), F32)
+    ahead_low, back_low, ahead_high, back_high, table = pl.pallas_call(
         window_kernel,
-        out_shape=[jax.ShapeDtypeStruct((2, FLAT, LANES), BF)] * 2,
-        in_specs=[SCALARS, ANYWHERE],
-        out_specs=whole(2),
-        scratch_shapes=[pltpu.VMEM(orbitals.shape, BF), pltpu.VMEM((FLAT * 8, LANES), F32),
-                        pltpu.SemaphoreType.DMA((2,))],
-        compiler_params=pltpu.CompilerParams(vmem_limit_bytes=66_300_000),
+        out_shape=[box] * 4 + [jax.ShapeDtypeStruct((table_layout(boxes)[-1],), jnp.int32)],
+        in_specs=[ANYWHERE] * 4,
+        out_specs=whole(4) + [SCALARS],
+        scratch_shapes=[pltpu.SMEM(dest.shape, jnp.int32), pltpu.SMEM(partners_t.shape, jnp.int32),
+                        pltpu.SMEM(anchors_t.shape, jnp.int32), pltpu.VMEM(orbitals.shape, BF),
+                        splitter, pltpu.SemaphoreType.DMA((5,))],
+        compiler_params=pltpu.CompilerParams(vmem_limit_bytes=12 << 20),
         name="window",
-    )(partners_t, orbitals)
-    from_prev = from_behind(windows[0], 1)
-    from_next = from_behind(windows[1], -1)
-
-    slabs = jax.ShapeDtypeStruct((boxes + 2, 2, TILES, ROWS, LANES), F32)
-    pad, kron, table = pl.pallas_call(
+    )(*map(in_place, (dest, partners_t, anchors_t, orbitals)))
+    prev_low = from_behind(ahead_low, 1)
+    next_low = from_behind(back_low, -1)
+    prev_high = from_behind(ahead_high, 1)
+    next_high = from_behind(back_high, -1)
+
+    slabs = jax.ShapeDtypeStruct((boxes + 2, TILES, ROWS, LANES), F32)
+    constants = np.stack([repeated, tiled])
+    *pads, kron = pl.pallas_call(
         prepare_kernel,
-        out_shape=[slabs,
-                   jax.ShapeDtypeStruct((WIDE, NWIDE), BF),
-                   jax.ShapeDtypeStruct((table_layout(boxes)[-1],), jnp.int32)],
-        in_specs=[SCALARS] * 3 + whole(2),
-        out_specs=whole(2) + [SCALARS],
-        scratch_shapes=[pltpu.VMEM((FLAT * 8, LANES), F32)],
+        out_shape=[slabs, slabs, jax.ShapeDtypeStruct((WIDE, NWIDE), BF)],
+        in_specs=[ANYWHERE] * 2,
+        out_specs=whole(3),
+        scratch_shapes=[pltpu.VMEM(orbitals.shape, BF), pltpu.VMEM(constants.shape, F32), splitter,
+                        pltpu.SemaphoreType.DMA((3,))],
         compiler_params=pltpu.CompilerParams(vmem_limit_bytes=20 << 20),
         cost_estimate=cost(10_000_000, 10_000_000),
         name="prepare",
-    )(dest, partners_t, anchors_t, orbitals, np.stack([repeated, tiled]))
-    pad = pl.pallas_call(
-        fill_kernel,
-        out_shape=slabs,
-        in_specs=whole(3),
-        out_specs=pl.BlockSpec(memory_space=pltpu.VMEM),
-        scratch_shapes=[pltpu.VMEM((FLAT, LANES), F32)],
-        input_output_aliases={0: 0},
-        compiler_params=pltpu.CompilerParams(vmem_limit_bytes=12 << 20),
-        cost_estimate=cost(1_000_000, 2_000_000),
-        name="fill",
-    )(pad, from_prev, from_next)
+    )(in_place(orbitals), in_place(constants))
+    for spin, halo in enumerate(((prev_low, next_low), (prev_high, next_high))):
+        pads[spin] = pl.pallas_call(
+            fill_kernel,
+            out_shape=slabs,
+            in_specs=whole(3),
+            out_specs=pl.BlockSpec(memory_space=pltpu.VMEM),
+            scratch_shapes=[pltpu.VMEM((FLAT, LANES), F32)],
+            input_output_aliases={0: 0},
+            compiler_params=pltpu.CompilerParams(vmem_limit_bytes=12 << 20),
+            cost_estimate=cost(1_000_000, 2_000_000),
+        )(pads[spin], *halo)
 
     moving = AHEAD + BACK
 
@@ -447,7 +464,7 @@
         return pl.pallas_call(
             lambda *refs: pair_kernel(start, held, spins, *refs),
             out_shape=shapes,
-            in_specs=[SCALARS] + whole(4),
+            in_specs=[SCALARS] + whole(3 + len(spins)),
             out_specs=whole(len(shapes)),
             scratch_shapes=[
                 pltpu.VMEM((held, len(spins), PARTNERS, TILES, EDGE, LANES), F32),
@@ -457,7 +474,7 @@
             ],
             compiler_params=pltpu.CompilerParams(vmem_limit_bytes=20 << 20),
             cost_estimate=cost(4 * cubes * EDGE * FACE * FACE, 10_000_000),
-        )(table, pad, kron, diag, inverse)
+        )(table, kron, diag, inverse, *[pads[spin] for spin in spins])
 
     terms, arrived = [], []
     for spin in range(2):
@@ -468,14 +485,13 @@
         arrived += [ahead, back]
     terms += solve(moving, boxes - moving, (0, 1), False)
 
-    shape = jax.ShapeDtypeStruct((CAP, 2, FLAT * LANES), F32)
+    shape = jax.ShapeDtypeStruct((CAP, 2 * FLAT, LANES), F32)
     kept = pl.pallas_call(
         keep_kernel,
         out_shape=shape,
         grid=(CAP,),
         in_specs=[SCALARS] + whole(3),
-        out_specs=pl.BlockSpec((1, 2, FLAT * LANES), lambda i: (i, 0, 0)),
-        scratch_shapes=[pltpu.VMEM((2 * FLAT, LANES), F32)],
+        out_specs=pl.BlockSpec((1, 2 * FLAT, LANES), lambda i: (i, 0, 0)),
         compiler_params=pltpu.CompilerParams(vmem_limit_bytes=8 << 20),
         cost_estimate=cost(1_000_000, 8_000_000),
         name="keep",
@@ -485,14 +501,15 @@
         out_shape=shape,
         in_specs=[SCALARS] + whole(4) + [ANYWHERE],
         out_specs=ANYWHERE,
-        scratch_shapes=[pltpu.VMEM((AHEAD + BACK, 2, FLAT * LANES), F32), pltpu.VMEM((2 * FLAT, LANES), F32),
+        scratch_shapes=[pltpu.VMEM((AHEAD + BACK, 2 * FLAT, LANES), F32),
                         pltpu.SemaphoreType.DMA((AHEAD + BACK,))],
         input_output_aliases={5: 0},
         compiler_params=pltpu.CompilerParams(vmem_limit_bytes=8 << 20),
         cost_estimate=cost(1_000_000, 4_000_000),
         name="place",
     )(table, *arrived, kept)
-    return jnp.transpose(placed, (1, 0, 2))
+    placed = placed.reshape(-1).reshape(CAP, FLAT, 2, LANES).transpose(0, 2, 1, 3)
+    return placed.reshape(CAP, 2, FLAT * LANES).transpose(1, 0, 2)
 
 
 def solution(mesh):

time: 61.8 us -> 56.8 us (0.919)
  the two profiles are of different devices: /device:TPU:1 before, /device:TPU:0 now
where the time goes in v4:
time: 56.8 us; the launch traced here: 56.6 us
  Pallas kernels  34.4 us (61%)
  starting transfers between devices  16 us (28%)
  waiting for transfers between devices  5.31 us (9%)
  local copies, waits for them, and re-layouts  0.82 us (1%)
    pallas_call x3, Pallas kernels, solve(): pl.pallas_call(lambda *refs: pair_kernel(start, held, spins, *refs), out_...  23.1 us
    ppermute x8, starting transfers between devices, from_behind(): lax.ppermute(value, AXES, [(source, (source + steps) % count) for source...  16 us
    ppermute x8, waiting for transfers between devices, from_behind(): lax.ppermute(value, AXES, [(source, (source + steps) % count) for source...  5.31 us
    pallas_call x1, Pallas kernels, shards(): pl.pallas_call(keep_kernel, out_shape=shape, grid=(CAP,), in_specs=[SCALA...  3.93 us
    pallas_call x1, Pallas kernels, shards(): pl.pallas_call(prepare_kernel, out_shape=[slabs, slabs, jax.ShapeDtypeStr...  3.13 us
    pallas_call x1, Pallas kernels, shards(): pl.pallas_call(window_kernel, out_shape=[box] * 4 + [jax.ShapeDtypeStruct...  2.52 us
    pallas_call x1, Pallas kernels, shards(): pl.pallas_call(lambda *refs: place_kernel(boxes, *refs), out_shape=shape,...  1.4 us
  transfers between devices with their start and end apart: 8, of which 3 were waited for; matrix products, arithmetic and copies ran while one was open for 0% of the time, Pallas kernels for 39%

profile of v4, /device:TPU:0, one launch (start us, length us, event | category | flops | bytes accessed | tf_op | source)
XLA Modules:
  0.0 56.6 jit_solution(1334928310732716832)
XLA Ops:
  0.0 2.5 %window.1 = (bf16[500,128]{1,0:T(8,128)(2,1)S(1)}, bf16[500,128]{1,0:T(8,128)(2,1)S(1)}, bf16[500,128]{1,0:T(8,128)(2,1)S(1)}, bf16[500,128]{1,0:T(8,128)(2,1)S(1)}, s32[52]{0:T(128)S(1)}) custom-call(s32[128]{0:T(128)} %dest_hbm.1, s32[2,128]{1,0:T(2,128)} %bitcast.10, s32[3,128]{1,0:T(4,128)} %bitcast.9, bf16[2,4,64000]{2,1,0:T(4,128)(2,1)} %orb_hbm.3), custom_call_target="tpu_custom_call" | custom-call | tf_op jit(solution)/shard_map/window/pallas_call | solution.py:415
  2.5 3.1 %collective-permute-start.4 = (bf16[500,128]{1,0:T(8,128)(2,1)S(1)}, bf16[500,128]{1,0:T(8,128)(2,1)S(1)}, u32[]{:S(2)}, u32[]{:S(2)}) collective-permute-start(bf16[500,128]{1,0:T(8,128)(2,1)S(1)} %get-tuple-element.27), channel_id=1, source_target_pairs={{0,1},{1,2},{2,3},{3,4},{4,5},{5,6},{6,7},{7,8},{8,9},{9,10},{10,1... | collective-permute-start | bytes 384008 | tf_op jit(solution)/shard_map/ppermute | solution.py:389
  5.6 3.4 %collective-permute-start.5 = (bf16[500,128]{1,0:T(8,128)(2,1)S(1)}, bf16[500,128]{1,0:T(8,128)(2,1)S(1)}, u32[]{:S(2)}, u32[]{:S(2)}) collective-permute-start(bf16[500,128]{1,0:T(8,128)(2,1)S(1)} %get-tuple-element.28), channel_id=1, source_target_pairs={{0,31},{1,0},{2,1},{3,2},{4,3},{5,4},{6,5},{7,6},{8,7},{9,8},{10,9... | collective-permute-start | bytes 384008 | tf_op jit(solution)/shard_map/ppermute | solution.py:389
  9.0 0.0 collective-permute-start
  9.1 5.3 %collective-permute-start.1 = (bf16[500,128]{1,0:T(8,128)(2,1)S(1)}, bf16[500,128]{1,0:T(8,128)(2,1)S(1)}, u32[]{:S(2)}, u32[]{:S(2)}) collective-permute-start(bf16[500,128]{1,0:T(8,128)(2,1)S(1)} %get-tuple-element.23), channel_id=1, source_target_pairs={{0,31},{1,0},{2,1},{3,2},{4,3},{5,4},{6,5},{7,6},{8,7},{9,8},{10,9... | collective-permute-start | bytes 384008 | tf_op jit(solution)/shard_map/ppermute | solution.py:389
  14.4 3.1 %prepare.1 = (f32[6,13,88,128]{3,2,1,0:T(8,128)S(1)}, f32[6,13,88,128]{3,2,1,0:T(8,128)S(1)}, bf16[1664,1792]{1,0:T(8,128)(2,1)S(1)}) custom-call(bf16[2,4,64000]{2,1,0:T(4,128)(2,1)} %orb_hbm.3, f32[2,40,1792]{2,1,0:T(8,128)} %constant.8.clone.rep_hbm), custom_call_target="tpu_custom_call" | custom-call | flops 10000000 | bytes 10000000 | tf_op jit(solution)/shard_map/prepare/pallas_call | solution.py:433
  17.5 0.0 collective-permute-done.4.prev_ref
  17.5 0.0 collective-permute-done.5.next_ref
  17.5 0.0 copy-start
  17.6 0.0 copy-start.1
  17.6 0.2 shard_map.93.refs_4_.refs_5_
  17.7 0.8 %copy-done = f32[40,1792]{1,0:T(8,128)S(1)} copy-done((f32[40,1792]{1,0:T(8,128)S(1)}, f32[40,1792]{1,0:T(8,128)}, u32[]{:S(2)}) %copy-start) | copy-done | bytes 286744
  18.5 0.0 copy-done.1
  18.5 8.3 %shard_map.94 = (f32[3,500,128]{2,1,0:T(8,128)S(1)}, bf16[1,500,128]{2,1,0:T(8,128)(2,1)S(1)}, bf16[2,500,128]{2,1,0:T(8,128)(2,1)S(1)}) custom-call(s32[52]{0:T(128)S(1)} %get-tuple-element.19.refs_0_.tab_ref, bf16[1664,1792]{1,0:T(8,128)(2,1)S(1)} %get-tuple-element.20.refs_1_, bf16[240,240]{1,0:T(8,128)(2,1)S(1)} %copy-done.1, f32[40,1792]{1,0:T(8,128)S(1)} %copy-done, ...), custom_call_target="tpu_custom_call" | custom-call | flops 2457600000 | bytes 10000000 | tf_op jit(solution)/shard_map/pallas_call | solution.py:464
  26.8 0.0 collective-permute-done.prev_ref
  26.8 0.0 collective-permute-done.1.next_ref
  26.8 0.2 shard_map.91.refs_4_
  27.0 0.0 copy-start.2
  27.0 8.3 %shard_map.92 = (f32[3,500,128]{2,1,0:T(8,128)S(1)}, bf16[1,500,128]{2,1,0:T(8,128)(2,1)S(1)}, bf16[2,500,128]{2,1,0:T(8,128)(2,1)S(1)}) custom-call(s32[52]{0:T(128)S(1)} %get-tuple-element.19.refs_0_.tab_ref, bf16[1664,1792]{1,0:T(8,128)(2,1)S(1)} %get-tuple-element.20.refs_1_, bf16[240,240]{1,0:T(8,128)(2,1)S(1)} %copy-done.1, f32[40,1792]{1,0:T(8,128)S(1)} %copy-done, ...), custom_call_target="tpu_custom_call" | custom-call | flops 2457600000 | bytes 10000000 | tf_op jit(solution)/shard_map/pallas_call | solution.py:464
  35.3 1.2 %collective-permute-start.7 = (bf16[2,500,128]{2,1,0:T(8,128)(2,1)S(1)}, bf16[2,500,128]{2,1,0:T(8,128)(2,1)S(1)}, u32[]{:S(2)}, u32[]{:S(2)}) collective-permute-start(bf16[2,500,128]{2,1,0:T(8,128)(2,1)S(1)} %get-tuple-element.30), channel_id=1, source_target_pairs={{0,31},{1,0},{2,1},{3,2},{4,3},{5,4},{6,5},{7,6},{8,7},{9,8},{10,9... | collective-permute-start | bytes 768008 | tf_op jit(solution)/shard_map/ppermute | solution.py:389
  36.5 0.1 collective-permute-start.3
  36.6 2.0 %collective-permute-start.6 = (bf16[1,500,128]{2,1,0:T(8,128)(2,1)S(1)}, bf16[1,500,128]{2,1,0:T(8,128)(2,1)S(1)}, u32[]{:S(2)}, u32[]{:S(2)}) collective-permute-start(bf16[1,500,128]{2,1,0:T(8,128)(2,1)S(1)} %get-tuple-element.29), channel_id=1, source_target_pairs={{0,1},{1,2},{2,3},{3,4},{4,5},{5,6},{6,7},{7,8},{8,9},{9,10},{10,1... | collective-permute-start | bytes 384008 | tf_op jit(solution)/shard_map/ppermute | solution.py:389
  38.5 0.9 %collective-permute-start.2 = (bf16[1,500,128]{2,1,0:T(8,128)(2,1)S(1)}, bf16[1,500,128]{2,1,0:T(8,128)(2,1)S(1)}, u32[]{:S(2)}, u32[]{:S(2)}) collective-permute-start(bf16[1,500,128]{2,1,0:T(8,128)(2,1)S(1)} %get-tuple-element.24), channel_id=1, source_target_pairs={{0,1},{1,2},{2,3},{3,4},{4,5},{5,6},{6,7},{7,8},{8,9},{9,10},{10,1... | collective-permute-start | bytes 384008 | tf_op jit(solution)/shard_map/ppermute | solution.py:389
  39.4 0.0 copy-done.2
  39.4 6.5 %shard_map.95.rest_ref = f32[2,500,128]{2,1,0:T(8,128)S(1)} custom-call(s32[52]{0:T(128)S(1)} %get-tuple-element.19.refs_0_.tab_ref, bf16[1664,1792]{1,0:T(8,128)(2,1)S(1)} %get-tuple-element.20.refs_1_, bf16[160,160]{1,0:T(8,128)(2,1)S(1)} %copy-done.2, f32[40,1792]{1,0:T(8,128)S(1)} %copy-done, f32[6,13,88,128]{3,2,1,0:T(8,128)S(1)} %shard_map.91.refs_4_, ...), custom_call_target="tpu_custom_call" | custom-call | flops 1638400000 | bytes 10000000 | tf_op jit(solution)/shard_map/pallas_call | solution.py:464
  46.0 3.9 %keep.1.refs_5_ = f32[7,1000,128]{2,1,0:T(8,128)} custom-call(s32[52]{0:T(128)S(1)} %get-tuple-element.19.refs_0_.tab_ref, f32[3,500,128]{2,1,0:T(8,128)S(1)} %get-tuple-element.31.low_ref, f32[3,500,128]{2,1,0:T(8,128)S(1)} %get-tuple-element.32.high_ref, f32[2,500,128]{2,1,0:T(8,128)S(1)} %shard_map.95.rest_ref), custom_call_target="tpu_custom_call" | custom-call | flops 1000000 | bytes 8000000 | tf_op jit(solution)/shard_map/keep/pallas_call | solution.py:489
  49.9 1.5 %collective-permute-done.6.refs_3_ = bf16[1,500,128]{2,1,0:T(8,128)(2,1)S(1)} collective-permute-done((bf16[1,500,128]{2,1,0:T(8,128)(2,1)S(1)}, bf16[1,500,128]{2,1,0:T(8,128)(2,1)S(1)}, u32[]{:S(2)}, u32[]{:S(2)}) %collective-permute-start.6) | collective-permute-done | bytes 128032 | tf_op jit(solution)/shard_map/ppermute | solution.py:389
  51.4 2.6 %collective-permute-done.2.refs_1_ = bf16[1,500,128]{2,1,0:T(8,128)(2,1)S(1)} collective-permute-done((bf16[1,500,128]{2,1,0:T(8,128)(2,1)S(1)}, bf16[1,500,128]{2,1,0:T(8,128)(2,1)S(1)}, u32[]{:S(2)}, u32[]{:S(2)}) %collective-permute-start.2) | collective-permute-done | bytes 128032 | tf_op jit(solution)/shard_map/ppermute | solution.py:389
  54.0 0.0 collective-permute-done.7.refs_4_
  54.0 1.2 %collective-permute-done.3.refs_2_ = bf16[2,500,128]{2,1,0:T(8,128)(2,1)S(1)} collective-permute-done((bf16[2,500,128]{2,1,0:T(8,128)(2,1)S(1)}, bf16[2,500,128]{2,1,0:T(8,128)(2,1)S(1)}, u32[]{:S(2)}, u32[]{:S(2)}) %collective-permute-start.3) | collective-permute-done | bytes 256032 | tf_op jit(solution)/shard_map/ppermute | solution.py:389
  55.2 1.4 %place.1 = f32[7,1000,128]{2,1,0:T(8,128)} custom-call(s32[52]{0:T(128)S(1)} %get-tuple-element.19.refs_0_.tab_ref, bf16[1,500,128]{2,1,0:T(8,128)(2,1)S(1)} %collective-permute-done.2.refs_1_, bf16[2,500,128]{2,1,0:T(8,128)(2,1)S(1)} %collective-permute-done.3.refs_2_, ...), custom_call_target="tpu_custom_call", output_to_operand_aliasing={{}: (5, {})} | custom-call | flops 1000000 | bytes 4000000 | tf_op jit(solution)/shard_map/place/pallas_call | solution.py:499
Async XLA Ops:
  2.5 15.0 %collective-permute-start.4 = (bf16[500,128]{1,0:T(8,128)(2,1)S(1)}, bf16[500,128]{1,0:T(8,128)(2,1)S(1)}, u32[]{:S(2)}, u32[]{:S(2)}) collective-permute-start(bf16[500,128]{1,0:T(8,128)(2,1)S(1)} %get-tuple-element.27), channel_id=1, source_target_pairs={{0,1},{1,2},{2,3},{3,4},{4,5},{5,6},{6,7},{7,8},{8,9},{9,10},{10,1... | collective-permute-start | bytes 384008 | tf_op jit(solution)/shard_map/ppermute | solution.py:389
  5.6 11.9 %collective-permute-start.5 = (bf16[500,128]{1,0:T(8,128)(2,1)S(1)}, bf16[500,128]{1,0:T(8,128)(2,1)S(1)}, u32[]{:S(2)}, u32[]{:S(2)}) collective-permute-start(bf16[500,128]{1,0:T(8,128)(2,1)S(1)} %get-tuple-element.28), channel_id=1, source_target_pairs={{0,31},{1,0},{2,1},{3,2},{4,3},{5,4},{6,5},{7,6},{8,7},{9,8},{10,9... | collective-permute-start | bytes 384008 | tf_op jit(solution)/shard_map/ppermute | solution.py:389
  9.0 17.8 %collective-permute-start = (bf16[500,128]{1,0:T(8,128)(2,1)S(1)}, bf16[500,128]{1,0:T(8,128)(2,1)S(1)}, u32[]{:S(2)}, u32[]{:S(2)}) collective-permute-start(bf16[500,128]{1,0:T(8,128)(2,1)S(1)} %get-tuple-element.22), channel_id=1, source_target_pairs={{0,1},{1,2},{2,3},{3,4},{4,5},{5,6},{6,7},{7,8},{8,9},{9,10},{10,1... | collective-permute-start | bytes 384008 | tf_op jit(solution)/shard_map/ppermute | solution.py:389
  9.1 17.8 %collective-permute-start.1 = (bf16[500,128]{1,0:T(8,128)(2,1)S(1)}, bf16[500,128]{1,0:T(8,128)(2,1)S(1)}, u32[]{:S(2)}, u32[]{:S(2)}) collective-permute-start(bf16[500,128]{1,0:T(8,128)(2,1)S(1)} %get-tuple-element.23), channel_id=1, source_target_pairs={{0,31},{1,0},{2,1},{3,2},{4,3},{5,4},{6,5},{7,6},{8,7},{9,8},{10,9... | collective-permute-start | bytes 384008 | tf_op jit(solution)/shard_map/ppermute | solution.py:389
  17.5 1.0 %copy-start = (f32[40,1792]{1,0:T(8,128)S(1)}, f32[40,1792]{1,0:T(8,128)}, u32[]{:S(2)}) copy-start(f32[40,1792]{1,0:T(8,128)} %constant.10.clone.refs_3_) | copy-start | bytes 860164
  17.6 1.0 %copy-start.1 = (bf16[240,240]{1,0:T(8,128)(2,1)S(1)}, bf16[240,240]{1,0:T(8,128)(2,1)}, u32[]{:S(2)}) copy-start(bf16[240,240]{1,0:T(8,128)(2,1)} %constant.9.clone.refs_2_) | copy-start | bytes 345604
  27.0 12.4 %copy-start.2 = (bf16[160,160]{1,0:T(8,128)(2,1)S(1)}, bf16[160,160]{1,0:T(8,128)(2,1)}, u32[]{:S(2)}) copy-start(bf16[160,160]{1,0:T(8,128)(2,1)} %constant.11.clone.refs_2_) | copy-start | bytes 153604
  35.3 18.7 %collective-permute-start.7 = (bf16[2,500,128]{2,1,0:T(8,128)(2,1)S(1)}, bf16[2,500,128]{2,1,0:T(8,128)(2,1)S(1)}, u32[]{:S(2)}, u32[]{:S(2)}) collective-permute-start(bf16[2,500,128]{2,1,0:T(8,128)(2,1)S(1)} %get-tuple-element.30), channel_id=1, source_target_pairs={{0,31},{1,0},{2,1},{3,2},{4,3},{5,4},{6,5},{7,6},{8,7},{9,8},{10,9... | collective-permute-start | bytes 768008 | tf_op jit(solution)/shard_map/ppermute | solution.py:389
  36.5 18.7 %collective-permute-start.3 = (bf16[2,500,128]{2,1,0:T(8,128)(2,1)S(1)}, bf16[2,500,128]{2,1,0:T(8,128)(2,1)S(1)}, u32[]{:S(2)}, u32[]{:S(2)}) collective-permute-start(bf16[2,500,128]{2,1,0:T(8,128)(2,1)S(1)} %get-tuple-element.25), channel_id=1, source_target_pairs={{0,31},{1,0},{2,1},{3,2},{4,3},{5,4},{6,5},{7,6},{8,7},{9,8},{10,9... | collective-permute-start | bytes 768008 | tf_op jit(solution)/shard_map/ppermute | solution.py:389
  36.6 14.9 %collective-permute-start.6 = (bf16[1,500,128]{2,1,0:T(8,128)(2,1)S(1)}, bf16[1,500,128]{2,1,0:T(8,128)(2,1)S(1)}, u32[]{:S(2)}, u32[]{:S(2)}) collective-permute-start(bf16[1,500,128]{2,1,0:T(8,128)(2,1)S(1)} %get-tuple-element.29), channel_id=1, source_target_pairs={{0,1},{1,2},{2,3},{3,4},{4,5},{5,6},{6,7},{7,8},{8,9},{9,10},{10,1... | collective-permute-start | bytes 384008 | tf_op jit(solution)/shard_map/ppermute | solution.py:389
  38.5 15.5 %collective-permute-start.2 = (bf16[1,500,128]{2,1,0:T(8,128)(2,1)S(1)}, bf16[1,500,128]{2,1,0:T(8,128)(2,1)S(1)}, u32[]{:S(2)}, u32[]{:S(2)}) collective-permute-start(bf16[1,500,128]{2,1,0:T(8,128)(2,1)S(1)} %get-tuple-element.24), channel_id=1, source_target_pairs={{0,1},{1,2},{2,3},{3,4},{4,5},{5,6},{6,7},{7,8},{8,9},{9,10},{10,1... | collective-permute-start | bytes 384008 | tf_op jit(solution)/shard_map/ppermute | solution.py:389

commit v5 on v4

--- a/solution.py
+++ b/solution.py
@@ -341,26 +341,53 @@
             sends[1][k] = out_ref[tab_ref[leaves + AHEAD + k]].astype(BF)
 
 
-def keep_kernel(tab_ref, low_ref, high_ref, rest_ref, out_ref):
+def keep_kernel(tab_ref, low_ref, high_ref, rest_ref, out_ref, form_ref, sems):
     first = low_ref.shape[0]
     boxes = first + rest_ref.shape[0] // 2
-    code = tab_ref[table_layout(boxes)[1] + pl.program_id(0)]
-
-    @pl.when(code < first)
-    def _():
-        spot = jnp.minimum(code, first - 1)
-        for spin, ref in enumerate((low_ref, high_ref)):
-            out_ref[0, pl.ds(spin, FLAT, stride=2), :] = ref[spot]
-
-    @pl.when((code >= first) & (code < boxes))
-    def _():
-        spot = jnp.clip(code - first, 0, boxes - first - 1)
-        for spin in range(2):
-            out_ref[0, pl.ds(spin, FLAT, stride=2), :] = rest_ref[2 * spot + spin]
-
-    @pl.when(code >= boxes + AHEAD + BACK)
-    def _():
-        out_ref[...] = jnp.zeros_like(out_ref)
+    codes = table_layout(boxes)[1]
+
+    def copy(slot):
+        return pltpu.make_async_copy(form_ref.at[slot], out_ref.at[slot], sems.at[slot])
+
+    def arrives(slot):
+        code = tab_ref[codes + slot]
+        return (code >= boxes) & (code < boxes + AHEAD + BACK)
+
+    def make(slot, _):
+        code = tab_ref[codes + slot]
+
+        @pl.when(code < first)
+        def _():
+            spot = jnp.minimum(code, first - 1)
+            for spin, ref in enumerate((low_ref, high_ref)):
+                form_ref[slot, pl.ds(spin, FLAT, stride=2), :] = ref[spot]
+
+        @pl.when((code >= first) & (code < boxes))
+        def _():
+            spot = jnp.clip(code - first, 0, boxes - first - 1)
+            for spin in range(2):
+                form_ref[slot, pl.ds(spin, FLAT, stride=2), :] = rest_ref[2 * spot + spin]
+
+        @pl.when(code >= boxes + AHEAD + BACK)
+        def _():
+            form_ref[slot] = jnp.zeros(form_ref.shape[1:], F32)
+
+        @pl.when(jnp.logical_not(arrives(slot)))
+        def _():
+            copy(slot).start()
+
+        return 0
+
+    lax.fori_loop(0, CAP, make, 0)
+
+    def finish(slot, _):
+        @pl.when(jnp.logical_not(arrives(slot)))
+        def _():
+            copy(slot).wait()
+
+        return 0
+
+    lax.fori_loop(0, CAP, finish, 0)
 
 
 def place_kernel(boxes, tab_ref, prev_low, next_low, prev_high, next_high, kept_ref, out_ref, form_ref, sems):
@@ -430,7 +457,7 @@
 
     slabs = jax.ShapeDtypeStruct((boxes + 2, TILES, ROWS, LANES), F32)
     constants = np.stack([repeated, tiled])
-    *pads, kron = pl.pallas_call(
+    prepare = pl.pallas_call(
         prepare_kernel,
         out_shape=[slabs, slabs, jax.ShapeDtypeStruct((WIDE, NWIDE), BF)],
         in_specs=[ANYWHERE] * 2,
@@ -440,7 +467,8 @@
         compiler_params=pltpu.CompilerParams(vmem_limit_bytes=20 << 20),
         cost_estimate=cost(10_000_000, 10_000_000),
         name="prepare",
-    )(in_place(orbitals), in_place(constants))
+    )
+    *pads, kron = prepare(in_place(orbitals), in_place(constants))
     for spin, halo in enumerate(((prev_low, next_low), (prev_high, next_high))):
         pads[spin] = pl.pallas_call(
             fill_kernel,
@@ -489,9 +517,9 @@
     kept = pl.pallas_call(
         keep_kernel,
         out_shape=shape,
-        grid=(CAP,),
         in_specs=[SCALARS] + whole(3),
-        out_specs=pl.BlockSpec((1, 2 * FLAT, LANES), lambda i: (i, 0, 0)),
+        out_specs=ANYWHERE,
+        scratch_shapes=[pltpu.VMEM((CAP, 2 * FLAT, LANES), F32), pltpu.SemaphoreType.DMA((CAP,))],
         compiler_params=pltpu.CompilerParams(vmem_limit_bytes=8 << 20),
         cost_estimate=cost(1_000_000, 8_000_000),
         name="keep",

time: 56.8 us -> 56.8 us (level)
  waiting for transfers between devices: 5.31 us -> 6.94 us
  Pallas kernels: 34.4 us -> 32.8 us
    pallas_call x2, Pallas kernels: 7.05 us -> 5.42 us  [the longest x1 3.13 us: shards(): *pads, kron = prepare(in_place(orbitals), in_place(constants))]
    ppermute x8, waiting for transfers between devices: 5.31 us -> 6.94 us  [from_behind(): lax.ppermute(value, AXES, [(source, (source + steps) % count) for source...]
  transfers between devices with their start and end apart: 8 -> 8, of which waited for: 3 -> 3; matrix products, arithmetic and copies ran while one was open for 0% -> 0% of each run, Pallas kernels for 39% -> 36%
where the time goes in v5:
time: 56.8 us; the launch traced here: 56.6 us
  Pallas kernels  32.8 us (58%)
  starting transfers between devices  16 us (28%)
  waiting for transfers between devices  6.94 us (12%)
  local copies, waits for them, and re-layouts  0.82 us (1%)
    pallas_call x3, Pallas kernels, solve(): pl.pallas_call(lambda *refs: pair_kernel(start, held, spins, *refs), out_...  23.1 us
    ppermute x8, starting transfers between devices, from_behind(): lax.ppermute(value, AXES, [(source, (source + steps) % count) for source...  16 us
    ppermute x8, waiting for transfers between devices, from_behind(): lax.ppermute(value, AXES, [(source, (source + steps) % count) for source...  6.94 us
    pallas_call x1, Pallas kernels, shards(): *pads, kron = prepare(in_place(orbitals), in_place(constants))  3.13 us
    pallas_call x1, Pallas kernels, shards(): pl.pallas_call(window_kernel, out_shape=[box] * 4 + [jax.ShapeDtypeStruct...  2.52 us
    pallas_call x1, Pallas kernels, shards(): pl.pallas_call(keep_kernel, out_shape=shape, in_specs=[SCALARS] + whole(3...  2.29 us
    pallas_call x1, Pallas kernels, shards(): pl.pallas_call(lambda *refs: place_kernel(boxes, *refs), out_shape=shape,...  1.4 us
  transfers between devices with their start and end apart: 8, of which 3 were waited for; matrix products, arithmetic and copies ran while one was open for 0% of the time, Pallas kernels for 36%

profile of v5, /device:TPU:0, one launch (start us, length us, event | category | flops | bytes accessed | tf_op | source)
XLA Modules:
  0.0 56.6 jit_solution(3684955772852780508)
XLA Ops:
  0.0 2.5 %window.1 = (bf16[500,128]{1,0:T(8,128)(2,1)S(1)}, bf16[500,128]{1,0:T(8,128)(2,1)S(1)}, bf16[500,128]{1,0:T(8,128)(2,1)S(1)}, bf16[500,128]{1,0:T(8,128)(2,1)S(1)}, s32[52]{0:T(128)S(1)}) custom-call(s32[128]{0:T(128)} %dest_hbm.1, s32[2,128]{1,0:T(2,128)} %bitcast.10, s32[3,128]{1,0:T(4,128)} %bitcast.9, bf16[2,4,64000]{2,1,0:T(4,128)(2,1)} %orb_hbm.3), custom_call_target="tpu_custom_call" | custom-call | tf_op jit(solution)/shard_map/window/pallas_call | solution.py:442
  2.5 3.1 %collective-permute-start.4 = (bf16[500,128]{1,0:T(8,128)(2,1)S(1)}, bf16[500,128]{1,0:T(8,128)(2,1)S(1)}, u32[]{:S(2)}, u32[]{:S(2)}) collective-permute-start(bf16[500,128]{1,0:T(8,128)(2,1)S(1)} %get-tuple-element.27), channel_id=1, source_target_pairs={{0,1},{1,2},{2,3},{3,4},{4,5},{5,6},{6,7},{7,8},{8,9},{9,10},{10,1... | collective-permute-start | bytes 384008 | tf_op jit(solution)/shard_map/ppermute | solution.py:416
  5.6 3.4 %collective-permute-start.5 = (bf16[500,128]{1,0:T(8,128)(2,1)S(1)}, bf16[500,128]{1,0:T(8,128)(2,1)S(1)}, u32[]{:S(2)}, u32[]{:S(2)}) collective-permute-start(bf16[500,128]{1,0:T(8,128)(2,1)S(1)} %get-tuple-element.28), channel_id=1, source_target_pairs={{0,31},{1,0},{2,1},{3,2},{4,3},{5,4},{6,5},{7,6},{8,7},{9,8},{10,9... | collective-permute-start | bytes 384008 | tf_op jit(solution)/shard_map/ppermute | solution.py:416
  9.0 0.0 collective-permute-start
  9.1 5.3 %collective-permute-start.1 = (bf16[500,128]{1,0:T(8,128)(2,1)S(1)}, bf16[500,128]{1,0:T(8,128)(2,1)S(1)}, u32[]{:S(2)}, u32[]{:S(2)}) collective-permute-start(bf16[500,128]{1,0:T(8,128)(2,1)S(1)} %get-tuple-element.23), channel_id=1, source_target_pairs={{0,31},{1,0},{2,1},{3,2},{4,3},{5,4},{6,5},{7,6},{8,7},{9,8},{10,9... | collective-permute-start | bytes 384008 | tf_op jit(solution)/shard_map/ppermute | solution.py:416
  14.4 3.1 %prepare.1 = (f32[6,13,88,128]{3,2,1,0:T(8,128)S(1)}, f32[6,13,88,128]{3,2,1,0:T(8,128)S(1)}, bf16[1664,1792]{1,0:T(8,128)(2,1)S(1)}) custom-call(bf16[2,4,64000]{2,1,0:T(4,128)(2,1)} %orb_hbm.3, f32[2,40,1792]{2,1,0:T(8,128)} %constant.8.clone.rep_hbm), custom_call_target="tpu_custom_call" | custom-call | flops 10000000 | bytes 10000000 | tf_op jit(solution)/shard_map/prepare/pallas_call | solution.py:471
  17.5 0.0 collective-permute-done.4.prev_ref
  17.5 0.0 collective-permute-done.5.next_ref
  17.5 0.0 copy-start
  17.6 0.0 copy-start.1
  17.6 0.2 shard_map.93.refs_4_.refs_5_
  17.7 0.8 %copy-done = f32[40,1792]{1,0:T(8,128)S(1)} copy-done((f32[40,1792]{1,0:T(8,128)S(1)}, f32[40,1792]{1,0:T(8,128)}, u32[]{:S(2)}) %copy-start) | copy-done | bytes 286744
  18.5 0.0 copy-done.1
  18.5 8.3 %shard_map.94 = (f32[3,500,128]{2,1,0:T(8,128)S(1)}, bf16[1,500,128]{2,1,0:T(8,128)(2,1)S(1)}, bf16[2,500,128]{2,1,0:T(8,128)(2,1)S(1)}) custom-call(s32[52]{0:T(128)S(1)} %get-tuple-element.19.refs_0_.tab_ref, bf16[1664,1792]{1,0:T(8,128)(2,1)S(1)} %get-tuple-element.20.refs_1_, bf16[240,240]{1,0:T(8,128)(2,1)S(1)} %copy-done.1, f32[40,1792]{1,0:T(8,128)S(1)} %copy-done, ...), custom_call_target="tpu_custom_call" | custom-call | flops 2457600000 | bytes 10000000 | tf_op jit(solution)/shard_map/pallas_call | solution.py:492
  26.8 0.0 collective-permute-done.prev_ref
  26.8 0.0 collective-permute-done.1.next_ref
  26.8 0.2 shard_map.91.refs_4_
  27.0 0.0 copy-start.2
  27.0 8.3 %shard_map.92 = (f32[3,500,128]{2,1,0:T(8,128)S(1)}, bf16[1,500,128]{2,1,0:T(8,128)(2,1)S(1)}, bf16[2,500,128]{2,1,0:T(8,128)(2,1)S(1)}) custom-call(s32[52]{0:T(128)S(1)} %get-tuple-element.19.refs_0_.tab_ref, bf16[1664,1792]{1,0:T(8,128)(2,1)S(1)} %get-tuple-element.20.refs_1_, bf16[240,240]{1,0:T(8,128)(2,1)S(1)} %copy-done.1, f32[40,1792]{1,0:T(8,128)S(1)} %copy-done, ...), custom_call_target="tpu_custom_call" | custom-call | flops 2457600000 | bytes 10000000 | tf_op jit(solution)/shard_map/pallas_call | solution.py:492
  35.3 1.2 %collective-permute-start.7 = (bf16[2,500,128]{2,1,0:T(8,128)(2,1)S(1)}, bf16[2,500,128]{2,1,0:T(8,128)(2,1)S(1)}, u32[]{:S(2)}, u32[]{:S(2)}) collective-permute-start(bf16[2,500,128]{2,1,0:T(8,128)(2,1)S(1)} %get-tuple-element.30), channel_id=1, source_target_pairs={{0,31},{1,0},{2,1},{3,2},{4,3},{5,4},{6,5},{7,6},{8,7},{9,8},{10,9... | collective-permute-start | bytes 768008 | tf_op jit(solution)/shard_map/ppermute | solution.py:416
  36.5 0.1 collective-permute-start.3
  36.6 2.0 %collective-permute-start.6 = (bf16[1,500,128]{2,1,0:T(8,128)(2,1)S(1)}, bf16[1,500,128]{2,1,0:T(8,128)(2,1)S(1)}, u32[]{:S(2)}, u32[]{:S(2)}) collective-permute-start(bf16[1,500,128]{2,1,0:T(8,128)(2,1)S(1)} %get-tuple-element.29), channel_id=1, source_target_pairs={{0,1},{1,2},{2,3},{3,4},{4,5},{5,6},{6,7},{7,8},{8,9},{9,10},{10,1... | collective-permute-start | bytes 384008 | tf_op jit(solution)/shard_map/ppermute | solution.py:416
  38.5 0.9 %collective-permute-start.2 = (bf16[1,500,128]{2,1,0:T(8,128)(2,1)S(1)}, bf16[1,500,128]{2,1,0:T(8,128)(2,1)S(1)}, u32[]{:S(2)}, u32[]{:S(2)}) collective-permute-start(bf16[1,500,128]{2,1,0:T(8,128)(2,1)S(1)} %get-tuple-element.24), channel_id=1, source_target_pairs={{0,1},{1,2},{2,3},{3,4},{4,5},{5,6},{6,7},{7,8},{8,9},{9,10},{10,1... | collective-permute-start | bytes 384008 | tf_op jit(solution)/shard_map/ppermute | solution.py:416
  39.4 0.0 copy-done.2
  39.4 6.5 %shard_map.95.rest_ref = f32[2,500,128]{2,1,0:T(8,128)S(1)} custom-call(s32[52]{0:T(128)S(1)} %get-tuple-element.19.refs_0_.tab_ref, bf16[1664,1792]{1,0:T(8,128)(2,1)S(1)} %get-tuple-element.20.refs_1_, bf16[160,160]{1,0:T(8,128)(2,1)S(1)} %copy-done.2, f32[40,1792]{1,0:T(8,128)S(1)} %copy-done, f32[6,13,88,128]{3,2,1,0:T(8,128)S(1)} %shard_map.91.refs_4_, ...), custom_call_target="tpu_custom_call" | custom-call | flops 1638400000 | bytes 10000000 | tf_op jit(solution)/shard_map/pallas_call | solution.py:492
  46.0 2.3 %keep.1.refs_5_ = f32[7,1000,128]{2,1,0:T(8,128)} custom-call(s32[52]{0:T(128)S(1)} %get-tuple-element.19.refs_0_.tab_ref, f32[3,500,128]{2,1,0:T(8,128)S(1)} %get-tuple-element.31.low_ref, f32[3,500,128]{2,1,0:T(8,128)S(1)} %get-tuple-element.32.high_ref, f32[2,500,128]{2,1,0:T(8,128)S(1)} %shard_map.95.rest_ref), custom_call_target="tpu_custom_call" | custom-call | flops 1000000 | bytes 8000000 | tf_op jit(solution)/shard_map/keep/pallas_call | solution.py:517
  48.3 3.2 %collective-permute-done.6.refs_3_ = bf16[1,500,128]{2,1,0:T(8,128)(2,1)S(1)} collective-permute-done((bf16[1,500,128]{2,1,0:T(8,128)(2,1)S(1)}, bf16[1,500,128]{2,1,0:T(8,128)(2,1)S(1)}, u32[]{:S(2)}, u32[]{:S(2)}) %collective-permute-start.6) | collective-permute-done | bytes 128032 | tf_op jit(solution)/shard_map/ppermute | solution.py:416
  51.4 2.6 %collective-permute-done.2.refs_1_ = bf16[1,500,128]{2,1,0:T(8,128)(2,1)S(1)} collective-permute-done((bf16[1,500,128]{2,1,0:T(8,128)(2,1)S(1)}, bf16[1,500,128]{2,1,0:T(8,128)(2,1)S(1)}, u32[]{:S(2)}, u32[]{:S(2)}) %collective-permute-start.2) | collective-permute-done | bytes 128032 | tf_op jit(solution)/shard_map/ppermute | solution.py:416
  54.0 0.0 collective-permute-done.7.refs_4_
  54.0 1.2 %collective-permute-done.3.refs_2_ = bf16[2,500,128]{2,1,0:T(8,128)(2,1)S(1)} collective-permute-done((bf16[2,500,128]{2,1,0:T(8,128)(2,1)S(1)}, bf16[2,500,128]{2,1,0:T(8,128)(2,1)S(1)}, u32[]{:S(2)}, u32[]{:S(2)}) %collective-permute-start.3) | collective-permute-done | bytes 256032 | tf_op jit(solution)/shard_map/ppermute | solution.py:416
  55.2 1.4 %place.1 = f32[7,1000,128]{2,1,0:T(8,128)} custom-call(s32[52]{0:T(128)S(1)} %get-tuple-element.19.refs_0_.tab_ref, bf16[1,500,128]{2,1,0:T(8,128)(2,1)S(1)} %collective-permute-done.2.refs_1_, bf16[2,500,128]{2,1,0:T(8,128)(2,1)S(1)} %collective-permute-done.3.refs_2_, ...), custom_call_target="tpu_custom_call", output_to_operand_aliasing={{}: (5, {})} | custom-call | flops 1000000 | bytes 4000000 | tf_op jit(solution)/shard_map/place/pallas_call | solution.py:527
Async XLA Ops:
  2.5 15.0 %collective-permute-start.4 = (bf16[500,128]{1,0:T(8,128)(2,1)S(1)}, bf16[500,128]{1,0:T(8,128)(2,1)S(1)}, u32[]{:S(2)}, u32[]{:S(2)}) collective-permute-start(bf16[500,128]{1,0:T(8,128)(2,1)S(1)} %get-tuple-element.27), channel_id=1, source_target_pairs={{0,1},{1,2},{2,3},{3,4},{4,5},{5,6},{6,7},{7,8},{8,9},{9,10},{10,1... | collective-permute-start | bytes 384008 | tf_op jit(solution)/shard_map/ppermute | solution.py:416
  5.6 11.9 %collective-permute-start.5 = (bf16[500,128]{1,0:T(8,128)(2,1)S(1)}, bf16[500,128]{1,0:T(8,128)(2,1)S(1)}, u32[]{:S(2)}, u32[]{:S(2)}) collective-permute-start(bf16[500,128]{1,0:T(8,128)(2,1)S(1)} %get-tuple-element.28), channel_id=1, source_target_pairs={{0,31},{1,0},{2,1},{3,2},{4,3},{5,4},{6,5},{7,6},{8,7},{9,8},{10,9... | collective-permute-start | bytes 384008 | tf_op jit(solution)/shard_map/ppermute | solution.py:416
  9.0 17.8 %collective-permute-start = (bf16[500,128]{1,0:T(8,128)(2,1)S(1)}, bf16[500,128]{1,0:T(8,128)(2,1)S(1)}, u32[]{:S(2)}, u32[]{:S(2)}) collective-permute-start(bf16[500,128]{1,0:T(8,128)(2,1)S(1)} %get-tuple-element.22), channel_id=1, source_target_pairs={{0,1},{1,2},{2,3},{3,4},{4,5},{5,6},{6,7},{7,8},{8,9},{9,10},{10,1... | collective-permute-start | bytes 384008 | tf_op jit(solution)/shard_map/ppermute | solution.py:416
  9.1 17.8 %collective-permute-start.1 = (bf16[500,128]{1,0:T(8,128)(2,1)S(1)}, bf16[500,128]{1,0:T(8,128)(2,1)S(1)}, u32[]{:S(2)}, u32[]{:S(2)}) collective-permute-start(bf16[500,128]{1,0:T(8,128)(2,1)S(1)} %get-tuple-element.23), channel_id=1, source_target_pairs={{0,31},{1,0},{2,1},{3,2},{4,3},{5,4},{6,5},{7,6},{8,7},{9,8},{10,9... | collective-permute-start | bytes 384008 | tf_op jit(solution)/shard_map/ppermute | solution.py:416
  17.5 1.0 %copy-start = (f32[40,1792]{1,0:T(8,128)S(1)}, f32[40,1792]{1,0:T(8,128)}, u32[]{:S(2)}) copy-start(f32[40,1792]{1,0:T(8,128)} %constant.10.clone.refs_3_) | copy-start | bytes 860164
  17.6 1.0 %copy-start.1 = (bf16[240,240]{1,0:T(8,128)(2,1)S(1)}, bf16[240,240]{1,0:T(8,128)(2,1)}, u32[]{:S(2)}) copy-start(bf16[240,240]{1,0:T(8,128)(2,1)} %constant.9.clone.refs_2_) | copy-start | bytes 345604
  27.0 12.4 %copy-start.2 = (bf16[160,160]{1,0:T(8,128)(2,1)S(1)}, bf16[160,160]{1,0:T(8,128)(2,1)}, u32[]{:S(2)}) copy-start(bf16[160,160]{1,0:T(8,128)(2,1)} %constant.11.clone.refs_2_) | copy-start | bytes 153604
  35.3 18.7 %collective-permute-start.7 = (bf16[2,500,128]{2,1,0:T(8,128)(2,1)S(1)}, bf16[2,500,128]{2,1,0:T(8,128)(2,1)S(1)}, u32[]{:S(2)}, u32[]{:S(2)}) collective-permute-start(bf16[2,500,128]{2,1,0:T(8,128)(2,1)S(1)} %get-tuple-element.30), channel_id=1, source_target_pairs={{0,31},{1,0},{2,1},{3,2},{4,3},{5,4},{6,5},{7,6},{8,7},{9,8},{10,9... | collective-permute-start | bytes 768008 | tf_op jit(solution)/shard_map/ppermute | solution.py:416
  36.5 18.7 %collective-permute-start.3 = (bf16[2,500,128]{2,1,0:T(8,128)(2,1)S(1)}, bf16[2,500,128]{2,1,0:T(8,128)(2,1)S(1)}, u32[]{:S(2)}, u32[]{:S(2)}) collective-permute-start(bf16[2,500,128]{2,1,0:T(8,128)(2,1)S(1)} %get-tuple-element.25), channel_id=1, source_target_pairs={{0,31},{1,0},{2,1},{3,2},{4,3},{5,4},{6,5},{7,6},{8,7},{9,8},{10,9... | collective-permute-start | bytes 768008 | tf_op jit(solution)/shard_map/ppermute | solution.py:416
  36.6 14.9 %collective-permute-start.6 = (bf16[1,500,128]{2,1,0:T(8,128)(2,1)S(1)}, bf16[1,500,128]{2,1,0:T(8,128)(2,1)S(1)}, u32[]{:S(2)}, u32[]{:S(2)}) collective-permute-start(bf16[1,500,128]{2,1,0:T(8,128)(2,1)S(1)} %get-tuple-element.29), channel_id=1, source_target_pairs={{0,1},{1,2},{2,3},{3,4},{4,5},{5,6},{6,7},{7,8},{8,9},{9,10},{10,1... | collective-permute-start | bytes 384008 | tf_op jit(solution)/shard_map/ppermute | solution.py:416
  38.5 15.5 %collective-permute-start.2 = (bf16[1,500,128]{2,1,0:T(8,128)(2,1)S(1)}, bf16[1,500,128]{2,1,0:T(8,128)(2,1)S(1)}, u32[]{:S(2)}, u32[]{:S(2)}) collective-permute-start(bf16[1,500,128]{2,1,0:T(8,128)(2,1)S(1)} %get-tuple-element.24), channel_id=1, source_target_pairs={{0,1},{1,2},{2,3},{3,4},{4,5},{5,6},{6,7},{7,8},{8,9},{9,10},{10,1... | collective-permute-start | bytes 384008 | tf_op jit(solution)/shard_map/ppermute | solution.py:416

commit v6 on v4

--- a/solution.py
+++ b/solution.py
@@ -133,16 +133,19 @@
     slots = codes + CAP + 1
     leaves = slots + AHEAD + BACK + 1
     order = leaves + AHEAD + BACK + 1
-    return pairs, codes, slots, leaves, order, order + boxes
+    homes = order + boxes
+    return pairs, codes, slots, leaves, order, homes, homes + boxes + 1
 
 
 def build_tables(dest_ref, part_ref, anc_ref, tab_ref, boxes):
     total = part_ref.shape[1]
     device = lax.axis_index(AXES)
-    pairs, codes, slots, leaves, order, _ = table_layout(boxes)
+    pairs, codes, slots, leaves, order, homes, _ = table_layout(boxes)
     one, none = jnp.int32(1), jnp.int32(0)
     for k in range(CAP + 1):
         tab_ref[codes + k] = boxes + AHEAD + BACK
+    for k in range(boxes + 1):
+        tab_ref[homes + k] = 0
     for k in range(AHEAD + BACK + 1):
         tab_ref[slots + k] = CAP
         tab_ref[leaves + k] = 0
@@ -172,6 +175,7 @@
             hit = (box >= 0) & (box < total) & (dest_ref[jnp.clip(box, 0, total - 1)] == device)
             if block == 1:
                 code = spots[k]
+                tab_ref[jnp.where(hit, homes + code, homes + boxes)] = jnp.minimum(count, CAP - 1)
             else:
                 first, most = (0, AHEAD) if block == 0 else (AHEAD, BACK)
                 where = first + jnp.minimum(arrived, most - 1)
@@ -193,10 +197,12 @@
                 tab_ref[base + 1 + axis] = jnp.clip(moved - extent // 2, -(PAD - 4), PAD - 4)
 
 
-def prepare_kernel(orb_hbm, rep_hbm, low_ref, high_ref, kron_ref, orb_ref, rep_ref, flat_ref, sems):
+def prepare_kernel(orb_hbm, rep_hbm, inv_hbm, diag_hbm, rest_hbm, low_ref, high_ref, kron_ref, inv_ref, diag_ref, rest_ref,
+                   orb_ref, rep_ref, flat_ref, sems):
     boxes = orb_ref.shape[1]
     copies = [pltpu.make_async_copy(orb_hbm.at[spin], orb_ref.at[spin], sems.at[spin]) for spin in range(2)]
-    copies.append(pltpu.make_async_copy(rep_hbm, rep_ref, sems.at[2]))
+    copies += [pltpu.make_async_copy(source, target, sems.at[2 + k]) for k, (source, target) in enumerate(
+        ((rep_hbm, rep_ref), (inv_hbm, inv_ref), (diag_hbm, diag_ref), (rest_hbm, rest_ref)))]
     for copy in copies:
         copy.start()
     for spin, pad_ref in enumerate((low_ref, high_ref)):
@@ -227,6 +233,8 @@
 
     lax.fori_loop(0, HALF, build, 0)
     kron_ref[FACE:, :] = jnp.zeros((WIDE - FACE, NWIDE), BF)
+    for copy in copies[3:]:
+        copy.wait()
 
 
 def fill_kernel(old_ref, prev_ref, next_ref, pad_ref, flat_ref):
@@ -240,11 +248,36 @@
         )
 
 
-def pair_kernel(start, held, spins, tab_ref, kron_ref, diag_ref, inv_ref, *refs):
-    pads, out_ref, sends = refs[:len(spins)], refs[len(spins)], refs[len(spins) + 1:-4]
-    mov_ref, x_ref, y_ref, res_ref = refs[-4:]
+def pair_kernel(start, held, spins, final, tab_ref, kron_ref, diag_ref, inv_ref, *refs):
+    pads, (mov_ref, x_ref, y_ref, res_ref) = refs[:len(spins)], refs[-4:]
     boxes = pads[0].shape[0] - 2
-    pairs, _, _, leaves, order, _ = table_layout(boxes)
+    pairs, codes, _, leaves, order, homes, _ = table_layout(boxes)
+    if final:
+        low_ref, high_ref, out_ref, form_ref, sems = refs[len(spins):-4]
+
+        def copy(slot):
+            return pltpu.make_async_copy(form_ref.at[slot], out_ref.at[slot], sems.at[slot])
+
+        def early(slot, _):
+            code = tab_ref[codes + slot]
+
+            @pl.when(code < start)
+            def _():
+                spot = jnp.minimum(code, start - 1)
+                for spin, ref in enumerate((low_ref, high_ref)):
+                    form_ref[slot, pl.ds(spin, FLAT, stride=2), :] = ref[spot]
+                copy(slot).start()
+
+            @pl.when(code >= boxes + AHEAD + BACK)
+            def _():
+                form_ref[slot] = jnp.zeros(form_ref.shape[1:], F32)
+                copy(slot).start()
+
+            return 0
+
+        lax.fori_loop(0, CAP, early, 0)
+    else:
+        out_ref, sends = refs[len(spins)], refs[len(spins) + 1:-4]
     lanes = lane_iota()
     rows = lax.broadcasted_iota(jnp.int32, (EDGE, 1), 0)
 
@@ -326,6 +359,29 @@
                     total = total + potential[first:first + EDGE] * mov_ref[index, at, number, u]
                 res_ref[index * len(spins) + at, u] = total
 
+    if final:
+        for index in range(held):
+            home = tab_ref[homes + start + index]
+            for at in range(len(spins)):
+                slabs_to_flat(
+                    lambda u, parity: res_ref[index * len(spins) + at, u, pl.ds(parity, HALF, stride=2), :],
+                    lambda t, x: form_ref.__setitem__(
+                        (home, pl.ds(2 * t + at, HALF, stride=2 * PAIRT), slice(None)), x),
+                )
+            copy(home).start()
+
+        def finish(slot, _):
+            code = tab_ref[codes + slot]
+
+            @pl.when((code < boxes) | (code >= boxes + AHEAD + BACK))
+            def _():
+                copy(slot).wait()
+
+            return 0
+
+        lax.fori_loop(0, CAP, finish, 0)
+        return
+
     def flatten(row, _):
         slabs_to_flat(
             lambda u, parity: res_ref[row, u, pl.ds(parity, HALF, stride=2), :],
@@ -334,33 +390,10 @@
         return 0
 
     lax.fori_loop(0, held * len(spins), flatten, 0)
-    if sends:
-        for k in range(AHEAD):
-            sends[0][k] = out_ref[tab_ref[leaves + k]].astype(BF)
-        for k in range(BACK):
-            sends[1][k] = out_ref[tab_ref[leaves + AHEAD + k]].astype(BF)
-
-
-def keep_kernel(tab_ref, low_ref, high_ref, rest_ref, out_ref):
-    first = low_ref.shape[0]
-    boxes = first + rest_ref.shape[0] // 2
-    code = tab_ref[table_layout(boxes)[1] + pl.program_id(0)]
-
-    @pl.when(code < first)
-    def _():
-        spot = jnp.minimum(code, first - 1)
-        for spin, ref in enumerate((low_ref, high_ref)):
-            out_ref[0, pl.ds(spin, FLAT, stride=2), :] = ref[spot]
-
-    @pl.when((code >= first) & (code < boxes))
-    def _():
-        spot = jnp.clip(code - first, 0, boxes - first - 1)
-        for spin in range(2):
-            out_ref[0, pl.ds(spin, FLAT, stride=2), :] = rest_ref[2 * spot + spin]
-
-    @pl.when(code >= boxes + AHEAD + BACK)
-    def _():
-        out_ref[...] = jnp.zeros_like(out_ref)
+    for k in range(AHEAD):
+        sends[0][k] = out_ref[tab_ref[leaves + k]].astype(BF)
+    for k in range(BACK):
+        sends[1][k] = out_ref[tab_ref[leaves + AHEAD + k]].astype(BF)
 
 
 def place_kernel(boxes, tab_ref, prev_low, next_low, prev_high, next_high, kept_ref, out_ref, form_ref, sems):
@@ -428,19 +461,26 @@
     prev_high = from_behind(ahead_high, 1)
     next_high = from_behind(back_high, -1)
 
+    moving = AHEAD + BACK
     slabs = jax.ShapeDtypeStruct((boxes + 2, TILES, ROWS, LANES), F32)
     constants = np.stack([repeated, tiled])
-    *pads, kron = pl.pallas_call(
+    diags = [np.kron(np.eye(cubes, dtype=np.float32), sine).astype(jnp.bfloat16)
+             for cubes in (moving * PARTNERS, (boxes - moving) * 2 * PARTNERS)]
+    handed = (inverse, *diags)
+    prepare = pl.pallas_call(
         prepare_kernel,
-        out_shape=[slabs, slabs, jax.ShapeDtypeStruct((WIDE, NWIDE), BF)],
-        in_specs=[ANYWHERE] * 2,
-        out_specs=whole(3),
+        out_shape=[slabs, slabs, jax.ShapeDtypeStruct((WIDE, NWIDE), BF)]
+        + [jax.ShapeDtypeStruct(value.shape, value.dtype) for value in handed],
+        in_specs=[ANYWHERE] * 5,
+        out_specs=whole(6),
         scratch_shapes=[pltpu.VMEM(orbitals.shape, BF), pltpu.VMEM(constants.shape, F32), splitter,
-                        pltpu.SemaphoreType.DMA((3,))],
+                        pltpu.SemaphoreType.DMA((6,))],
         compiler_params=pltpu.CompilerParams(vmem_limit_bytes=20 << 20),
         cost_estimate=cost(10_000_000, 10_000_000),
         name="prepare",
-    )(in_place(orbitals), in_place(constants))
+    )
+    low, high, kron, inverse, *diags = prepare(*map(in_place, (orbitals, constants, *handed)))
+    pads = [low, high]
     for spin, halo in enumerate(((prev_low, next_low), (prev_high, next_high))):
         pads[spin] = pl.pallas_call(
             fill_kernel,
@@ -453,20 +493,25 @@
             cost_estimate=cost(1_000_000, 2_000_000),
         )(pads[spin], *halo)
 
-    moving = AHEAD + BACK
-
-    def solve(start, held, spins, send):
+    shape = jax.ShapeDtypeStruct((CAP, 2 * FLAT, LANES), F32)
+
+    def solve(start, held, spins, terms=None):
         cubes = held * len(spins) * PARTNERS
-        diag = np.kron(np.eye(cubes, dtype=np.float32), sine).astype(jnp.bfloat16)
-        shapes = [jax.ShapeDtypeStruct((held * len(spins), FLAT, LANES), F32)]
-        if send:
+        final = terms is not None
+        if final:
+            shapes, specs = [shape], [ANYWHERE]
+            extra = [pltpu.VMEM(shape.shape, F32), pltpu.SemaphoreType.DMA((CAP,))]
+        else:
+            shapes = [jax.ShapeDtypeStruct((held * len(spins), FLAT, LANES), F32)]
             shapes += [jax.ShapeDtypeStruct((count, FLAT, LANES), BF) for count in (AHEAD, BACK)]
+            specs, extra = whole(3), []
+        operands = [table, kron, diags[final], inverse] + [pads[spin] for spin in spins] + (terms or [])
         return pl.pallas_call(
-            lambda *refs: pair_kernel(start, held, spins, *refs),
+            lambda *refs: pair_kernel(start, held, spins, final, *refs),
             out_shape=shapes,
-            in_specs=[SCALARS] + whole(3 + len(spins)),
-            out_specs=whole(len(shapes)),
-            scratch_shapes=[
+            in_specs=[SCALARS] + whole(len(operands) - 1),
+            out_specs=specs,
+            scratch_shapes=extra + [
                 pltpu.VMEM((held, len(spins), PARTNERS, TILES, EDGE, LANES), F32),
                 pltpu.VMEM((cubes * EDGE, NWIDE), BF),
                 pltpu.VMEM((cubes * EDGE, NWIDE), BF),
@@ -474,28 +519,16 @@
             ],
             compiler_params=pltpu.CompilerParams(vmem_limit_bytes=20 << 20),
             cost_estimate=cost(4 * cubes * EDGE * FACE * FACE, 10_000_000),
-        )(table, kron, diag, inverse, *[pads[spin] for spin in spins])
+        )(*operands)
 
     terms, arrived = [], []
     for spin in range(2):
-        mine, sent_ahead, sent_back = solve(0, moving, (spin,), True)
+        mine, sent_ahead, sent_back = solve(0, moving, (spin,))
         terms.append(mine)
         ahead = from_behind(sent_ahead, 1)
         back = from_behind(sent_back, -1)
         arrived += [ahead, back]
-    terms += solve(moving, boxes - moving, (0, 1), False)
-
-    shape = jax.ShapeDtypeStruct((CAP, 2 * FLAT, LANES), F32)
-    kept = pl.pallas_call(
-        keep_kernel,
-        out_shape=shape,
-        grid=(CAP,),
-        in_specs=[SCALARS] + whole(3),
-        out_specs=pl.BlockSpec((1, 2 * FLAT, LANES), lambda i: (i, 0, 0)),
-        compiler_params=pltpu.CompilerParams(vmem_limit_bytes=8 << 20),
-        cost_estimate=cost(1_000_000, 8_000_000),
-        name="keep",
-    )(table, *terms)
+    kept, = solve(moving, boxes - moving, (0, 1), terms)
     placed = pl.pallas_call(
         lambda *refs: place_kernel(boxes, *refs),
         out_shape=shape,

time: 56.8 us -> 50.9 us (0.90)
  Pallas kernels: 34.4 us -> 31.6 us
  waiting for transfers between devices: 5.31 us -> 3.06 us
  local copies, waits for them, and re-layouts: 0.82 us -> 0 us
    pallas_call x5 -> x4, Pallas kernels: 30.2 us -> 27.3 us  [the longest x3 24.2 us: solve(): pl.pallas_call(lambda *refs: pair_kernel(start, held, spins, final, *refs...]
    ppermute x8, waiting for transfers between devices: 5.31 us -> 3.06 us  [from_behind(): lax.ppermute(value, AXES, [(source, (source + steps) % count) for source...]
    unnamed x6 -> x0, local copies, waits for them, and re-layouts: 0.82 us -> none
  transfers between devices with their start and end apart: 8 -> 8, of which waited for: 3 -> 2; matrix products, arithmetic and copies ran while one was open for 0% -> 0% of each run, Pallas kernels for 39% -> 55%
where the time goes in v6:
time: 50.9 us; the launch traced here: 50.7 us
  Pallas kernels  31.6 us (62%)
  starting transfers between devices  16 us (31%)
  waiting for transfers between devices  3.06 us (6%)
    pallas_call x3, Pallas kernels, solve(): pl.pallas_call(lambda *refs: pair_kernel(start, held, spins, final, *refs...  24.2 us
    ppermute x8, starting transfers between devices, from_behind(): lax.ppermute(value, AXES, [(source, (source + steps) % count) for source...  16 us
    pallas_call x1, Pallas kernels, shards(): prepare(*map(in_place, (orbitals, constants, *handed)))  3.16 us
    ppermute x8, waiting for transfers between devices, from_behind(): lax.ppermute(value, AXES, [(source, (source + steps) % count) for source...  3.06 us
    pallas_call x1, Pallas kernels, shards(): pl.pallas_call(window_kernel, out_shape=[box] * 4 + [jax.ShapeDtypeStruct...  2.53 us
    pallas_call x1, Pallas kernels, shards(): pl.pallas_call(lambda *refs: place_kernel(boxes, *refs), out_shape=shape,...  1.4 us
  transfers between devices with their start and end apart: 8, of which 2 were waited for; matrix products, arithmetic and copies ran while one was open for 0% of the time, Pallas kernels for 55%

profile of v6, /device:TPU:0, one launch (start us, length us, event | category | flops | bytes accessed | tf_op | source)
XLA Modules:
  0.0 50.7 jit_solution(12366174830542270661)
XLA Ops:
  0.0 2.5 %window.1 = (bf16[500,128]{1,0:T(8,128)(2,1)S(1)}, bf16[500,128]{1,0:T(8,128)(2,1)S(1)}, bf16[500,128]{1,0:T(8,128)(2,1)S(1)}, bf16[500,128]{1,0:T(8,128)(2,1)S(1)}, s32[57]{0:T(128)S(1)}) custom-call(s32[128]{0:T(128)} %dest_hbm.1, s32[2,128]{1,0:T(2,128)} %bitcast.10, s32[3,128]{1,0:T(4,128)} %bitcast.9, bf16[2,4,64000]{2,1,0:T(4,128)(2,1)} %orb_hbm.3), custom_call_target="tpu_custom_call" | custom-call | tf_op jit(solution)/shard_map/window/pallas_call | solution.py:448
  2.5 3.1 %collective-permute-start = (bf16[500,128]{1,0:T(8,128)(2,1)S(1)}, bf16[500,128]{1,0:T(8,128)(2,1)S(1)}, u32[]{:S(2)}, u32[]{:S(2)}) collective-permute-start(bf16[500,128]{1,0:T(8,128)(2,1)S(1)} %get-tuple-element.27), channel_id=1, source_target_pairs={{0,1},{1,2},{2,3},{3,4},{4,5},{5,6},{6,7},{7,8},{8,9},{9,10},{10,1... | collective-permute-start | bytes 384008 | tf_op jit(solution)/shard_map/ppermute | solution.py:422
  5.6 3.4 %collective-permute-start.1 = (bf16[500,128]{1,0:T(8,128)(2,1)S(1)}, bf16[500,128]{1,0:T(8,128)(2,1)S(1)}, u32[]{:S(2)}, u32[]{:S(2)}) collective-permute-start(bf16[500,128]{1,0:T(8,128)(2,1)S(1)} %get-tuple-element.28), channel_id=1, source_target_pairs={{0,31},{1,0},{2,1},{3,2},{4,3},{5,4},{6,5},{7,6},{8,7},{9,8},{10,9... | collective-permute-start | bytes 384008 | tf_op jit(solution)/shard_map/ppermute | solution.py:422
  9.1 0.0 collective-permute-start.4
  9.1 5.3 %collective-permute-start.5 = (bf16[500,128]{1,0:T(8,128)(2,1)S(1)}, bf16[500,128]{1,0:T(8,128)(2,1)S(1)}, u32[]{:S(2)}, u32[]{:S(2)}) collective-permute-start(bf16[500,128]{1,0:T(8,128)(2,1)S(1)} %get-tuple-element.33), channel_id=1, source_target_pairs={{0,31},{1,0},{2,1},{3,2},{4,3},{5,4},{6,5},{7,6},{8,7},{9,8},{10,9... | collective-permute-start | bytes 384008 | tf_op jit(solution)/shard_map/ppermute | solution.py:422
  14.4 3.2 %prepare.1 = (f32[6,13,88,128]{3,2,1,0:T(8,128)S(1)}, f32[6,13,88,128]{3,2,1,0:T(8,128)S(1)}, bf16[1664,1792]{1,0:T(8,128)(2,1)S(1)}, f32[40,1792]{1,0:T(8,128)S...) custom-call(bf16[2,4,64000]{2,1,0:T(4,128)(2,1)} %orb_hbm.3, f32[2,40,1792]{2,1,0:T(8,128)} %constant.8.clone.rep_hbm, ...), custom_call_target="tpu_custom_call" | custom-call | flops 10000000 | bytes 10000000 | tf_op jit(solution)/shard_map/prepare/pallas_call | solution.py:482
  17.6 0.0 collective-permute-done.prev_ref
  17.6 0.0 collective-permute-done.1.next_ref
  17.6 0.2 shard_map.82.refs_4_
  17.7 8.3 %shard_map.83 = (f32[3,500,128]{2,1,0:T(8,128)S(1)}, bf16[1,500,128]{2,1,0:T(8,128)(2,1)S(1)}, bf16[2,500,128]{2,1,0:T(8,128)(2,1)S(1)}) custom-call(s32[57]{0:T(128)S(1)} %get-tuple-element.22.refs_0_, bf16[1664,1792]{1,0:T(8,128)(2,1)S(1)} %get-tuple-element.23.refs_1_, bf16[240,240]{1,0:T(8,128)(2,1)S(1)} %get-tuple-element.24.refs_2_, ...), custom_call_target="tpu_custom_call" | custom-call | flops 2457600000 | bytes 10000000 | tf_op jit(solution)/shard_map/pallas_call | solution.py:509
  26.0 1.2 %collective-permute-start.3 = (bf16[2,500,128]{2,1,0:T(8,128)(2,1)S(1)}, bf16[2,500,128]{2,1,0:T(8,128)(2,1)S(1)}, u32[]{:S(2)}, u32[]{:S(2)}) collective-permute-start(bf16[2,500,128]{2,1,0:T(8,128)(2,1)S(1)} %get-tuple-element.30), channel_id=1, source_target_pairs={{0,31},{1,0},{2,1},{3,2},{4,3},{5,4},{6,5},{7,6},{8,7},{9,8},{10,9... | collective-permute-start | bytes 768008 | tf_op jit(solution)/shard_map/ppermute | solution.py:422
  27.2 0.0 collective-permute-done.4.prev_ref
  27.2 0.0 collective-permute-done.5.next_ref
  27.2 0.2 shard_map.84.refs_4_.refs_5_
  27.4 8.3 %shard_map.85 = (f32[3,500,128]{2,1,0:T(8,128)S(1)}, bf16[1,500,128]{2,1,0:T(8,128)(2,1)S(1)}, bf16[2,500,128]{2,1,0:T(8,128)(2,1)S(1)}) custom-call(s32[57]{0:T(128)S(1)} %get-tuple-element.22.refs_0_, bf16[1664,1792]{1,0:T(8,128)(2,1)S(1)} %get-tuple-element.23.refs_1_, bf16[240,240]{1,0:T(8,128)(2,1)S(1)} %get-tuple-element.24.refs_2_, ...), custom_call_target="tpu_custom_call" | custom-call | flops 2457600000 | bytes 10000000 | tf_op jit(solution)/shard_map/pallas_call | solution.py:509
  35.7 0.1 collective-permute-start.7
  35.7 2.0 %collective-permute-start.2 = (bf16[1,500,128]{2,1,0:T(8,128)(2,1)S(1)}, bf16[1,500,128]{2,1,0:T(8,128)(2,1)S(1)}, u32[]{:S(2)}, u32[]{:S(2)}) collective-permute-start(bf16[1,500,128]{2,1,0:T(8,128)(2,1)S(1)} %get-tuple-element.29), channel_id=1, source_target_pairs={{0,1},{1,2},{2,3},{3,4},{4,5},{5,6},{6,7},{7,8},{8,9},{9,10},{10,1... | collective-permute-start | bytes 384008 | tf_op jit(solution)/shard_map/ppermute | solution.py:422
  37.8 0.9 %collective-permute-start.6 = (bf16[1,500,128]{2,1,0:T(8,128)(2,1)S(1)}, bf16[1,500,128]{2,1,0:T(8,128)(2,1)S(1)}, u32[]{:S(2)}, u32[]{:S(2)}) collective-permute-start(bf16[1,500,128]{2,1,0:T(8,128)(2,1)S(1)} %get-tuple-element.34), channel_id=1, source_target_pairs={{0,1},{1,2},{2,3},{3,4},{4,5},{5,6},{6,7},{7,8},{8,9},{9,10},{10,1... | collective-permute-start | bytes 384008 | tf_op jit(solution)/shard_map/ppermute | solution.py:422
  38.7 7.6 %shard_map.86.refs_5_ = f32[7,1000,128]{2,1,0:T(8,128)} custom-call(s32[57]{0:T(128)S(1)} %get-tuple-element.22.refs_0_, bf16[1664,1792]{1,0:T(8,128)(2,1)S(1)} %get-tuple-element.23.refs_1_, bf16[160,160]{1,0:T(8,128)(2,1)S(1)} %get-tuple-element.36.refs_2_, f32[40,1792]{1,0:T(8,128)S(1)} %get-tuple-element.25.refs_3_, ...), custom_call_target="tpu_custom_call" | custom-call | flops 1638400000 | bytes 10000000 | tf_op jit(solution)/shard_map/pallas_call | solution.py:509
  46.3 0.0 collective-permute-done.2.refs_1_
  46.3 1.4 %collective-permute-done.6.refs_3_ = bf16[1,500,128]{2,1,0:T(8,128)(2,1)S(1)} collective-permute-done((bf16[1,500,128]{2,1,0:T(8,128)(2,1)S(1)}, bf16[1,500,128]{2,1,0:T(8,128)(2,1)S(1)}, u32[]{:S(2)}, u32[]{:S(2)}) %collective-permute-start.6) | collective-permute-done | bytes 128032 | tf_op jit(solution)/shard_map/ppermute | solution.py:422
  47.7 0.0 collective-permute-done.3.refs_2_
  47.7 1.6 %collective-permute-done.7.refs_4_ = bf16[2,500,128]{2,1,0:T(8,128)(2,1)S(1)} collective-permute-done((bf16[2,500,128]{2,1,0:T(8,128)(2,1)S(1)}, bf16[2,500,128]{2,1,0:T(8,128)(2,1)S(1)}, u32[]{:S(2)}, u32[]{:S(2)}) %collective-permute-start.7) | collective-permute-done | bytes 256032 | tf_op jit(solution)/shard_map/ppermute | solution.py:422
  49.3 1.4 %place.1 = f32[7,1000,128]{2,1,0:T(8,128)} custom-call(s32[57]{0:T(128)S(1)} %get-tuple-element.22.refs_0_, bf16[1,500,128]{2,1,0:T(8,128)(2,1)S(1)} %collective-permute-done.2.refs_1_, bf16[2,500,128]{2,1,0:T(8,128)(2,1)S(1)} %collective-permute-done.3.refs_2_, ...), custom_call_target="tpu_custom_call", output_to_operand_aliasing={{}: (5, {})} | custom-call | flops 1000000 | bytes 4000000 | tf_op jit(solution)/shard_map/place/pallas_call | solution.py:532
Async XLA Ops:
  2.5 15.0 %collective-permute-start = (bf16[500,128]{1,0:T(8,128)(2,1)S(1)}, bf16[500,128]{1,0:T(8,128)(2,1)S(1)}, u32[]{:S(2)}, u32[]{:S(2)}) collective-permute-start(bf16[500,128]{1,0:T(8,128)(2,1)S(1)} %get-tuple-element.27), channel_id=1, source_target_pairs={{0,1},{1,2},{2,3},{3,4},{4,5},{5,6},{6,7},{7,8},{8,9},{9,10},{10,1... | collective-permute-start | bytes 384008 | tf_op jit(solution)/shard_map/ppermute | solution.py:422
  5.6 11.9 %collective-permute-start.1 = (bf16[500,128]{1,0:T(8,128)(2,1)S(1)}, bf16[500,128]{1,0:T(8,128)(2,1)S(1)}, u32[]{:S(2)}, u32[]{:S(2)}) collective-permute-start(bf16[500,128]{1,0:T(8,128)(2,1)S(1)} %get-tuple-element.28), channel_id=1, source_target_pairs={{0,31},{1,0},{2,1},{3,2},{4,3},{5,4},{6,5},{7,6},{8,7},{9,8},{10,9... | collective-permute-start | bytes 384008 | tf_op jit(solution)/shard_map/ppermute | solution.py:422
  9.1 18.2 %collective-permute-start.4 = (bf16[500,128]{1,0:T(8,128)(2,1)S(1)}, bf16[500,128]{1,0:T(8,128)(2,1)S(1)}, u32[]{:S(2)}, u32[]{:S(2)}) collective-permute-start(bf16[500,128]{1,0:T(8,128)(2,1)S(1)} %get-tuple-element.32), channel_id=1, source_target_pairs={{0,1},{1,2},{2,3},{3,4},{4,5},{5,6},{6,7},{7,8},{8,9},{9,10},{10,1... | collective-permute-start | bytes 384008 | tf_op jit(solution)/shard_map/ppermute | solution.py:422
  9.1 18.2 %collective-permute-start.5 = (bf16[500,128]{1,0:T(8,128)(2,1)S(1)}, bf16[500,128]{1,0:T(8,128)(2,1)S(1)}, u32[]{:S(2)}, u32[]{:S(2)}) collective-permute-start(bf16[500,128]{1,0:T(8,128)(2,1)S(1)} %get-tuple-element.33), channel_id=1, source_target_pairs={{0,31},{1,0},{2,1},{3,2},{4,3},{5,4},{6,5},{7,6},{8,7},{9,8},{10,9... | collective-permute-start | bytes 384008 | tf_op jit(solution)/shard_map/ppermute | solution.py:422
  26.0 21.6 %collective-permute-start.3 = (bf16[2,500,128]{2,1,0:T(8,128)(2,1)S(1)}, bf16[2,500,128]{2,1,0:T(8,128)(2,1)S(1)}, u32[]{:S(2)}, u32[]{:S(2)}) collective-permute-start(bf16[2,500,128]{2,1,0:T(8,128)(2,1)S(1)} %get-tuple-element.30), channel_id=1, source_target_pairs={{0,31},{1,0},{2,1},{3,2},{4,3},{5,4},{6,5},{7,6},{8,7},{9,8},{10,9... | collective-permute-start | bytes 768008 | tf_op jit(solution)/shard_map/ppermute | solution.py:422
  35.7 13.6 %collective-permute-start.7 = (bf16[2,500,128]{2,1,0:T(8,128)(2,1)S(1)}, bf16[2,500,128]{2,1,0:T(8,128)(2,1)S(1)}, u32[]{:S(2)}, u32[]{:S(2)}) collective-permute-start(bf16[2,500,128]{2,1,0:T(8,128)(2,1)S(1)} %get-tuple-element.35), channel_id=1, source_target_pairs={{0,31},{1,0},{2,1},{3,2},{4,3},{5,4},{6,5},{7,6},{8,7},{9,8},{10,9... | collective-permute-start | bytes 768008 | tf_op jit(solution)/shard_map/ppermute | solution.py:422
  35.7 10.5 %collective-permute-start.2 = (bf16[1,500,128]{2,1,0:T(8,128)(2,1)S(1)}, bf16[1,500,128]{2,1,0:T(8,128)(2,1)S(1)}, u32[]{:S(2)}, u32[]{:S(2)}) collective-permute-start(bf16[1,500,128]{2,1,0:T(8,128)(2,1)S(1)} %get-tuple-element.29), channel_id=1, source_target_pairs={{0,1},{1,2},{2,3},{3,4},{4,5},{5,6},{6,7},{7,8},{8,9},{9,10},{10,1... | collective-permute-start | bytes 384008 | tf_op jit(solution)/shard_map/ppermute | solution.py:422
  37.8 9.9 %collective-permute-start.6 = (bf16[1,500,128]{2,1,0:T(8,128)(2,1)S(1)}, bf16[1,500,128]{2,1,0:T(8,128)(2,1)S(1)}, u32[]{:S(2)}, u32[]{:S(2)}) collective-permute-start(bf16[1,500,128]{2,1,0:T(8,128)(2,1)S(1)} %get-tuple-element.34), channel_id=1, source_target_pairs={{0,1},{1,2},{2,3},{3,4},{4,5},{5,6},{6,7},{7,8},{8,9},{9,10},{10,1... | collective-permute-start | bytes 384008 | tf_op jit(solution)/shard_map/ppermute | solution.py:422

commit v7 on v6

--- a/solution.py
+++ b/solution.py
@@ -21,10 +21,11 @@
 LANES = 128
 FACE = EDGE * EDGE
 TILES = -(-FACE // LANES)
-WIDE = TILES * LANES
 NCHUNK = 256
-NSTEPS = -(-FACE // NCHUNK)
-NWIDE = NSTEPS * NCHUNK
+FOLD = FACE // 2
+FTILES = -(-FOLD // LANES)
+FWIDE = FTILES * LANES
+CHUNKS = [(min(first, FWIDE - NCHUNK), NCHUNK) for first in range(0, FWIDE, NCHUNK)]
 FLAT = EDGE ** 3 // LANES
 HALF = EDGE // 2
 PAIRT = 2 * FACE // LANES
@@ -41,14 +42,22 @@
     sine = (np.sqrt(np.float32(2.0 / (EDGE + 1.0))) * np.sin(angles)).astype(jnp.bfloat16)
     sine = sine.astype(np.float32)
     levels = 2.0 - 2.0 * np.cos(np.pi * counter.astype(np.float64) / (EDGE + 1.0))
-    lam = levels[:, None, None] + levels[None, :, None] + levels[None, None, :] + SCREEN
-    inverse = np.zeros((EDGE, NWIDE), np.float32)
-    inverse[:, :FACE] = (1.0 / lam).reshape(EDGE, FACE)
-    repeated = np.zeros((EDGE, NWIDE), np.float32)
-    repeated[:, :FACE] = np.repeat(sine, EDGE, axis=1)
-    tiled = np.zeros((EDGE, NWIDE), np.float32)
-    tiled[:, :FACE] = np.tile(sine, (1, EDGE))
-    return sine, inverse, repeated, tiled
+    number = np.arange(FOLD)
+    second, step = number // HALF, number % HALF
+    thirds = [2 * step + second % 2, 2 * step + 1 - second % 2]
+    inverse = np.zeros((EDGE, 2 * FWIDE), np.float32)
+    for part, third in enumerate(thirds):
+        lam = levels[:, None] + levels[second] + levels[third] + SCREEN
+        inverse[:, part * FWIDE:part * FWIDE + FOLD] = 1.0 / lam
+    factors = np.zeros((6, EDGE, FWIDE), np.float32)
+    factors[0, :HALF, :FOLD] = sine[:HALF][:, second]
+    for part, third in enumerate(thirds):
+        factors[1 + part, :, :FOLD] = sine[:, third]
+    factors[3, :, :FOLD] = np.repeat(sine[:HALF], EDGE, axis=0).T
+    lines = np.tile(sine, (HALF, 1)).T
+    factors[4, :, :FOLD] = np.concatenate([lines[0::2], lines[1::2]])
+    factors[5, :, :FOLD] = np.concatenate([lines[1::2], lines[0::2]])
+    return sine, inverse, factors
 
 
 def lane_iota():
@@ -79,6 +88,19 @@
                 store(t - TILES, 1, jnp.where(low, rolled, turned))
             rolled = turned
     store(TILES - 1, 1, rolled)
+
+
+def turn(x):
+    source = (LANES // 2 - 1 - lax.broadcasted_iota(jnp.int32, x.shape, 1)) & (LANES - 1)
+    return jnp.take_along_axis(x, source, axis=1)
+
+
+def reverse_slabs(load, store, first, count):
+    low = lane_iota() < LANES // 2
+    turned = [turn(load(v)) for v in range(count)]
+    for u in range(first, TILES):
+        v = TILES - 1 - u
+        store(u, jnp.where(low, turned[v], turned[v - 1]) if v > 0 else turned[v])
 
 
 def slabs_to_flat(load, store):
@@ -197,12 +219,18 @@
                 tab_ref[base + 1 + axis] = jnp.clip(moved - extent // 2, -(PAD - 4), PAD - 4)
 
 
-def prepare_kernel(orb_hbm, rep_hbm, inv_hbm, diag_hbm, rest_hbm, low_ref, high_ref, kron_ref, inv_ref, diag_ref, rest_ref,
-                   orb_ref, rep_ref, flat_ref, sems):
+def reverse_box(pad_ref, box):
+    body = pl.ds(PAD, EDGE)
+    reverse_slabs(lambda v: pad_ref[0, box, v, body, :],
+                  lambda u, x: pad_ref.__setitem__((1, box, u, body, slice(None)), x), 0, TILES)
+
+
+def prepare_kernel(orb_hbm, fac_hbm, inv_hbm, diag_hbm, rest_hbm, low_ref, high_ref, to_ref, from_ref, inv_ref, diag_ref,
+                   rest_ref, orb_ref, fac_ref, flat_ref, sems):
     boxes = orb_ref.shape[1]
     copies = [pltpu.make_async_copy(orb_hbm.at[spin], orb_ref.at[spin], sems.at[spin]) for spin in range(2)]
     copies += [pltpu.make_async_copy(source, target, sems.at[2 + k]) for k, (source, target) in enumerate(
-        ((rep_hbm, rep_ref), (inv_hbm, inv_ref), (diag_hbm, diag_ref), (rest_hbm, rest_ref)))]
+        ((fac_hbm, fac_ref), (inv_hbm, inv_ref), (diag_hbm, diag_ref), (rest_hbm, rest_ref)))]
     for copy in copies:
         copy.start()
     for spin, pad_ref in enumerate((low_ref, high_ref)):
@@ -213,47 +241,56 @@
             flat_to_slabs(
                 lambda t: flat_ref[pl.ds(box + 8 * t, HALF, stride=8 * PAIRT), :],
                 lambda u, parity, x: pad_ref.__setitem__(
-                    (box, u, pl.ds(PAD + parity, HALF, stride=2), slice(None)), x),
+                    (0, box, u, pl.ds(PAD + parity, HALF, stride=2), slice(None)), x),
             )
+            reverse_box(pad_ref, box)
             return 0
 
         lax.fori_loop(0, boxes, slabs, 0)
 
     copies[2].wait()
+    front = lax.broadcasted_iota(jnp.int32, (EDGE, 1), 0) < HALF
 
     def build(i, _):
-        row = pl.multiple_of(i * 2 * EDGE, 16)
-        for c in range(NSTEPS):
-            cols = slice(c * NCHUNK, (c + 1) * NCHUNK)
-            til = rep_ref[1, :, cols]
-            first = rep_ref[0, pl.ds(2 * i, 1), cols] * til
-            second = rep_ref[0, pl.ds(2 * i + 1, 1), cols] * til
-            kron_ref[pl.ds(row, 2 * EDGE), cols] = jnp.concatenate([first, second], axis=0).astype(BF)
+        where = pl.ds(pl.multiple_of(i * 2 * EDGE, 16), 2 * EDGE)
+        for first, size in CHUNKS:
+            cols = slice(first, first + size)
+            line = [fac_ref[0, pl.ds(2 * i + k, 1), cols] for k in range(2)]
+            mode = [fac_ref[3, pl.ds(4 * i + k, 1), cols] for k in range(4)]
+            modes = [jnp.where(front, mode[2 * k], mode[2 * k + 1]) for k in range(2)]
+            for part in range(2):
+                right = fac_ref[1 + part, :, cols]
+                to_ref[part, where, cols] = jnp.concatenate([x * right for x in line], axis=0).astype(BF)
+                right = fac_ref[4 + part, :, cols]
+                from_ref[part, where, cols] = jnp.concatenate([x * right for x in modes], axis=0).astype(BF)
         return 0
 
-    lax.fori_loop(0, HALF, build, 0)
-    kron_ref[FACE:, :] = jnp.zeros((WIDE - FACE, NWIDE), BF)
+    lax.fori_loop(0, HALF // 2, build, 0)
+    for part in range(2):
+        to_ref[part, FOLD:, :] = jnp.zeros((FWIDE - FOLD, FWIDE), BF)
+        from_ref[part, FOLD:, :] = jnp.zeros((FWIDE - FOLD, FWIDE), BF)
     for copy in copies[3:]:
         copy.wait()
 
 
 def fill_kernel(old_ref, prev_ref, next_ref, pad_ref, flat_ref):
-    boxes = pad_ref.shape[0] - 2
+    boxes = pad_ref.shape[1] - 2
     for side, ref in ((0, prev_ref), (1, next_ref)):
         flat_ref[...] = ref[...].astype(F32)
         flat_to_slabs(
             lambda t: flat_ref[pl.ds(t, HALF, stride=PAIRT), :],
             lambda u, parity, x: pad_ref.__setitem__(
-                (boxes + side, u, pl.ds(PAD + parity, HALF, stride=2), slice(None)), x),
+                (0, boxes + side, u, pl.ds(PAD + parity, HALF, stride=2), slice(None)), x),
         )
-
-
-def pair_kernel(start, held, spins, final, tab_ref, kron_ref, diag_ref, inv_ref, *refs):
-    pads, (mov_ref, x_ref, y_ref, res_ref) = refs[:len(spins)], refs[-4:]
-    boxes = pads[0].shape[0] - 2
+        reverse_box(pad_ref, boxes + side)
+
+
+def pair_kernel(start, held, spins, final, tab_ref, to_ref, from_ref, diag_ref, inv_ref, *refs):
+    pads, (mov_ref, x_ref, y_ref, half_ref, res_ref) = refs[:len(spins)], refs[-5:]
+    boxes = pads[0].shape[1] - 2
     pairs, codes, _, leaves, order, homes, _ = table_layout(boxes)
     if final:
-        low_ref, high_ref, out_ref, form_ref, sems = refs[len(spins):-4]
+        low_ref, high_ref, out_ref, form_ref, sems = refs[len(spins):-5]
 
         def copy(slot):
             return pltpu.make_async_copy(form_ref.at[slot], out_ref.at[slot], sems.at[slot])
@@ -277,7 +314,7 @@
 
         lax.fori_loop(0, CAP, early, 0)
     else:
-        out_ref, sends = refs[len(spins)], refs[len(spins) + 1:-4]
+        out_ref, sends = refs[len(spins)], refs[len(spins) + 1:-5]
     lanes = lane_iota()
     rows = lax.broadcasted_iota(jnp.int32, (EDGE, 1), 0)
 
@@ -288,76 +325,102 @@
             base = pairs + (box * PARTNERS + number) * 4
             source = tab_ref[base]
             da, db, dc = tab_ref[base + 1], tab_ref[base + 2], tab_ref[base + 3]
-            offset = ZERO_TILES * LANES - (db * EDGE + dc)
             row_ok = jnp.abs(2 * (rows - da) - (EDGE - 1)) < EDGE
-            places.append((source, da, db, dc, offset // LANES, offset % LANES, row_ok))
-        last = [[None] * PARTNERS for _ in spins]
-        for u in range(TILES + 1):
+            for b_by, c_by in ((db, dc), (-db, -dc)):
+                offset = ZERO_TILES * LANES - (b_by * EDGE + c_by)
+                places.append((source, da, b_by, c_by, offset // LANES, offset % LANES, row_ok))
+        last = [[None] * len(places) for _ in spins]
+        for u in range(FTILES + 1):
             keep = []
-            for number in range(PARTNERS):
-                source, da, db, dc, quotient, rest, row_ok = places[number]
+            for source, da, b_by, c_by, quotient, rest, row_ok in places:
                 if u > 0:
                     cell = lanes + (u - 1) * LANES
                     b = (cell * 52429) >> 21
                     c = cell - b * EDGE
-                    ok = (jnp.abs(2 * (b - db) - (EDGE - 1)) < EDGE) & (jnp.abs(2 * (c - dc) - (EDGE - 1)) < EDGE)
-                    if u == TILES:
-                        ok = ok & (lanes < FACE - (TILES - 1) * LANES)
+                    ok = (jnp.abs(2 * (b - b_by) - (EDGE - 1)) < EDGE) & (jnp.abs(2 * (c - c_by) - (EDGE - 1)) < EDGE)
+                    if u == FTILES:
+                        ok = ok & (lanes < FOLD - (FTILES - 1) * LANES)
                     keep.append(row_ok & ok)
             for at, pad_ref in enumerate(pads):
                 values = []
-                for number in range(PARTNERS):
-                    source, da, db, dc, quotient, rest, row_ok = places[number]
+                for which, (source, da, b_by, c_by, quotient, rest, row_ok) in enumerate(places):
+                    part = which % 2
                     tile = jnp.clip(quotient + (u - ZERO_TILES), 0, TILES - 1)
-                    x = pad_ref[source, tile, pl.ds(PAD - da, EDGE), :]
+                    x = pad_ref[part, source, tile, pl.ds(PAD - da, EDGE), :]
                     turned = pltpu.roll(x, (LANES - rest) % LANES, 1)
                     if u > 0:
-                        moved = jnp.where(keep[number], jnp.where(lanes < LANES - rest, last[at][number], turned), 0.0)
-                        mov_ref[index, at, number, u - 1] = moved
-                        values.append(pad_ref[box, u - 1, pl.ds(PAD, EDGE), :] * moved)
-                    last[at][number] = turned
+                        moved = jnp.where(keep[which], jnp.where(lanes < LANES - rest, last[at][which], turned), 0.0)
+                        mov_ref[index, at, which // 2, part, u - 1] = moved
+                        values.append(pad_ref[part, box, u - 1, pl.ds(PAD, EDGE), :] * moved)
+                    last[at][which] = turned
                 if u > 0:
-                    both = jnp.concatenate(values, axis=0)
-                    if u == TILES:
-                        both = jnp.where(lanes < FACE - (TILES - 1) * LANES, both, 0.0)
-                    first = (index * len(spins) + at) * PARTNERS * EDGE
-                    x_ref[pl.ds(pl.multiple_of(first, 16), PARTNERS * EDGE),
-                          (u - 1) * LANES:u * LANES] = both.astype(BF)
+                    where = pl.ds(pl.multiple_of((index * len(spins) + at) * PARTNERS * EDGE, 16), PARTNERS * EDGE)
+                    front = jnp.concatenate(values[0::2], axis=0)
+                    behind = jnp.concatenate(values[1::2], axis=0)
+                    x_ref[where, (u - 1) * LANES:u * LANES] = (front + behind).astype(BF)
+                    x_ref[where, FWIDE + (u - 1) * LANES:FWIDE + u * LANES] = (front - behind).astype(BF)
         return 0
 
     lax.fori_loop(0, held, dense, 0)
 
     cubes = held * len(spins) * PARTNERS
     diag = diag_ref[...]
-    for c in range(NSTEPS):
-        cols = slice(c * NCHUNK, min((c + 1) * NCHUNK, WIDE))
+    for first in range(0, 2 * FWIDE, NCHUNK):
+        cols = slice(first, first + NCHUNK)
         y_ref[:, cols] = jnp.dot(diag, x_ref[:, cols], preferred_element_type=F32).astype(BF)
 
-    def forward(n, _):
-        cols = pl.ds(pl.multiple_of(n * NCHUNK, NCHUNK), NCHUNK)
-        z = jnp.dot(y_ref[:, :WIDE], kron_ref[:, cols], preferred_element_type=F32)
-        z = z.reshape(cubes, EDGE, NCHUNK) * inv_ref[:, cols][None]
-        x_ref[:, cols] = z.reshape(cubes * EDGE, NCHUNK).astype(BF)
+    def forward(first, size):
+        for part in range(2):
+            z = jnp.dot(y_ref[:, part * FWIDE:(part + 1) * FWIDE], to_ref[part, :, pl.ds(first, size)],
+                        preferred_element_type=F32)
+            cols = pl.ds(pl.multiple_of(part * FWIDE + first, LANES), size)
+            z = z.reshape(cubes, EDGE, size) * inv_ref[:, cols][None]
+            x_ref[:, cols] = z.reshape(cubes * EDGE, size).astype(BF)
+
+    def backward(first, size):
+        even, odd = [jnp.dot(x_ref[:, part * FWIDE:(part + 1) * FWIDE], from_ref[part, :, pl.ds(first, size)],
+                             preferred_element_type=F32) for part in range(2)]
+        y_ref[:, pl.ds(first, size)] = (even + odd).astype(BF)
+        y_ref[:, pl.ds(pl.multiple_of(FWIDE + first, LANES), size)] = (even - odd).astype(BF)
+
+    for step in (forward, backward):
+        whole_steps = FWIDE // NCHUNK
+
+        def looped(n, _):
+            step(pl.multiple_of(n * NCHUNK, NCHUNK), NCHUNK)
+            return 0
+
+        lax.fori_loop(0, whole_steps, looped, 0)
+        if FWIDE % NCHUNK:
+            step(whole_steps * NCHUNK, FWIDE % NCHUNK)
+
+    for first in range(0, 2 * FTILES, 2):
+        potential = jnp.dot(diag, y_ref[:, first * LANES:(first + 2) * LANES], preferred_element_type=F32)
+        for u in (first, first + 1):
+            side = slice((u - first) * LANES, (u - first + 1) * LANES)
+            for index in range(held):
+                for at in range(len(spins)):
+                    total = 0.0
+                    for number in range(PARTNERS):
+                        row = ((index * len(spins) + at) * PARTNERS + number) * EDGE
+                        total = total + potential[row:row + EDGE, side] * mov_ref[index, at, number, u // FTILES, u % FTILES]
+                    if u < FTILES:
+                        res_ref[index * len(spins) + at, u] = total
+                    else:
+                        half_ref[index * len(spins) + at, u - FTILES] = total
+
+    def unfold(row, _):
+        middle = FTILES - 1
+
+        def store(u, x):
+            if u == middle:
+                x = jnp.where(lanes < FOLD - middle * LANES, res_ref[row, middle], x)
+            res_ref[row, u] = x
+
+        reverse_slabs(lambda v: half_ref[row, v], store, middle, FTILES)
         return 0
 
-    lax.fori_loop(0, NSTEPS, forward, 0)
-
-    def backward(n, _):
-        cols = pl.ds(pl.multiple_of(n * NCHUNK, NCHUNK), NCHUNK)
-        y_ref[:, cols] = jnp.dot(x_ref[:, :WIDE], kron_ref[:, cols], preferred_element_type=F32).astype(BF)
-        return 0
-
-    lax.fori_loop(0, NSTEPS, backward, 0)
-
-    for u in range(TILES):
-        potential = jnp.dot(diag, y_ref[:, u * LANES:(u + 1) * LANES], preferred_element_type=F32)
-        for index in range(held):
-            for at in range(len(spins)):
-                total = 0.0
-                for number in range(PARTNERS):
-                    first = ((index * len(spins) + at) * PARTNERS + number) * EDGE
-                    total = total + potential[first:first + EDGE] * mov_ref[index, at, number, u]
-                res_ref[index * len(spins) + at, u] = total
+    lax.fori_loop(0, held * len(spins), unfold, 0)
 
     if final:
         for index in range(held):
@@ -440,7 +503,7 @@
 
 def shards(orbitals, dest, partners, anchors):
     boxes = orbitals.shape[1]
-    sine, inverse, repeated, tiled = tables()
+    sine, inverse, factors = tables()
     partners_t, anchors_t = partners.T, anchors.T
 
     box = jax.ShapeDtypeStruct((FLAT, LANES), BF)
@@ -462,24 +525,24 @@
     next_high = from_behind(back_high, -1)
 
     moving = AHEAD + BACK
-    slabs = jax.ShapeDtypeStruct((boxes + 2, TILES, ROWS, LANES), F32)
-    constants = np.stack([repeated, tiled])
+    slabs = jax.ShapeDtypeStruct((2, boxes + 2, TILES, ROWS, LANES), F32)
+    folded = jax.ShapeDtypeStruct((2, FWIDE, FWIDE), BF)
     diags = [np.kron(np.eye(cubes, dtype=np.float32), sine).astype(jnp.bfloat16)
              for cubes in (moving * PARTNERS, (boxes - moving) * 2 * PARTNERS)]
     handed = (inverse, *diags)
     prepare = pl.pallas_call(
         prepare_kernel,
-        out_shape=[slabs, slabs, jax.ShapeDtypeStruct((WIDE, NWIDE), BF)]
+        out_shape=[slabs, slabs, folded, folded]
         + [jax.ShapeDtypeStruct(value.shape, value.dtype) for value in handed],
         in_specs=[ANYWHERE] * 5,
-        out_specs=whole(6),
-        scratch_shapes=[pltpu.VMEM(orbitals.shape, BF), pltpu.VMEM(constants.shape, F32), splitter,
+        out_specs=whole(7),
+        scratch_shapes=[pltpu.VMEM(orbitals.shape, BF), pltpu.VMEM(factors.shape, F32), splitter,
                         pltpu.SemaphoreType.DMA((6,))],
         compiler_params=pltpu.CompilerParams(vmem_limit_bytes=20 << 20),
         cost_estimate=cost(10_000_000, 10_000_000),
         name="prepare",
     )
-    low, high, kron, inverse, *diags = prepare(*map(in_place, (orbitals, constants, *handed)))
+    low, high, to_modes, from_modes, inverse, *diags = prepare(*map(in_place, (orbitals, factors, *handed)))
     pads = [low, high]
     for spin, halo in enumerate(((prev_low, next_low), (prev_high, next_high))):
         pads[spin] = pl.pallas_call(
@@ -505,20 +568,21 @@
             shapes = [jax.ShapeDtypeStruct((held * len(spins), FLAT, LANES), F32)]
             shapes += [jax.ShapeDtypeStruct((count, FLAT, LANES), BF) for count in (AHEAD, BACK)]
             specs, extra = whole(3), []
-        operands = [table, kron, diags[final], inverse] + [pads[spin] for spin in spins] + (terms or [])
+        operands = [table, to_modes, from_modes, diags[final], inverse] + [pads[spin] for spin in spins] + (terms or [])
         return pl.pallas_call(
             lambda *refs: pair_kernel(start, held, spins, final, *refs),
             out_shape=shapes,
             in_specs=[SCALARS] + whole(len(operands) - 1),
             out_specs=specs,
             scratch_shapes=extra + [
-                pltpu.VMEM((held, len(spins), PARTNERS, TILES, EDGE, LANES), F32),
-                pltpu.VMEM((cubes * EDGE, NWIDE), BF),
-                pltpu.VMEM((cubes * EDGE, NWIDE), BF),
+                pltpu.VMEM((held, len(spins), PARTNERS, 2, FTILES, EDGE, LANES), F32),
+                pltpu.VMEM((cubes * EDGE, 2 * FWIDE), BF),
+                pltpu.VMEM((cubes * EDGE, 2 * FWIDE), BF),
+                pltpu.VMEM((held * len(spins), FTILES, EDGE, LANES), F32),
                 pltpu.VMEM((held * len(spins), TILES, EDGE, LANES), F32),
             ],
             compiler_params=pltpu.CompilerParams(vmem_limit_bytes=20 << 20),
-            cost_estimate=cost(4 * cubes * EDGE * FACE * FACE, 10_000_000),
+            cost_estimate=cost(2 * cubes * EDGE * FACE * FACE, 10_000_000),
         )(*operands)
 
     terms, arrived = [], []

time: 50.9 us -> 48.1 us (0.945)
  Pallas kernels: 31.6 us -> 27.5 us
  waiting for transfers between devices: 3.06 us -> 4.43 us
    pallas_call x3, Pallas kernels: 24.2 us -> 18.6 us  [solve(): pl.pallas_call(lambda *refs: pair_kernel(start, held, spins, final, *refs...]
    ppermute x8, waiting for transfers between devices: 3.06 us -> 4.43 us  [from_behind(): lax.ppermute(value, AXES, [(source, (source + steps) % count) for source...]
    pallas_call x1, Pallas kernels: 3.16 us -> 4.39 us  [shards(): prepare(*map(in_place, (orbitals, factors, *handed)))]
  transfers between devices with their start and end apart: 8 -> 8, of which waited for: 2 -> 2; matrix products, arithmetic and copies ran while one was open for 0% -> 0% of each run, Pallas kernels for 55% -> 49%
where the time goes in v7:
time: 48.1 us; the launch traced here: 48 us
  Pallas kernels  27.5 us (57%)
  starting transfers between devices  16 us (33%)
  waiting for transfers between devices  4.43 us (9%)
    pallas_call x3, Pallas kernels, solve(): pl.pallas_call(lambda *refs: pair_kernel(start, held, spins, final, *refs...  18.6 us
    ppermute x8, starting transfers between devices, from_behind(): lax.ppermute(value, AXES, [(source, (source + steps) % count) for source...  16 us
    ppermute x8, waiting for transfers between devices, from_behind(): lax.ppermute(value, AXES, [(source, (source + steps) % count) for source...  4.43 us
    pallas_call x1, Pallas kernels, shards(): prepare(*map(in_place, (orbitals, factors, *handed)))  4.39 us
    pallas_call x1, Pallas kernels, shards(): pl.pallas_call(window_kernel, out_shape=[box] * 4 + [jax.ShapeDtypeStruct...  2.53 us
    pallas_call x1, Pallas kernels, shards(): pl.pallas_call(lambda *refs: place_kernel(boxes, *refs), out_shape=shape,...  1.4 us
  transfers between devices with their start and end apart: 8, of which 2 were waited for; matrix products, arithmetic and copies ran while one was open for 0% of the time, Pallas kernels for 49%

profile of v7, /device:TPU:0, one launch (start us, length us, event | category | flops | bytes accessed | tf_op | source)
XLA Modules:
  0.0 48.0 jit_solution(3224513394695303070)
XLA Ops:
  0.0 2.5 %window.1 = (bf16[500,128]{1,0:T(8,128)(2,1)S(1)}, bf16[500,128]{1,0:T(8,128)(2,1)S(1)}, bf16[500,128]{1,0:T(8,128)(2,1)S(1)}, bf16[500,128]{1,0:T(8,128)(2,1)S(1)}, s32[57]{0:T(128)S(1)}) custom-call(s32[128]{0:T(128)} %dest_hbm.1, s32[2,128]{1,0:T(2,128)} %bitcast.10, s32[3,128]{1,0:T(4,128)} %bitcast.9, bf16[2,4,64000]{2,1,0:T(4,128)(2,1)} %orb_hbm.3), custom_call_target="tpu_custom_call" | custom-call | tf_op jit(solution)/shard_map/window/pallas_call | solution.py:511
  2.5 3.1 %collective-permute-start = (bf16[500,128]{1,0:T(8,128)(2,1)S(1)}, bf16[500,128]{1,0:T(8,128)(2,1)S(1)}, u32[]{:S(2)}, u32[]{:S(2)}) collective-permute-start(bf16[500,128]{1,0:T(8,128)(2,1)S(1)} %get-tuple-element.29), channel_id=1, source_target_pairs={{0,1},{1,2},{2,3},{3,4},{4,5},{5,6},{6,7},{7,8},{8,9},{9,10},{10,1... | collective-permute-start | bytes 384008 | tf_op jit(solution)/shard_map/ppermute | solution.py:485
  5.6 3.4 %collective-permute-start.1 = (bf16[500,128]{1,0:T(8,128)(2,1)S(1)}, bf16[500,128]{1,0:T(8,128)(2,1)S(1)}, u32[]{:S(2)}, u32[]{:S(2)}) collective-permute-start(bf16[500,128]{1,0:T(8,128)(2,1)S(1)} %get-tuple-element.30), channel_id=1, source_target_pairs={{0,31},{1,0},{2,1},{3,2},{4,3},{5,4},{6,5},{7,6},{8,7},{9,8},{10,9... | collective-permute-start | bytes 384008 | tf_op jit(solution)/shard_map/ppermute | solution.py:485
  9.1 0.0 collective-permute-start.4
  9.1 5.3 %collective-permute-start.5 = (bf16[500,128]{1,0:T(8,128)(2,1)S(1)}, bf16[500,128]{1,0:T(8,128)(2,1)S(1)}, u32[]{:S(2)}, u32[]{:S(2)}) collective-permute-start(bf16[500,128]{1,0:T(8,128)(2,1)S(1)} %get-tuple-element.35), channel_id=1, source_target_pairs={{0,31},{1,0},{2,1},{3,2},{4,3},{5,4},{6,5},{7,6},{8,7},{9,8},{10,9... | collective-permute-start | bytes 384008 | tf_op jit(solution)/shard_map/ppermute | solution.py:485
  14.4 4.4 %prepare.1 = (f32[2,6,13,88,128]{4,3,2,1,0:T(8,128)S(1)}, f32[2,6,13,88,128]{4,3,2,1,0:T(8,128)S(1)}, bf16[2,896,896]{2,1,0:T(8,128)(2,1)S(1)}, bf16[2,896,896]{...) custom-call(bf16[2,4,64000]{2,1,0:T(4,128)(2,1)} %orb_hbm.3, ...), custom_call_target="tpu_custom_call" | custom-call | flops 10000000 | bytes 10000000 | tf_op jit(solution)/shard_map/prepare/pallas_call | solution.py:545
  18.8 0.0 collective-permute-done.prev_ref
  18.8 0.0 collective-permute-done.1.next_ref
  18.8 0.3 shard_map.82.refs_5_
  19.1 6.4 %shard_map.83 = (f32[3,500,128]{2,1,0:T(8,128)S(1)}, bf16[1,500,128]{2,1,0:T(8,128)(2,1)S(1)}, bf16[2,500,128]{2,1,0:T(8,128)(2,1)S(1)}) custom-call(s32[57]{0:T(128)S(1)} %get-tuple-element.23.refs_0_, bf16[2,896,896]{2,1,0:T(8,128)(2,1)S(1)} %get-tuple-element.24.refs_1_, bf16[2,896,896]{2,1,0:T(8,128)(2,1)S(1)} %get-tuple-element.25.refs_2_, ...), custom_call_target="tpu_custom_call" | custom-call | flops 1228800000 | bytes 10000000 | tf_op jit(solution)/shard_map/pallas_call | solution.py:572
  25.5 0.1 collective-permute-start.3
  25.5 0.0 collective-permute-done.4.prev_ref
  25.5 0.0 collective-permute-done.5.next_ref
  25.6 0.3 shard_map.84.refs_5_.refs_6_
  25.8 6.4 %shard_map.85 = (f32[3,500,128]{2,1,0:T(8,128)S(1)}, bf16[1,500,128]{2,1,0:T(8,128)(2,1)S(1)}, bf16[2,500,128]{2,1,0:T(8,128)(2,1)S(1)}) custom-call(s32[57]{0:T(128)S(1)} %get-tuple-element.23.refs_0_, bf16[2,896,896]{2,1,0:T(8,128)(2,1)S(1)} %get-tuple-element.24.refs_1_, bf16[2,896,896]{2,1,0:T(8,128)(2,1)S(1)} %get-tuple-element.25.refs_2_, ...), custom_call_target="tpu_custom_call" | custom-call | flops 1228800000 | bytes 10000000 | tf_op jit(solution)/shard_map/pallas_call | solution.py:572
  32.2 0.1 collective-permute-start.7
  32.3 2.0 %collective-permute-start.2 = (bf16[1,500,128]{2,1,0:T(8,128)(2,1)S(1)}, bf16[1,500,128]{2,1,0:T(8,128)(2,1)S(1)}, u32[]{:S(2)}, u32[]{:S(2)}) collective-permute-start(bf16[1,500,128]{2,1,0:T(8,128)(2,1)S(1)} %get-tuple-element.31), channel_id=1, source_target_pairs={{0,1},{1,2},{2,3},{3,4},{4,5},{5,6},{6,7},{7,8},{8,9},{9,10},{10,1... | collective-permute-start | bytes 384008 | tf_op jit(solution)/shard_map/ppermute | solution.py:485
  34.3 2.0 %collective-permute-start.6 = (bf16[1,500,128]{2,1,0:T(8,128)(2,1)S(1)}, bf16[1,500,128]{2,1,0:T(8,128)(2,1)S(1)}, u32[]{:S(2)}, u32[]{:S(2)}) collective-permute-start(bf16[1,500,128]{2,1,0:T(8,128)(2,1)S(1)} %get-tuple-element.36), channel_id=1, source_target_pairs={{0,1},{1,2},{2,3},{3,4},{4,5},{5,6},{6,7},{7,8},{8,9},{9,10},{10,1... | collective-permute-start | bytes 384008 | tf_op jit(solution)/shard_map/ppermute | solution.py:485
  36.3 5.9 %shard_map.86.refs_5_ = f32[7,1000,128]{2,1,0:T(8,128)} custom-call(s32[57]{0:T(128)S(1)} %get-tuple-element.23.refs_0_, bf16[2,896,896]{2,1,0:T(8,128)(2,1)S(1)} %get-tuple-element.24.refs_1_, bf16[2,896,896]{2,1,0:T(8,128)(2,1)S(1)} %get-tuple-element.25.refs_2_, bf16[160,160]{1,0:T(8,128)(2,1)S(1)} %get-tuple-element.38.refs_3_, ...), custom_call_target="tpu_custom_call" | custom-call | flops 819200000 | bytes 10000000 | tf_op jit(solution)/shard_map/pallas_call | solution.py:572
  42.2 0.0 collective-permute-done.2.refs_1_
  42.2 2.3 %collective-permute-done.6.refs_3_ = bf16[1,500,128]{2,1,0:T(8,128)(2,1)S(1)} collective-permute-done((bf16[1,500,128]{2,1,0:T(8,128)(2,1)S(1)}, bf16[1,500,128]{2,1,0:T(8,128)(2,1)S(1)}, u32[]{:S(2)}, u32[]{:S(2)}) %collective-permute-start.6) | collective-permute-done | bytes 128032 | tf_op jit(solution)/shard_map/ppermute | solution.py:485
  44.4 0.0 collective-permute-done.3.refs_2_
  44.4 2.1 %collective-permute-done.7.refs_4_ = bf16[2,500,128]{2,1,0:T(8,128)(2,1)S(1)} collective-permute-done((bf16[2,500,128]{2,1,0:T(8,128)(2,1)S(1)}, bf16[2,500,128]{2,1,0:T(8,128)(2,1)S(1)}, u32[]{:S(2)}, u32[]{:S(2)}) %collective-permute-start.7) | collective-permute-done | bytes 256032 | tf_op jit(solution)/shard_map/ppermute | solution.py:485
  46.6 1.4 %place.1 = f32[7,1000,128]{2,1,0:T(8,128)} custom-call(s32[57]{0:T(128)S(1)} %get-tuple-element.23.refs_0_, bf16[1,500,128]{2,1,0:T(8,128)(2,1)S(1)} %collective-permute-done.2.refs_1_, bf16[2,500,128]{2,1,0:T(8,128)(2,1)S(1)} %collective-permute-done.3.refs_2_, ...), custom_call_target="tpu_custom_call", output_to_operand_aliasing={{}: (5, {})} | custom-call | flops 1000000 | bytes 4000000 | tf_op jit(solution)/shard_map/place/pallas_call | solution.py:596
Async XLA Ops:
  2.5 16.3 %collective-permute-start = (bf16[500,128]{1,0:T(8,128)(2,1)S(1)}, bf16[500,128]{1,0:T(8,128)(2,1)S(1)}, u32[]{:S(2)}, u32[]{:S(2)}) collective-permute-start(bf16[500,128]{1,0:T(8,128)(2,1)S(1)} %get-tuple-element.29), channel_id=1, source_target_pairs={{0,1},{1,2},{2,3},{3,4},{4,5},{5,6},{6,7},{7,8},{8,9},{9,10},{10,1... | collective-permute-start | bytes 384008 | tf_op jit(solution)/shard_map/ppermute | solution.py:485
  5.6 13.2 %collective-permute-start.1 = (bf16[500,128]{1,0:T(8,128)(2,1)S(1)}, bf16[500,128]{1,0:T(8,128)(2,1)S(1)}, u32[]{:S(2)}, u32[]{:S(2)}) collective-permute-start(bf16[500,128]{1,0:T(8,128)(2,1)S(1)} %get-tuple-element.30), channel_id=1, source_target_pairs={{0,31},{1,0},{2,1},{3,2},{4,3},{5,4},{6,5},{7,6},{8,7},{9,8},{10,9... | collective-permute-start | bytes 384008 | tf_op jit(solution)/shard_map/ppermute | solution.py:485
  9.1 16.5 %collective-permute-start.4 = (bf16[500,128]{1,0:T(8,128)(2,1)S(1)}, bf16[500,128]{1,0:T(8,128)(2,1)S(1)}, u32[]{:S(2)}, u32[]{:S(2)}) collective-permute-start(bf16[500,128]{1,0:T(8,128)(2,1)S(1)} %get-tuple-element.34), channel_id=1, source_target_pairs={{0,1},{1,2},{2,3},{3,4},{4,5},{5,6},{6,7},{7,8},{8,9},{9,10},{10,1... | collective-permute-start | bytes 384008 | tf_op jit(solution)/shard_map/ppermute | solution.py:485
  9.1 16.5 %collective-permute-start.5 = (bf16[500,128]{1,0:T(8,128)(2,1)S(1)}, bf16[500,128]{1,0:T(8,128)(2,1)S(1)}, u32[]{:S(2)}, u32[]{:S(2)}) collective-permute-start(bf16[500,128]{1,0:T(8,128)(2,1)S(1)} %get-tuple-element.35), channel_id=1, source_target_pairs={{0,31},{1,0},{2,1},{3,2},{4,3},{5,4},{6,5},{7,6},{8,7},{9,8},{10,9... | collective-permute-start | bytes 384008 | tf_op jit(solution)/shard_map/ppermute | solution.py:485
  25.5 19.0 %collective-permute-start.3 = (bf16[2,500,128]{2,1,0:T(8,128)(2,1)S(1)}, bf16[2,500,128]{2,1,0:T(8,128)(2,1)S(1)}, u32[]{:S(2)}, u32[]{:S(2)}) collective-permute-start(bf16[2,500,128]{2,1,0:T(8,128)(2,1)S(1)} %get-tuple-element.32), channel_id=1, source_target_pairs={{0,31},{1,0},{2,1},{3,2},{4,3},{5,4},{6,5},{7,6},{8,7},{9,8},{10,9... | collective-permute-start | bytes 768008 | tf_op jit(solution)/shard_map/ppermute | solution.py:485
  32.2 14.4 %collective-permute-start.7 = (bf16[2,500,128]{2,1,0:T(8,128)(2,1)S(1)}, bf16[2,500,128]{2,1,0:T(8,128)(2,1)S(1)}, u32[]{:S(2)}, u32[]{:S(2)}) collective-permute-start(bf16[2,500,128]{2,1,0:T(8,128)(2,1)S(1)} %get-tuple-element.37), channel_id=1, source_target_pairs={{0,31},{1,0},{2,1},{3,2},{4,3},{5,4},{6,5},{7,6},{8,7},{9,8},{10,9... | collective-permute-start | bytes 768008 | tf_op jit(solution)/shard_map/ppermute | solution.py:485
  32.3 9.9 %collective-permute-start.2 = (bf16[1,500,128]{2,1,0:T(8,128)(2,1)S(1)}, bf16[1,500,128]{2,1,0:T(8,128)(2,1)S(1)}, u32[]{:S(2)}, u32[]{:S(2)}) collective-permute-start(bf16[1,500,128]{2,1,0:T(8,128)(2,1)S(1)} %get-tuple-element.31), channel_id=1, source_target_pairs={{0,1},{1,2},{2,3},{3,4},{4,5},{5,6},{6,7},{7,8},{8,9},{9,10},{10,1... | collective-permute-start | bytes 384008 | tf_op jit(solution)/shard_map/ppermute | solution.py:485
  34.3 10.1 %collective-permute-start.6 = (bf16[1,500,128]{2,1,0:T(8,128)(2,1)S(1)}, bf16[1,500,128]{2,1,0:T(8,128)(2,1)S(1)}, u32[]{:S(2)}, u32[]{:S(2)}) collective-permute-start(bf16[1,500,128]{2,1,0:T(8,128)(2,1)S(1)} %get-tuple-element.36), channel_id=1, source_target_pairs={{0,1},{1,2},{2,3},{3,4},{4,5},{5,6},{6,7},{7,8},{8,9},{9,10},{10,1... | collective-permute-start | bytes 384008 | tf_op jit(solution)/shard_map/ppermute | solution.py:485

commit v8 on v7

--- a/solution.py
+++ b/solution.py
@@ -37,11 +37,13 @@
 
 
 def tables():
-    counter = np.arange(EDGE, dtype=np.float32) + 1.0
-    angles = np.float32(np.pi) * counter[:, None] * counter[None, :] / np.float32(EDGE + 1.0)
-    sine = (np.sqrt(np.float32(2.0 / (EDGE + 1.0))) * np.sin(angles)).astype(jnp.bfloat16)
-    sine = sine.astype(np.float32)
-    levels = 2.0 - 2.0 * np.cos(np.pi * counter.astype(np.float64) / (EDGE + 1.0))
+    counter = np.arange(EDGE) + 1
+    turns = np.outer(counter, counter) % (2 * (EDGE + 1))
+    sine = (np.sqrt(2.0 / (EDGE + 1.0)) * np.sin(np.pi * turns / (EDGE + 1.0))).astype(np.float32)
+    sine = sine.astype(jnp.bfloat16).astype(np.float32)
+    flipped = sine[::-1] * np.where(np.arange(EDGE) % 2 == 0, 1.0, -1.0)
+    assert np.array_equal(sine, flipped)
+    levels = 2.0 - 2.0 * np.cos(np.pi * counter / (EDGE + 1.0))
     number = np.arange(FOLD)
     second, step = number // HALF, number % HALF
     thirds = [2 * step + second % 2, 2 * step + 1 - second % 2]
@@ -130,23 +132,18 @@
     return wanted
 
 
-def window_kernel(dest_hbm, part_hbm, anc_hbm, orb_hbm, ahead_low, back_low, ahead_high, back_high, tab_ref,
-                  dest_ref, part_ref, anc_ref, orb_ref, flat_ref, sems):
-    boxes = orb_ref.shape[1]
-    small = [pltpu.make_async_copy(source, target, sems.at[k]) for k, (source, target) in enumerate(
-        ((part_hbm, part_ref), (dest_hbm, dest_ref), (anc_hbm, anc_ref)))]
-    large = [pltpu.make_async_copy(orb_hbm.at[spin], orb_ref.at[spin], sems.at[3 + spin]) for spin in range(2)]
-    for copy in (small[0], large[0], small[1], small[2], large[1]):
-        copy.start()
-    for copy in small:
-        copy.wait()
+def window_kernel(part_hbm, orb_hbm, ahead_ref, back_ref, part_ref, orb_ref, flat_ref, sems):
+    boxes = orb_ref.shape[0]
+    small = pltpu.make_async_copy(part_hbm, part_ref, sems.at[0])
+    large = pltpu.make_async_copy(orb_hbm.at[0], orb_ref, sems.at[1])
+    small.start()
+    large.start()
+    small.wait()
     wanted = wanted_boxes(part_ref, boxes)
-    build_tables(dest_ref, part_ref, anc_ref, tab_ref, boxes)
-    for spin, refs in enumerate(((ahead_low, back_low), (ahead_high, back_high))):
-        large[spin].wait()
-        split_boxes(orb_ref.at[spin], flat_ref, boxes)
-        for side, ref in enumerate(refs):
-            ref[...] = flat_ref[pl.ds(wanted[side], FLAT, stride=8), :].astype(BF)
+    large.wait()
+    split_boxes(orb_ref, flat_ref, boxes)
+    for side, ref in enumerate((ahead_ref, back_ref)):
+        ref[...] = flat_ref[pl.ds(wanted[side], FLAT, stride=8), :].astype(BF)
 
 
 def table_layout(boxes):
@@ -225,17 +222,26 @@
                   lambda u, x: pad_ref.__setitem__((1, box, u, body, slice(None)), x), 0, TILES)
 
 
-def prepare_kernel(orb_hbm, fac_hbm, inv_hbm, diag_hbm, rest_hbm, low_ref, high_ref, to_ref, from_ref, inv_ref, diag_ref,
-                   rest_ref, orb_ref, fac_ref, flat_ref, sems):
+def prepare_kernel(dest_hbm, part_hbm, anc_hbm, orb_hbm, inv_hbm, diag_hbm, rest_hbm,
+                   low_ref, high_ref, ahead_ref, back_ref, tab_ref, inv_ref, diag_ref, rest_ref,
+                   dest_ref, part_ref, anc_ref, orb_ref, flat_ref, sems):
     boxes = orb_ref.shape[1]
-    copies = [pltpu.make_async_copy(orb_hbm.at[spin], orb_ref.at[spin], sems.at[spin]) for spin in range(2)]
-    copies += [pltpu.make_async_copy(source, target, sems.at[2 + k]) for k, (source, target) in enumerate(
-        ((fac_hbm, fac_ref), (inv_hbm, inv_ref), (diag_hbm, diag_ref), (rest_hbm, rest_ref)))]
+    pieces = [(part_hbm, part_ref), (dest_hbm, dest_ref), (anc_hbm, anc_ref)]
+    pieces += [(orb_hbm.at[spin], orb_ref.at[spin]) for spin in range(2)]
+    pieces += [(inv_hbm, inv_ref), (diag_hbm, diag_ref), (rest_hbm, rest_ref)]
+    copies = [pltpu.make_async_copy(source, target, sems.at[k]) for k, (source, target) in enumerate(pieces)]
     for copy in copies:
         copy.start()
+    for copy in copies[:3]:
+        copy.wait()
+    build_tables(dest_ref, part_ref, anc_ref, tab_ref, boxes)
+    wanted = wanted_boxes(part_ref, boxes)
     for spin, pad_ref in enumerate((low_ref, high_ref)):
-        copies[spin].wait()
+        copies[3 + spin].wait()
         split_boxes(orb_ref.at[spin], flat_ref, boxes)
+        if spin == 1:
+            for side, ref in enumerate((ahead_ref, back_ref)):
+                ref[...] = flat_ref[pl.ds(wanted[side], FLAT, stride=8), :].astype(BF)
 
         def slabs(box, _):
             flat_to_slabs(
@@ -247,30 +253,39 @@
             return 0
 
         lax.fori_loop(0, boxes, slabs, 0)
-
-    copies[2].wait()
-    front = lax.broadcasted_iota(jnp.int32, (EDGE, 1), 0) < HALF
-
-    def build(i, _):
-        where = pl.ds(pl.multiple_of(i * 2 * EDGE, 16), 2 * EDGE)
-        for first, size in CHUNKS:
-            cols = slice(first, first + size)
-            line = [fac_ref[0, pl.ds(2 * i + k, 1), cols] for k in range(2)]
-            mode = [fac_ref[3, pl.ds(4 * i + k, 1), cols] for k in range(4)]
-            modes = [jnp.where(front, mode[2 * k], mode[2 * k + 1]) for k in range(2)]
-            for part in range(2):
-                right = fac_ref[1 + part, :, cols]
-                to_ref[part, where, cols] = jnp.concatenate([x * right for x in line], axis=0).astype(BF)
-                right = fac_ref[4 + part, :, cols]
-                from_ref[part, where, cols] = jnp.concatenate([x * right for x in modes], axis=0).astype(BF)
-        return 0
-
-    lax.fori_loop(0, HALF // 2, build, 0)
-    for part in range(2):
-        to_ref[part, FOLD:, :] = jnp.zeros((FWIDE - FOLD, FWIDE), BF)
-        from_ref[part, FOLD:, :] = jnp.zeros((FWIDE - FOLD, FWIDE), BF)
-    for copy in copies[3:]:
+    for copy in copies[5:]:
         copy.wait()
+
+
+def modes_kernel(early, fac_hbm, *refs):
+    to_ref, from_ref, fac_ref, sem = refs[-4:]
+    first = lax.axis_index(AXES[-1]) == 0
+
+    @pl.when(first if early else jnp.logical_not(first))
+    def _():
+        copy = pltpu.make_async_copy(fac_hbm, fac_ref, sem)
+        copy.start()
+        for part in range(2):
+            to_ref[part, FOLD:, :] = jnp.zeros((FWIDE - FOLD, FWIDE), BF)
+            from_ref[part, FOLD:, :] = jnp.zeros((FWIDE - FOLD, FWIDE), BF)
+        front = lax.broadcasted_iota(jnp.int32, (EDGE, 1), 0) < HALF
+        copy.wait()
+
+        def build(i, _):
+            where = pl.ds(pl.multiple_of(i * 2 * EDGE, 16), 2 * EDGE)
+            for start, size in CHUNKS:
+                cols = slice(start, start + size)
+                line = [fac_ref[0, pl.ds(2 * i + k, 1), cols] for k in range(2)]
+                mode = [fac_ref[3, pl.ds(4 * i + k, 1), cols] for k in range(4)]
+                modes = [jnp.where(front, mode[2 * k], mode[2 * k + 1]) for k in range(2)]
+                for part in range(2):
+                    right = fac_ref[1 + part, :, cols]
+                    to_ref[part, where, cols] = jnp.concatenate([x * right for x in line], axis=0).astype(BF)
+                    right = fac_ref[4 + part, :, cols]
+                    from_ref[part, where, cols] = jnp.concatenate([x * right for x in modes], axis=0).astype(BF)
+            return 0
+
+        lax.fori_loop(0, HALF // 2, build, 0)
 
 
 def fill_kernel(old_ref, prev_ref, next_ref, pad_ref, flat_ref):
@@ -508,41 +523,57 @@
 
     box = jax.ShapeDtypeStruct((FLAT, LANES), BF)
     splitter = pltpu.VMEM((FLAT * 8, LANES), F32)
-    ahead_low, back_low, ahead_high, back_high, table = pl.pallas_call(
+    ahead, back = pl.pallas_call(
         window_kernel,
-        out_shape=[box] * 4 + [jax.ShapeDtypeStruct((table_layout(boxes)[-1],), jnp.int32)],
-        in_specs=[ANYWHERE] * 4,
-        out_specs=whole(4) + [SCALARS],
-        scratch_shapes=[pltpu.SMEM(dest.shape, jnp.int32), pltpu.SMEM(partners_t.shape, jnp.int32),
-                        pltpu.SMEM(anchors_t.shape, jnp.int32), pltpu.VMEM(orbitals.shape, BF),
-                        splitter, pltpu.SemaphoreType.DMA((5,))],
+        out_shape=[box] * 2,
+        in_specs=[ANYWHERE] * 2,
+        out_specs=whole(2),
+        scratch_shapes=[pltpu.SMEM(partners_t.shape, jnp.int32), pltpu.VMEM(orbitals.shape[1:], BF),
+                        splitter, pltpu.SemaphoreType.DMA((2,))],
         compiler_params=pltpu.CompilerParams(vmem_limit_bytes=12 << 20),
         name="window",
-    )(*map(in_place, (dest, partners_t, anchors_t, orbitals)))
-    prev_low = from_behind(ahead_low, 1)
-    next_low = from_behind(back_low, -1)
-    prev_high = from_behind(ahead_high, 1)
-    next_high = from_behind(back_high, -1)
-
+    )(*map(in_place, (partners_t, orbitals)))
+    prev_low = from_behind(ahead, 1)
+    next_low = from_behind(back, -1)
+
+    folded = jax.ShapeDtypeStruct((2, FWIDE, FWIDE), BF)
+
+    def build_modes(early, *before):
+        return pl.pallas_call(
+            lambda *refs: modes_kernel(early, *refs),
+            out_shape=[folded] * 2,
+            in_specs=[ANYWHERE] + whole(len(before)),
+            out_specs=whole(2),
+            scratch_shapes=[pltpu.VMEM(factors.shape, F32), pltpu.SemaphoreType.DMA],
+            input_output_aliases={1: 0, 2: 1} if before else {},
+            compiler_params=pltpu.CompilerParams(vmem_limit_bytes=12 << 20),
+            cost_estimate=cost(4_000_000, 4_000_000),
+        )(in_place(factors), *before)
+
+    modes = build_modes(True)
     moving = AHEAD + BACK
     slabs = jax.ShapeDtypeStruct((2, boxes + 2, TILES, ROWS, LANES), F32)
-    folded = jax.ShapeDtypeStruct((2, FWIDE, FWIDE), BF)
     diags = [np.kron(np.eye(cubes, dtype=np.float32), sine).astype(jnp.bfloat16)
              for cubes in (moving * PARTNERS, (boxes - moving) * 2 * PARTNERS)]
     handed = (inverse, *diags)
     prepare = pl.pallas_call(
         prepare_kernel,
-        out_shape=[slabs, slabs, folded, folded]
+        out_shape=[slabs, slabs, box, box, jax.ShapeDtypeStruct((table_layout(boxes)[-1],), jnp.int32)]
         + [jax.ShapeDtypeStruct(value.shape, value.dtype) for value in handed],
-        in_specs=[ANYWHERE] * 5,
-        out_specs=whole(7),
-        scratch_shapes=[pltpu.VMEM(orbitals.shape, BF), pltpu.VMEM(factors.shape, F32), splitter,
-                        pltpu.SemaphoreType.DMA((6,))],
+        in_specs=[ANYWHERE] * 7,
+        out_specs=whole(4) + [SCALARS] + whole(3),
+        scratch_shapes=[pltpu.SMEM(dest.shape, jnp.int32), pltpu.SMEM(partners_t.shape, jnp.int32),
+                        pltpu.SMEM(anchors_t.shape, jnp.int32), pltpu.VMEM(orbitals.shape, BF), splitter,
+                        pltpu.SemaphoreType.DMA((8,))],
         compiler_params=pltpu.CompilerParams(vmem_limit_bytes=20 << 20),
         cost_estimate=cost(10_000_000, 10_000_000),
         name="prepare",
     )
-    low, high, to_modes, from_modes, inverse, *diags = prepare(*map(in_place, (orbitals, factors, *handed)))
+    low, high, ahead, back, table, inverse, *diags = prepare(
+        *map(in_place, (dest, partners_t, anchors_t, orbitals, *handed)))
+    prev_high = from_behind(ahead, 1)
+    next_high = from_behind(back, -1)
+    to_modes, from_modes = build_modes(False, *modes)
     pads = [low, high]
     for spin, halo in enumerate(((prev_low, next_low), (prev_high, next_high))):
         pads[spin] = pl.pallas_call(

time: 48.1 us -> 49.5 us (1.029)
  waiting for transfers between devices: 4.43 us -> 5.06 us
  Pallas kernels: 27.5 us -> 28.1 us
    pallas_call x2 -> x4, Pallas kernels: 6.92 us -> 7.67 us  [the longest x1 4.29 us: shards(): prepare(*map(in_place, (dest, partners_t, anchors_t, orbitals, *handed)))]
    ppermute x8, waiting for transfers between devices: 4.43 us -> 5.06 us  [from_behind(): lax.ppermute(value, AXES, [(source, (source + steps) % count) for source...]
  transfers between devices with their start and end apart: 8 -> 8, of which waited for: 2 -> 3; matrix products, arithmetic and copies ran while one was open for 0% -> 0% of each run, Pallas kernels for 49% -> 45%
where the time goes in v8:
time: 49.5 us; the launch traced here: 49.3 us
  Pallas kernels  28.1 us (57%)
  starting transfers between devices  16.1 us (33%)
  waiting for transfers between devices  5.06 us (10%)
    pallas_call x3, Pallas kernels, solve(): pl.pallas_call(lambda *refs: pair_kernel(start, held, spins, final, *refs...  18.5 us
    ppermute x8, starting transfers between devices, from_behind(): lax.ppermute(value, AXES, [(source, (source + steps) % count) for source...  16.1 us
    ppermute x8, waiting for transfers between devices, from_behind(): lax.ppermute(value, AXES, [(source, (source + steps) % count) for source...  5.06 us
    pallas_call x1, Pallas kernels, shards(): prepare(*map(in_place, (dest, partners_t, anchors_t, orbitals, *handed)))  4.29 us
    pallas_call x2, Pallas kernels, build_modes(): pl.pallas_call(lambda *refs: modes_kernel(early, *refs), out_shape=[folde...  1.98 us
    pallas_call x1, Pallas kernels, shards(): pl.pallas_call(window_kernel, out_shape=[box] * 2, in_specs=[ANYWHERE] *...  1.4 us
    pallas_call x1, Pallas kernels, shards(): pl.pallas_call(lambda *refs: place_kernel(boxes, *refs), out_shape=shape,...  1.4 us
  transfers between devices with their start and end apart: 8, of which 3 were waited for; matrix products, arithmetic and copies ran while one was open for 0% of the time, Pallas kernels for 45%

profile of v8, /device:TPU:0, one launch (start us, length us, event | category | flops | bytes accessed | tf_op | source)
XLA Modules:
  0.0 49.3 jit_solution(7405272314623056753)
XLA Ops:
  0.0 4.3 %prepare.1 = (f32[2,6,13,88,128]{4,3,2,1,0:T(8,128)S(1)}, f32[2,6,13,88,128]{4,3,2,1,0:T(8,128)S(1)}, bf16[500,128]{1,0:T(8,128)(2,1)S(1)}, bf16[500,128]{1,0:T(...) custom-call(s32[128]{0:T(128)} %dest_hbm.1, ...), custom_call_target="tpu_custom_call" | custom-call | flops 10000000 | bytes 10000000 | tf_op jit(solution)/shard_map/prepare/pallas_call | solution.py:572
  4.3 3.1 %collective-permute-start.4 = (bf16[500,128]{1,0:T(8,128)(2,1)S(1)}, bf16[500,128]{1,0:T(8,128)(2,1)S(1)}, u32[]{:S(2)}, u32[]{:S(2)}) collective-permute-start(bf16[500,128]{1,0:T(8,128)(2,1)S(1)} %get-tuple-element.38), channel_id=1, source_target_pairs={{0,1},{1,2},{2,3},{3,4},{4,5},{5,6},{6,7},{7,8},{8,9},{9,10},{10,1... | collective-permute-start | bytes 384008 | tf_op jit(solution)/shard_map/ppermute | solution.py:500
  7.4 3.4 %collective-permute-start.5 = (bf16[500,128]{1,0:T(8,128)(2,1)S(1)}, bf16[500,128]{1,0:T(8,128)(2,1)S(1)}, u32[]{:S(2)}, u32[]{:S(2)}) collective-permute-start(bf16[500,128]{1,0:T(8,128)(2,1)S(1)} %get-tuple-element.39), channel_id=1, source_target_pairs={{0,31},{1,0},{2,1},{3,2},{4,3},{5,4},{6,5},{7,6},{8,7},{9,8},{10,9... | collective-permute-start | bytes 384008 | tf_op jit(solution)/shard_map/ppermute | solution.py:500
  10.8 1.4 %window.1 = (bf16[500,128]{1,0:T(8,128)(2,1)S(1)}, bf16[500,128]{1,0:T(8,128)(2,1)S(1)}) custom-call(s32[2,128]{1,0:T(2,128)} %bitcast.10, bf16[2,4,64000]{2,1,0:T(4,128)(2,1)} %orb_hbm.3), custom_call_target="tpu_custom_call" | custom-call | tf_op jit(solution)/shard_map/window/pallas_call | solution.py:526
  12.2 0.1 collective-permute-start
  12.3 5.3 %collective-permute-start.1 = (bf16[500,128]{1,0:T(8,128)(2,1)S(1)}, bf16[500,128]{1,0:T(8,128)(2,1)S(1)}, u32[]{:S(2)}, u32[]{:S(2)}) collective-permute-start(bf16[500,128]{1,0:T(8,128)(2,1)S(1)} %get-tuple-element.34), channel_id=1, source_target_pairs={{0,31},{1,0},{2,1},{3,2},{4,3},{5,4},{6,5},{7,6},{8,7},{9,8},{10,9... | collective-permute-start | bytes 384008 | tf_op jit(solution)/shard_map/ppermute | solution.py:500
  17.6 2.0 %shard_map.82 = (bf16[2,896,896]{2,1,0:T(8,128)(2,1)S(1)}, bf16[2,896,896]{2,1,0:T(8,128)(2,1)S(1)}) custom-call(f32[6,40,896]{2,1,0:T(8,128)} %constant.8.clone.refs_0_), custom_call_target="tpu_custom_call" | custom-call | flops 4000000 | bytes 4000000 | tf_op jit(solution)/shard_map/pallas_call | solution.py:542
  19.6 0.0 collective-permute-done.4.prev_ref
  19.6 0.0 collective-permute-done.5.next_ref
  19.6 0.3 shard_map.86.refs_5_.refs_6_
  19.9 6.3 %shard_map.87 = (f32[3,500,128]{2,1,0:T(8,128)S(1)}, bf16[1,500,128]{2,1,0:T(8,128)(2,1)S(1)}, bf16[2,500,128]{2,1,0:T(8,128)(2,1)S(1)}) custom-call(s32[57]{0:T(128)S(1)} %get-tuple-element.25.refs_0_, bf16[2,896,896]{2,1,0:T(8,128)(2,1)S(1)} %get-tuple-element.28.refs_1_, bf16[2,896,896]{2,1,0:T(8,128)(2,1)S(1)} %get-tuple-element.29.refs_2_, ...), custom_call_target="tpu_custom_call" | custom-call | flops 1228800000 | bytes 10000000 | tf_op jit(solution)/shard_map/pallas_call | solution.py:603
  26.3 0.9 %collective-permute-start.7 = (bf16[2,500,128]{2,1,0:T(8,128)(2,1)S(1)}, bf16[2,500,128]{2,1,0:T(8,128)(2,1)S(1)}, u32[]{:S(2)}, u32[]{:S(2)}) collective-permute-start(bf16[2,500,128]{2,1,0:T(8,128)(2,1)S(1)} %get-tuple-element.41), channel_id=1, source_target_pairs={{0,31},{1,0},{2,1},{3,2},{4,3},{5,4},{6,5},{7,6},{8,7},{9,8},{10,9... | collective-permute-start | bytes 768008 | tf_op jit(solution)/shard_map/ppermute | solution.py:500
  27.1 0.0 collective-permute-done.prev_ref
  27.1 0.0 collective-permute-done.1.next_ref
  27.1 0.3 shard_map.84.refs_5_
  27.4 6.3 %shard_map.85 = (f32[3,500,128]{2,1,0:T(8,128)S(1)}, bf16[1,500,128]{2,1,0:T(8,128)(2,1)S(1)}, bf16[2,500,128]{2,1,0:T(8,128)(2,1)S(1)}) custom-call(s32[57]{0:T(128)S(1)} %get-tuple-element.25.refs_0_, bf16[2,896,896]{2,1,0:T(8,128)(2,1)S(1)} %get-tuple-element.28.refs_1_, bf16[2,896,896]{2,1,0:T(8,128)(2,1)S(1)} %get-tuple-element.29.refs_2_, ...), custom_call_target="tpu_custom_call" | custom-call | flops 1228800000 | bytes 10000000 | tf_op jit(solution)/shard_map/pallas_call | solution.py:603
  33.8 0.1 collective-permute-start.3
  33.9 1.9 %collective-permute-start.6 = (bf16[1,500,128]{2,1,0:T(8,128)(2,1)S(1)}, bf16[1,500,128]{2,1,0:T(8,128)(2,1)S(1)}, u32[]{:S(2)}, u32[]{:S(2)}) collective-permute-start(bf16[1,500,128]{2,1,0:T(8,128)(2,1)S(1)} %get-tuple-element.40), channel_id=1, source_target_pairs={{0,1},{1,2},{2,3},{3,4},{4,5},{5,6},{6,7},{7,8},{8,9},{9,10},{10,1... | collective-permute-start | bytes 384008 | tf_op jit(solution)/shard_map/ppermute | solution.py:500
  35.8 1.2 %collective-permute-start.2 = (bf16[1,500,128]{2,1,0:T(8,128)(2,1)S(1)}, bf16[1,500,128]{2,1,0:T(8,128)(2,1)S(1)}, u32[]{:S(2)}, u32[]{:S(2)}) collective-permute-start(bf16[1,500,128]{2,1,0:T(8,128)(2,1)S(1)} %get-tuple-element.35), channel_id=1, source_target_pairs={{0,1},{1,2},{2,3},{3,4},{4,5},{5,6},{6,7},{7,8},{8,9},{9,10},{10,1... | collective-permute-start | bytes 384008 | tf_op jit(solution)/shard_map/ppermute | solution.py:500
  37.0 5.8 %shard_map.88.refs_5_ = f32[7,1000,128]{2,1,0:T(8,128)} custom-call(s32[57]{0:T(128)S(1)} %get-tuple-element.25.refs_0_, bf16[2,896,896]{2,1,0:T(8,128)(2,1)S(1)} %get-tuple-element.28.refs_1_, bf16[2,896,896]{2,1,0:T(8,128)(2,1)S(1)} %get-tuple-element.29.refs_2_, bf16[160,160]{1,0:T(8,128)(2,1)S(1)} %get-tuple-element.42.refs_3_, ...), custom_call_target="tpu_custom_call" | custom-call | flops 819200000 | bytes 10000000 | tf_op jit(solution)/shard_map/pallas_call | solution.py:603
  42.9 0.5 collective-permute-done.6.refs_3_
  43.4 2.5 %collective-permute-done.2.refs_1_ = bf16[1,500,128]{2,1,0:T(8,128)(2,1)S(1)} collective-permute-done((bf16[1,500,128]{2,1,0:T(8,128)(2,1)S(1)}, bf16[1,500,128]{2,1,0:T(8,128)(2,1)S(1)}, u32[]{:S(2)}, u32[]{:S(2)}) %collective-permute-start.2) | collective-permute-done | bytes 128032 | tf_op jit(solution)/shard_map/ppermute | solution.py:500
  45.9 0.0 collective-permute-done.7.refs_4_
  45.9 2.1 %collective-permute-done.3.refs_2_ = bf16[2,500,128]{2,1,0:T(8,128)(2,1)S(1)} collective-permute-done((bf16[2,500,128]{2,1,0:T(8,128)(2,1)S(1)}, bf16[2,500,128]{2,1,0:T(8,128)(2,1)S(1)}, u32[]{:S(2)}, u32[]{:S(2)}) %collective-permute-start.3) | collective-permute-done | bytes 256032 | tf_op jit(solution)/shard_map/ppermute | solution.py:500
  47.9 1.4 %place.1 = f32[7,1000,128]{2,1,0:T(8,128)} custom-call(s32[57]{0:T(128)S(1)} %get-tuple-element.25.refs_0_, bf16[1,500,128]{2,1,0:T(8,128)(2,1)S(1)} %collective-permute-done.2.refs_1_, bf16[2,500,128]{2,1,0:T(8,128)(2,1)S(1)} %collective-permute-done.3.refs_2_, ...), custom_call_target="tpu_custom_call", output_to_operand_aliasing={{}: (5, {})} | custom-call | flops 1000000 | bytes 4000000 | tf_op jit(solution)/shard_map/place/pallas_call | solution.py:627
  (1 shorter events, 0.0 us)
Async XLA Ops:
  4.3 15.3 %collective-permute-start.4 = (bf16[500,128]{1,0:T(8,128)(2,1)S(1)}, bf16[500,128]{1,0:T(8,128)(2,1)S(1)}, u32[]{:S(2)}, u32[]{:S(2)}) collective-permute-start(bf16[500,128]{1,0:T(8,128)(2,1)S(1)} %get-tuple-element.38), channel_id=1, source_target_pairs={{0,1},{1,2},{2,3},{3,4},{4,5},{5,6},{6,7},{7,8},{8,9},{9,10},{10,1... | collective-permute-start | bytes 384008 | tf_op jit(solution)/shard_map/ppermute | solution.py:500
  7.4 12.2 %collective-permute-start.5 = (bf16[500,128]{1,0:T(8,128)(2,1)S(1)}, bf16[500,128]{1,0:T(8,128)(2,1)S(1)}, u32[]{:S(2)}, u32[]{:S(2)}) collective-permute-start(bf16[500,128]{1,0:T(8,128)(2,1)S(1)} %get-tuple-element.39), channel_id=1, source_target_pairs={{0,31},{1,0},{2,1},{3,2},{4,3},{5,4},{6,5},{7,6},{8,7},{9,8},{10,9... | collective-permute-start | bytes 384008 | tf_op jit(solution)/shard_map/ppermute | solution.py:500
  12.2 14.9 %collective-permute-start = (bf16[500,128]{1,0:T(8,128)(2,1)S(1)}, bf16[500,128]{1,0:T(8,128)(2,1)S(1)}, u32[]{:S(2)}, u32[]{:S(2)}) collective-permute-start(bf16[500,128]{1,0:T(8,128)(2,1)S(1)} %get-tuple-element.33), channel_id=1, source_target_pairs={{0,1},{1,2},{2,3},{3,4},{4,5},{5,6},{6,7},{7,8},{8,9},{9,10},{10,1... | collective-permute-start | bytes 384008 | tf_op jit(solution)/shard_map/ppermute | solution.py:500
  12.3 14.8 %collective-permute-start.1 = (bf16[500,128]{1,0:T(8,128)(2,1)S(1)}, bf16[500,128]{1,0:T(8,128)(2,1)S(1)}, u32[]{:S(2)}, u32[]{:S(2)}) collective-permute-start(bf16[500,128]{1,0:T(8,128)(2,1)S(1)} %get-tuple-element.34), channel_id=1, source_target_pairs={{0,31},{1,0},{2,1},{3,2},{4,3},{5,4},{6,5},{7,6},{8,7},{9,8},{10,9... | collective-permute-start | bytes 384008 | tf_op jit(solution)/shard_map/ppermute | solution.py:500
  26.3 19.6 %collective-permute-start.7 = (bf16[2,500,128]{2,1,0:T(8,128)(2,1)S(1)}, bf16[2,500,128]{2,1,0:T(8,128)(2,1)S(1)}, u32[]{:S(2)}, u32[]{:S(2)}) collective-permute-start(bf16[2,500,128]{2,1,0:T(8,128)(2,1)S(1)} %get-tuple-element.41), channel_id=1, source_target_pairs={{0,31},{1,0},{2,1},{3,2},{4,3},{5,4},{6,5},{7,6},{8,7},{9,8},{10,9... | collective-permute-start | bytes 768008 | tf_op jit(solution)/shard_map/ppermute | solution.py:500
  33.8 14.2 %collective-permute-start.3 = (bf16[2,500,128]{2,1,0:T(8,128)(2,1)S(1)}, bf16[2,500,128]{2,1,0:T(8,128)(2,1)S(1)}, u32[]{:S(2)}, u32[]{:S(2)}) collective-permute-start(bf16[2,500,128]{2,1,0:T(8,128)(2,1)S(1)} %get-tuple-element.36), channel_id=1, source_target_pairs={{0,31},{1,0},{2,1},{3,2},{4,3},{5,4},{6,5},{7,6},{8,7},{9,8},{10,9... | collective-permute-start | bytes 768008 | tf_op jit(solution)/shard_map/ppermute | solution.py:500
  33.9 9.5 %collective-permute-start.6 = (bf16[1,500,128]{2,1,0:T(8,128)(2,1)S(1)}, bf16[1,500,128]{2,1,0:T(8,128)(2,1)S(1)}, u32[]{:S(2)}, u32[]{:S(2)}) collective-permute-start(bf16[1,500,128]{2,1,0:T(8,128)(2,1)S(1)} %get-tuple-element.40), channel_id=1, source_target_pairs={{0,1},{1,2},{2,3},{3,4},{4,5},{5,6},{6,7},{7,8},{8,9},{9,10},{10,1... | collective-permute-start | bytes 384008 | tf_op jit(solution)/shard_map/ppermute | solution.py:500
  35.8 10.0 %collective-permute-start.2 = (bf16[1,500,128]{2,1,0:T(8,128)(2,1)S(1)}, bf16[1,500,128]{2,1,0:T(8,128)(2,1)S(1)}, u32[]{:S(2)}, u32[]{:S(2)}) collective-permute-start(bf16[1,500,128]{2,1,0:T(8,128)(2,1)S(1)} %get-tuple-element.35), channel_id=1, source_target_pairs={{0,1},{1,2},{2,3},{3,4},{4,5},{5,6},{6,7},{7,8},{8,9},{9,10},{10,1... | collective-permute-start | bytes 384008 | tf_op jit(solution)/shard_map/ppermute | solution.py:500

commit v9 on v8

--- a/solution.py
+++ b/solution.py
@@ -222,12 +222,12 @@
                   lambda u, x: pad_ref.__setitem__((1, box, u, body, slice(None)), x), 0, TILES)
 
 
-def prepare_kernel(dest_hbm, part_hbm, anc_hbm, orb_hbm, inv_hbm, diag_hbm, rest_hbm,
-                   low_ref, high_ref, ahead_ref, back_ref, tab_ref, inv_ref, diag_ref, rest_ref,
-                   dest_ref, part_ref, anc_ref, orb_ref, flat_ref, sems):
+def second_kernel(dest_hbm, part_hbm, anc_hbm, orb_hbm, inv_hbm, diag_hbm, rest_hbm,
+                  orb_ref, ahead_ref, back_ref, tab_ref, inv_ref, diag_ref, rest_ref,
+                  dest_ref, part_ref, anc_ref, flat_ref, sems):
     boxes = orb_ref.shape[1]
     pieces = [(part_hbm, part_ref), (dest_hbm, dest_ref), (anc_hbm, anc_ref)]
-    pieces += [(orb_hbm.at[spin], orb_ref.at[spin]) for spin in range(2)]
+    pieces += [(orb_hbm.at[spin], orb_ref.at[spin]) for spin in (1, 0)]
     pieces += [(inv_hbm, inv_ref), (diag_hbm, diag_ref), (rest_hbm, rest_ref)]
     copies = [pltpu.make_async_copy(source, target, sems.at[k]) for k, (source, target) in enumerate(pieces)]
     for copy in copies:
@@ -236,12 +236,22 @@
         copy.wait()
     build_tables(dest_ref, part_ref, anc_ref, tab_ref, boxes)
     wanted = wanted_boxes(part_ref, boxes)
-    for spin, pad_ref in enumerate((low_ref, high_ref)):
-        copies[3 + spin].wait()
+    copies[3].wait()
+    split_boxes(orb_ref.at[1], flat_ref, boxes)
+    for side, ref in enumerate((ahead_ref, back_ref)):
+        ref[...] = flat_ref[pl.ds(wanted[side], FLAT, stride=8), :].astype(BF)
+    for copy in copies[4:]:
+        copy.wait()
+
+
+def slabs_kernel(spin, near, orb_ref, *refs):
+    pad_ref, flat_ref = refs[-2:]
+    boxes = orb_ref.shape[1]
+    low_half = 2 * lax.axis_index(AXES[-1]) < lax.axis_size(AXES[-1])
+
+    @pl.when(low_half if near else jnp.logical_not(low_half))
+    def _():
         split_boxes(orb_ref.at[spin], flat_ref, boxes)
-        if spin == 1:
-            for side, ref in enumerate((ahead_ref, back_ref)):
-                ref[...] = flat_ref[pl.ds(wanted[side], FLAT, stride=8), :].astype(BF)
 
         def slabs(box, _):
             flat_to_slabs(
@@ -253,8 +263,6 @@
             return 0
 
         lax.fori_loop(0, boxes, slabs, 0)
-    for copy in copies[5:]:
-        copy.wait()
 
 
 def modes_kernel(early, fac_hbm, *refs):
@@ -556,25 +564,38 @@
     diags = [np.kron(np.eye(cubes, dtype=np.float32), sine).astype(jnp.bfloat16)
              for cubes in (moving * PARTNERS, (boxes - moving) * 2 * PARTNERS)]
     handed = (inverse, *diags)
-    prepare = pl.pallas_call(
-        prepare_kernel,
-        out_shape=[slabs, slabs, box, box, jax.ShapeDtypeStruct((table_layout(boxes)[-1],), jnp.int32)]
+    second = pl.pallas_call(
+        second_kernel,
+        out_shape=[jax.ShapeDtypeStruct(orbitals.shape, BF), box, box,
+                   jax.ShapeDtypeStruct((table_layout(boxes)[-1],), jnp.int32)]
         + [jax.ShapeDtypeStruct(value.shape, value.dtype) for value in handed],
         in_specs=[ANYWHERE] * 7,
-        out_specs=whole(4) + [SCALARS] + whole(3),
+        out_specs=whole(3) + [SCALARS] + whole(3),
         scratch_shapes=[pltpu.SMEM(dest.shape, jnp.int32), pltpu.SMEM(partners_t.shape, jnp.int32),
-                        pltpu.SMEM(anchors_t.shape, jnp.int32), pltpu.VMEM(orbitals.shape, BF), splitter,
-                        pltpu.SemaphoreType.DMA((8,))],
-        compiler_params=pltpu.CompilerParams(vmem_limit_bytes=20 << 20),
-        cost_estimate=cost(10_000_000, 10_000_000),
-        name="prepare",
+                        pltpu.SMEM(anchors_t.shape, jnp.int32), splitter, pltpu.SemaphoreType.DMA((8,))],
+        compiler_params=pltpu.CompilerParams(vmem_limit_bytes=12 << 20),
+        cost_estimate=cost(1_000_000, 2_000_000),
+        name="second",
     )
-    low, high, ahead, back, table, inverse, *diags = prepare(
+    held, ahead, back, table, inverse, *diags = second(
         *map(in_place, (dest, partners_t, anchors_t, orbitals, *handed)))
     prev_high = from_behind(ahead, 1)
     next_high = from_behind(back, -1)
     to_modes, from_modes = build_modes(False, *modes)
-    pads = [low, high]
+
+    def build_slabs(spin, near, *before):
+        return pl.pallas_call(
+            lambda *refs: slabs_kernel(spin, near, *refs),
+            out_shape=slabs,
+            in_specs=whole(1 + len(before)),
+            out_specs=pl.BlockSpec(memory_space=pltpu.VMEM),
+            scratch_shapes=[splitter],
+            input_output_aliases={1: 0} if before else {},
+            compiler_params=pltpu.CompilerParams(vmem_limit_bytes=12 << 20),
+            cost_estimate=cost(2_000_000, 4_000_000),
+        )(held, *before)
+
+    pads = [build_slabs(0, True, build_slabs(0, False)), build_slabs(1, False, build_slabs(1, True))]
     for spin, halo in enumerate(((prev_low, next_low), (prev_high, next_high))):
         pads[spin] = pl.pallas_call(
             fill_kernel,

time: 49.5 us -> 54.8 us (1.11)
  waiting for transfers between devices: 5.06 us -> 9.94 us
    ppermute x8, waiting for transfers between devices: 5.06 us -> 9.94 us  [from_behind(): lax.ppermute(value, AXES, [(source, (source + steps) % count) for source...]
    pallas_call x1 -> x5, Pallas kernels: 4.29 us -> 4.57 us  [the longest x4 2.47 us: build_slabs(): pl.pallas_call(lambda *refs: slabs_kernel(spin, near, *refs), out_shape=s...]
  transfers between devices with their start and end apart: 8 -> 8, of which waited for: 3 -> 3; matrix products, arithmetic and copies ran while one was open for 0% -> 0% of each run, Pallas kernels for 45% -> 34%
where the time goes in v9:
time: 54.8 us; the launch traced here: 54.6 us
  Pallas kernels  28.5 us (52%)
  starting transfers between devices  16 us (29%)
  waiting for transfers between devices  9.94 us (18%)
    pallas_call x3, Pallas kernels, solve(): pl.pallas_call(lambda *refs: pair_kernel(start, held, spins, final, *refs...  18.6 us
    ppermute x8, starting transfers between devices, from_behind(): lax.ppermute(value, AXES, [(source, (source + steps) % count) for source...  16 us
    ppermute x8, waiting for transfers between devices, from_behind(): lax.ppermute(value, AXES, [(source, (source + steps) % count) for source...  9.94 us
    pallas_call x4, Pallas kernels, build_slabs(): pl.pallas_call(lambda *refs: slabs_kernel(spin, near, *refs), out_shape=s...  2.47 us
    pallas_call x1, Pallas kernels, shards(): second(*map(in_place, (dest, partners_t, anchors_t, orbitals, *handed)))  2.09 us
    pallas_call x2, Pallas kernels, build_modes(): pl.pallas_call(lambda *refs: modes_kernel(early, *refs), out_shape=[folde...  2 us
    pallas_call x1, Pallas kernels, shards(): pl.pallas_call(window_kernel, out_shape=[box] * 2, in_specs=[ANYWHERE] *...  1.4 us
    pallas_call x1, Pallas kernels, shards(): pl.pallas_call(lambda *refs: place_kernel(boxes, *refs), out_shape=shape,...  1.4 us
  transfers between devices with their start and end apart: 8, of which 3 were waited for; matrix products, arithmetic and copies ran while one was open for 0% of the time, Pallas kernels for 34%

profile of v9, /device:TPU:0, one launch (start us, length us, event | category | flops | bytes accessed | tf_op | source)
XLA Modules:
  0.0 54.6 jit_solution(8586273453130266550)
XLA Ops:
  0.0 2.1 %second.1 = (bf16[2,4,64000]{2,1,0:T(4,128)(2,1)S(1)}, bf16[500,128]{1,0:T(8,128)(2,1)S(1)}, bf16[500,128]{1,0:T(8,128)(2,1)S(1)}, s32[57]{0:T(128)S(1)}, f32[40...) custom-call(s32[128]{0:T(128)} %dest_hbm.1, s32[2,128]{1,0:T(2,128)} %bitcast.9, ...), custom_call_target="tpu_custom_call" | custom-call | flops 1000000 | bytes 2000000 | tf_op jit(solution)/shard_map/second/pallas_call | solution.py:580
  2.1 3.1 %collective-permute-start.4 = (bf16[500,128]{1,0:T(8,128)(2,1)S(1)}, bf16[500,128]{1,0:T(8,128)(2,1)S(1)}, u32[]{:S(2)}, u32[]{:S(2)}) collective-permute-start(bf16[500,128]{1,0:T(8,128)(2,1)S(1)} %get-tuple-element.36), channel_id=1, source_target_pairs={{0,1},{1,2},{2,3},{3,4},{4,5},{5,6},{6,7},{7,8},{8,9},{9,10},{10,1... | collective-permute-start | bytes 384008 | tf_op jit(solution)/shard_map/ppermute | solution.py:508
  5.2 3.4 %collective-permute-start.5 = (bf16[500,128]{1,0:T(8,128)(2,1)S(1)}, bf16[500,128]{1,0:T(8,128)(2,1)S(1)}, u32[]{:S(2)}, u32[]{:S(2)}) collective-permute-start(bf16[500,128]{1,0:T(8,128)(2,1)S(1)} %get-tuple-element.37), channel_id=1, source_target_pairs={{0,31},{1,0},{2,1},{3,2},{4,3},{5,4},{6,5},{7,6},{8,7},{9,8},{10,9... | collective-permute-start | bytes 384008 | tf_op jit(solution)/shard_map/ppermute | solution.py:508
  8.6 1.4 %window.1 = (bf16[500,128]{1,0:T(8,128)(2,1)S(1)}, bf16[500,128]{1,0:T(8,128)(2,1)S(1)}) custom-call(s32[2,128]{1,0:T(2,128)} %bitcast.10, bf16[2,4,64000]{2,1,0:T(4,128)(2,1)} %orb_hbm.3), custom_call_target="tpu_custom_call" | custom-call | tf_op jit(solution)/shard_map/window/pallas_call | solution.py:534
  10.0 0.1 collective-permute-start
  10.1 5.3 %collective-permute-start.1 = (bf16[500,128]{1,0:T(8,128)(2,1)S(1)}, bf16[500,128]{1,0:T(8,128)(2,1)S(1)}, u32[]{:S(2)}, u32[]{:S(2)}) collective-permute-start(bf16[500,128]{1,0:T(8,128)(2,1)S(1)} %get-tuple-element.33), channel_id=1, source_target_pairs={{0,31},{1,0},{2,1},{3,2},{4,3},{5,4},{6,5},{7,6},{8,7},{9,8},{10,9... | collective-permute-start | bytes 384008 | tf_op jit(solution)/shard_map/ppermute | solution.py:508
  15.4 1.2 %shard_map.88.refs_1_ = f32[2,6,13,88,128]{4,3,2,1,0:T(8,128)S(1)} custom-call(bf16[2,4,64000]{2,1,0:T(4,128)(2,1)S(1)} %get-tuple-element.31.refs_0_), custom_call_target="tpu_custom_call" | custom-call | flops 2000000 | bytes 4000000 | tf_op jit(solution)/shard_map/pallas_call | solution.py:587
  16.7 1.2 %shard_map.85.old_ref = f32[2,6,13,88,128]{4,3,2,1,0:T(8,128)S(1)} custom-call(bf16[2,4,64000]{2,1,0:T(4,128)(2,1)S(1)} %get-tuple-element.31.refs_0_, f32[2,6,13,88,128]{4,3,2,1,0:T(8,128)S(1)} %shard_map.84.refs_1_), custom_call_target="tpu_custom_call", output_to_operand_aliasing={{}: (1, {})} | custom-call | flops 2000000 | bytes 4000000 | tf_op jit(solution)/shard_map/pallas_call | solution.py:587
  17.9 2.0 %shard_map.82 = (bf16[2,896,896]{2,1,0:T(8,128)(2,1)S(1)}, bf16[2,896,896]{2,1,0:T(8,128)(2,1)S(1)}) custom-call(f32[6,40,896]{2,1,0:T(8,128)} %constant.8.clone.refs_0_), custom_call_target="tpu_custom_call" | custom-call | flops 4000000 | bytes 4000000 | tf_op jit(solution)/shard_map/pallas_call | solution.py:550
  19.9 0.0 collective-permute-done.4.prev_ref
  20.0 0.0 collective-permute-done.5.next_ref
  20.0 0.3 shard_map.90.refs_5_.refs_6_
  20.2 6.4 %shard_map.91 = (f32[3,500,128]{2,1,0:T(8,128)S(1)}, bf16[1,500,128]{2,1,0:T(8,128)(2,1)S(1)}, bf16[2,500,128]{2,1,0:T(8,128)(2,1)S(1)}) custom-call(s32[57]{0:T(128)S(1)} %get-tuple-element.24.refs_0_, bf16[2,896,896]{2,1,0:T(8,128)(2,1)S(1)} %get-tuple-element.27.refs_1_, bf16[2,896,896]{2,1,0:T(8,128)(2,1)S(1)} %get-tuple-element.28.refs_2_, ...), custom_call_target="tpu_custom_call" | custom-call | flops 1228800000 | bytes 10000000 | tf_op jit(solution)/shard_map/pallas_call | solution.py:624
  26.6 0.0 collective-permute-done.prev_ref
  26.6 0.0 collective-permute-done.1.next_ref
  26.6 0.3 shard_map.86.refs_5_
  26.9 6.3 %shard_map.87 = (f32[3,500,128]{2,1,0:T(8,128)S(1)}, bf16[1,500,128]{2,1,0:T(8,128)(2,1)S(1)}, bf16[2,500,128]{2,1,0:T(8,128)(2,1)S(1)}) custom-call(s32[57]{0:T(128)S(1)} %get-tuple-element.24.refs_0_, bf16[2,896,896]{2,1,0:T(8,128)(2,1)S(1)} %get-tuple-element.27.refs_1_, bf16[2,896,896]{2,1,0:T(8,128)(2,1)S(1)} %get-tuple-element.28.refs_2_, ...), custom_call_target="tpu_custom_call" | custom-call | flops 1228800000 | bytes 10000000 | tf_op jit(solution)/shard_map/pallas_call | solution.py:624
  33.3 0.1 collective-permute-start.7
  33.3 0.1 collective-permute-start.3
  33.4 2.0 %collective-permute-start.6 = (bf16[1,500,128]{2,1,0:T(8,128)(2,1)S(1)}, bf16[1,500,128]{2,1,0:T(8,128)(2,1)S(1)}, u32[]{:S(2)}, u32[]{:S(2)}) collective-permute-start(bf16[1,500,128]{2,1,0:T(8,128)(2,1)S(1)} %get-tuple-element.38), channel_id=1, source_target_pairs={{0,1},{1,2},{2,3},{3,4},{4,5},{5,6},{6,7},{7,8},{8,9},{9,10},{10,1... | collective-permute-start | bytes 384008 | tf_op jit(solution)/shard_map/ppermute | solution.py:508
  35.4 2.0 %collective-permute-start.2 = (bf16[1,500,128]{2,1,0:T(8,128)(2,1)S(1)}, bf16[1,500,128]{2,1,0:T(8,128)(2,1)S(1)}, u32[]{:S(2)}, u32[]{:S(2)}) collective-permute-start(bf16[1,500,128]{2,1,0:T(8,128)(2,1)S(1)} %get-tuple-element.34), channel_id=1, source_target_pairs={{0,1},{1,2},{2,3},{3,4},{4,5},{5,6},{6,7},{7,8},{8,9},{9,10},{10,1... | collective-permute-start | bytes 384008 | tf_op jit(solution)/shard_map/ppermute | solution.py:508
  37.4 5.9 %shard_map.92.refs_5_ = f32[7,1000,128]{2,1,0:T(8,128)} custom-call(s32[57]{0:T(128)S(1)} %get-tuple-element.24.refs_0_, bf16[2,896,896]{2,1,0:T(8,128)(2,1)S(1)} %get-tuple-element.27.refs_1_, bf16[2,896,896]{2,1,0:T(8,128)(2,1)S(1)} %get-tuple-element.28.refs_2_, bf16[160,160]{1,0:T(8,128)(2,1)S(1)} %get-tuple-element.40.refs_3_, ...), custom_call_target="tpu_custom_call" | custom-call | flops 819200000 | bytes 10000000 | tf_op jit(solution)/shard_map/pallas_call | solution.py:624
  43.2 5.0 %collective-permute-done.6.refs_3_ = bf16[1,500,128]{2,1,0:T(8,128)(2,1)S(1)} collective-permute-done((bf16[1,500,128]{2,1,0:T(8,128)(2,1)S(1)}, bf16[1,500,128]{2,1,0:T(8,128)(2,1)S(1)}, u32[]{:S(2)}, u32[]{:S(2)}) %collective-permute-start.6) | collective-permute-done | bytes 128032 | tf_op jit(solution)/shard_map/ppermute | solution.py:508
  48.3 2.8 %collective-permute-done.2.refs_1_ = bf16[1,500,128]{2,1,0:T(8,128)(2,1)S(1)} collective-permute-done((bf16[1,500,128]{2,1,0:T(8,128)(2,1)S(1)}, bf16[1,500,128]{2,1,0:T(8,128)(2,1)S(1)}, u32[]{:S(2)}, u32[]{:S(2)}) %collective-permute-start.2) | collective-permute-done | bytes 128032 | tf_op jit(solution)/shard_map/ppermute | solution.py:508
  51.0 0.0 collective-permute-done.7.refs_4_
  51.0 2.1 %collective-permute-done.3.refs_2_ = bf16[2,500,128]{2,1,0:T(8,128)(2,1)S(1)} collective-permute-done((bf16[2,500,128]{2,1,0:T(8,128)(2,1)S(1)}, bf16[2,500,128]{2,1,0:T(8,128)(2,1)S(1)}, u32[]{:S(2)}, u32[]{:S(2)}) %collective-permute-start.3) | collective-permute-done | bytes 256032 | tf_op jit(solution)/shard_map/ppermute | solution.py:508
  53.2 1.4 %place.1 = f32[7,1000,128]{2,1,0:T(8,128)} custom-call(s32[57]{0:T(128)S(1)} %get-tuple-element.24.refs_0_, bf16[1,500,128]{2,1,0:T(8,128)(2,1)S(1)} %collective-permute-done.2.refs_1_, bf16[2,500,128]{2,1,0:T(8,128)(2,1)S(1)} %collective-permute-done.3.refs_2_, ...), custom_call_target="tpu_custom_call", output_to_operand_aliasing={{}: (5, {})} | custom-call | flops 1000000 | bytes 4000000 | tf_op jit(solution)/shard_map/place/pallas_call | solution.py:648
  (3 shorter events, 0.1 us)
Async XLA Ops:
  2.1 17.9 %collective-permute-start.4 = (bf16[500,128]{1,0:T(8,128)(2,1)S(1)}, bf16[500,128]{1,0:T(8,128)(2,1)S(1)}, u32[]{:S(2)}, u32[]{:S(2)}) collective-permute-start(bf16[500,128]{1,0:T(8,128)(2,1)S(1)} %get-tuple-element.36), channel_id=1, source_target_pairs={{0,1},{1,2},{2,3},{3,4},{4,5},{5,6},{6,7},{7,8},{8,9},{9,10},{10,1... | collective-permute-start | bytes 384008 | tf_op jit(solution)/shard_map/ppermute | solution.py:508
  5.2 14.8 %collective-permute-start.5 = (bf16[500,128]{1,0:T(8,128)(2,1)S(1)}, bf16[500,128]{1,0:T(8,128)(2,1)S(1)}, u32[]{:S(2)}, u32[]{:S(2)}) collective-permute-start(bf16[500,128]{1,0:T(8,128)(2,1)S(1)} %get-tuple-element.37), channel_id=1, source_target_pairs={{0,31},{1,0},{2,1},{3,2},{4,3},{5,4},{6,5},{7,6},{8,7},{9,8},{10,9... | collective-permute-start | bytes 384008 | tf_op jit(solution)/shard_map/ppermute | solution.py:508
  10.0 16.6 %collective-permute-start = (bf16[500,128]{1,0:T(8,128)(2,1)S(1)}, bf16[500,128]{1,0:T(8,128)(2,1)S(1)}, u32[]{:S(2)}, u32[]{:S(2)}) collective-permute-start(bf16[500,128]{1,0:T(8,128)(2,1)S(1)} %get-tuple-element.32), channel_id=1, source_target_pairs={{0,1},{1,2},{2,3},{3,4},{4,5},{5,6},{6,7},{7,8},{8,9},{9,10},{10,1... | collective-permute-start | bytes 384008 | tf_op jit(solution)/shard_map/ppermute | solution.py:508
  10.1 16.5 %collective-permute-start.1 = (bf16[500,128]{1,0:T(8,128)(2,1)S(1)}, bf16[500,128]{1,0:T(8,128)(2,1)S(1)}, u32[]{:S(2)}, u32[]{:S(2)}) collective-permute-start(bf16[500,128]{1,0:T(8,128)(2,1)S(1)} %get-tuple-element.33), channel_id=1, source_target_pairs={{0,31},{1,0},{2,1},{3,2},{4,3},{5,4},{6,5},{7,6},{8,7},{9,8},{10,9... | collective-permute-start | bytes 384008 | tf_op jit(solution)/shard_map/ppermute | solution.py:508
  33.3 17.8 %collective-permute-start.7 = (bf16[2,500,128]{2,1,0:T(8,128)(2,1)S(1)}, bf16[2,500,128]{2,1,0:T(8,128)(2,1)S(1)}, u32[]{:S(2)}, u32[]{:S(2)}) collective-permute-start(bf16[2,500,128]{2,1,0:T(8,128)(2,1)S(1)} %get-tuple-element.39), channel_id=1, source_target_pairs={{0,31},{1,0},{2,1},{3,2},{4,3},{5,4},{6,5},{7,6},{8,7},{9,8},{10,9... | collective-permute-start | bytes 768008 | tf_op jit(solution)/shard_map/ppermute | solution.py:508
  33.3 19.9 %collective-permute-start.3 = (bf16[2,500,128]{2,1,0:T(8,128)(2,1)S(1)}, bf16[2,500,128]{2,1,0:T(8,128)(2,1)S(1)}, u32[]{:S(2)}, u32[]{:S(2)}) collective-permute-start(bf16[2,500,128]{2,1,0:T(8,128)(2,1)S(1)} %get-tuple-element.35), channel_id=1, source_target_pairs={{0,31},{1,0},{2,1},{3,2},{4,3},{5,4},{6,5},{7,6},{8,7},{9,8},{10,9... | collective-permute-start | bytes 768008 | tf_op jit(solution)/shard_map/ppermute | solution.py:508
  33.4 14.9 %collective-permute-start.6 = (bf16[1,500,128]{2,1,0:T(8,128)(2,1)S(1)}, bf16[1,500,128]{2,1,0:T(8,128)(2,1)S(1)}, u32[]{:S(2)}, u32[]{:S(2)}) collective-permute-start(bf16[1,500,128]{2,1,0:T(8,128)(2,1)S(1)} %get-tuple-element.38), channel_id=1, source_target_pairs={{0,1},{1,2},{2,3},{3,4},{4,5},{5,6},{6,7},{7,8},{8,9},{9,10},{10,1... | collective-permute-start | bytes 384008 | tf_op jit(solution)/shard_map/ppermute | solution.py:508
  35.4 15.6 %collective-permute-start.2 = (bf16[1,500,128]{2,1,0:T(8,128)(2,1)S(1)}, bf16[1,500,128]{2,1,0:T(8,128)(2,1)S(1)}, u32[]{:S(2)}, u32[]{:S(2)}) collective-permute-start(bf16[1,500,128]{2,1,0:T(8,128)(2,1)S(1)} %get-tuple-element.34), channel_id=1, source_target_pairs={{0,1},{1,2},{2,3},{3,4},{4,5},{5,6},{6,7},{7,8},{8,9},{9,10},{10,1... | collective-permute-start | bytes 384008 | tf_op jit(solution)/shard_map/ppermute | solution.py:508

commit v10 on v9

--- a/solution.py
+++ b/solution.py
@@ -132,18 +132,20 @@
     return wanted
 
 
-def window_kernel(part_hbm, orb_hbm, ahead_ref, back_ref, part_ref, orb_ref, flat_ref, sems):
-    boxes = orb_ref.shape[0]
+def window_kernel(part_hbm, orb_hbm, ahead_ref, back_ref, orb_ref, part_ref, flat_ref, sems):
+    boxes = orb_ref.shape[1]
     small = pltpu.make_async_copy(part_hbm, part_ref, sems.at[0])
-    large = pltpu.make_async_copy(orb_hbm.at[0], orb_ref, sems.at[1])
+    large = [pltpu.make_async_copy(orb_hbm.at[spin], orb_ref.at[spin], sems.at[1 + spin]) for spin in range(2)]
     small.start()
-    large.start()
+    for copy in large:
+        copy.start()
     small.wait()
     wanted = wanted_boxes(part_ref, boxes)
-    large.wait()
-    split_boxes(orb_ref, flat_ref, boxes)
+    large[0].wait()
+    split_boxes(orb_ref.at[0], flat_ref, boxes)
     for side, ref in enumerate((ahead_ref, back_ref)):
         ref[...] = flat_ref[pl.ds(wanted[side], FLAT, stride=8), :].astype(BF)
+    large[1].wait()
 
 
 def table_layout(boxes):
@@ -222,34 +224,35 @@
                   lambda u, x: pad_ref.__setitem__((1, box, u, body, slice(None)), x), 0, TILES)
 
 
-def second_kernel(dest_hbm, part_hbm, anc_hbm, orb_hbm, inv_hbm, diag_hbm, rest_hbm,
-                  orb_ref, ahead_ref, back_ref, tab_ref, inv_ref, diag_ref, rest_ref,
+def second_kernel(dest_hbm, part_hbm, anc_hbm, inv_hbm, diag_hbm, rest_hbm, orb_ref,
+                  ahead_ref, back_ref, tab_ref, inv_ref, diag_ref, rest_ref,
                   dest_ref, part_ref, anc_ref, flat_ref, sems):
     boxes = orb_ref.shape[1]
     pieces = [(part_hbm, part_ref), (dest_hbm, dest_ref), (anc_hbm, anc_ref)]
-    pieces += [(orb_hbm.at[spin], orb_ref.at[spin]) for spin in (1, 0)]
     pieces += [(inv_hbm, inv_ref), (diag_hbm, diag_ref), (rest_hbm, rest_ref)]
     copies = [pltpu.make_async_copy(source, target, sems.at[k]) for k, (source, target) in enumerate(pieces)]
     for copy in copies:
         copy.start()
+    split_boxes(orb_ref.at[1], flat_ref, boxes)
     for copy in copies[:3]:
         copy.wait()
-    build_tables(dest_ref, part_ref, anc_ref, tab_ref, boxes)
     wanted = wanted_boxes(part_ref, boxes)
-    copies[3].wait()
-    split_boxes(orb_ref.at[1], flat_ref, boxes)
     for side, ref in enumerate((ahead_ref, back_ref)):
         ref[...] = flat_ref[pl.ds(wanted[side], FLAT, stride=8), :].astype(BF)
-    for copy in copies[4:]:
+    build_tables(dest_ref, part_ref, anc_ref, tab_ref, boxes)
+    for copy in copies[3:]:
         copy.wait()
+
+
+def low_half():
+    return 2 * lax.axis_index(AXES[-1]) < lax.axis_size(AXES[-1])
 
 
 def slabs_kernel(spin, near, orb_ref, *refs):
     pad_ref, flat_ref = refs[-2:]
     boxes = orb_ref.shape[1]
-    low_half = 2 * lax.axis_index(AXES[-1]) < lax.axis_size(AXES[-1])
-
-    @pl.when(low_half if near else jnp.logical_not(low_half))
+
+    @pl.when(low_half() if near else jnp.logical_not(low_half()))
     def _():
         split_boxes(orb_ref.at[spin], flat_ref, boxes)
 
@@ -267,9 +270,8 @@
 
 def modes_kernel(early, fac_hbm, *refs):
     to_ref, from_ref, fac_ref, sem = refs[-4:]
-    first = lax.axis_index(AXES[-1]) == 0
-
-    @pl.when(first if early else jnp.logical_not(first))
+
+    @pl.when(low_half() if early else jnp.logical_not(low_half()))
     def _():
         copy = pltpu.make_async_copy(fac_hbm, fac_ref, sem)
         copy.start()
@@ -531,13 +533,12 @@
 
     box = jax.ShapeDtypeStruct((FLAT, LANES), BF)
     splitter = pltpu.VMEM((FLAT * 8, LANES), F32)
-    ahead, back = pl.pallas_call(
+    ahead, back, held = pl.pallas_call(
         window_kernel,
-        out_shape=[box] * 2,
+        out_shape=[box] * 2 + [jax.ShapeDtypeStruct(orbitals.shape, BF)],
         in_specs=[ANYWHERE] * 2,
-        out_specs=whole(2),
-        scratch_shapes=[pltpu.SMEM(partners_t.shape, jnp.int32), pltpu.VMEM(orbitals.shape[1:], BF),
-                        splitter, pltpu.SemaphoreType.DMA((2,))],
+        out_specs=whole(3),
+        scratch_shapes=[pltpu.SMEM(partners_t.shape, jnp.int32), splitter, pltpu.SemaphoreType.DMA((3,))],
         compiler_params=pltpu.CompilerParams(vmem_limit_bytes=12 << 20),
         name="window",
     )(*map(in_place, (partners_t, orbitals)))
@@ -566,19 +567,18 @@
     handed = (inverse, *diags)
     second = pl.pallas_call(
         second_kernel,
-        out_shape=[jax.ShapeDtypeStruct(orbitals.shape, BF), box, box,
-                   jax.ShapeDtypeStruct((table_layout(boxes)[-1],), jnp.int32)]
+        out_shape=[box, box, jax.ShapeDtypeStruct((table_layout(boxes)[-1],), jnp.int32)]
         + [jax.ShapeDtypeStruct(value.shape, value.dtype) for value in handed],
-        in_specs=[ANYWHERE] * 7,
-        out_specs=whole(3) + [SCALARS] + whole(3),
+        in_specs=[ANYWHERE] * 6 + whole(1),
+        out_specs=whole(2) + [SCALARS] + whole(3),
         scratch_shapes=[pltpu.SMEM(dest.shape, jnp.int32), pltpu.SMEM(partners_t.shape, jnp.int32),
-                        pltpu.SMEM(anchors_t.shape, jnp.int32), splitter, pltpu.SemaphoreType.DMA((8,))],
+                        pltpu.SMEM(anchors_t.shape, jnp.int32), splitter, pltpu.SemaphoreType.DMA((6,))],
         compiler_params=pltpu.CompilerParams(vmem_limit_bytes=12 << 20),
         cost_estimate=cost(1_000_000, 2_000_000),
         name="second",
     )
-    held, ahead, back, table, inverse, *diags = second(
-        *map(in_place, (dest, partners_t, anchors_t, orbitals, *handed)))
+    ahead, back, table, inverse, *diags = second(
+        *map(in_place, (dest, partners_t, anchors_t, *handed)), held)
     prev_high = from_behind(ahead, 1)
     next_high = from_behind(back, -1)
     to_modes, from_modes = build_modes(False, *modes)

time: 54.8 us -> 48.9 us (0.89)
  waiting for transfers between devices: 9.94 us -> 4.43 us
    ppermute x8, waiting for transfers between devices: 9.94 us -> 4.43 us  [from_behind(): lax.ppermute(value, AXES, [(source, (source + steps) % count) for source...]
  transfers between devices with their start and end apart: 8 -> 8, of which waited for: 3 -> 2; matrix products, arithmetic and copies ran while one was open for 0% -> 0% of each run, Pallas kernels for 34% -> 48%
where the time goes in v10:
time: 48.9 us; the launch traced here: 48.7 us
  Pallas kernels  28.1 us (57%)
  starting transfers between devices  16 us (33%)
  waiting for transfers between devices  4.43 us (9%)
    pallas_call x3, Pallas kernels, solve(): pl.pallas_call(lambda *refs: pair_kernel(start, held, spins, final, *refs...  18.6 us
    ppermute x8, starting transfers between devices, from_behind(): lax.ppermute(value, AXES, [(source, (source + steps) % count) for source...  16 us
    ppermute x8, waiting for transfers between devices, from_behind(): lax.ppermute(value, AXES, [(source, (source + steps) % count) for source...  4.43 us
    pallas_call x4, Pallas kernels, build_slabs(): pl.pallas_call(lambda *refs: slabs_kernel(spin, near, *refs), out_shape=s...  2.47 us
    pallas_call x2, Pallas kernels, build_modes(): pl.pallas_call(lambda *refs: modes_kernel(early, *refs), out_shape=[folde...  2 us
    pallas_call x1, Pallas kernels, shards(): second(*map(in_place, (dest, partners_t, anchors_t, *handed)), held)  1.74 us
    pallas_call x1, Pallas kernels, shards(): pl.pallas_call(window_kernel, out_shape=[box] * 2 + [jax.ShapeDtypeStruct...  1.41 us
    pallas_call x1, Pallas kernels, shards(): pl.pallas_call(lambda *refs: place_kernel(boxes, *refs), out_shape=shape,...  1.4 us
  transfers between devices with their start and end apart: 8, of which 2 were waited for; matrix products, arithmetic and copies ran while one was open for 0% of the time, Pallas kernels for 48%

profile of v10, /device:TPU:0, one launch (start us, length us, event | category | flops | bytes accessed | tf_op | source)
XLA Modules:
  0.0 48.7 jit_solution(13109667050324556485)
XLA Ops:
  0.0 1.4 %window.1 = (bf16[500,128]{1,0:T(8,128)(2,1)S(1)}, bf16[500,128]{1,0:T(8,128)(2,1)S(1)}, bf16[2,4,64000]{2,1,0:T(4,128)(2,1)S(1)}) custom-call(s32[2,128]{1,0:T(2,128)} %bitcast.9, bf16[2,4,64000]{2,1,0:T(4,128)(2,1)} %orb_hbm.1), custom_call_target="tpu_custom_call" | custom-call | tf_op jit(solution)/shard_map/window/pallas_call | solution.py:536
  1.4 1.7 %second.1 = (bf16[500,128]{1,0:T(8,128)(2,1)S(1)}, bf16[500,128]{1,0:T(8,128)(2,1)S(1)}, s32[57]{0:T(128)S(1)}, f32[40,1792]{1,0:T(8,128)S(1)}, bf16[240,240]{1,...) custom-call(s32[128]{0:T(128)} %dest_hbm.1, s32[2,128]{1,0:T(2,128)} %bitcast.10, s32[3,128]{1,0:T(4,128)} %bitcast.11, ...), custom_call_target="tpu_custom_call" | custom-call | flops 1000000 | bytes 2000000 | tf_op jit(solution)/shard_map/second/pallas_call | solution.py:580
  3.2 3.1 %collective-permute-start.4 = (bf16[500,128]{1,0:T(8,128)(2,1)S(1)}, bf16[500,128]{1,0:T(8,128)(2,1)S(1)}, u32[]{:S(2)}, u32[]{:S(2)}) collective-permute-start(bf16[500,128]{1,0:T(8,128)(2,1)S(1)} %get-tuple-element.36), channel_id=1, source_target_pairs={{0,1},{1,2},{2,3},{3,4},{4,5},{5,6},{6,7},{7,8},{8,9},{9,10},{10,1... | collective-permute-start | bytes 384008 | tf_op jit(solution)/shard_map/ppermute | solution.py:510
  6.3 3.4 %collective-permute-start.5 = (bf16[500,128]{1,0:T(8,128)(2,1)S(1)}, bf16[500,128]{1,0:T(8,128)(2,1)S(1)}, u32[]{:S(2)}, u32[]{:S(2)}) collective-permute-start(bf16[500,128]{1,0:T(8,128)(2,1)S(1)} %get-tuple-element.37), channel_id=1, source_target_pairs={{0,31},{1,0},{2,1},{3,2},{4,3},{5,4},{6,5},{7,6},{8,7},{9,8},{10,9... | collective-permute-start | bytes 384008 | tf_op jit(solution)/shard_map/ppermute | solution.py:510
  9.7 0.0 collective-permute-start
  9.7 5.3 %collective-permute-start.1 = (bf16[500,128]{1,0:T(8,128)(2,1)S(1)}, bf16[500,128]{1,0:T(8,128)(2,1)S(1)}, u32[]{:S(2)}, u32[]{:S(2)}) collective-permute-start(bf16[500,128]{1,0:T(8,128)(2,1)S(1)} %get-tuple-element.33), channel_id=1, source_target_pairs={{0,31},{1,0},{2,1},{3,2},{4,3},{5,4},{6,5},{7,6},{8,7},{9,8},{10,9... | collective-permute-start | bytes 384008 | tf_op jit(solution)/shard_map/ppermute | solution.py:510
  15.0 1.2 %shard_map.88.refs_1_ = f32[2,6,13,88,128]{4,3,2,1,0:T(8,128)S(1)} custom-call(bf16[2,4,64000]{2,1,0:T(4,128)(2,1)S(1)} %get-tuple-element.24.orb_ref.refs_0_), custom_call_target="tpu_custom_call" | custom-call | flops 2000000 | bytes 4000000 | tf_op jit(solution)/shard_map/pallas_call | solution.py:587
  16.3 1.2 %shard_map.85.old_ref = f32[2,6,13,88,128]{4,3,2,1,0:T(8,128)S(1)} custom-call(bf16[2,4,64000]{2,1,0:T(4,128)(2,1)S(1)} %get-tuple-element.24.orb_ref.refs_0_, f32[2,6,13,88,128]{4,3,2,1,0:T(8,128)S(1)} %shard_map.84.refs_1_), custom_call_target="tpu_custom_call", output_to_operand_aliasing={{}: (1, {})} | custom-call | flops 2000000 | bytes 4000000 | tf_op jit(solution)/shard_map/pallas_call | solution.py:587
  17.5 2.0 %shard_map.82 = (bf16[2,896,896]{2,1,0:T(8,128)(2,1)S(1)}, bf16[2,896,896]{2,1,0:T(8,128)(2,1)S(1)}) custom-call(f32[6,40,896]{2,1,0:T(8,128)} %constant.8.clone.refs_0_), custom_call_target="tpu_custom_call" | custom-call | flops 4000000 | bytes 4000000 | tf_op jit(solution)/shard_map/pallas_call | solution.py:551
  19.6 0.0 collective-permute-done.4.prev_ref
  19.6 0.0 collective-permute-done.5.next_ref
  19.6 0.3 shard_map.90.refs_5_.refs_6_
  19.8 6.4 %shard_map.91 = (f32[3,500,128]{2,1,0:T(8,128)S(1)}, bf16[1,500,128]{2,1,0:T(8,128)(2,1)S(1)}, bf16[2,500,128]{2,1,0:T(8,128)(2,1)S(1)}) custom-call(s32[57]{0:T(128)S(1)} %get-tuple-element.25.refs_0_, bf16[2,896,896]{2,1,0:T(8,128)(2,1)S(1)} %get-tuple-element.28.refs_1_, bf16[2,896,896]{2,1,0:T(8,128)(2,1)S(1)} %get-tuple-element.29.refs_2_, ...), custom_call_target="tpu_custom_call" | custom-call | flops 1228800000 | bytes 10000000 | tf_op jit(solution)/shard_map/pallas_call | solution.py:624
  26.2 0.1 collective-permute-start.7
  26.3 0.0 collective-permute-done.prev_ref
  26.3 0.0 collective-permute-done.1.next_ref
  26.3 0.3 shard_map.86.refs_5_
  26.6 6.4 %shard_map.87 = (f32[3,500,128]{2,1,0:T(8,128)S(1)}, bf16[1,500,128]{2,1,0:T(8,128)(2,1)S(1)}, bf16[2,500,128]{2,1,0:T(8,128)(2,1)S(1)}) custom-call(s32[57]{0:T(128)S(1)} %get-tuple-element.25.refs_0_, bf16[2,896,896]{2,1,0:T(8,128)(2,1)S(1)} %get-tuple-element.28.refs_1_, bf16[2,896,896]{2,1,0:T(8,128)(2,1)S(1)} %get-tuple-element.29.refs_2_, ...), custom_call_target="tpu_custom_call" | custom-call | flops 1228800000 | bytes 10000000 | tf_op jit(solution)/shard_map/pallas_call | solution.py:624
  32.9 0.1 collective-permute-start.3
  33.0 2.0 %collective-permute-start.6 = (bf16[1,500,128]{2,1,0:T(8,128)(2,1)S(1)}, bf16[1,500,128]{2,1,0:T(8,128)(2,1)S(1)}, u32[]{:S(2)}, u32[]{:S(2)}) collective-permute-start(bf16[1,500,128]{2,1,0:T(8,128)(2,1)S(1)} %get-tuple-element.38), channel_id=1, source_target_pairs={{0,1},{1,2},{2,3},{3,4},{4,5},{5,6},{6,7},{7,8},{8,9},{9,10},{10,1... | collective-permute-start | bytes 384008 | tf_op jit(solution)/shard_map/ppermute | solution.py:510
  35.1 2.0 %collective-permute-start.2 = (bf16[1,500,128]{2,1,0:T(8,128)(2,1)S(1)}, bf16[1,500,128]{2,1,0:T(8,128)(2,1)S(1)}, u32[]{:S(2)}, u32[]{:S(2)}) collective-permute-start(bf16[1,500,128]{2,1,0:T(8,128)(2,1)S(1)} %get-tuple-element.34), channel_id=1, source_target_pairs={{0,1},{1,2},{2,3},{3,4},{4,5},{5,6},{6,7},{7,8},{8,9},{9,10},{10,1... | collective-permute-start | bytes 384008 | tf_op jit(solution)/shard_map/ppermute | solution.py:510
  37.0 5.9 %shard_map.92.refs_5_ = f32[7,1000,128]{2,1,0:T(8,128)} custom-call(s32[57]{0:T(128)S(1)} %get-tuple-element.25.refs_0_, bf16[2,896,896]{2,1,0:T(8,128)(2,1)S(1)} %get-tuple-element.28.refs_1_, bf16[2,896,896]{2,1,0:T(8,128)(2,1)S(1)} %get-tuple-element.29.refs_2_, bf16[160,160]{1,0:T(8,128)(2,1)S(1)} %get-tuple-element.40.refs_3_, ...), custom_call_target="tpu_custom_call" | custom-call | flops 819200000 | bytes 10000000 | tf_op jit(solution)/shard_map/pallas_call | solution.py:624
  42.9 0.0 collective-permute-done.6.refs_3_
  42.9 2.3 %collective-permute-done.2.refs_1_ = bf16[1,500,128]{2,1,0:T(8,128)(2,1)S(1)} collective-permute-done((bf16[1,500,128]{2,1,0:T(8,128)(2,1)S(1)}, bf16[1,500,128]{2,1,0:T(8,128)(2,1)S(1)}, u32[]{:S(2)}, u32[]{:S(2)}) %collective-permute-start.2) | collective-permute-done | bytes 128032 | tf_op jit(solution)/shard_map/ppermute | solution.py:510
  45.2 0.0 collective-permute-done.7.refs_4_
  45.2 2.1 %collective-permute-done.3.refs_2_ = bf16[2,500,128]{2,1,0:T(8,128)(2,1)S(1)} collective-permute-done((bf16[2,500,128]{2,1,0:T(8,128)(2,1)S(1)}, bf16[2,500,128]{2,1,0:T(8,128)(2,1)S(1)}, u32[]{:S(2)}, u32[]{:S(2)}) %collective-permute-start.3) | collective-permute-done | bytes 256032 | tf_op jit(solution)/shard_map/ppermute | solution.py:510
  47.3 1.4 %place.1 = f32[7,1000,128]{2,1,0:T(8,128)} custom-call(s32[57]{0:T(128)S(1)} %get-tuple-element.25.refs_0_, bf16[1,500,128]{2,1,0:T(8,128)(2,1)S(1)} %collective-permute-done.2.refs_1_, bf16[2,500,128]{2,1,0:T(8,128)(2,1)S(1)} %collective-permute-done.3.refs_2_, ...), custom_call_target="tpu_custom_call", output_to_operand_aliasing={{}: (5, {})} | custom-call | flops 1000000 | bytes 4000000 | tf_op jit(solution)/shard_map/place/pallas_call | solution.py:648
  (3 shorter events, 0.1 us)
Async XLA Ops:
  3.2 16.4 %collective-permute-start.4 = (bf16[500,128]{1,0:T(8,128)(2,1)S(1)}, bf16[500,128]{1,0:T(8,128)(2,1)S(1)}, u32[]{:S(2)}, u32[]{:S(2)}) collective-permute-start(bf16[500,128]{1,0:T(8,128)(2,1)S(1)} %get-tuple-element.36), channel_id=1, source_target_pairs={{0,1},{1,2},{2,3},{3,4},{4,5},{5,6},{6,7},{7,8},{8,9},{9,10},{10,1... | collective-permute-start | bytes 384008 | tf_op jit(solution)/shard_map/ppermute | solution.py:510
  6.3 13.3 %collective-permute-start.5 = (bf16[500,128]{1,0:T(8,128)(2,1)S(1)}, bf16[500,128]{1,0:T(8,128)(2,1)S(1)}, u32[]{:S(2)}, u32[]{:S(2)}) collective-permute-start(bf16[500,128]{1,0:T(8,128)(2,1)S(1)} %get-tuple-element.37), channel_id=1, source_target_pairs={{0,31},{1,0},{2,1},{3,2},{4,3},{5,4},{6,5},{7,6},{8,7},{9,8},{10,9... | collective-permute-start | bytes 384008 | tf_op jit(solution)/shard_map/ppermute | solution.py:510
  9.7 16.6 %collective-permute-start = (bf16[500,128]{1,0:T(8,128)(2,1)S(1)}, bf16[500,128]{1,0:T(8,128)(2,1)S(1)}, u32[]{:S(2)}, u32[]{:S(2)}) collective-permute-start(bf16[500,128]{1,0:T(8,128)(2,1)S(1)} %get-tuple-element.32), channel_id=1, source_target_pairs={{0,1},{1,2},{2,3},{3,4},{4,5},{5,6},{6,7},{7,8},{8,9},{9,10},{10,1... | collective-permute-start | bytes 384008 | tf_op jit(solution)/shard_map/ppermute | solution.py:510
  9.7 16.6 %collective-permute-start.1 = (bf16[500,128]{1,0:T(8,128)(2,1)S(1)}, bf16[500,128]{1,0:T(8,128)(2,1)S(1)}, u32[]{:S(2)}, u32[]{:S(2)}) collective-permute-start(bf16[500,128]{1,0:T(8,128)(2,1)S(1)} %get-tuple-element.33), channel_id=1, source_target_pairs={{0,31},{1,0},{2,1},{3,2},{4,3},{5,4},{6,5},{7,6},{8,7},{9,8},{10,9... | collective-permute-start | bytes 384008 | tf_op jit(solution)/shard_map/ppermute | solution.py:510
  26.2 19.0 %collective-permute-start.7 = (bf16[2,500,128]{2,1,0:T(8,128)(2,1)S(1)}, bf16[2,500,128]{2,1,0:T(8,128)(2,1)S(1)}, u32[]{:S(2)}, u32[]{:S(2)}) collective-permute-start(bf16[2,500,128]{2,1,0:T(8,128)(2,1)S(1)} %get-tuple-element.39), channel_id=1, source_target_pairs={{0,31},{1,0},{2,1},{3,2},{4,3},{5,4},{6,5},{7,6},{8,7},{9,8},{10,9... | collective-permute-start | bytes 768008 | tf_op jit(solution)/shard_map/ppermute | solution.py:510
  32.9 14.4 %collective-permute-start.3 = (bf16[2,500,128]{2,1,0:T(8,128)(2,1)S(1)}, bf16[2,500,128]{2,1,0:T(8,128)(2,1)S(1)}, u32[]{:S(2)}, u32[]{:S(2)}) collective-permute-start(bf16[2,500,128]{2,1,0:T(8,128)(2,1)S(1)} %get-tuple-element.35), channel_id=1, source_target_pairs={{0,31},{1,0},{2,1},{3,2},{4,3},{5,4},{6,5},{7,6},{8,7},{9,8},{10,9... | collective-permute-start | bytes 768008 | tf_op jit(solution)/shard_map/ppermute | solution.py:510
  33.0 9.9 %collective-permute-start.6 = (bf16[1,500,128]{2,1,0:T(8,128)(2,1)S(1)}, bf16[1,500,128]{2,1,0:T(8,128)(2,1)S(1)}, u32[]{:S(2)}, u32[]{:S(2)}) collective-permute-start(bf16[1,500,128]{2,1,0:T(8,128)(2,1)S(1)} %get-tuple-element.38), channel_id=1, source_target_pairs={{0,1},{1,2},{2,3},{3,4},{4,5},{5,6},{6,7},{7,8},{8,9},{9,10},{10,1... | collective-permute-start | bytes 384008 | tf_op jit(solution)/shard_map/ppermute | solution.py:510
  35.1 10.1 %collective-permute-start.2 = (bf16[1,500,128]{2,1,0:T(8,128)(2,1)S(1)}, bf16[1,500,128]{2,1,0:T(8,128)(2,1)S(1)}, u32[]{:S(2)}, u32[]{:S(2)}) collective-permute-start(bf16[1,500,128]{2,1,0:T(8,128)(2,1)S(1)} %get-tuple-element.34), channel_id=1, source_target_pairs={{0,1},{1,2},{2,3},{3,4},{4,5},{5,6},{6,7},{7,8},{8,9},{9,10},{10,1... | collective-permute-start | bytes 384008 | tf_op jit(solution)/shard_map/ppermute | solution.py:510

commit v11 on v10

--- a/solution.py
+++ b/solution.py
@@ -244,15 +244,25 @@
         copy.wait()
 
 
+def place_along():
+    return lax.axis_index(AXES[-1]), lax.axis_size(AXES[-1])
+
+
 def low_half():
-    return 2 * lax.axis_index(AXES[-1]) < lax.axis_size(AXES[-1])
-
-
-def slabs_kernel(spin, near, orb_ref, *refs):
+    place, count = place_along()
+    return 2 * place < count
+
+
+def at_end():
+    place, count = place_along()
+    return place == count - 1
+
+
+def slabs_kernel(spin, chosen, orb_ref, *refs):
     pad_ref, flat_ref = refs[-2:]
     boxes = orb_ref.shape[1]
 
-    @pl.when(low_half() if near else jnp.logical_not(low_half()))
+    @pl.when(chosen())
     def _():
         split_boxes(orb_ref.at[spin], flat_ref, boxes)
 
@@ -271,7 +281,7 @@
 def modes_kernel(early, fac_hbm, *refs):
     to_ref, from_ref, fac_ref, sem = refs[-4:]
 
-    @pl.when(low_half() if early else jnp.logical_not(low_half()))
+    @pl.when(jnp.logical_not(at_end()) if early else at_end())
     def _():
         copy = pltpu.make_async_copy(fac_hbm, fac_ref, sem)
         copy.start()
@@ -343,7 +353,7 @@
     lanes = lane_iota()
     rows = lax.broadcasted_iota(jnp.int32, (EDGE, 1), 0)
 
-    def dense(index, _):
+    def dense(index):
         box = tab_ref[order + start + index]
         places = []
         for number in range(PARTNERS):
@@ -379,14 +389,15 @@
                         values.append(pad_ref[part, box, u - 1, pl.ds(PAD, EDGE), :] * moved)
                     last[at][which] = turned
                 if u > 0:
-                    where = pl.ds(pl.multiple_of((index * len(spins) + at) * PARTNERS * EDGE, 16), PARTNERS * EDGE)
+                    where = pl.ds((index * len(spins) + at) * PARTNERS * EDGE, PARTNERS * EDGE)
                     front = jnp.concatenate(values[0::2], axis=0)
                     behind = jnp.concatenate(values[1::2], axis=0)
                     x_ref[where, (u - 1) * LANES:u * LANES] = (front + behind).astype(BF)
                     x_ref[where, FWIDE + (u - 1) * LANES:FWIDE + u * LANES] = (front - behind).astype(BF)
         return 0
 
-    lax.fori_loop(0, held, dense, 0)
+    for index in range(held):
+        dense(index)
 
     cubes = held * len(spins) * PARTNERS
     diag = diag_ref[...]
@@ -409,15 +420,7 @@
         y_ref[:, pl.ds(pl.multiple_of(FWIDE + first, LANES), size)] = (even - odd).astype(BF)
 
     for step in (forward, backward):
-        whole_steps = FWIDE // NCHUNK
-
-        def looped(n, _):
-            step(pl.multiple_of(n * NCHUNK, NCHUNK), NCHUNK)
-            return 0
-
-        lax.fori_loop(0, whole_steps, looped, 0)
-        if FWIDE % NCHUNK:
-            step(whole_steps * NCHUNK, FWIDE % NCHUNK)
+        step(0, FWIDE)
 
     for first in range(0, 2 * FTILES, 2):
         potential = jnp.dot(diag, y_ref[:, first * LANES:(first + 2) * LANES], preferred_element_type=F32)
@@ -434,7 +437,7 @@
                     else:
                         half_ref[index * len(spins) + at, u - FTILES] = total
 
-    def unfold(row, _):
+    def unfold(row):
         middle = FTILES - 1
 
         def store(u, x):
@@ -445,7 +448,8 @@
         reverse_slabs(lambda v: half_ref[row, v], store, middle, FTILES)
         return 0
 
-    lax.fori_loop(0, held * len(spins), unfold, 0)
+    for row in range(held * len(spins)):
+        unfold(row)
 
     if final:
         for index in range(held):
@@ -470,14 +474,15 @@
         lax.fori_loop(0, CAP, finish, 0)
         return
 
-    def flatten(row, _):
+    def flatten(row):
         slabs_to_flat(
             lambda u, parity: res_ref[row, u, pl.ds(parity, HALF, stride=2), :],
             lambda t, x: out_ref.__setitem__((row, pl.ds(t, HALF, stride=PAIRT), slice(None)), x),
         )
         return 0
 
-    lax.fori_loop(0, held * len(spins), flatten, 0)
+    for row in range(held * len(spins)):
+        flatten(row)
     for k in range(AHEAD):
         sends[0][k] = out_ref[tab_ref[leaves + k]].astype(BF)
     for k in range(BACK):
@@ -583,9 +588,18 @@
     next_high = from_behind(back, -1)
     to_modes, from_modes = build_modes(False, *modes)
 
-    def build_slabs(spin, near, *before):
+    def inner():
+        return jnp.logical_not(low_half() | at_end())
+
+    def build_slabs(spin, *before):
+        here = (inner, low_half)[spin]
+        late = len(before) > 0
+
+        def chosen():
+            return jnp.logical_not(here()) if late else here()
+
         return pl.pallas_call(
-            lambda *refs: slabs_kernel(spin, near, *refs),
+            lambda *refs: slabs_kernel(spin, chosen, *refs),
             out_shape=slabs,
             in_specs=whole(1 + len(before)),
             out_specs=pl.BlockSpec(memory_space=pltpu.VMEM),
@@ -595,7 +609,7 @@
             cost_estimate=cost(2_000_000, 4_000_000),
         )(held, *before)
 
-    pads = [build_slabs(0, True, build_slabs(0, False)), build_slabs(1, False, build_slabs(1, True))]
+    pads = [build_slabs(0, build_slabs(0)), build_slabs(1, build_slabs(1))]
     for spin, halo in enumerate(((prev_low, next_low), (prev_high, next_high))):
         pads[spin] = pl.pallas_call(
             fill_kernel,

time: 48.9 us -> 45.9 us (0.939)
  Pallas kernels: 28.1 us -> 22.7 us
  waiting for transfers between devices: 4.43 us -> 6.72 us
    pallas_call x3, Pallas kernels: 18.6 us -> 13.1 us  [solve(): pl.pallas_call(lambda *refs: pair_kernel(start, held, spins, final, *refs...]
    ppermute x8, waiting for transfers between devices: 4.43 us -> 6.72 us  [from_behind(): lax.ppermute(value, AXES, [(source, (source + steps) % count) for source...]
  transfers between devices with their start and end apart: 8 -> 8, of which waited for: 2 -> 3; matrix products, arithmetic and copies ran while one was open for 0% -> 0% of each run, Pallas kernels for 48% -> 40%
where the time goes in v11:
time: 45.9 us; the launch traced here: 45.7 us
  Pallas kernels  22.7 us (49%)
  starting transfers between devices  16 us (35%)
  waiting for transfers between devices  6.72 us (15%)
    ppermute x8, starting transfers between devices, from_behind(): lax.ppermute(value, AXES, [(source, (source + steps) % count) for source...  16 us
    pallas_call x3, Pallas kernels, solve(): pl.pallas_call(lambda *refs: pair_kernel(start, held, spins, final, *refs...  13.1 us
    ppermute x8, waiting for transfers between devices, from_behind(): lax.ppermute(value, AXES, [(source, (source + steps) % count) for source...  6.72 us
    pallas_call x4, Pallas kernels, build_slabs(): pl.pallas_call(lambda *refs: slabs_kernel(spin, chosen, *refs), out_shape...  2.48 us
    pallas_call x2, Pallas kernels, build_modes(): pl.pallas_call(lambda *refs: modes_kernel(early, *refs), out_shape=[folde...  2 us
    pallas_call x1, Pallas kernels, shards(): second(*map(in_place, (dest, partners_t, anchors_t, *handed)), held)  1.74 us
    pallas_call x1, Pallas kernels, shards(): pl.pallas_call(window_kernel, out_shape=[box] * 2 + [jax.ShapeDtypeStruct...  1.41 us
    pallas_call x1, Pallas kernels, shards(): pl.pallas_call(lambda *refs: place_kernel(boxes, *refs), out_shape=shape,...  1.4 us
  transfers between devices with their start and end apart: 8, of which 3 were waited for; matrix products, arithmetic and copies ran while one was open for 0% of the time, Pallas kernels for 40%

profile of v11, /device:TPU:0, one launch (start us, length us, event | category | flops | bytes accessed | tf_op | source)
XLA Modules:
  0.0 45.7 jit_solution(15741618625465991356)
XLA Ops:
  0.0 1.4 %window.1 = (bf16[500,128]{1,0:T(8,128)(2,1)S(1)}, bf16[500,128]{1,0:T(8,128)(2,1)S(1)}, bf16[2,4,64000]{2,1,0:T(4,128)(2,1)S(1)}) custom-call(s32[2,128]{1,0:T(2,128)} %bitcast.9, bf16[2,4,64000]{2,1,0:T(4,128)(2,1)} %orb_hbm.1), custom_call_target="tpu_custom_call" | custom-call | tf_op jit(solution)/shard_map/window/pallas_call | solution.py:541
  1.4 1.7 %second.1 = (bf16[500,128]{1,0:T(8,128)(2,1)S(1)}, bf16[500,128]{1,0:T(8,128)(2,1)S(1)}, s32[57]{0:T(128)S(1)}, f32[40,1792]{1,0:T(8,128)S(1)}, bf16[240,240]{1,...) custom-call(s32[128]{0:T(128)} %dest_hbm.1, s32[2,128]{1,0:T(2,128)} %bitcast.10, s32[3,128]{1,0:T(4,128)} %bitcast.11, ...), custom_call_target="tpu_custom_call" | custom-call | flops 1000000 | bytes 2000000 | tf_op jit(solution)/shard_map/second/pallas_call | solution.py:585
  3.2 3.1 %collective-permute-start.4 = (bf16[500,128]{1,0:T(8,128)(2,1)S(1)}, bf16[500,128]{1,0:T(8,128)(2,1)S(1)}, u32[]{:S(2)}, u32[]{:S(2)}) collective-permute-start(bf16[500,128]{1,0:T(8,128)(2,1)S(1)} %get-tuple-element.36), channel_id=1, source_target_pairs={{0,1},{1,2},{2,3},{3,4},{4,5},{5,6},{6,7},{7,8},{8,9},{9,10},{10,1... | collective-permute-start | bytes 384008 | tf_op jit(solution)/shard_map/ppermute | solution.py:515
  6.3 3.4 %collective-permute-start.5 = (bf16[500,128]{1,0:T(8,128)(2,1)S(1)}, bf16[500,128]{1,0:T(8,128)(2,1)S(1)}, u32[]{:S(2)}, u32[]{:S(2)}) collective-permute-start(bf16[500,128]{1,0:T(8,128)(2,1)S(1)} %get-tuple-element.37), channel_id=1, source_target_pairs={{0,31},{1,0},{2,1},{3,2},{4,3},{5,4},{6,5},{7,6},{8,7},{9,8},{10,9... | collective-permute-start | bytes 384008 | tf_op jit(solution)/shard_map/ppermute | solution.py:515
  9.7 0.0 collective-permute-start
  9.7 5.3 %collective-permute-start.1 = (bf16[500,128]{1,0:T(8,128)(2,1)S(1)}, bf16[500,128]{1,0:T(8,128)(2,1)S(1)}, u32[]{:S(2)}, u32[]{:S(2)}) collective-permute-start(bf16[500,128]{1,0:T(8,128)(2,1)S(1)} %get-tuple-element.33), channel_id=1, source_target_pairs={{0,31},{1,0},{2,1},{3,2},{4,3},{5,4},{6,5},{7,6},{8,7},{9,8},{10,9... | collective-permute-start | bytes 384008 | tf_op jit(solution)/shard_map/ppermute | solution.py:515
  15.0 1.2 %shard_map.88.refs_1_ = f32[2,6,13,88,128]{4,3,2,1,0:T(8,128)S(1)} custom-call(bf16[2,4,64000]{2,1,0:T(4,128)(2,1)S(1)} %get-tuple-element.24.orb_ref.refs_0_), custom_call_target="tpu_custom_call" | custom-call | flops 2000000 | bytes 4000000 | tf_op jit(solution)/shard_map/pallas_call | solution.py:601
  16.3 1.2 %shard_map.85.old_ref = f32[2,6,13,88,128]{4,3,2,1,0:T(8,128)S(1)} custom-call(bf16[2,4,64000]{2,1,0:T(4,128)(2,1)S(1)} %get-tuple-element.24.orb_ref.refs_0_, f32[2,6,13,88,128]{4,3,2,1,0:T(8,128)S(1)} %shard_map.84.refs_1_), custom_call_target="tpu_custom_call", output_to_operand_aliasing={{}: (1, {})} | custom-call | flops 2000000 | bytes 4000000 | tf_op jit(solution)/shard_map/pallas_call | solution.py:601
  17.5 2.0 %shard_map.82 = (bf16[2,896,896]{2,1,0:T(8,128)(2,1)S(1)}, bf16[2,896,896]{2,1,0:T(8,128)(2,1)S(1)}) custom-call(f32[6,40,896]{2,1,0:T(8,128)} %constant.8.clone.refs_0_), custom_call_target="tpu_custom_call" | custom-call | flops 4000000 | bytes 4000000 | tf_op jit(solution)/shard_map/pallas_call | solution.py:556
  19.6 0.0 collective-permute-done.4.prev_ref
  19.6 0.0 collective-permute-done.5.next_ref
  19.6 0.3 shard_map.90.refs_5_.refs_6_
  19.8 4.4 %shard_map.91 = (f32[3,500,128]{2,1,0:T(8,128)S(1)}, bf16[1,500,128]{2,1,0:T(8,128)(2,1)S(1)}, bf16[2,500,128]{2,1,0:T(8,128)(2,1)S(1)}) custom-call(s32[57]{0:T(128)S(1)} %get-tuple-element.25.refs_0_, bf16[2,896,896]{2,1,0:T(8,128)(2,1)S(1)} %get-tuple-element.28.refs_1_, bf16[2,896,896]{2,1,0:T(8,128)(2,1)S(1)} %get-tuple-element.29.refs_2_, ...), custom_call_target="tpu_custom_call" | custom-call | flops 1228800000 | bytes 10000000 | tf_op jit(solution)/shard_map/pallas_call | solution.py:638
  24.2 0.1 collective-permute-start.7
  24.3 0.0 collective-permute-done.prev_ref
  24.3 0.0 collective-permute-done.1.next_ref
  24.3 0.3 shard_map.86.refs_5_
  24.6 4.4 %shard_map.87 = (f32[3,500,128]{2,1,0:T(8,128)S(1)}, bf16[1,500,128]{2,1,0:T(8,128)(2,1)S(1)}, bf16[2,500,128]{2,1,0:T(8,128)(2,1)S(1)}) custom-call(s32[57]{0:T(128)S(1)} %get-tuple-element.25.refs_0_, bf16[2,896,896]{2,1,0:T(8,128)(2,1)S(1)} %get-tuple-element.28.refs_1_, bf16[2,896,896]{2,1,0:T(8,128)(2,1)S(1)} %get-tuple-element.29.refs_2_, ...), custom_call_target="tpu_custom_call" | custom-call | flops 1228800000 | bytes 10000000 | tf_op jit(solution)/shard_map/pallas_call | solution.py:638
  28.9 0.6 %collective-permute-start.3 = (bf16[2,500,128]{2,1,0:T(8,128)(2,1)S(1)}, bf16[2,500,128]{2,1,0:T(8,128)(2,1)S(1)}, u32[]{:S(2)}, u32[]{:S(2)}) collective-permute-start(bf16[2,500,128]{2,1,0:T(8,128)(2,1)S(1)} %get-tuple-element.35), channel_id=1, source_target_pairs={{0,31},{1,0},{2,1},{3,2},{4,3},{5,4},{6,5},{7,6},{8,7},{9,8},{10,9... | collective-permute-start | bytes 768008 | tf_op jit(solution)/shard_map/ppermute | solution.py:515
  29.6 1.5 %collective-permute-start.6 = (bf16[1,500,128]{2,1,0:T(8,128)(2,1)S(1)}, bf16[1,500,128]{2,1,0:T(8,128)(2,1)S(1)}, u32[]{:S(2)}, u32[]{:S(2)}) collective-permute-start(bf16[1,500,128]{2,1,0:T(8,128)(2,1)S(1)} %get-tuple-element.38), channel_id=1, source_target_pairs={{0,1},{1,2},{2,3},{3,4},{4,5},{5,6},{6,7},{7,8},{8,9},{9,10},{10,1... | collective-permute-start | bytes 384008 | tf_op jit(solution)/shard_map/ppermute | solution.py:515
  31.1 2.0 %collective-permute-start.2 = (bf16[1,500,128]{2,1,0:T(8,128)(2,1)S(1)}, bf16[1,500,128]{2,1,0:T(8,128)(2,1)S(1)}, u32[]{:S(2)}, u32[]{:S(2)}) collective-permute-start(bf16[1,500,128]{2,1,0:T(8,128)(2,1)S(1)} %get-tuple-element.34), channel_id=1, source_target_pairs={{0,1},{1,2},{2,3},{3,4},{4,5},{5,6},{6,7},{7,8},{8,9},{9,10},{10,1... | collective-permute-start | bytes 384008 | tf_op jit(solution)/shard_map/ppermute | solution.py:515
  33.0 4.4 %shard_map.92.refs_5_ = f32[7,1000,128]{2,1,0:T(8,128)} custom-call(s32[57]{0:T(128)S(1)} %get-tuple-element.25.refs_0_, bf16[2,896,896]{2,1,0:T(8,128)(2,1)S(1)} %get-tuple-element.28.refs_1_, bf16[2,896,896]{2,1,0:T(8,128)(2,1)S(1)} %get-tuple-element.29.refs_2_, bf16[160,160]{1,0:T(8,128)(2,1)S(1)} %get-tuple-element.40.refs_3_, ...), custom_call_target="tpu_custom_call" | custom-call | flops 819200000 | bytes 10000000 | tf_op jit(solution)/shard_map/pallas_call | solution.py:638
  37.4 1.8 %collective-permute-done.6.refs_3_ = bf16[1,500,128]{2,1,0:T(8,128)(2,1)S(1)} collective-permute-done((bf16[1,500,128]{2,1,0:T(8,128)(2,1)S(1)}, bf16[1,500,128]{2,1,0:T(8,128)(2,1)S(1)}, u32[]{:S(2)}, u32[]{:S(2)}) %collective-permute-start.6) | collective-permute-done | bytes 128032 | tf_op jit(solution)/shard_map/ppermute | solution.py:515
  39.2 2.8 %collective-permute-done.2.refs_1_ = bf16[1,500,128]{2,1,0:T(8,128)(2,1)S(1)} collective-permute-done((bf16[1,500,128]{2,1,0:T(8,128)(2,1)S(1)}, bf16[1,500,128]{2,1,0:T(8,128)(2,1)S(1)}, u32[]{:S(2)}, u32[]{:S(2)}) %collective-permute-start.2) | collective-permute-done | bytes 128032 | tf_op jit(solution)/shard_map/ppermute | solution.py:515
  42.0 0.0 collective-permute-done.7.refs_4_
  42.0 2.1 %collective-permute-done.3.refs_2_ = bf16[2,500,128]{2,1,0:T(8,128)(2,1)S(1)} collective-permute-done((bf16[2,500,128]{2,1,0:T(8,128)(2,1)S(1)}, bf16[2,500,128]{2,1,0:T(8,128)(2,1)S(1)}, u32[]{:S(2)}, u32[]{:S(2)}) %collective-permute-start.3) | collective-permute-done | bytes 256032 | tf_op jit(solution)/shard_map/ppermute | solution.py:515
  44.1 1.4 %place.1 = f32[7,1000,128]{2,1,0:T(8,128)} custom-call(s32[57]{0:T(128)S(1)} %get-tuple-element.25.refs_0_, bf16[1,500,128]{2,1,0:T(8,128)(2,1)S(1)} %collective-permute-done.2.refs_1_, bf16[2,500,128]{2,1,0:T(8,128)(2,1)S(1)} %collective-permute-done.3.refs_2_, ...), custom_call_target="tpu_custom_call", output_to_operand_aliasing={{}: (5, {})} | custom-call | flops 1000000 | bytes 4000000 | tf_op jit(solution)/shard_map/place/pallas_call | solution.py:662
  (3 shorter events, 0.1 us)
Async XLA Ops:
  3.2 16.4 %collective-permute-start.4 = (bf16[500,128]{1,0:T(8,128)(2,1)S(1)}, bf16[500,128]{1,0:T(8,128)(2,1)S(1)}, u32[]{:S(2)}, u32[]{:S(2)}) collective-permute-start(bf16[500,128]{1,0:T(8,128)(2,1)S(1)} %get-tuple-element.36), channel_id=1, source_target_pairs={{0,1},{1,2},{2,3},{3,4},{4,5},{5,6},{6,7},{7,8},{8,9},{9,10},{10,1... | collective-permute-start | bytes 384008 | tf_op jit(solution)/shard_map/ppermute | solution.py:515
  6.3 13.3 %collective-permute-start.5 = (bf16[500,128]{1,0:T(8,128)(2,1)S(1)}, bf16[500,128]{1,0:T(8,128)(2,1)S(1)}, u32[]{:S(2)}, u32[]{:S(2)}) collective-permute-start(bf16[500,128]{1,0:T(8,128)(2,1)S(1)} %get-tuple-element.37), channel_id=1, source_target_pairs={{0,31},{1,0},{2,1},{3,2},{4,3},{5,4},{6,5},{7,6},{8,7},{9,8},{10,9... | collective-permute-start | bytes 384008 | tf_op jit(solution)/shard_map/ppermute | solution.py:515
  9.7 14.6 %collective-permute-start = (bf16[500,128]{1,0:T(8,128)(2,1)S(1)}, bf16[500,128]{1,0:T(8,128)(2,1)S(1)}, u32[]{:S(2)}, u32[]{:S(2)}) collective-permute-start(bf16[500,128]{1,0:T(8,128)(2,1)S(1)} %get-tuple-element.32), channel_id=1, source_target_pairs={{0,1},{1,2},{2,3},{3,4},{4,5},{5,6},{6,7},{7,8},{8,9},{9,10},{10,1... | collective-permute-start | bytes 384008 | tf_op jit(solution)/shard_map/ppermute | solution.py:515
  9.7 14.6 %collective-permute-start.1 = (bf16[500,128]{1,0:T(8,128)(2,1)S(1)}, bf16[500,128]{1,0:T(8,128)(2,1)S(1)}, u32[]{:S(2)}, u32[]{:S(2)}) collective-permute-start(bf16[500,128]{1,0:T(8,128)(2,1)S(1)} %get-tuple-element.33), channel_id=1, source_target_pairs={{0,31},{1,0},{2,1},{3,2},{4,3},{5,4},{6,5},{7,6},{8,7},{9,8},{10,9... | collective-permute-start | bytes 384008 | tf_op jit(solution)/shard_map/ppermute | solution.py:515
  24.2 17.8 %collective-permute-start.7 = (bf16[2,500,128]{2,1,0:T(8,128)(2,1)S(1)}, bf16[2,500,128]{2,1,0:T(8,128)(2,1)S(1)}, u32[]{:S(2)}, u32[]{:S(2)}) collective-permute-start(bf16[2,500,128]{2,1,0:T(8,128)(2,1)S(1)} %get-tuple-element.39), channel_id=1, source_target_pairs={{0,31},{1,0},{2,1},{3,2},{4,3},{5,4},{6,5},{7,6},{8,7},{9,8},{10,9... | collective-permute-start | bytes 768008 | tf_op jit(solution)/shard_map/ppermute | solution.py:515
  28.9 15.2 %collective-permute-start.3 = (bf16[2,500,128]{2,1,0:T(8,128)(2,1)S(1)}, bf16[2,500,128]{2,1,0:T(8,128)(2,1)S(1)}, u32[]{:S(2)}, u32[]{:S(2)}) collective-permute-start(bf16[2,500,128]{2,1,0:T(8,128)(2,1)S(1)} %get-tuple-element.35), channel_id=1, source_target_pairs={{0,31},{1,0},{2,1},{3,2},{4,3},{5,4},{6,5},{7,6},{8,7},{9,8},{10,9... | collective-permute-start | bytes 768008 | tf_op jit(solution)/shard_map/ppermute | solution.py:515
  29.6 9.7 %collective-permute-start.6 = (bf16[1,500,128]{2,1,0:T(8,128)(2,1)S(1)}, bf16[1,500,128]{2,1,0:T(8,128)(2,1)S(1)}, u32[]{:S(2)}, u32[]{:S(2)}) collective-permute-start(bf16[1,500,128]{2,1,0:T(8,128)(2,1)S(1)} %get-tuple-element.38), channel_id=1, source_target_pairs={{0,1},{1,2},{2,3},{3,4},{4,5},{5,6},{6,7},{7,8},{8,9},{9,10},{10,1... | collective-permute-start | bytes 384008 | tf_op jit(solution)/shard_map/ppermute | solution.py:515
  31.1 10.9 %collective-permute-start.2 = (bf16[1,500,128]{2,1,0:T(8,128)(2,1)S(1)}, bf16[1,500,128]{2,1,0:T(8,128)(2,1)S(1)}, u32[]{:S(2)}, u32[]{:S(2)}) collective-permute-start(bf16[1,500,128]{2,1,0:T(8,128)(2,1)S(1)} %get-tuple-element.34), channel_id=1, source_target_pairs={{0,1},{1,2},{2,3},{3,4},{4,5},{5,6},{6,7},{7,8},{8,9},{9,10},{10,1... | collective-permute-start | bytes 384008 | tf_op jit(solution)/shard_map/ppermute | solution.py:515

commit v12 on v11

--- a/solution.py
+++ b/solution.py
@@ -244,25 +244,15 @@
         copy.wait()
 
 
-def place_along():
-    return lax.axis_index(AXES[-1]), lax.axis_size(AXES[-1])
-
-
 def low_half():
-    place, count = place_along()
-    return 2 * place < count
-
-
-def at_end():
-    place, count = place_along()
-    return place == count - 1
+    return 2 * lax.axis_index(AXES[-1]) < lax.axis_size(AXES[-1])
 
 
 def slabs_kernel(spin, chosen, orb_ref, *refs):
     pad_ref, flat_ref = refs[-2:]
     boxes = orb_ref.shape[1]
 
-    @pl.when(chosen())
+    @pl.when(chosen() if chosen else True)
     def _():
         split_boxes(orb_ref.at[spin], flat_ref, boxes)
 
@@ -281,7 +271,7 @@
 def modes_kernel(early, fac_hbm, *refs):
     to_ref, from_ref, fac_ref, sem = refs[-4:]
 
-    @pl.when(jnp.logical_not(at_end()) if early else at_end())
+    @pl.when(low_half() if early else jnp.logical_not(low_half()))
     def _():
         copy = pltpu.make_async_copy(fac_hbm, fac_ref, sem)
         copy.start()
@@ -588,16 +578,7 @@
     next_high = from_behind(back, -1)
     to_modes, from_modes = build_modes(False, *modes)
 
-    def inner():
-        return jnp.logical_not(low_half() | at_end())
-
-    def build_slabs(spin, *before):
-        here = (inner, low_half)[spin]
-        late = len(before) > 0
-
-        def chosen():
-            return jnp.logical_not(here()) if late else here()
-
+    def build_slabs(spin, *before, chosen=None):
         return pl.pallas_call(
             lambda *refs: slabs_kernel(spin, chosen, *refs),
             out_shape=slabs,
@@ -609,7 +590,7 @@
             cost_estimate=cost(2_000_000, 4_000_000),
         )(held, *before)
 
-    pads = [build_slabs(0, build_slabs(0)), build_slabs(1, build_slabs(1))]
+    pads = [build_slabs(0), build_slabs(1, build_slabs(1, chosen=low_half), chosen=lambda: jnp.logical_not(low_half()))]
     for spin, halo in enumerate(((prev_low, next_low), (prev_high, next_high))):
         pads[spin] = pl.pallas_call(
             fill_kernel,

time: 45.9 us -> 45.8 us (level)
    pallas_call x4 -> x3, Pallas kernels: 2.48 us -> 2.45 us  [build_slabs(): pl.pallas_call(lambda *refs: slabs_kernel(spin, chosen, *refs), out_shape...]
where the time goes in v12:
time: 45.8 us; the launch traced here: 45.7 us
  Pallas kernels  22.6 us (49%)
  starting transfers between devices  16 us (35%)
  waiting for transfers between devices  6.72 us (15%)
    ppermute x8, starting transfers between devices, from_behind(): lax.ppermute(value, AXES, [(source, (source + steps) % count) for source...  16 us
    pallas_call x3, Pallas kernels, solve(): pl.pallas_call(lambda *refs: pair_kernel(start, held, spins, final, *refs...  13.1 us
    ppermute x8, waiting for transfers between devices, from_behind(): lax.ppermute(value, AXES, [(source, (source + steps) % count) for source...  6.72 us
    pallas_call x3, Pallas kernels, build_slabs(): pl.pallas_call(lambda *refs: slabs_kernel(spin, chosen, *refs), out_shape...  2.45 us
    pallas_call x2, Pallas kernels, build_modes(): pl.pallas_call(lambda *refs: modes_kernel(early, *refs), out_shape=[folde...  2 us
    pallas_call x1, Pallas kernels, shards(): second(*map(in_place, (dest, partners_t, anchors_t, *handed)), held)  1.74 us
    pallas_call x1, Pallas kernels, shards(): pl.pallas_call(window_kernel, out_shape=[box] * 2 + [jax.ShapeDtypeStruct...  1.41 us
    pallas_call x1, Pallas kernels, shards(): pl.pallas_call(lambda *refs: place_kernel(boxes, *refs), out_shape=shape,...  1.4 us
  transfers between devices with their start and end apart: 8, of which 3 were waited for; matrix products, arithmetic and copies ran while one was open for 0% of the time, Pallas kernels for 40%

profile of v12, /device:TPU:0, one launch (start us, length us, event | category | flops | bytes accessed | tf_op | source)
XLA Modules:
  0.0 45.7 jit_solution(3291606136667072567)
XLA Ops:
  0.0 1.4 %window.1 = (bf16[500,128]{1,0:T(8,128)(2,1)S(1)}, bf16[500,128]{1,0:T(8,128)(2,1)S(1)}, bf16[2,4,64000]{2,1,0:T(4,128)(2,1)S(1)}) custom-call(s32[2,128]{1,0:T(2,128)} %bitcast.9, bf16[2,4,64000]{2,1,0:T(4,128)(2,1)} %orb_hbm.1), custom_call_target="tpu_custom_call" | custom-call | tf_op jit(solution)/shard_map/window/pallas_call | solution.py:531
  1.4 1.7 %second.1 = (bf16[500,128]{1,0:T(8,128)(2,1)S(1)}, bf16[500,128]{1,0:T(8,128)(2,1)S(1)}, s32[57]{0:T(128)S(1)}, f32[40,1792]{1,0:T(8,128)S(1)}, bf16[240,240]{1,...) custom-call(s32[128]{0:T(128)} %dest_hbm.1, s32[2,128]{1,0:T(2,128)} %bitcast.10, s32[3,128]{1,0:T(4,128)} %bitcast.11, ...), custom_call_target="tpu_custom_call" | custom-call | flops 1000000 | bytes 2000000 | tf_op jit(solution)/shard_map/second/pallas_call | solution.py:575
  3.2 3.1 %collective-permute-start.4 = (bf16[500,128]{1,0:T(8,128)(2,1)S(1)}, bf16[500,128]{1,0:T(8,128)(2,1)S(1)}, u32[]{:S(2)}, u32[]{:S(2)}) collective-permute-start(bf16[500,128]{1,0:T(8,128)(2,1)S(1)} %get-tuple-element.36), channel_id=1, source_target_pairs={{0,1},{1,2},{2,3},{3,4},{4,5},{5,6},{6,7},{7,8},{8,9},{9,10},{10,1... | collective-permute-start | bytes 384008 | tf_op jit(solution)/shard_map/ppermute | solution.py:505
  6.3 3.4 %collective-permute-start.5 = (bf16[500,128]{1,0:T(8,128)(2,1)S(1)}, bf16[500,128]{1,0:T(8,128)(2,1)S(1)}, u32[]{:S(2)}, u32[]{:S(2)}) collective-permute-start(bf16[500,128]{1,0:T(8,128)(2,1)S(1)} %get-tuple-element.37), channel_id=1, source_target_pairs={{0,31},{1,0},{2,1},{3,2},{4,3},{5,4},{6,5},{7,6},{8,7},{9,8},{10,9... | collective-permute-start | bytes 384008 | tf_op jit(solution)/shard_map/ppermute | solution.py:505
  9.7 0.0 collective-permute-start
  9.7 5.3 %collective-permute-start.1 = (bf16[500,128]{1,0:T(8,128)(2,1)S(1)}, bf16[500,128]{1,0:T(8,128)(2,1)S(1)}, u32[]{:S(2)}, u32[]{:S(2)}) collective-permute-start(bf16[500,128]{1,0:T(8,128)(2,1)S(1)} %get-tuple-element.33), channel_id=1, source_target_pairs={{0,31},{1,0},{2,1},{3,2},{4,3},{5,4},{6,5},{7,6},{8,7},{9,8},{10,9... | collective-permute-start | bytes 384008 | tf_op jit(solution)/shard_map/ppermute | solution.py:505
  15.0 1.2 %shard_map.87.refs_1_ = f32[2,6,13,88,128]{4,3,2,1,0:T(8,128)S(1)} custom-call(bf16[2,4,64000]{2,1,0:T(4,128)(2,1)S(1)} %get-tuple-element.24.orb_ref.refs_0_), custom_call_target="tpu_custom_call" | custom-call | flops 2000000 | bytes 4000000 | tf_op jit(solution)/shard_map/pallas_call | solution.py:582
  16.3 1.2 %shard_map.84.old_ref = f32[2,6,13,88,128]{4,3,2,1,0:T(8,128)S(1)} custom-call(bf16[2,4,64000]{2,1,0:T(4,128)(2,1)S(1)} %get-tuple-element.24.orb_ref.refs_0_), custom_call_target="tpu_custom_call" | custom-call | flops 2000000 | bytes 4000000 | tf_op jit(solution)/shard_map/pallas_call | solution.py:582
  17.5 2.0 %shard_map.82 = (bf16[2,896,896]{2,1,0:T(8,128)(2,1)S(1)}, bf16[2,896,896]{2,1,0:T(8,128)(2,1)S(1)}) custom-call(f32[6,40,896]{2,1,0:T(8,128)} %constant.8.clone.refs_0_), custom_call_target="tpu_custom_call" | custom-call | flops 4000000 | bytes 4000000 | tf_op jit(solution)/shard_map/pallas_call | solution.py:546
  19.5 0.0 collective-permute-done.4.prev_ref
  19.5 0.0 collective-permute-done.5.next_ref
  19.5 0.3 shard_map.89.refs_5_.refs_6_
  19.8 4.4 %shard_map.90 = (f32[3,500,128]{2,1,0:T(8,128)S(1)}, bf16[1,500,128]{2,1,0:T(8,128)(2,1)S(1)}, bf16[2,500,128]{2,1,0:T(8,128)(2,1)S(1)}) custom-call(s32[57]{0:T(128)S(1)} %get-tuple-element.25.refs_0_, bf16[2,896,896]{2,1,0:T(8,128)(2,1)S(1)} %get-tuple-element.28.refs_1_, bf16[2,896,896]{2,1,0:T(8,128)(2,1)S(1)} %get-tuple-element.29.refs_2_, ...), custom_call_target="tpu_custom_call" | custom-call | flops 1228800000 | bytes 10000000 | tf_op jit(solution)/shard_map/pallas_call | solution.py:619
  24.2 0.1 collective-permute-start.7
  24.2 0.0 collective-permute-done.prev_ref
  24.3 0.0 collective-permute-done.1.next_ref
  24.3 0.3 shard_map.85.refs_5_
  24.5 4.4 %shard_map.86 = (f32[3,500,128]{2,1,0:T(8,128)S(1)}, bf16[1,500,128]{2,1,0:T(8,128)(2,1)S(1)}, bf16[2,500,128]{2,1,0:T(8,128)(2,1)S(1)}) custom-call(s32[57]{0:T(128)S(1)} %get-tuple-element.25.refs_0_, bf16[2,896,896]{2,1,0:T(8,128)(2,1)S(1)} %get-tuple-element.28.refs_1_, bf16[2,896,896]{2,1,0:T(8,128)(2,1)S(1)} %get-tuple-element.29.refs_2_, ...), custom_call_target="tpu_custom_call" | custom-call | flops 1228800000 | bytes 10000000 | tf_op jit(solution)/shard_map/pallas_call | solution.py:619
  28.9 0.7 %collective-permute-start.3 = (bf16[2,500,128]{2,1,0:T(8,128)(2,1)S(1)}, bf16[2,500,128]{2,1,0:T(8,128)(2,1)S(1)}, u32[]{:S(2)}, u32[]{:S(2)}) collective-permute-start(bf16[2,500,128]{2,1,0:T(8,128)(2,1)S(1)} %get-tuple-element.35), channel_id=1, source_target_pairs={{0,31},{1,0},{2,1},{3,2},{4,3},{5,4},{6,5},{7,6},{8,7},{9,8},{10,9... | collective-permute-start | bytes 768008 | tf_op jit(solution)/shard_map/ppermute | solution.py:505
  29.6 1.5 %collective-permute-start.6 = (bf16[1,500,128]{2,1,0:T(8,128)(2,1)S(1)}, bf16[1,500,128]{2,1,0:T(8,128)(2,1)S(1)}, u32[]{:S(2)}, u32[]{:S(2)}) collective-permute-start(bf16[1,500,128]{2,1,0:T(8,128)(2,1)S(1)} %get-tuple-element.38), channel_id=1, source_target_pairs={{0,1},{1,2},{2,3},{3,4},{4,5},{5,6},{6,7},{7,8},{8,9},{9,10},{10,1... | collective-permute-start | bytes 384008 | tf_op jit(solution)/shard_map/ppermute | solution.py:505
  31.0 2.0 %collective-permute-start.2 = (bf16[1,500,128]{2,1,0:T(8,128)(2,1)S(1)}, bf16[1,500,128]{2,1,0:T(8,128)(2,1)S(1)}, u32[]{:S(2)}, u32[]{:S(2)}) collective-permute-start(bf16[1,500,128]{2,1,0:T(8,128)(2,1)S(1)} %get-tuple-element.34), channel_id=1, source_target_pairs={{0,1},{1,2},{2,3},{3,4},{4,5},{5,6},{6,7},{7,8},{8,9},{9,10},{10,1... | collective-permute-start | bytes 384008 | tf_op jit(solution)/shard_map/ppermute | solution.py:505
  33.0 4.4 %shard_map.91.refs_5_ = f32[7,1000,128]{2,1,0:T(8,128)} custom-call(s32[57]{0:T(128)S(1)} %get-tuple-element.25.refs_0_, bf16[2,896,896]{2,1,0:T(8,128)(2,1)S(1)} %get-tuple-element.28.refs_1_, bf16[2,896,896]{2,1,0:T(8,128)(2,1)S(1)} %get-tuple-element.29.refs_2_, bf16[160,160]{1,0:T(8,128)(2,1)S(1)} %get-tuple-element.40.refs_3_, ...), custom_call_target="tpu_custom_call" | custom-call | flops 819200000 | bytes 10000000 | tf_op jit(solution)/shard_map/pallas_call | solution.py:619
  37.4 1.8 %collective-permute-done.6.refs_3_ = bf16[1,500,128]{2,1,0:T(8,128)(2,1)S(1)} collective-permute-done((bf16[1,500,128]{2,1,0:T(8,128)(2,1)S(1)}, bf16[1,500,128]{2,1,0:T(8,128)(2,1)S(1)}, u32[]{:S(2)}, u32[]{:S(2)}) %collective-permute-start.6) | collective-permute-done | bytes 128032 | tf_op jit(solution)/shard_map/ppermute | solution.py:505
  39.2 2.8 %collective-permute-done.2.refs_1_ = bf16[1,500,128]{2,1,0:T(8,128)(2,1)S(1)} collective-permute-done((bf16[1,500,128]{2,1,0:T(8,128)(2,1)S(1)}, bf16[1,500,128]{2,1,0:T(8,128)(2,1)S(1)}, u32[]{:S(2)}, u32[]{:S(2)}) %collective-permute-start.2) | collective-permute-done | bytes 128032 | tf_op jit(solution)/shard_map/ppermute | solution.py:505
  42.0 0.0 collective-permute-done.7.refs_4_
  42.0 2.1 %collective-permute-done.3.refs_2_ = bf16[2,500,128]{2,1,0:T(8,128)(2,1)S(1)} collective-permute-done((bf16[2,500,128]{2,1,0:T(8,128)(2,1)S(1)}, bf16[2,500,128]{2,1,0:T(8,128)(2,1)S(1)}, u32[]{:S(2)}, u32[]{:S(2)}) %collective-permute-start.3) | collective-permute-done | bytes 256032 | tf_op jit(solution)/shard_map/ppermute | solution.py:505
  44.1 1.4 %place.1 = f32[7,1000,128]{2,1,0:T(8,128)} custom-call(s32[57]{0:T(128)S(1)} %get-tuple-element.25.refs_0_, bf16[1,500,128]{2,1,0:T(8,128)(2,1)S(1)} %collective-permute-done.2.refs_1_, bf16[2,500,128]{2,1,0:T(8,128)(2,1)S(1)} %collective-permute-done.3.refs_2_, ...), custom_call_target="tpu_custom_call", output_to_operand_aliasing={{}: (5, {})} | custom-call | flops 1000000 | bytes 4000000 | tf_op jit(solution)/shard_map/place/pallas_call | solution.py:643
  (2 shorter events, 0.0 us)
Async XLA Ops:
  3.2 16.4 %collective-permute-start.4 = (bf16[500,128]{1,0:T(8,128)(2,1)S(1)}, bf16[500,128]{1,0:T(8,128)(2,1)S(1)}, u32[]{:S(2)}, u32[]{:S(2)}) collective-permute-start(bf16[500,128]{1,0:T(8,128)(2,1)S(1)} %get-tuple-element.36), channel_id=1, source_target_pairs={{0,1},{1,2},{2,3},{3,4},{4,5},{5,6},{6,7},{7,8},{8,9},{9,10},{10,1... | collective-permute-start | bytes 384008 | tf_op jit(solution)/shard_map/ppermute | solution.py:505
  6.3 13.3 %collective-permute-start.5 = (bf16[500,128]{1,0:T(8,128)(2,1)S(1)}, bf16[500,128]{1,0:T(8,128)(2,1)S(1)}, u32[]{:S(2)}, u32[]{:S(2)}) collective-permute-start(bf16[500,128]{1,0:T(8,128)(2,1)S(1)} %get-tuple-element.37), channel_id=1, source_target_pairs={{0,31},{1,0},{2,1},{3,2},{4,3},{5,4},{6,5},{7,6},{8,7},{9,8},{10,9... | collective-permute-start | bytes 384008 | tf_op jit(solution)/shard_map/ppermute | solution.py:505
  9.7 14.6 %collective-permute-start = (bf16[500,128]{1,0:T(8,128)(2,1)S(1)}, bf16[500,128]{1,0:T(8,128)(2,1)S(1)}, u32[]{:S(2)}, u32[]{:S(2)}) collective-permute-start(bf16[500,128]{1,0:T(8,128)(2,1)S(1)} %get-tuple-element.32), channel_id=1, source_target_pairs={{0,1},{1,2},{2,3},{3,4},{4,5},{5,6},{6,7},{7,8},{8,9},{9,10},{10,1... | collective-permute-start | bytes 384008 | tf_op jit(solution)/shard_map/ppermute | solution.py:505
  9.7 14.6 %collective-permute-start.1 = (bf16[500,128]{1,0:T(8,128)(2,1)S(1)}, bf16[500,128]{1,0:T(8,128)(2,1)S(1)}, u32[]{:S(2)}, u32[]{:S(2)}) collective-permute-start(bf16[500,128]{1,0:T(8,128)(2,1)S(1)} %get-tuple-element.33), channel_id=1, source_target_pairs={{0,31},{1,0},{2,1},{3,2},{4,3},{5,4},{6,5},{7,6},{8,7},{9,8},{10,9... | collective-permute-start | bytes 384008 | tf_op jit(solution)/shard_map/ppermute | solution.py:505
  24.2 17.8 %collective-permute-start.7 = (bf16[2,500,128]{2,1,0:T(8,128)(2,1)S(1)}, bf16[2,500,128]{2,1,0:T(8,128)(2,1)S(1)}, u32[]{:S(2)}, u32[]{:S(2)}) collective-permute-start(bf16[2,500,128]{2,1,0:T(8,128)(2,1)S(1)} %get-tuple-element.39), channel_id=1, source_target_pairs={{0,31},{1,0},{2,1},{3,2},{4,3},{5,4},{6,5},{7,6},{8,7},{9,8},{10,9... | collective-permute-start | bytes 768008 | tf_op jit(solution)/shard_map/ppermute | solution.py:505
  28.9 15.2 %collective-permute-start.3 = (bf16[2,500,128]{2,1,0:T(8,128)(2,1)S(1)}, bf16[2,500,128]{2,1,0:T(8,128)(2,1)S(1)}, u32[]{:S(2)}, u32[]{:S(2)}) collective-permute-start(bf16[2,500,128]{2,1,0:T(8,128)(2,1)S(1)} %get-tuple-element.35), channel_id=1, source_target_pairs={{0,31},{1,0},{2,1},{3,2},{4,3},{5,4},{6,5},{7,6},{8,7},{9,8},{10,9... | collective-permute-start | bytes 768008 | tf_op jit(solution)/shard_map/ppermute | solution.py:505
  29.6 9.6 %collective-permute-start.6 = (bf16[1,500,128]{2,1,0:T(8,128)(2,1)S(1)}, bf16[1,500,128]{2,1,0:T(8,128)(2,1)S(1)}, u32[]{:S(2)}, u32[]{:S(2)}) collective-permute-start(bf16[1,500,128]{2,1,0:T(8,128)(2,1)S(1)} %get-tuple-element.38), channel_id=1, source_target_pairs={{0,1},{1,2},{2,3},{3,4},{4,5},{5,6},{6,7},{7,8},{8,9},{9,10},{10,1... | collective-permute-start | bytes 384008 | tf_op jit(solution)/shard_map/ppermute | solution.py:505
  31.0 10.9 %collective-permute-start.2 = (bf16[1,500,128]{2,1,0:T(8,128)(2,1)S(1)}, bf16[1,500,128]{2,1,0:T(8,128)(2,1)S(1)}, u32[]{:S(2)}, u32[]{:S(2)}) collective-permute-start(bf16[1,500,128]{2,1,0:T(8,128)(2,1)S(1)} %get-tuple-element.34), channel_id=1, source_target_pairs={{0,1},{1,2},{2,3},{3,4},{4,5},{5,6},{6,7},{7,8},{8,9},{9,10},{10,1... | collective-permute-start | bytes 384008 | tf_op jit(solution)/shard_map/ppermute | solution.py:505

commit v13 on v12

--- a/solution.py
+++ b/solution.py
@@ -132,12 +132,13 @@
     return wanted
 
 
-def window_kernel(part_hbm, orb_hbm, ahead_ref, back_ref, orb_ref, part_ref, flat_ref, sems):
+def window_kernel(part_hbm, orb_hbm, fac_hbm, ahead_ref, back_ref, orb_ref, fac_ref, part_ref, flat_ref, sems):
     boxes = orb_ref.shape[1]
     small = pltpu.make_async_copy(part_hbm, part_ref, sems.at[0])
     large = [pltpu.make_async_copy(orb_hbm.at[spin], orb_ref.at[spin], sems.at[1 + spin]) for spin in range(2)]
+    factors = pltpu.make_async_copy(fac_hbm, fac_ref, sems.at[3])
     small.start()
-    for copy in large:
+    for copy in (*large, factors):
         copy.start()
     small.wait()
     wanted = wanted_boxes(part_ref, boxes)
@@ -146,6 +147,7 @@
     for side, ref in enumerate((ahead_ref, back_ref)):
         ref[...] = flat_ref[pl.ds(wanted[side], FLAT, stride=8), :].astype(BF)
     large[1].wait()
+    factors.wait()
 
 
 def table_layout(boxes):
@@ -256,30 +258,21 @@
     def _():
         split_boxes(orb_ref.at[spin], flat_ref, boxes)
 
-        def slabs(box, _):
+        for box in range(boxes):
             flat_to_slabs(
                 lambda t: flat_ref[pl.ds(box + 8 * t, HALF, stride=8 * PAIRT), :],
                 lambda u, parity, x: pad_ref.__setitem__(
                     (0, box, u, pl.ds(PAD + parity, HALF, stride=2), slice(None)), x),
             )
             reverse_box(pad_ref, box)
-            return 0
-
-        lax.fori_loop(0, boxes, slabs, 0)
-
-
-def modes_kernel(early, fac_hbm, *refs):
-    to_ref, from_ref, fac_ref, sem = refs[-4:]
+
+
+def modes_kernel(early, fac_ref, *refs):
+    to_ref, from_ref = refs[-2:]
 
     @pl.when(low_half() if early else jnp.logical_not(low_half()))
     def _():
-        copy = pltpu.make_async_copy(fac_hbm, fac_ref, sem)
-        copy.start()
-        for part in range(2):
-            to_ref[part, FOLD:, :] = jnp.zeros((FWIDE - FOLD, FWIDE), BF)
-            from_ref[part, FOLD:, :] = jnp.zeros((FWIDE - FOLD, FWIDE), BF)
         front = lax.broadcasted_iota(jnp.int32, (EDGE, 1), 0) < HALF
-        copy.wait()
 
         def build(i, _):
             where = pl.ds(pl.multiple_of(i * 2 * EDGE, 16), 2 * EDGE)
@@ -296,6 +289,9 @@
             return 0
 
         lax.fori_loop(0, HALF // 2, build, 0)
+        for part in range(2):
+            to_ref[part, FOLD:, :] = jnp.zeros((FWIDE - FOLD, FWIDE), BF)
+            from_ref[part, FOLD:, :] = jnp.zeros((FWIDE - FOLD, FWIDE), BF)
 
 
 def fill_kernel(old_ref, prev_ref, next_ref, pad_ref, flat_ref):
@@ -528,15 +524,15 @@
 
     box = jax.ShapeDtypeStruct((FLAT, LANES), BF)
     splitter = pltpu.VMEM((FLAT * 8, LANES), F32)
-    ahead, back, held = pl.pallas_call(
+    ahead, back, held, factors = pl.pallas_call(
         window_kernel,
-        out_shape=[box] * 2 + [jax.ShapeDtypeStruct(orbitals.shape, BF)],
-        in_specs=[ANYWHERE] * 2,
-        out_specs=whole(3),
-        scratch_shapes=[pltpu.SMEM(partners_t.shape, jnp.int32), splitter, pltpu.SemaphoreType.DMA((3,))],
+        out_shape=[box] * 2 + [jax.ShapeDtypeStruct(orbitals.shape, BF), jax.ShapeDtypeStruct(factors.shape, F32)],
+        in_specs=[ANYWHERE] * 3,
+        out_specs=whole(4),
+        scratch_shapes=[pltpu.SMEM(partners_t.shape, jnp.int32), splitter, pltpu.SemaphoreType.DMA((4,))],
         compiler_params=pltpu.CompilerParams(vmem_limit_bytes=12 << 20),
         name="window",
-    )(*map(in_place, (partners_t, orbitals)))
+    )(*map(in_place, (partners_t, orbitals, factors)))
     prev_low = from_behind(ahead, 1)
     next_low = from_behind(back, -1)
 
@@ -546,13 +542,12 @@
         return pl.pallas_call(
             lambda *refs: modes_kernel(early, *refs),
             out_shape=[folded] * 2,
-            in_specs=[ANYWHERE] + whole(len(before)),
+            in_specs=whole(1 + len(before)),
             out_specs=whole(2),
-            scratch_shapes=[pltpu.VMEM(factors.shape, F32), pltpu.SemaphoreType.DMA],
             input_output_aliases={1: 0, 2: 1} if before else {},
             compiler_params=pltpu.CompilerParams(vmem_limit_bytes=12 << 20),
             cost_estimate=cost(4_000_000, 4_000_000),
-        )(in_place(factors), *before)
+        )(factors, *before)
 
     modes = build_modes(True)
     moving = AHEAD + BACK

time: 45.8 us -> 44.3 us (0.967)
  Pallas kernels: 22.6 us -> 21 us
    pallas_call x2, Pallas kernels: 2 us -> 0.87 us  [build_modes(): pl.pallas_call(lambda *refs: modes_kernel(early, *refs), out_shape=[folde...]
    pallas_call x3, Pallas kernels: 2.45 us -> 1.89 us  [build_slabs(): pl.pallas_call(lambda *refs: slabs_kernel(spin, chosen, *refs), out_shape...]
  transfers between devices with their start and end apart: 8 -> 8, of which waited for: 3 -> 3; matrix products, arithmetic and copies ran while one was open for 0% -> 0% of each run, Pallas kernels for 40% -> 37%
where the time goes in v13:
time: 44.3 us; the launch traced here: 44.1 us
  Pallas kernels  21 us (47%)
  starting transfers between devices  16 us (36%)
  waiting for transfers between devices  6.81 us (15%)
    ppermute x8, starting transfers between devices, from_behind(): lax.ppermute(value, AXES, [(source, (source + steps) % count) for source...  16 us
    pallas_call x3, Pallas kernels, solve(): pl.pallas_call(lambda *refs: pair_kernel(start, held, spins, final, *refs...  13.1 us
    ppermute x8, waiting for transfers between devices, from_behind(): lax.ppermute(value, AXES, [(source, (source + steps) % count) for source...  6.81 us
    pallas_call x3, Pallas kernels, build_slabs(): pl.pallas_call(lambda *refs: slabs_kernel(spin, chosen, *refs), out_shape...  1.89 us
    pallas_call x1, Pallas kernels, shards(): second(*map(in_place, (dest, partners_t, anchors_t, *handed)), held)  1.74 us
    pallas_call x1, Pallas kernels, shards(): pl.pallas_call(window_kernel, out_shape=[box] * 2 + [jax.ShapeDtypeStruct...  1.51 us
    pallas_call x1, Pallas kernels, shards(): pl.pallas_call(lambda *refs: place_kernel(boxes, *refs), out_shape=shape,...  1.4 us
  transfers between devices with their start and end apart: 8, of which 3 were waited for; matrix products, arithmetic and copies ran while one was open for 0% of the time, Pallas kernels for 37%

profile of v13, /device:TPU:0, one launch (start us, length us, event | category | flops | bytes accessed | tf_op | source)
XLA Modules:
  0.0 44.1 jit_solution(16421987064516254801)
XLA Ops:
  0.0 1.5 %window.1 = (bf16[500,128]{1,0:T(8,128)(2,1)S(1)}, bf16[500,128]{1,0:T(8,128)(2,1)S(1)}, bf16[2,4,64000]{2,1,0:T(4,128)(2,1)S(1)}, f32[6,40,896]{2,1,0:T(8,128)S(1)}) custom-call(s32[2,128]{1,0:T(2,128)} %bitcast.9, bf16[2,4,64000]{2,1,0:T(4,128)(2,1)} %orb_hbm.1, f32[6,40,896]{2,1,0:T(8,128)} %constant.8.clone.fac_hbm), custom_call_target="tpu_custom_call" | custom-call | tf_op jit(solution)/shard_map/window/pallas_call | solution.py:527
  1.5 1.7 %second.1 = (bf16[500,128]{1,0:T(8,128)(2,1)S(1)}, bf16[500,128]{1,0:T(8,128)(2,1)S(1)}, s32[57]{0:T(128)S(1)}, f32[40,1792]{1,0:T(8,128)S(1)}, bf16[240,240]{1,...) custom-call(s32[128]{0:T(128)} %dest_hbm.1, s32[2,128]{1,0:T(2,128)} %bitcast.10, s32[3,128]{1,0:T(4,128)} %bitcast.11, ...), custom_call_target="tpu_custom_call" | custom-call | flops 1000000 | bytes 2000000 | tf_op jit(solution)/shard_map/second/pallas_call | solution.py:570
  3.3 3.1 %collective-permute-start.4 = (bf16[500,128]{1,0:T(8,128)(2,1)S(1)}, bf16[500,128]{1,0:T(8,128)(2,1)S(1)}, u32[]{:S(2)}, u32[]{:S(2)}) collective-permute-start(bf16[500,128]{1,0:T(8,128)(2,1)S(1)} %get-tuple-element.38), channel_id=1, source_target_pairs={{0,1},{1,2},{2,3},{3,4},{4,5},{5,6},{6,7},{7,8},{8,9},{9,10},{10,1... | collective-permute-start | bytes 384008 | tf_op jit(solution)/shard_map/ppermute | solution.py:501
  6.4 3.4 %collective-permute-start.5 = (bf16[500,128]{1,0:T(8,128)(2,1)S(1)}, bf16[500,128]{1,0:T(8,128)(2,1)S(1)}, u32[]{:S(2)}, u32[]{:S(2)}) collective-permute-start(bf16[500,128]{1,0:T(8,128)(2,1)S(1)} %get-tuple-element.39), channel_id=1, source_target_pairs={{0,31},{1,0},{2,1},{3,2},{4,3},{5,4},{6,5},{7,6},{8,7},{9,8},{10,9... | collective-permute-start | bytes 384008 | tf_op jit(solution)/shard_map/ppermute | solution.py:501
  9.8 0.0 collective-permute-start
  9.8 5.3 %collective-permute-start.1 = (bf16[500,128]{1,0:T(8,128)(2,1)S(1)}, bf16[500,128]{1,0:T(8,128)(2,1)S(1)}, u32[]{:S(2)}, u32[]{:S(2)}) collective-permute-start(bf16[500,128]{1,0:T(8,128)(2,1)S(1)} %get-tuple-element.35), channel_id=1, source_target_pairs={{0,31},{1,0},{2,1},{3,2},{4,3},{5,4},{6,5},{7,6},{8,7},{9,8},{10,9... | collective-permute-start | bytes 384008 | tf_op jit(solution)/shard_map/ppermute | solution.py:501
  15.1 0.9 %shard_map.87.refs_1_ = f32[2,6,13,88,128]{4,3,2,1,0:T(8,128)S(1)} custom-call(bf16[2,4,64000]{2,1,0:T(4,128)(2,1)S(1)} %get-tuple-element.25.orb_ref.refs_0_), custom_call_target="tpu_custom_call" | custom-call | flops 2000000 | bytes 4000000 | tf_op jit(solution)/shard_map/pallas_call | solution.py:577
  16.1 0.9 %shard_map.84.old_ref = f32[2,6,13,88,128]{4,3,2,1,0:T(8,128)S(1)} custom-call(bf16[2,4,64000]{2,1,0:T(4,128)(2,1)S(1)} %get-tuple-element.25.orb_ref.refs_0_), custom_call_target="tpu_custom_call" | custom-call | flops 2000000 | bytes 4000000 | tf_op jit(solution)/shard_map/pallas_call | solution.py:577
  17.0 0.9 %shard_map.82 = (bf16[2,896,896]{2,1,0:T(8,128)(2,1)S(1)}, bf16[2,896,896]{2,1,0:T(8,128)(2,1)S(1)}) custom-call(f32[6,40,896]{2,1,0:T(8,128)S(1)} %get-tuple-element.27.refs_0_), custom_call_target="tpu_custom_call" | custom-call | flops 4000000 | bytes 4000000 | tf_op jit(solution)/shard_map/pallas_call | solution.py:542
  17.9 0.0 collective-permute-done.4.prev_ref
  17.9 0.0 collective-permute-done.5.next_ref
  17.9 0.3 shard_map.89.refs_5_.refs_6_
  18.2 4.4 %shard_map.90 = (f32[3,500,128]{2,1,0:T(8,128)S(1)}, bf16[1,500,128]{2,1,0:T(8,128)(2,1)S(1)}, bf16[2,500,128]{2,1,0:T(8,128)(2,1)S(1)}) custom-call(s32[57]{0:T(128)S(1)} %get-tuple-element.26.refs_0_, bf16[2,896,896]{2,1,0:T(8,128)(2,1)S(1)} %get-tuple-element.30.refs_1_, bf16[2,896,896]{2,1,0:T(8,128)(2,1)S(1)} %get-tuple-element.31.refs_2_, ...), custom_call_target="tpu_custom_call" | custom-call | flops 1228800000 | bytes 10000000 | tf_op jit(solution)/shard_map/pallas_call | solution.py:614
  22.6 1.5 %collective-permute-start.7 = (bf16[2,500,128]{2,1,0:T(8,128)(2,1)S(1)}, bf16[2,500,128]{2,1,0:T(8,128)(2,1)S(1)}, u32[]{:S(2)}, u32[]{:S(2)}) collective-permute-start(bf16[2,500,128]{2,1,0:T(8,128)(2,1)S(1)} %get-tuple-element.41), channel_id=1, source_target_pairs={{0,31},{1,0},{2,1},{3,2},{4,3},{5,4},{6,5},{7,6},{8,7},{9,8},{10,9... | collective-permute-start | bytes 768008 | tf_op jit(solution)/shard_map/ppermute | solution.py:501
  24.1 0.0 collective-permute-done.prev_ref
  24.1 0.0 collective-permute-done.1.next_ref
  24.1 0.3 shard_map.85.refs_5_
  24.4 4.3 %shard_map.86 = (f32[3,500,128]{2,1,0:T(8,128)S(1)}, bf16[1,500,128]{2,1,0:T(8,128)(2,1)S(1)}, bf16[2,500,128]{2,1,0:T(8,128)(2,1)S(1)}) custom-call(s32[57]{0:T(128)S(1)} %get-tuple-element.26.refs_0_, bf16[2,896,896]{2,1,0:T(8,128)(2,1)S(1)} %get-tuple-element.30.refs_1_, bf16[2,896,896]{2,1,0:T(8,128)(2,1)S(1)} %get-tuple-element.31.refs_2_, ...), custom_call_target="tpu_custom_call" | custom-call | flops 1228800000 | bytes 10000000 | tf_op jit(solution)/shard_map/pallas_call | solution.py:614
  28.8 0.9 %collective-permute-start.3 = (bf16[2,500,128]{2,1,0:T(8,128)(2,1)S(1)}, bf16[2,500,128]{2,1,0:T(8,128)(2,1)S(1)}, u32[]{:S(2)}, u32[]{:S(2)}) collective-permute-start(bf16[2,500,128]{2,1,0:T(8,128)(2,1)S(1)} %get-tuple-element.37), channel_id=1, source_target_pairs={{0,31},{1,0},{2,1},{3,2},{4,3},{5,4},{6,5},{7,6},{8,7},{9,8},{10,9... | collective-permute-start | bytes 768008 | tf_op jit(solution)/shard_map/ppermute | solution.py:501
  29.7 1.2 %collective-permute-start.6 = (bf16[1,500,128]{2,1,0:T(8,128)(2,1)S(1)}, bf16[1,500,128]{2,1,0:T(8,128)(2,1)S(1)}, u32[]{:S(2)}, u32[]{:S(2)}) collective-permute-start(bf16[1,500,128]{2,1,0:T(8,128)(2,1)S(1)} %get-tuple-element.40), channel_id=1, source_target_pairs={{0,1},{1,2},{2,3},{3,4},{4,5},{5,6},{6,7},{7,8},{8,9},{9,10},{10,1... | collective-permute-start | bytes 384008 | tf_op jit(solution)/shard_map/ppermute | solution.py:501
  30.8 0.5 %collective-permute-start.2 = (bf16[1,500,128]{2,1,0:T(8,128)(2,1)S(1)}, bf16[1,500,128]{2,1,0:T(8,128)(2,1)S(1)}, u32[]{:S(2)}, u32[]{:S(2)}) collective-permute-start(bf16[1,500,128]{2,1,0:T(8,128)(2,1)S(1)} %get-tuple-element.36), channel_id=1, source_target_pairs={{0,1},{1,2},{2,3},{3,4},{4,5},{5,6},{6,7},{7,8},{8,9},{9,10},{10,1... | collective-permute-start | bytes 384008 | tf_op jit(solution)/shard_map/ppermute | solution.py:501
  31.4 4.4 %shard_map.91.refs_5_ = f32[7,1000,128]{2,1,0:T(8,128)} custom-call(s32[57]{0:T(128)S(1)} %get-tuple-element.26.refs_0_, bf16[2,896,896]{2,1,0:T(8,128)(2,1)S(1)} %get-tuple-element.30.refs_1_, bf16[2,896,896]{2,1,0:T(8,128)(2,1)S(1)} %get-tuple-element.31.refs_2_, bf16[160,160]{1,0:T(8,128)(2,1)S(1)} %get-tuple-element.42.refs_3_, ...), custom_call_target="tpu_custom_call" | custom-call | flops 819200000 | bytes 10000000 | tf_op jit(solution)/shard_map/pallas_call | solution.py:614
  35.8 3.3 %collective-permute-done.6.refs_3_ = bf16[1,500,128]{2,1,0:T(8,128)(2,1)S(1)} collective-permute-done((bf16[1,500,128]{2,1,0:T(8,128)(2,1)S(1)}, bf16[1,500,128]{2,1,0:T(8,128)(2,1)S(1)}, u32[]{:S(2)}, u32[]{:S(2)}) %collective-permute-start.6) | collective-permute-done | bytes 128032 | tf_op jit(solution)/shard_map/ppermute | solution.py:501
  39.1 2.5 %collective-permute-done.2.refs_1_ = bf16[1,500,128]{2,1,0:T(8,128)(2,1)S(1)} collective-permute-done((bf16[1,500,128]{2,1,0:T(8,128)(2,1)S(1)}, bf16[1,500,128]{2,1,0:T(8,128)(2,1)S(1)}, u32[]{:S(2)}, u32[]{:S(2)}) %collective-permute-start.2) | collective-permute-done | bytes 128032 | tf_op jit(solution)/shard_map/ppermute | solution.py:501
  41.6 0.0 collective-permute-done.7.refs_4_
  41.6 1.0 %collective-permute-done.3.refs_2_ = bf16[2,500,128]{2,1,0:T(8,128)(2,1)S(1)} collective-permute-done((bf16[2,500,128]{2,1,0:T(8,128)(2,1)S(1)}, bf16[2,500,128]{2,1,0:T(8,128)(2,1)S(1)}, u32[]{:S(2)}, u32[]{:S(2)}) %collective-permute-start.3) | collective-permute-done | bytes 256032 | tf_op jit(solution)/shard_map/ppermute | solution.py:501
  42.6 1.4 %place.1 = f32[7,1000,128]{2,1,0:T(8,128)} custom-call(s32[57]{0:T(128)S(1)} %get-tuple-element.26.refs_0_, bf16[1,500,128]{2,1,0:T(8,128)(2,1)S(1)} %collective-permute-done.2.refs_1_, bf16[2,500,128]{2,1,0:T(8,128)(2,1)S(1)} %collective-permute-done.3.refs_2_, ...), custom_call_target="tpu_custom_call", output_to_operand_aliasing={{}: (5, {})} | custom-call | flops 1000000 | bytes 4000000 | tf_op jit(solution)/shard_map/place/pallas_call | solution.py:638
  (2 shorter events, 0.0 us)
Async XLA Ops:
  3.3 14.7 %collective-permute-start.4 = (bf16[500,128]{1,0:T(8,128)(2,1)S(1)}, bf16[500,128]{1,0:T(8,128)(2,1)S(1)}, u32[]{:S(2)}, u32[]{:S(2)}) collective-permute-start(bf16[500,128]{1,0:T(8,128)(2,1)S(1)} %get-tuple-element.38), channel_id=1, source_target_pairs={{0,1},{1,2},{2,3},{3,4},{4,5},{5,6},{6,7},{7,8},{8,9},{9,10},{10,1... | collective-permute-start | bytes 384008 | tf_op jit(solution)/shard_map/ppermute | solution.py:501
  6.4 11.6 %collective-permute-start.5 = (bf16[500,128]{1,0:T(8,128)(2,1)S(1)}, bf16[500,128]{1,0:T(8,128)(2,1)S(1)}, u32[]{:S(2)}, u32[]{:S(2)}) collective-permute-start(bf16[500,128]{1,0:T(8,128)(2,1)S(1)} %get-tuple-element.39), channel_id=1, source_target_pairs={{0,31},{1,0},{2,1},{3,2},{4,3},{5,4},{6,5},{7,6},{8,7},{9,8},{10,9... | collective-permute-start | bytes 384008 | tf_op jit(solution)/shard_map/ppermute | solution.py:501
  9.8 14.3 %collective-permute-start = (bf16[500,128]{1,0:T(8,128)(2,1)S(1)}, bf16[500,128]{1,0:T(8,128)(2,1)S(1)}, u32[]{:S(2)}, u32[]{:S(2)}) collective-permute-start(bf16[500,128]{1,0:T(8,128)(2,1)S(1)} %get-tuple-element.34), channel_id=1, source_target_pairs={{0,1},{1,2},{2,3},{3,4},{4,5},{5,6},{6,7},{7,8},{8,9},{9,10},{10,1... | collective-permute-start | bytes 384008 | tf_op jit(solution)/shard_map/ppermute | solution.py:501
  9.8 14.3 %collective-permute-start.1 = (bf16[500,128]{1,0:T(8,128)(2,1)S(1)}, bf16[500,128]{1,0:T(8,128)(2,1)S(1)}, u32[]{:S(2)}, u32[]{:S(2)}) collective-permute-start(bf16[500,128]{1,0:T(8,128)(2,1)S(1)} %get-tuple-element.35), channel_id=1, source_target_pairs={{0,31},{1,0},{2,1},{3,2},{4,3},{5,4},{6,5},{7,6},{8,7},{9,8},{10,9... | collective-permute-start | bytes 384008 | tf_op jit(solution)/shard_map/ppermute | solution.py:501
  22.6 19.0 %collective-permute-start.7 = (bf16[2,500,128]{2,1,0:T(8,128)(2,1)S(1)}, bf16[2,500,128]{2,1,0:T(8,128)(2,1)S(1)}, u32[]{:S(2)}, u32[]{:S(2)}) collective-permute-start(bf16[2,500,128]{2,1,0:T(8,128)(2,1)S(1)} %get-tuple-element.41), channel_id=1, source_target_pairs={{0,31},{1,0},{2,1},{3,2},{4,3},{5,4},{6,5},{7,6},{8,7},{9,8},{10,9... | collective-permute-start | bytes 768008 | tf_op jit(solution)/shard_map/ppermute | solution.py:501
  28.8 13.8 %collective-permute-start.3 = (bf16[2,500,128]{2,1,0:T(8,128)(2,1)S(1)}, bf16[2,500,128]{2,1,0:T(8,128)(2,1)S(1)}, u32[]{:S(2)}, u32[]{:S(2)}) collective-permute-start(bf16[2,500,128]{2,1,0:T(8,128)(2,1)S(1)} %get-tuple-element.37), channel_id=1, source_target_pairs={{0,31},{1,0},{2,1},{3,2},{4,3},{5,4},{6,5},{7,6},{8,7},{9,8},{10,9... | collective-permute-start | bytes 768008 | tf_op jit(solution)/shard_map/ppermute | solution.py:501
  29.7 9.4 %collective-permute-start.6 = (bf16[1,500,128]{2,1,0:T(8,128)(2,1)S(1)}, bf16[1,500,128]{2,1,0:T(8,128)(2,1)S(1)}, u32[]{:S(2)}, u32[]{:S(2)}) collective-permute-start(bf16[1,500,128]{2,1,0:T(8,128)(2,1)S(1)} %get-tuple-element.40), channel_id=1, source_target_pairs={{0,1},{1,2},{2,3},{3,4},{4,5},{5,6},{6,7},{7,8},{8,9},{9,10},{10,1... | collective-permute-start | bytes 384008 | tf_op jit(solution)/shard_map/ppermute | solution.py:501
  30.8 10.8 %collective-permute-start.2 = (bf16[1,500,128]{2,1,0:T(8,128)(2,1)S(1)}, bf16[1,500,128]{2,1,0:T(8,128)(2,1)S(1)}, u32[]{:S(2)}, u32[]{:S(2)}) collective-permute-start(bf16[1,500,128]{2,1,0:T(8,128)(2,1)S(1)} %get-tuple-element.36), channel_id=1, source_target_pairs={{0,1},{1,2},{2,3},{3,4},{4,5},{5,6},{6,7},{7,8},{8,9},{9,10},{10,1... | collective-permute-start | bytes 384008 | tf_op jit(solution)/shard_map/ppermute | solution.py:501

commit v14 on v13

--- a/solution.py
+++ b/solution.py
@@ -250,6 +250,14 @@
     return 2 * lax.axis_index(AXES[-1]) < lax.axis_size(AXES[-1])
 
 
+def at_start():
+    return lax.axis_index(AXES[-1]) == 0
+
+
+def at_end():
+    return lax.axis_index(AXES[-1]) == lax.axis_size(AXES[-1]) - 1
+
+
 def slabs_kernel(spin, chosen, orb_ref, *refs):
     pad_ref, flat_ref = refs[-2:]
     boxes = orb_ref.shape[1]
@@ -267,10 +275,10 @@
             reverse_box(pad_ref, box)
 
 
-def modes_kernel(early, fac_ref, *refs):
+def modes_kernel(chosen, fac_ref, *refs):
     to_ref, from_ref = refs[-2:]
 
-    @pl.when(low_half() if early else jnp.logical_not(low_half()))
+    @pl.when(chosen())
     def _():
         front = lax.broadcasted_iota(jnp.int32, (EDGE, 1), 0) < HALF
 
@@ -538,9 +546,10 @@
 
     folded = jax.ShapeDtypeStruct((2, FWIDE, FWIDE), BF)
 
-    def build_modes(early, *before):
+    def build_modes(place, *before):
+        chosen = (at_start, lambda: low_half() & jnp.logical_not(at_start()), lambda: jnp.logical_not(low_half()))[place]
         return pl.pallas_call(
-            lambda *refs: modes_kernel(early, *refs),
+            lambda *refs: modes_kernel(chosen, *refs),
             out_shape=[folded] * 2,
             in_specs=whole(1 + len(before)),
             out_specs=whole(2),
@@ -549,7 +558,7 @@
             cost_estimate=cost(4_000_000, 4_000_000),
         )(factors, *before)
 
-    modes = build_modes(True)
+    modes = build_modes(0)
     moving = AHEAD + BACK
     slabs = jax.ShapeDtypeStruct((2, boxes + 2, TILES, ROWS, LANES), F32)
     diags = [np.kron(np.eye(cubes, dtype=np.float32), sine).astype(jnp.bfloat16)
@@ -571,7 +580,7 @@
         *map(in_place, (dest, partners_t, anchors_t, *handed)), held)
     prev_high = from_behind(ahead, 1)
     next_high = from_behind(back, -1)
-    to_modes, from_modes = build_modes(False, *modes)
+    to_modes, from_modes = build_modes(2, *build_modes(1, *modes))
 
     def build_slabs(spin, *before, chosen=None):
         return pl.pallas_call(
@@ -585,7 +594,7 @@
             cost_estimate=cost(2_000_000, 4_000_000),
         )(held, *before)
 
-    pads = [build_slabs(0), build_slabs(1, build_slabs(1, chosen=low_half), chosen=lambda: jnp.logical_not(low_half()))]
+    pads = [build_slabs(0, build_slabs(0, chosen=at_end), chosen=lambda: jnp.logical_not(at_end())), build_slabs(1, build_slabs(1, chosen=at_start), chosen=lambda: jnp.logical_not(at_start()))]
     for spin, halo in enumerate(((prev_low, next_low), (prev_high, next_high))):
         pads[spin] = pl.pallas_call(
             fill_kernel,

time: 44.3 us -> 44.3 us (level)
    pallas_call x3 -> x4, Pallas kernels: 1.89 us -> 1.91 us  [build_slabs(): pl.pallas_call(lambda *refs: slabs_kernel(spin, chosen, *refs), out_shape...]
    pallas_call x2 -> x3, Pallas kernels: 0.87 us -> 0.89 us  [build_modes(): pl.pallas_call(lambda *refs: modes_kernel(chosen, *refs), out_shape=[fold...]
where the time goes in v14:
time: 44.3 us; the launch traced here: 44.1 us
  Pallas kernels  21.1 us (48%)
  starting transfers between devices  16 us (36%)
  waiting for transfers between devices  6.76 us (15%)
    ppermute x8, starting transfers between devices, from_behind(): lax.ppermute(value, AXES, [(source, (source + steps) % count) for source...  16 us
    pallas_call x3, Pallas kernels, solve(): pl.pallas_call(lambda *refs: pair_kernel(start, held, spins, final, *refs...  13.1 us
    ppermute x8, waiting for transfers between devices, from_behind(): lax.ppermute(value, AXES, [(source, (source + steps) % count) for source...  6.76 us
    pallas_call x4, Pallas kernels, build_slabs(): pl.pallas_call(lambda *refs: slabs_kernel(spin, chosen, *refs), out_shape...  1.91 us
    pallas_call x1, Pallas kernels, shards(): second(*map(in_place, (dest, partners_t, anchors_t, *handed)), held)  1.74 us
    pallas_call x1, Pallas kernels, shards(): pl.pallas_call(window_kernel, out_shape=[box] * 2 + [jax.ShapeDtypeStruct...  1.51 us
    pallas_call x1, Pallas kernels, shards(): pl.pallas_call(lambda *refs: place_kernel(boxes, *refs), out_shape=shape,...  1.4 us
    pallas_call x3, Pallas kernels, build_modes(): pl.pallas_call(lambda *refs: modes_kernel(chosen, *refs), out_shape=[fold...  0.89 us
  transfers between devices with their start and end apart: 8, of which 3 were waited for; matrix products, arithmetic and copies ran while one was open for 0% of the time, Pallas kernels for 37%

profile of v14, /device:TPU:0, one launch (start us, length us, event | category | flops | bytes accessed | tf_op | source)
XLA Modules:
  0.0 44.1 jit_solution(14710224494962971759)
XLA Ops:
  0.0 1.5 %window.1 = (bf16[500,128]{1,0:T(8,128)(2,1)S(1)}, bf16[500,128]{1,0:T(8,128)(2,1)S(1)}, bf16[2,4,64000]{2,1,0:T(4,128)(2,1)S(1)}, f32[6,40,896]{2,1,0:T(8,128)S(1)}) custom-call(s32[2,128]{1,0:T(2,128)} %bitcast.9, bf16[2,4,64000]{2,1,0:T(4,128)(2,1)} %orb_hbm.1, f32[6,40,896]{2,1,0:T(8,128)} %constant.8.clone.fac_hbm), custom_call_target="tpu_custom_call" | custom-call | tf_op jit(solution)/shard_map/window/pallas_call | solution.py:535
  1.5 1.7 %second.1 = (bf16[500,128]{1,0:T(8,128)(2,1)S(1)}, bf16[500,128]{1,0:T(8,128)(2,1)S(1)}, s32[57]{0:T(128)S(1)}, f32[40,1792]{1,0:T(8,128)S(1)}, bf16[240,240]{1,...) custom-call(s32[128]{0:T(128)} %dest_hbm.1, s32[2,128]{1,0:T(2,128)} %bitcast.10, s32[3,128]{1,0:T(4,128)} %bitcast.11, ...), custom_call_target="tpu_custom_call" | custom-call | flops 1000000 | bytes 2000000 | tf_op jit(solution)/shard_map/second/pallas_call | solution.py:579
  3.3 3.1 %collective-permute-start.4 = (bf16[500,128]{1,0:T(8,128)(2,1)S(1)}, bf16[500,128]{1,0:T(8,128)(2,1)S(1)}, u32[]{:S(2)}, u32[]{:S(2)}) collective-permute-start(bf16[500,128]{1,0:T(8,128)(2,1)S(1)} %get-tuple-element.42), channel_id=1, source_target_pairs={{0,1},{1,2},{2,3},{3,4},{4,5},{5,6},{6,7},{7,8},{8,9},{9,10},{10,1... | collective-permute-start | bytes 384008 | tf_op jit(solution)/shard_map/ppermute | solution.py:509
  6.4 3.4 %collective-permute-start.5 = (bf16[500,128]{1,0:T(8,128)(2,1)S(1)}, bf16[500,128]{1,0:T(8,128)(2,1)S(1)}, u32[]{:S(2)}, u32[]{:S(2)}) collective-permute-start(bf16[500,128]{1,0:T(8,128)(2,1)S(1)} %get-tuple-element.43), channel_id=1, source_target_pairs={{0,31},{1,0},{2,1},{3,2},{4,3},{5,4},{6,5},{7,6},{8,7},{9,8},{10,9... | collective-permute-start | bytes 384008 | tf_op jit(solution)/shard_map/ppermute | solution.py:509
  9.8 0.0 collective-permute-start
  9.8 5.3 %collective-permute-start.1 = (bf16[500,128]{1,0:T(8,128)(2,1)S(1)}, bf16[500,128]{1,0:T(8,128)(2,1)S(1)}, u32[]{:S(2)}, u32[]{:S(2)}) collective-permute-start(bf16[500,128]{1,0:T(8,128)(2,1)S(1)} %get-tuple-element.39), channel_id=1, source_target_pairs={{0,31},{1,0},{2,1},{3,2},{4,3},{5,4},{6,5},{7,6},{8,7},{9,8},{10,9... | collective-permute-start | bytes 384008 | tf_op jit(solution)/shard_map/ppermute | solution.py:509
  15.1 0.9 %shard_map.89.refs_1_ = f32[2,6,13,88,128]{4,3,2,1,0:T(8,128)S(1)} custom-call(bf16[2,4,64000]{2,1,0:T(4,128)(2,1)S(1)} %get-tuple-element.27.orb_ref.refs_0_), custom_call_target="tpu_custom_call" | custom-call | flops 2000000 | bytes 4000000 | tf_op jit(solution)/shard_map/pallas_call | solution.py:586
  16.1 1.0 %shard_map.86.old_ref = f32[2,6,13,88,128]{4,3,2,1,0:T(8,128)S(1)} custom-call(bf16[2,4,64000]{2,1,0:T(4,128)(2,1)S(1)} %get-tuple-element.27.orb_ref.refs_0_, f32[2,6,13,88,128]{4,3,2,1,0:T(8,128)S(1)} %shard_map.85.refs_1_), custom_call_target="tpu_custom_call", output_to_operand_aliasing={{}: (1, {})} | custom-call | flops 2000000 | bytes 4000000 | tf_op jit(solution)/shard_map/pallas_call | solution.py:586
  17.1 0.9 %shard_map.82 = (bf16[2,896,896]{2,1,0:T(8,128)(2,1)S(1)}, bf16[2,896,896]{2,1,0:T(8,128)(2,1)S(1)}) custom-call(f32[6,40,896]{2,1,0:T(8,128)S(1)} %get-tuple-element.29.refs_0_), custom_call_target="tpu_custom_call" | custom-call | flops 4000000 | bytes 4000000 | tf_op jit(solution)/shard_map/pallas_call | solution.py:551
  18.0 0.0 collective-permute-done.4.prev_ref
  18.0 0.0 collective-permute-done.5.next_ref
  18.0 0.3 shard_map.91.refs_5_.refs_6_
  18.3 4.4 %shard_map.92 = (f32[3,500,128]{2,1,0:T(8,128)S(1)}, bf16[1,500,128]{2,1,0:T(8,128)(2,1)S(1)}, bf16[2,500,128]{2,1,0:T(8,128)(2,1)S(1)}) custom-call(s32[57]{0:T(128)S(1)} %get-tuple-element.28.refs_0_, bf16[2,896,896]{2,1,0:T(8,128)(2,1)S(1)} %get-tuple-element.34.refs_1_, bf16[2,896,896]{2,1,0:T(8,128)(2,1)S(1)} %get-tuple-element.35.refs_2_, ...), custom_call_target="tpu_custom_call" | custom-call | flops 1228800000 | bytes 10000000 | tf_op jit(solution)/shard_map/pallas_call | solution.py:623
  22.6 1.5 %collective-permute-start.7 = (bf16[2,500,128]{2,1,0:T(8,128)(2,1)S(1)}, bf16[2,500,128]{2,1,0:T(8,128)(2,1)S(1)}, u32[]{:S(2)}, u32[]{:S(2)}) collective-permute-start(bf16[2,500,128]{2,1,0:T(8,128)(2,1)S(1)} %get-tuple-element.45), channel_id=1, source_target_pairs={{0,31},{1,0},{2,1},{3,2},{4,3},{5,4},{6,5},{7,6},{8,7},{9,8},{10,9... | collective-permute-start | bytes 768008 | tf_op jit(solution)/shard_map/ppermute | solution.py:509
  24.1 0.0 collective-permute-done.prev_ref
  24.1 0.0 collective-permute-done.1.next_ref
  24.1 0.3 shard_map.87.refs_5_
  24.4 4.3 %shard_map.88 = (f32[3,500,128]{2,1,0:T(8,128)S(1)}, bf16[1,500,128]{2,1,0:T(8,128)(2,1)S(1)}, bf16[2,500,128]{2,1,0:T(8,128)(2,1)S(1)}) custom-call(s32[57]{0:T(128)S(1)} %get-tuple-element.28.refs_0_, bf16[2,896,896]{2,1,0:T(8,128)(2,1)S(1)} %get-tuple-element.34.refs_1_, bf16[2,896,896]{2,1,0:T(8,128)(2,1)S(1)} %get-tuple-element.35.refs_2_, ...), custom_call_target="tpu_custom_call" | custom-call | flops 1228800000 | bytes 10000000 | tf_op jit(solution)/shard_map/pallas_call | solution.py:623
  28.8 0.9 %collective-permute-start.3 = (bf16[2,500,128]{2,1,0:T(8,128)(2,1)S(1)}, bf16[2,500,128]{2,1,0:T(8,128)(2,1)S(1)}, u32[]{:S(2)}, u32[]{:S(2)}) collective-permute-start(bf16[2,500,128]{2,1,0:T(8,128)(2,1)S(1)} %get-tuple-element.41), channel_id=1, source_target_pairs={{0,31},{1,0},{2,1},{3,2},{4,3},{5,4},{6,5},{7,6},{8,7},{9,8},{10,9... | collective-permute-start | bytes 768008 | tf_op jit(solution)/shard_map/ppermute | solution.py:509
  29.7 1.2 %collective-permute-start.6 = (bf16[1,500,128]{2,1,0:T(8,128)(2,1)S(1)}, bf16[1,500,128]{2,1,0:T(8,128)(2,1)S(1)}, u32[]{:S(2)}, u32[]{:S(2)}) collective-permute-start(bf16[1,500,128]{2,1,0:T(8,128)(2,1)S(1)} %get-tuple-element.44), channel_id=1, source_target_pairs={{0,1},{1,2},{2,3},{3,4},{4,5},{5,6},{6,7},{7,8},{8,9},{9,10},{10,1... | collective-permute-start | bytes 384008 | tf_op jit(solution)/shard_map/ppermute | solution.py:509
  30.8 0.6 %collective-permute-start.2 = (bf16[1,500,128]{2,1,0:T(8,128)(2,1)S(1)}, bf16[1,500,128]{2,1,0:T(8,128)(2,1)S(1)}, u32[]{:S(2)}, u32[]{:S(2)}) collective-permute-start(bf16[1,500,128]{2,1,0:T(8,128)(2,1)S(1)} %get-tuple-element.40), channel_id=1, source_target_pairs={{0,1},{1,2},{2,3},{3,4},{4,5},{5,6},{6,7},{7,8},{8,9},{9,10},{10,1... | collective-permute-start | bytes 384008 | tf_op jit(solution)/shard_map/ppermute | solution.py:509
  31.4 4.4 %shard_map.93.refs_5_ = f32[7,1000,128]{2,1,0:T(8,128)} custom-call(s32[57]{0:T(128)S(1)} %get-tuple-element.28.refs_0_, bf16[2,896,896]{2,1,0:T(8,128)(2,1)S(1)} %get-tuple-element.34.refs_1_, bf16[2,896,896]{2,1,0:T(8,128)(2,1)S(1)} %get-tuple-element.35.refs_2_, bf16[160,160]{1,0:T(8,128)(2,1)S(1)} %get-tuple-element.46.refs_3_, ...), custom_call_target="tpu_custom_call" | custom-call | flops 819200000 | bytes 10000000 | tf_op jit(solution)/shard_map/pallas_call | solution.py:623
  35.8 3.2 %collective-permute-done.6.refs_3_ = bf16[1,500,128]{2,1,0:T(8,128)(2,1)S(1)} collective-permute-done((bf16[1,500,128]{2,1,0:T(8,128)(2,1)S(1)}, bf16[1,500,128]{2,1,0:T(8,128)(2,1)S(1)}, u32[]{:S(2)}, u32[]{:S(2)}) %collective-permute-start.6) | collective-permute-done | bytes 128032 | tf_op jit(solution)/shard_map/ppermute | solution.py:509
  39.1 2.5 %collective-permute-done.2.refs_1_ = bf16[1,500,128]{2,1,0:T(8,128)(2,1)S(1)} collective-permute-done((bf16[1,500,128]{2,1,0:T(8,128)(2,1)S(1)}, bf16[1,500,128]{2,1,0:T(8,128)(2,1)S(1)}, u32[]{:S(2)}, u32[]{:S(2)}) %collective-permute-start.2) | collective-permute-done | bytes 128032 | tf_op jit(solution)/shard_map/ppermute | solution.py:509
  41.6 0.0 collective-permute-done.7.refs_4_
  41.6 1.0 %collective-permute-done.3.refs_2_ = bf16[2,500,128]{2,1,0:T(8,128)(2,1)S(1)} collective-permute-done((bf16[2,500,128]{2,1,0:T(8,128)(2,1)S(1)}, bf16[2,500,128]{2,1,0:T(8,128)(2,1)S(1)}, u32[]{:S(2)}, u32[]{:S(2)}) %collective-permute-start.3) | collective-permute-done | bytes 256032 | tf_op jit(solution)/shard_map/ppermute | solution.py:509
  42.6 1.4 %place.1 = f32[7,1000,128]{2,1,0:T(8,128)} custom-call(s32[57]{0:T(128)S(1)} %get-tuple-element.28.refs_0_, bf16[1,500,128]{2,1,0:T(8,128)(2,1)S(1)} %collective-permute-done.2.refs_1_, bf16[2,500,128]{2,1,0:T(8,128)(2,1)S(1)} %collective-permute-done.3.refs_2_, ...), custom_call_target="tpu_custom_call", output_to_operand_aliasing={{}: (5, {})} | custom-call | flops 1000000 | bytes 4000000 | tf_op jit(solution)/shard_map/place/pallas_call | solution.py:647
  (4 shorter events, 0.1 us)
Async XLA Ops:
  3.3 14.7 %collective-permute-start.4 = (bf16[500,128]{1,0:T(8,128)(2,1)S(1)}, bf16[500,128]{1,0:T(8,128)(2,1)S(1)}, u32[]{:S(2)}, u32[]{:S(2)}) collective-permute-start(bf16[500,128]{1,0:T(8,128)(2,1)S(1)} %get-tuple-element.42), channel_id=1, source_target_pairs={{0,1},{1,2},{2,3},{3,4},{4,5},{5,6},{6,7},{7,8},{8,9},{9,10},{10,1... | collective-permute-start | bytes 384008 | tf_op jit(solution)/shard_map/ppermute | solution.py:509
  6.4 11.6 %collective-permute-start.5 = (bf16[500,128]{1,0:T(8,128)(2,1)S(1)}, bf16[500,128]{1,0:T(8,128)(2,1)S(1)}, u32[]{:S(2)}, u32[]{:S(2)}) collective-permute-start(bf16[500,128]{1,0:T(8,128)(2,1)S(1)} %get-tuple-element.43), channel_id=1, source_target_pairs={{0,31},{1,0},{2,1},{3,2},{4,3},{5,4},{6,5},{7,6},{8,7},{9,8},{10,9... | collective-permute-start | bytes 384008 | tf_op jit(solution)/shard_map/ppermute | solution.py:509
  9.8 14.3 %collective-permute-start = (bf16[500,128]{1,0:T(8,128)(2,1)S(1)}, bf16[500,128]{1,0:T(8,128)(2,1)S(1)}, u32[]{:S(2)}, u32[]{:S(2)}) collective-permute-start(bf16[500,128]{1,0:T(8,128)(2,1)S(1)} %get-tuple-element.38), channel_id=1, source_target_pairs={{0,1},{1,2},{2,3},{3,4},{4,5},{5,6},{6,7},{7,8},{8,9},{9,10},{10,1... | collective-permute-start | bytes 384008 | tf_op jit(solution)/shard_map/ppermute | solution.py:509
  9.8 14.3 %collective-permute-start.1 = (bf16[500,128]{1,0:T(8,128)(2,1)S(1)}, bf16[500,128]{1,0:T(8,128)(2,1)S(1)}, u32[]{:S(2)}, u32[]{:S(2)}) collective-permute-start(bf16[500,128]{1,0:T(8,128)(2,1)S(1)} %get-tuple-element.39), channel_id=1, source_target_pairs={{0,31},{1,0},{2,1},{3,2},{4,3},{5,4},{6,5},{7,6},{8,7},{9,8},{10,9... | collective-permute-start | bytes 384008 | tf_op jit(solution)/shard_map/ppermute | solution.py:509
  22.6 19.0 %collective-permute-start.7 = (bf16[2,500,128]{2,1,0:T(8,128)(2,1)S(1)}, bf16[2,500,128]{2,1,0:T(8,128)(2,1)S(1)}, u32[]{:S(2)}, u32[]{:S(2)}) collective-permute-start(bf16[2,500,128]{2,1,0:T(8,128)(2,1)S(1)} %get-tuple-element.45), channel_id=1, source_target_pairs={{0,31},{1,0},{2,1},{3,2},{4,3},{5,4},{6,5},{7,6},{8,7},{9,8},{10,9... | collective-permute-start | bytes 768008 | tf_op jit(solution)/shard_map/ppermute | solution.py:509
  28.8 13.8 %collective-permute-start.3 = (bf16[2,500,128]{2,1,0:T(8,128)(2,1)S(1)}, bf16[2,500,128]{2,1,0:T(8,128)(2,1)S(1)}, u32[]{:S(2)}, u32[]{:S(2)}) collective-permute-start(bf16[2,500,128]{2,1,0:T(8,128)(2,1)S(1)} %get-tuple-element.41), channel_id=1, source_target_pairs={{0,31},{1,0},{2,1},{3,2},{4,3},{5,4},{6,5},{7,6},{8,7},{9,8},{10,9... | collective-permute-start | bytes 768008 | tf_op jit(solution)/shard_map/ppermute | solution.py:509
  29.7 9.4 %collective-permute-start.6 = (bf16[1,500,128]{2,1,0:T(8,128)(2,1)S(1)}, bf16[1,500,128]{2,1,0:T(8,128)(2,1)S(1)}, u32[]{:S(2)}, u32[]{:S(2)}) collective-permute-start(bf16[1,500,128]{2,1,0:T(8,128)(2,1)S(1)} %get-tuple-element.44), channel_id=1, source_target_pairs={{0,1},{1,2},{2,3},{3,4},{4,5},{5,6},{6,7},{7,8},{8,9},{9,10},{10,1... | collective-permute-start | bytes 384008 | tf_op jit(solution)/shard_map/ppermute | solution.py:509
  30.8 10.8 %collective-permute-start.2 = (bf16[1,500,128]{2,1,0:T(8,128)(2,1)S(1)}, bf16[1,500,128]{2,1,0:T(8,128)(2,1)S(1)}, u32[]{:S(2)}, u32[]{:S(2)}) collective-permute-start(bf16[1,500,128]{2,1,0:T(8,128)(2,1)S(1)} %get-tuple-element.40), channel_id=1, source_target_pairs={{0,1},{1,2},{2,3},{3,4},{4,5},{5,6},{6,7},{7,8},{8,9},{9,10},{10,1... | collective-permute-start | bytes 384008 | tf_op jit(solution)/shard_map/ppermute | solution.py:509
